TPU v7x, 32 devices: a whole 2x2x4 slice. The times are simulated.
32 devices in a mesh: shard: 8 (over y, x, core), seq: 4 (over z).
Axes of the slice: x: 2, y: 2, z: 4, core: 2. Of those that a mesh axis runs over, the one named last changes fastest.
Arguments:
- tokens: bfloat16 [9216, 1536], P(('shard', 'seq')), may hold values from -6 to 6
- routes: int32 [9216, 8], P(('shard', 'seq')), may hold values from 0 to 15, all different within a row; in each aligned block of 288 rows (0 to 287, 288 to 575, ...) at most 216 rows name the same one
- w_query: bfloat16 [1536, 1536], P('shard', 'seq'), may hold values from -0.15625 to 0.15625
- key_projection: bfloat16 [1536, 512], P('shard', 'seq'), may hold values from -0.15625 to 0.15625
- value_projection: bfloat16 [1536, 512], P('shard', 'seq'), may hold values from -0.15625 to 0.15625
- w_out: bfloat16 [1536, 1536], P('seq', 'shard'), may hold values from -2.5 to 2.5
- gain_attn: bfloat16 [1536], P(('shard', 'seq')), may hold values from 0.5 to 1.5
- gain_ffn: bfloat16 [1536], P(('shard', 'seq')), may hold values from 0.5 to 1.5
- w_router: bfloat16 [1536, 16], P(('shard', 'seq')), may hold values from -0.078125 to 0.078125
- w_gate: bfloat16 [16, 1536, 512], P('shard'), may hold values from -0.15625 to 0.15625
- w_up: bfloat16 [16, 1536, 512], P('shard'), may hold values from -0.15625 to 0.15625
- w_down: bfloat16 [16, 512, 1536], P('shard'), may hold values from -0.5 to 0.5
- out_grad: bfloat16 [9216, 1536], P(('shard', 'seq')), may hold values from -6 to 6
Outputs:
- output: bfloat16 [9216, 1536], P(('shard', 'seq'))
- grad_tokens: float32 [9216, 1536], P(('shard', 'seq'))
- grad_query: float32 [1536, 1536], P('shard', 'seq')
- grad_key: float32 [1536, 512], P('shard', 'seq')
- grad_value: float32 [1536, 512], P('shard', 'seq')
- grad_out: float32 [1536, 1536], P('seq', 'shard')
- grad_gain_attn: float32 [1536], P(('shard', 'seq'))
- grad_gain_ffn: float32 [1536], P(('shard', 'seq'))
- grad_router: float32 [1536, 16], P(('shard', 'seq'))
- grad_gate: float32 [16, 1536, 512], P('shard', 'seq')
- grad_up: float32 [16, 1536, 512], P('shard', 'seq')
- grad_down: float32 [16, 512, 1536], P('shard', None, 'seq')
Inputs may be any that keep to these rules, and one draw needn't show every extreme that they name: `routes`: each row names 8 different experts; among the rows of one device no expert is named by more than 216 rows, and in every draw some expert is named by exactly 216 rows of some device.
All inputs are finite; a program needn't handle non-finite values.
Results may differ from a plain program's by a relative error of at most 0.023.
Values may be sent and summed in bfloat16 or wider, within the bound.
No kernel may reach another device: no remote copies, remote signals or barrier semaphores. Data moves between devices by JAX's collectives and lax.ppermute only.
A program may use at most 320 MiB of HBM per device.

v0:
```python
import jax
import jax.numpy as jnp
from jax import lax
from jax.sharding import PartitionSpec as P

HEAD_DIMENSION = 64
CONT_LEN = 512
PROMPT_BLK = 128


norm_eps = 1e-05
negative = -1e30
rope_base = 10000.0
highest = lax.Precision.HIGHEST


def rms_norm(values, scaling):
    factor = lax.rsqrt(jnp.mean(values * values, axis=-1, keepdims=True) + norm_eps)
    return values * factor * scaling


def swiglu(gate_pre, up_pre):
    return jax.nn.silu(gate_pre) * up_pre


def softmax_last(values):
    return jax.nn.softmax(values, axis=-1)


def rotary_tables(places, head_size):
    half_size = head_size // 2
    frequency = jnp.exp(
        jnp.arange(half_size, dtype=jnp.float32) * (-2.0 * jnp.log(rope_base) / head_size)
    )
    angles = places.astype(jnp.float32)[:, None] * frequency[None, :]
    return (jnp.cos(angles)[:, None, :], jnp.sin(angles)[:, None, :])


def rotate(values, cosine, sine, head_size):
    total_row_count = values.shape[0]
    by_head = values.reshape(total_row_count, -1, head_size)
    half_size = head_size // 2
    first_half = by_head[..., :half_size]
    second_half = by_head[..., half_size:]
    turned = jnp.concatenate(
        [first_half * cosine - second_half * sine, second_half * cosine + first_half * sine],
        axis=-1,
    )
    return turned.reshape(total_row_count, -1)


def place_of(within, block_index, prompt_len):
    return jnp.where(
        within < PROMPT_BLK,
        block_index * PROMPT_BLK + within,
        prompt_len + (within - PROMPT_BLK) % CONT_LEN,
    )


def times_transposed(left_side, right_side, precision=None):
    return lax.dot_general(
        left_side,
        right_side,
        (((1,), (1,)), ((), ())),
        precision=precision,
        preferred_element_type=jnp.float32,
    )


def transposed_times(left_side, right_side, precision=None):
    return lax.dot_general(
        left_side,
        right_side,
        (((0,), (0,)), ((), ())),
        precision=precision,
        preferred_element_type=jnp.float32,
    )


def head_scores(query_matrix, key_matrix_rows, allowed, head_size):
    total_row_count = query_matrix.shape[0]
    kv_heads = key_matrix_rows.shape[1] // head_size
    grouped_heads = query_matrix.reshape(total_row_count, kv_heads, -1, head_size)
    key_head_split = key_matrix_rows.reshape(key_matrix_rows.shape[0], kv_heads, head_size)
    scores = jnp.einsum(
        "rhgd,khd->hgrk", grouped_heads, key_head_split, preferred_element_type=jnp.float32
    ) * head_size ** (-0.5)
    return jnp.where(allowed, scores, negative)


def attend_forward(query_matrix, key_matrix_rows, value_matrix_rows, allowed, head_size):
    scores = head_scores(query_matrix, key_matrix_rows, allowed, head_size)
    row_max = jnp.max(scores, axis=-1, keepdims=True)
    weights = jnp.exp(scores - row_max)
    row_total = jnp.sum(weights, axis=-1, keepdims=True)
    probs_low = (weights / row_total).astype(jnp.bfloat16)
    kv_heads = key_matrix_rows.shape[1] // head_size
    value_heads_split = value_matrix_rows.reshape(value_matrix_rows.shape[0], kv_heads, head_size)
    mixed_out = jnp.einsum(
        "hgrk,khd->rhgd", probs_low, value_heads_split, preferred_element_type=jnp.float32
    )
    return (mixed_out.reshape(query_matrix.shape[0], -1), row_max + jnp.log(row_total))


def attend_backward(
    query_matrix, key_matrix_rows, value_matrix_rows, allowed, log_total, mixed_grad, head_size
):
    total_row_count = query_matrix.shape[0]
    kv_heads = key_matrix_rows.shape[1] // head_size
    scores = head_scores(query_matrix, key_matrix_rows, allowed, head_size)
    probs = jnp.exp(scores - log_total)
    value_heads_split = value_matrix_rows.reshape(-1, kv_heads, head_size)
    key_head_split = key_matrix_rows.reshape(-1, kv_heads, head_size)
    grouped_heads = query_matrix.reshape(total_row_count, kv_heads, -1, head_size)
    grad_grouped = mixed_grad.reshape(total_row_count, kv_heads, -1, head_size)
    prob_grad = jnp.einsum(
        "rhgd,khd->hgrk", grad_grouped, value_heads_split, preferred_element_type=jnp.float32
    )
    inner_sum = jnp.sum(probs * prob_grad, axis=-1, keepdims=True)
    score_grad = (probs * (prob_grad - inner_sum)).astype(jnp.bfloat16)
    score_scale = head_size ** (-0.5)
    query_grad = (
        jnp.einsum("hgrk,khd->rhgd", score_grad, key_head_split, preferred_element_type=jnp.float32)
        * score_scale
    )
    key_grad = (
        jnp.einsum("hgrk,rhgd->khd", score_grad, grouped_heads, preferred_element_type=jnp.float32)
        * score_scale
    )
    value_grad = jnp.einsum(
        "hgrk,rhgd->khd",
        probs.astype(jnp.bfloat16),
        grad_grouped,
        preferred_element_type=jnp.float32,
    )
    return (
        query_grad.reshape(total_row_count, -1),
        key_grad.reshape(key_matrix_rows.shape[0], -1),
        value_grad.reshape(value_matrix_rows.shape[0], -1),
    )


def on_device(
    tokens,
    routes,
    w_query,
    key_projection,
    value_projection,
    w_out,
    gain_attn,
    gain_ffn,
    w_router,
    w_gate,
    w_up,
    w_down,
    out_grad,
):
    shard_count = lax.axis_size("shard")
    seq_count = lax.axis_size("seq")
    shard_index = lax.axis_index("shard")
    seq_index = lax.axis_index("seq")
    tok_count = tokens.shape[0]
    model_width = tokens.shape[1]
    top_count = routes.shape[1]
    block_len = tok_count * seq_count
    prompt_len = PROMPT_BLK * shard_count
    query_weight, key_weight, value_weight, out_weight, first_gain, second_gain, router_weight = (
        lax.all_gather(w_query, "seq", axis=1, tiled=True),
        lax.all_gather(key_projection, "seq", axis=1, tiled=True),
        lax.all_gather(value_projection, "seq", axis=1, tiled=True),
        lax.all_gather(w_out, "seq", axis=0, tiled=True),
        lax.all_gather(gain_attn, "seq", axis=0, tiled=True),
        lax.all_gather(gain_ffn, "seq", axis=0, tiled=True),
        lax.all_gather(w_router, "seq", axis=0, tiled=True),
    )
    query_weight, key_weight, value_weight, out_weight, first_gain, second_gain, router_weight = (
        lax.all_gather(query_weight, "shard", axis=0, tiled=True),
        lax.all_gather(key_weight, "shard", axis=0, tiled=True),
        lax.all_gather(value_weight, "shard", axis=0, tiled=True),
        lax.all_gather(out_weight, "shard", axis=1, tiled=True),
        lax.all_gather(first_gain, "shard", axis=0, tiled=True),
        lax.all_gather(second_gain, "shard", axis=0, tiled=True),
        lax.all_gather(router_weight, "shard", axis=0, tiled=True),
    )
    inputs = tokens.astype(jnp.float32)
    upstream = out_grad.astype(jnp.float32)
    own_rows = seq_index * tok_count + jnp.arange(tok_count, dtype=jnp.int32)
    token_cos, token_sin = rotary_tables(
        place_of(own_rows, shard_index, prompt_len), HEAD_DIMENSION
    )
    normed, first_back = jax.vjp(rms_norm, inputs, first_gain.astype(jnp.float32))
    normed_low = normed.astype(jnp.bfloat16)
    query_send = rotate(
        jnp.dot(normed_low, query_weight, preferred_element_type=jnp.float32),
        token_cos,
        token_sin,
        HEAD_DIMENSION,
    ).astype(jnp.bfloat16)
    key_send = rotate(
        jnp.dot(normed_low, key_weight, preferred_element_type=jnp.float32),
        token_cos,
        token_sin,
        HEAD_DIMENSION,
    ).astype(jnp.bfloat16)
    value_send = jnp.dot(normed_low, value_weight, preferred_element_type=jnp.float32).astype(
        jnp.bfloat16
    )
    query_heads, key_heads, value_heads = (
        lax.all_to_all(query_send, "seq", split_axis=1, concat_axis=0, tiled=True),
        lax.all_to_all(key_send, "seq", split_axis=1, concat_axis=0, tiled=True),
        lax.all_to_all(value_send, "seq", split_axis=1, concat_axis=0, tiled=True),
    )
    prompt_keys, prompt_values = (
        lax.all_gather(key_heads[:PROMPT_BLK], "shard", axis=0, tiled=True),
        lax.all_gather(value_heads[:PROMPT_BLK], "shard", axis=0, tiled=True),
    )
    key_places = jnp.arange(prompt_len, dtype=jnp.int32)
    prompt_allowed = (
        key_places[None, :]
        <= shard_index * PROMPT_BLK + jnp.arange(PROMPT_BLK, dtype=jnp.int32)[:, None]
    )
    wide_places = jnp.arange(prompt_len + CONT_LEN, dtype=jnp.int32)
    cont_allowed = (wide_places[None, :] < prompt_len) | (
        wide_places[None, :] - prompt_len <= jnp.arange(CONT_LEN, dtype=jnp.int32)[:, None]
    )
    cont_count = (block_len - PROMPT_BLK) // CONT_LEN
    mixed_piece, prompt_level = attend_forward(
        query_heads[:PROMPT_BLK], prompt_keys, prompt_values, prompt_allowed, HEAD_DIMENSION
    )
    mixed_parts = [mixed_piece]
    cont_levels = []
    cont_keys = []
    cont_values = []
    for number in range(cont_count):
        first_row = PROMPT_BLK + number * CONT_LEN
        last_row = first_row + CONT_LEN
        keys_all = jnp.concatenate([prompt_keys, key_heads[first_row:last_row]], axis=0)
        values_all = jnp.concatenate([prompt_values, value_heads[first_row:last_row]], axis=0)
        mixed_piece, cont_level = attend_forward(
            query_heads[first_row:last_row], keys_all, values_all, cont_allowed, HEAD_DIMENSION
        )
        mixed_parts.append(mixed_piece)
        cont_levels.append(cont_level)
        cont_keys.append(keys_all)
        cont_values.append(values_all)
    mixed_heads = jnp.concatenate(mixed_parts, axis=0).astype(jnp.bfloat16)
    mixed_tokens = lax.all_to_all(mixed_heads, "seq", split_axis=0, concat_axis=1, tiled=True)
    residual = inputs + jnp.dot(mixed_tokens, out_weight, preferred_element_type=jnp.float32)
    second_normed, second_back = jax.vjp(rms_norm, residual, second_gain.astype(jnp.float32))
    second_low = second_normed.astype(jnp.bfloat16)
    logits = jnp.dot(second_low, router_weight, preferred_element_type=jnp.float32)
    experts_all = router_weight.shape[1]
    capacity = max(2, 3 * tok_count * top_count // (2 * experts_all))
    chosen = routes[:, :, None] == jnp.arange(experts_all, dtype=jnp.int32)[None, None, :]
    route_mask = chosen.astype(jnp.float32)
    selected = jnp.sum(route_mask * logits[:, None, :], axis=-1)
    gate_weights, gate_back = jax.vjp(softmax_last, selected)
    entry_count = tok_count * top_count
    expert_hits = chosen.reshape(entry_count, experts_all).astype(jnp.int32)
    order_in_expert = jnp.sum((jnp.cumsum(expert_hits, axis=0) - expert_hits) * expert_hits, axis=1)
    target_slot = routes.reshape(-1) * capacity + order_in_expert
    entry_of_slot = (
        jnp.full((experts_all * capacity,), entry_count, jnp.int32)
        .at[target_slot]
        .set(jnp.arange(entry_count, dtype=jnp.int32))
    )
    row_of_slot = entry_of_slot // top_count
    blank_row = jnp.zeros((1, model_width), jnp.bfloat16)
    slot_rows = jnp.concatenate([second_low, blank_row], axis=0)[row_of_slot]
    entry_grads = (
        (gate_weights[:, :, None] * upstream[:, None, :])
        .astype(jnp.bfloat16)
        .reshape(entry_count, model_width)
    )
    slot_grads = jnp.concatenate([entry_grads, blank_row], axis=0)[entry_of_slot]
    arrived_rows, arrived_grads = (
        lax.all_to_all(
            slot_rows.reshape(shard_count, -1, model_width),
            "shard",
            split_axis=0,
            concat_axis=0,
            tiled=True,
        ),
        lax.all_to_all(
            slot_grads.reshape(shard_count, -1, model_width),
            "shard",
            split_axis=0,
            concat_axis=0,
            tiled=True,
        ),
    )
    local_experts = w_gate.shape[0]
    expert_in = arrived_rows.reshape(shard_count, local_experts, capacity, model_width)
    expert_grad_in = arrived_grads.reshape(shard_count, local_experts, capacity, model_width)
    gate_pre = jnp.einsum("secd,edf->secf", expert_in, w_gate, preferred_element_type=jnp.float32)
    up_pre = jnp.einsum("secd,edf->secf", expert_in, w_up, preferred_element_type=jnp.float32)
    hidden, swiglu_back = jax.vjp(swiglu, gate_pre, up_pre)
    hidden_low = hidden.astype(jnp.bfloat16)
    expert_out = jnp.einsum(
        "secf,efd->secd", hidden_low, w_down, preferred_element_type=jnp.float32
    ).astype(jnp.bfloat16)
    hidden_grad = jnp.einsum(
        "secd,efd->secf", expert_grad_in, w_down, preferred_element_type=jnp.float32
    )
    gate_pre_grad, up_pre_grad = swiglu_back(hidden_grad)
    gate_pre_low = gate_pre_grad.astype(jnp.bfloat16)
    up_pre_low = up_pre_grad.astype(jnp.bfloat16)
    grad_down = jnp.einsum(
        "secf,secd->efd", hidden_low, expert_grad_in, preferred_element_type=jnp.float32
    )
    grad_gate = jnp.einsum(
        "secd,secf->edf", expert_in, gate_pre_low, preferred_element_type=jnp.float32
    )
    grad_up = jnp.einsum(
        "secd,secf->edf", expert_in, up_pre_low, preferred_element_type=jnp.float32
    )
    row_grad = (
        jnp.einsum("secf,edf->secd", gate_pre_low, w_gate, preferred_element_type=jnp.float32)
        + jnp.einsum("secf,edf->secd", up_pre_low, w_up, preferred_element_type=jnp.float32)
    ).astype(jnp.bfloat16)
    back_out, back_rows = (
        lax.all_to_all(
            expert_out.reshape(shard_count, -1, model_width),
            "shard",
            split_axis=0,
            concat_axis=0,
            tiled=True,
        ),
        lax.all_to_all(
            row_grad.reshape(shard_count, -1, model_width),
            "shard",
            split_axis=0,
            concat_axis=0,
            tiled=True,
        ),
    )
    out_slots = (
        back_out.reshape(-1, model_width)[target_slot]
        .reshape(tok_count, top_count, model_width)
        .astype(jnp.float32)
    )
    grad_slots = (
        back_rows.reshape(-1, model_width)[target_slot]
        .reshape(tok_count, top_count, model_width)
        .astype(jnp.float32)
    )
    expert_sum = jnp.sum(gate_weights[:, :, None] * out_slots, axis=1)
    output = (residual + expert_sum).astype(jnp.bfloat16)
    gate_grad = jnp.sum(out_slots * upstream[:, None, :], axis=-1)
    (selected_grad,) = gate_back(gate_grad)
    logit_grad = jnp.sum(route_mask * selected_grad[:, :, None], axis=1)
    grad_router = transposed_times(second_low.astype(jnp.float32), logit_grad, highest)
    second_grad = jnp.sum(grad_slots, axis=1) + times_transposed(
        logit_grad, router_weight.astype(jnp.float32), highest
    )
    residual_part, grad_gain_ffn = second_back(second_grad)
    residual_grad = upstream + residual_part
    residual_low = residual_grad.astype(jnp.bfloat16)
    mixed_grad_tokens = times_transposed(residual_low, out_weight).astype(jnp.bfloat16)
    mixed_grad = lax.all_to_all(mixed_grad_tokens, "seq", split_axis=1, concat_axis=0, tiled=True)
    query_piece, prompt_key_grad, prompt_value_grad = attend_backward(
        query_heads[:PROMPT_BLK],
        prompt_keys,
        prompt_values,
        prompt_allowed,
        prompt_level,
        mixed_grad[:PROMPT_BLK],
        HEAD_DIMENSION,
    )
    query_parts = [query_piece]
    self_key_grads = []
    self_value_grads = []
    for number in range(cont_count):
        first_row = PROMPT_BLK + number * CONT_LEN
        last_row = first_row + CONT_LEN
        query_piece, key_piece, value_piece = attend_backward(
            query_heads[first_row:last_row],
            cont_keys[number],
            cont_values[number],
            cont_allowed,
            cont_levels[number],
            mixed_grad[first_row:last_row],
            HEAD_DIMENSION,
        )
        query_parts.append(query_piece)
        prompt_key_grad = prompt_key_grad + key_piece[:prompt_len]
        prompt_value_grad = prompt_value_grad + value_piece[:prompt_len]
        self_key_grads.append(key_piece[prompt_len:])
        self_value_grads.append(value_piece[prompt_len:])
    own_key_grad, own_value_grad = (
        lax.psum_scatter(
            prompt_key_grad.astype(jnp.bfloat16), "shard", scatter_dimension=0, tiled=True
        ).astype(jnp.float32),
        lax.psum_scatter(
            prompt_value_grad.astype(jnp.bfloat16), "shard", scatter_dimension=0, tiled=True
        ).astype(jnp.float32),
    )
    query_low = jnp.concatenate(query_parts, axis=0).astype(jnp.bfloat16)
    key_low = jnp.concatenate([own_key_grad] + self_key_grads, axis=0).astype(jnp.bfloat16)
    value_low = jnp.concatenate([own_value_grad] + self_value_grads, axis=0).astype(jnp.bfloat16)
    send_query, send_key, send_value = (query_low, key_low, value_low)
    back_query, back_key, back_value = (
        lax.all_to_all(send_query, "seq", split_axis=0, concat_axis=1, tiled=True),
        lax.all_to_all(send_key, "seq", split_axis=0, concat_axis=1, tiled=True),
        lax.all_to_all(send_value, "seq", split_axis=0, concat_axis=1, tiled=True),
    )
    lin_query = rotate(
        back_query.astype(jnp.float32), token_cos, -token_sin, HEAD_DIMENSION
    ).astype(jnp.bfloat16)
    lin_key = rotate(back_key.astype(jnp.float32), token_cos, -token_sin, HEAD_DIMENSION).astype(
        jnp.bfloat16
    )
    whole_query = transposed_times(normed_low, lin_query)
    whole_key = transposed_times(normed_low, lin_key)
    whole_value = transposed_times(normed_low, back_value)
    whole_out = transposed_times(mixed_tokens, residual_low)
    grad_query, grad_key, grad_value, grad_out = (
        lax.psum_scatter(
            whole_query.astype(jnp.bfloat16), "seq", scatter_dimension=1, tiled=True
        ).astype(jnp.float32),
        lax.psum_scatter(
            whole_key.astype(jnp.bfloat16), "seq", scatter_dimension=1, tiled=True
        ).astype(jnp.float32),
        lax.psum_scatter(
            whole_value.astype(jnp.bfloat16), "seq", scatter_dimension=1, tiled=True
        ).astype(jnp.float32),
        lax.psum_scatter(
            whole_out.astype(jnp.bfloat16), "seq", scatter_dimension=0, tiled=True
        ).astype(jnp.float32),
    )
    normed_grad = (
        times_transposed(lin_query, query_weight)
        + times_transposed(lin_key, key_weight)
        + times_transposed(back_value, value_weight)
    )
    input_part, grad_gain_attn = first_back(normed_grad)
    tokens_grad = residual_grad + input_part
    grad_query, grad_key, grad_value, grad_out, first_part, second_part, router_part = (
        lax.psum_scatter(
            grad_query.astype(jnp.bfloat16), "shard", scatter_dimension=0, tiled=True
        ).astype(jnp.float32),
        lax.psum_scatter(
            grad_key.astype(jnp.bfloat16), "shard", scatter_dimension=0, tiled=True
        ).astype(jnp.float32),
        lax.psum_scatter(
            grad_value.astype(jnp.bfloat16), "shard", scatter_dimension=0, tiled=True
        ).astype(jnp.float32),
        lax.psum_scatter(
            grad_out.astype(jnp.bfloat16), "shard", scatter_dimension=1, tiled=True
        ).astype(jnp.float32),
        lax.psum_scatter(
            grad_gain_attn.astype(jnp.bfloat16), "shard", scatter_dimension=0, tiled=True
        ).astype(jnp.float32),
        lax.psum_scatter(
            grad_gain_ffn.astype(jnp.bfloat16), "shard", scatter_dimension=0, tiled=True
        ).astype(jnp.float32),
        lax.psum_scatter(
            grad_router.astype(jnp.bfloat16), "shard", scatter_dimension=0, tiled=True
        ).astype(jnp.float32),
    )
    grad_gate, grad_up, grad_down, first_final, second_final, router_final = (
        lax.psum_scatter(
            grad_gate.astype(jnp.bfloat16), "seq", scatter_dimension=1, tiled=True
        ).astype(jnp.float32),
        lax.psum_scatter(
            grad_up.astype(jnp.bfloat16), "seq", scatter_dimension=1, tiled=True
        ).astype(jnp.float32),
        lax.psum_scatter(
            grad_down.astype(jnp.bfloat16), "seq", scatter_dimension=2, tiled=True
        ).astype(jnp.float32),
        lax.psum_scatter(
            first_part.astype(jnp.bfloat16), "seq", scatter_dimension=0, tiled=True
        ).astype(jnp.float32),
        lax.psum_scatter(
            second_part.astype(jnp.bfloat16), "seq", scatter_dimension=0, tiled=True
        ).astype(jnp.float32),
        lax.psum_scatter(
            router_part.astype(jnp.bfloat16), "seq", scatter_dimension=0, tiled=True
        ).astype(jnp.float32),
    )
    return (
        output,
        tokens_grad,
        grad_query,
        grad_key,
        grad_value,
        grad_out,
        first_final,
        second_final,
        router_final,
        grad_gate,
        grad_up,
        grad_down,
    )


def solution(mesh):
    return jax.shard_map(
        on_device,
        mesh=mesh,
        in_specs=(
            P(("shard", "seq"), None),
            P(("shard", "seq"), None),
            P("shard", "seq"),
            P("shard", "seq"),
            P("shard", "seq"),
            P("seq", "shard"),
            P(("shard", "seq")),
            P(("shard", "seq")),
            P(("shard", "seq"), None),
            P("shard", None, None),
            P("shard", None, None),
            P("shard", None, None),
            P(("shard", "seq"), None),
        ),
        out_specs=(
            P(("shard", "seq"), None),
            P(("shard", "seq"), None),
            P("shard", "seq"),
            P("shard", "seq"),
            P("shard", "seq"),
            P("seq", "shard"),
            P(("shard", "seq")),
            P(("shard", "seq")),
            P(("shard", "seq"), None),
            P("shard", "seq", None),
            P("shard", "seq", None),
            P("shard", None, "seq"),
        ),
        check_vma=False,
    )
```

profile of v0, /device:TPU:0, one launch (start us, length us, event | category | flops | bytes accessed | tf_op | source)
XLA Modules:
  0.0 1770.6 jit_solution(17996026511332895665)
XLA Ops:
  7.3 16.4 all_gather.50
  23.8 13.4 all_gather.53
  37.3 17.2 all_gather.56
  54.5 16.6 all_gather.58
  75.1 10.4 all-reduce.13
  86.0 12.7 all-reduce.11
  112.6 5.8 all-to-all-done
  139.4 10.5 all_gather.52
  157.4 9.0 all_gather.55
  182.5 8.8 fusion.140
  191.3 9.5 fusion.7
  206.9 10.4 fusion.79
  219.2 20.6 %fusion.141 = (f32[2,3,512]{2,1,0:T(4,128)}, f32[2,3,512,1536]{2,3,1,0:T(8,128)}) fusion(bf16[1536,2,64,1]{0,2,3,1:T(8,128)(2,1)} %bitcast.417, bf16[512,2,3,64]{0,3,2,1:T(8,128)(2,1)S(1)} %bitcast.407, pred[512,1536]{0,1:T(8,128)(4,1)} %fusion.52), kind=kOutput, calls=%fused_computation.258 | convolution fusion | flops 618132480 | bytes 20459520 | tf_op jit(solution)/shard_map/rhgd,khd->hgrk/dot_general | solution.py:85
  239.8 9.5 fusion.6
  249.3 8.9 fusion.80
  275.6 9.0 scatter_custom_fusion
  299.5 23.5 %gather_fusion = bf16[3456,1536]{1,0:T(8,128)(2,1)} fusion(bf16[289,1536]{1,0:T(8,128)(2,1)} %concatenate.57, s32[4096]{0:T(1024)S(1)} %get-tuple-element.151), kind=kCustom, calls=%fused_computation | custom fusion | bytes 21247488 | tf_op jit(solution)/shard_map/gather | solution.py:269
  328.2 13.2 all-gather
  341.5 107.9 %all-gather.1 = bf16[8,192,16]{1,2,0:T(8,128)(2,1)S(1)} all-gather(bf16[1,192,16]{1,2,0:T(8,128)(2,1)S(1)} %reshape.654), channel_id=1, replica_groups=mesh['shard'=8,'seq'=4] {'shard'}, dimensions={0}, use_global_device_ids=true | all-gather | bytes 55296 | tf_op jit(solution)/shard_map/all_gather | solution.py:183
  460.0 6.4 concatenate.58
  466.4 26.1 %gather_fusion.2 = bf16[3456,1536]{1,0:T(8,128)(2,1)} fusion(bf16[2305,1536]{1,0:T(8,128)(2,1)} %concatenate.58, s32[4096]{0:T(1024)S(1)} %get-tuple-element.150), kind=kCustom, calls=%fused_computation.2 | custom fusion | bytes 21247488 | tf_op jit(solution)/shard_map/gather | solution.py:275
  498.1 12.3 fusion.25
  510.5 12.0 fusion.27
  522.4 93.6 %all-to-all-done.6 = bf16[8,432,1536]{2,1,0:T(8,128)(2,1)} async-done(((bf16[8,432,1536]{2,1,0:T(8,128)(2,1)}), bf16[8,432,1536]{2,1,0:T(8,128)(2,1)}, u32[]{:S(2)}, u32[]{:S(2)}) %all-to-all-start.6) | async-done | bytes 10616864 | tf_op jit(solution)/shard_map/all_to_all | solution.py:284
  616.1 16.1 fusion.33
  632.2 7.9 convert_bitcast_fusion
  650.4 12.2 fusion.47
  662.6 14.4 fusion.29
  677.0 9.5 copy.323
  686.5 81.9 %all-to-all-done.5 = bf16[8,432,1536]{2,1,0:T(8,128)(2,1)} async-done(((bf16[8,432,1536]{2,1,0:T(8,128)(2,1)}), bf16[8,432,1536]{2,1,0:T(8,128)(2,1)}, u32[]{:S(2)}, u32[]{:S(2)}) %all-to-all-start.5) | async-done | bytes 10616864 | tf_op jit(solution)/shard_map/all_to_all | solution.py:322
  773.7 20.4 %gather_fusion.1 = bf16[2304,1536]{1,0:T(8,128)(2,1)} fusion(bf16[3456,1536]{1,0:T(8,128)(2,1)} %bitcast.61, s32[3072]{0:T(1024)S(1)} %pad_clamp_fusion.2), kind=kCustom, calls=%fused_computation.1 | custom fusion | bytes 14164992 | tf_op jit(solution)/shard_map/gather | solution.py:338
  794.1 8.5 fusion.11
  802.8 88.7 %all-to-all-done.7 = bf16[8,432,1536]{2,1,0:T(8,128)(2,1)} async-done(((bf16[8,432,1536]{2,1,0:T(8,128)(2,1)}), bf16[8,432,1536]{2,1,0:T(8,128)(2,1)}, u32[]{:S(2)}, u32[]{:S(2)}) %all-to-all-start.7) | async-done | bytes 10616864 | tf_op jit(solution)/shard_map/all_to_all | solution.py:329
  891.6 20.5 %gather_fusion.3 = bf16[2304,1536]{1,0:T(8,128)(2,1)} fusion(bf16[3456,1536]{1,0:T(8,128)(2,1)} %bitcast.72, s32[3072]{0:T(1024)S(1)} %pad_clamp_fusion.2), kind=kCustom, calls=%fused_computation.3 | custom fusion | bytes 14164992 | tf_op jit(solution)/shard_map/gather | solution.py:343
  912.1 7.8 convert_reduce_fusion
  930.8 18.2 %all-to-all-done.8 = bf16[288,4,384]{2,0,1:T(8,128)(2,1)S(1)} async-done(((bf16[288,4,384]{2,0,1:T(8,128)(2,1)}), bf16[288,4,384]{2,0,1:T(8,128)(2,1)S(1)}, u32[]{:S(2)}, u32[]{:S(2)}) %all-to-all-start.8) | async-done | bytes 884768 | tf_op jit(solution)/shard_map/all_to_all | solution.py:360
  950.2 8.4 fusion.57
  959.3 8.1 fusion.54
  972.5 12.4 fusion.3
  984.9 12.4 fusion
  1000.0 19.2 %fusion.5 = bf16[2,3,512,1536]{2,3,1,0:T(8,128)(2,1)} fusion(f32[2,1536,512,3]{2,1,3,0:T(8,128)} %get-tuple-element.144, f32[2,3,512,1536]{2,3,1,0:T(8,128)} %get-tuple-element.135, f32[2,3,512]{2,1,0:T(4,128)} %get-tuple-element.143, f32[2,3,512]{2,1,0:T(4,128)} %log_add_fusion.1), kind=kLoop, calls=%fused_computation.15 | loop fusion | flops 18874368 | bytes 47210496 | tf_op jit(solution)/shard_map/convert_element_type | solution.py:120
  1019.3 8.2 fusion.63
  1027.5 13.7 fusion.2
  1041.2 7.7 fusion.61
  1071.5 24.9 %reduce-scatter.30.cloned.1.call-done = bf16[128,128]{1,0:T(8,128)(2,1)} async-done(((bf16[1024,128]{1,0:T(8,128)(2,1)}), bf16[128,128]{1,0:T(8,128)(2,1)}) %reduce-scatter.30.cloned.1.call-update) | async-done | bytes 32784 | tf_op jit(solution)/shard_map/reduce_scatter | solution.py:391
  1097.2 13.4 all_to_all.142
  1120.6 11.9 bitcast_convert_fusion
  1132.5 7.1 copy.397
  1142.2 11.1 bitcast_convert_fusion.1
  1153.4 10.9 bitcast_convert_fusion.2
  1182.9 42.2 %all-to-all-done.9 = bf16[4,288,384]{2,1,0:T(8,128)(2,1)S(1)} async-done(((bf16[4,288,384]{2,1,0:T(8,128)(2,1)}), bf16[4,288,384]{2,1,0:T(8,128)(2,1)S(1)}, u32[]{:S(2)}, u32[]{:S(2)}) %all-to-all-start.9) | async-done | bytes 884768 | tf_op jit(solution)/shard_map/all_to_all | solution.py:403
  1234.1 6.7 copy.385
  1245.2 67.5 %reduce-scatter.40.cloned.1.call-done = bf16[384,1536]{1,0:T(8,128)(2,1)} async-done(((bf16[1536,1536]{1,0:T(8,128)(2,1)}), bf16[384,1536]{1,0:T(8,128)(2,1)}) %reduce-scatter.40.cloned.1.call-update) | async-done | bytes 1179664 | tf_op jit(solution)/shard_map/reduce_scatter | solution.py:427
  1316.4 59.6 %reduce-scatter.58.cloned.1.call-done = bf16[384,1024]{1,0:T(8,128)(2,1)} async-done(((bf16[1536,1024]{1,0:T(8,128)(2,1)}), bf16[384,1024]{1,0:T(8,128)(2,1)}) %reduce-scatter.58.cloned.1.call-update) | async-done | bytes 786448
  1380.5 58.0 %reduce-scatter.44.cloned.1.call-done = bf16[2,384,512]{2,1,0:T(8,128)(2,1)} async-done(((bf16[2,1536,512]{2,1,0:T(8,128)(2,1)}), bf16[2,384,512]{2,1,0:T(8,128)(2,1)}) %reduce-scatter.44.cloned.1.call-update) | async-done | bytes 786448 | tf_op jit(solution)/shard_map/reduce_scatter | solution.py:465
  1441.0 60.2 %reduce-scatter.42.cloned.1.call-done = bf16[2,384,512]{2,1,0:T(8,128)(2,1)} async-done(((bf16[2,1536,512]{2,1,0:T(8,128)(2,1)}), bf16[2,384,512]{2,1,0:T(8,128)(2,1)}) %reduce-scatter.42.cloned.1.call-update) | async-done | bytes 786448 | tf_op jit(solution)/shard_map/reduce_scatter | solution.py:462
  1503.6 18.8 %reduce-scatter.56.cloned.1.call-done = bf16[48,16]{1,0:T(8,128)(2,1)} async-done(((bf16[192,16]{1,0:T(8,128)(2,1)}), bf16[48,16]{1,0:T(8,128)(2,1)}) %reduce-scatter.56.cloned.1.call-update) | async-done | bytes 1552
  1523.8 5.7 fusion.144
  1529.5 78.6 %reduce-scatter.46.cloned.1.call-done = bf16[384,1536]{1,0:T(8,128)(2,1)} async-done(((bf16[1536,1536]{1,0:T(8,128)(2,1)}), bf16[384,1536]{1,0:T(8,128)(2,1)}) %reduce-scatter.46.cloned.1.call-update) | async-done | bytes 1179664
  1615.6 13.8 all-reduce.10
  1629.6 11.2 all-reduce.12
  1647.5 34.8 %reduce-scatter.36.cloned.1.call-done = bf16[192,128]{1,0:T(8,128)(2,1)} async-done(((bf16[1536,128]{1,0:T(8,128)(2,1)}), bf16[192,128]{1,0:T(8,128)(2,1)}) %reduce-scatter.36.cloned.1.call-update) | async-done | bytes 49168 | tf_op jit(solution)/shard_map/reduce_scatter | solution.py:442
  1683.7 38.4 %reduce-scatter.52.cloned.1.call-done = bf16[192,384]{1,0:T(8,128)(2,1)} async-done(((bf16[1536,384]{1,0:T(8,128)(2,1)}), bf16[192,384]{1,0:T(8,128)(2,1)}) %reduce-scatter.52.cloned.1.call-update) | async-done | bytes 147472
  1724.0 38.0 %reduce-scatter.34.cloned.1.call-done = bf16[192,384]{1,0:T(8,128)(2,1)} async-done(((bf16[1536,384]{1,0:T(8,128)(2,1)}), bf16[192,384]{1,0:T(8,128)(2,1)}) %reduce-scatter.34.cloned.1.call-update) | async-done | bytes 147472 | tf_op jit(solution)/shard_map/reduce_scatter | solution.py:439
  (455 shorter events, 259.5 us)
Async XLA Ops:
  7.2 608.9 %copy-start = (bf16[2,512,1536]{2,1,0:T(8,128)(2,1)S(1)}, bf16[2,512,1536]{2,1,0:T(8,128)(2,1)}, u32[]{:S(2)}) copy-start(bf16[2,512,1536]{2,1,0:T(8,128)(2,1)} %param.24) | copy-start | bytes 9437188
  7.2 65.5 %copy-start.95 = (u32[32]{0:T(128)S(1)}, u32[32]{0:T(128)}, u32[]{:S(2)}) copy-start(u32[32]{0:T(128)} %constant.119) | copy-start | bytes 388
  7.2 65.5 %copy-start.96 = (u32[32]{0:T(128)S(1)}, u32[32]{0:T(128)}, u32[]{:S(2)}) copy-start(u32[32]{0:T(128)} %constant.114) | copy-start | bytes 388
  7.2 67.4 %copy-start.99 = (bf16[48]{0:T(256)(128)(2,1)S(1)}, bf16[48]{0:T(256)(128)(2,1)}, u32[]{:S(2)}) copy-start(bf16[48]{0:T(256)(128)(2,1)} %param.20) | copy-start | bytes 292
  7.2 67.6 %copy-start.100 = (bf16[48]{0:T(256)(128)(2,1)S(1)}, bf16[48]{0:T(256)(128)(2,1)}, u32[]{:S(2)}) copy-start(bf16[48]{0:T(256)(128)(2,1)} %param.19) | copy-start | bytes 292
  7.2 94.2 %all-gather.7.cloned.1.call-start = ((), (), s32[]{:S(2)}) async-start(), calls=%async_computation.27 | async-start | bytes 1769472 | tf_op jit(solution)/shard_map/all_gather | solution.py:179
  23.8 85.0 %all-gather.9.cloned.1.call-start = ((), (), s32[]{:S(2)}) async-start(), calls=%async_computation.28 | async-start | bytes 1769472 | tf_op jit(solution)/shard_map/all_gather | solution.py:178
  37.2 84.7 %all-gather.11.cloned.1.call-start = ((), (), s32[]{:S(2)}) async-start(), calls=%async_computation.29 | async-start | bytes 5308416 | tf_op jit(solution)/shard_map/all_gather | solution.py:177
  54.5 237.1 %all-gather.13.cloned.1.call-start = ((), (), s32[]{:S(2)}) async-start(), calls=%async_computation.30 | async-start | bytes 5308416 | tf_op jit(solution)/shard_map/all_gather | solution.py:180
  72.6 31.2 %copy-start.86 = (f32[288]{0:T(512)}, f32[288]{0:T(512)S(1)}, u32[]{:S(2)}) copy-start(f32[288]{0:T(512)S(1)} %fusion.71) | copy-start | bytes 3460
  72.6 49.3 %copy-start.84 = (f32[288]{0:T(512)}, f32[288]{0:T(512)S(1)}, u32[]{:S(2)}) copy-start(f32[288]{0:T(512)S(1)} %fusion.124) | copy-start | bytes 3460
  98.7 23.2 %copy-start.69 = (f32[1536]{0:T(1024)}, f32[1536]{0:T(1024)S(1)}, u32[]{:S(2)}) copy-start(f32[1536]{0:T(1024)S(1)} %convert_element_type.262) | copy-start | bytes 18436
  104.6 13.8 all-to-all-start
  118.4 12.3 all-to-all-start.1
  130.7 42.3 %all-to-all-start.2 = ((bf16[288,4,384]{2,0,1:T(8,128)(2,1)}), bf16[288,4,384]{2,0,1:T(8,128)(2,1)}, u32[]{:S(2)}, u32[]{:S(2)}) async-start(bf16[288,4,384]{2,0,1:T(8,128)(2,1)} %copy.297), calls=%async_computation.2 | async-start | bytes 1769472 | tf_op jit(solution)/shard_map/all_to_all | solution.py:209
  179.8 21.0 %copy-start.80 = (f32[2,3,128]{2,1,0:T(4,128)}, f32[2,3,128]{2,1,0:T(4,128)S(1)}, u32[]{:S(2)}) copy-start(f32[2,3,128]{2,1,0:T(4,128)S(1)} %get-tuple-element.136) | copy-start | bytes 9220
  205.1 14.1 copy-start.20
  261.5 28.0 %all-to-all-start.3 = ((bf16[4,288,384]{2,1,0:T(8,128)(2,1)}), bf16[4,288,384]{2,1,0:T(8,128)(2,1)}, u32[]{:S(2)}, u32[]{:S(2)}) async-start(bf16[4,288,384]{2,1,0:T(8,128)(2,1)} %bitcast.419), calls=%async_computation.3 | async-start | bytes 1769472 | tf_op jit(solution)/shard_map/all_to_all | solution.py:247
  296.2 26.8 %copy-start.92 = (f32[288]{0:T(512)}, f32[288]{0:T(512)S(1)}, u32[]{:S(2)}) copy-start(f32[288]{0:T(512)S(1)} %get-tuple-element.138) | copy-start | bytes 3460
  296.2 26.8 %copy-start.82 = (f32[288]{0:T(512)}, f32[288]{0:T(512)S(1)}, u32[]{:S(2)}) copy-start(f32[288]{0:T(512)S(1)} %fusion.125) | copy-start | bytes 3460
  323.0 169.5 %all-to-all-start.4 = ((bf16[8,432,1536]{2,1,0:T(8,128)(2,1)}), bf16[8,432,1536]{2,1,0:T(8,128)(2,1)}, u32[]{:S(2)}, u32[]{:S(2)}) async-start(bf16[8,432,1536]{2,1,0:T(8,128)(2,1)} %bitcast.395), calls=%async_computation.4 | async-start | bytes 21233664 | tf_op jit(solution)/shard_map/all_to_all | solution.py:277
  492.6 123.5 %all-to-all-start.6 = ((bf16[8,432,1536]{2,1,0:T(8,128)(2,1)}), bf16[8,432,1536]{2,1,0:T(8,128)(2,1)}, u32[]{:S(2)}, u32[]{:S(2)}) async-start(bf16[8,432,1536]{2,1,0:T(8,128)(2,1)} %bitcast.396), calls=%async_computation.6 | async-start | bytes 21233664 | tf_op jit(solution)/shard_map/all_to_all | solution.py:284
  498.1 12.3 copy-start.97
  644.8 123.5 %all-to-all-start.5 = ((bf16[8,432,1536]{2,1,0:T(8,128)(2,1)}), bf16[8,432,1536]{2,1,0:T(8,128)(2,1)}, u32[]{:S(2)}, u32[]{:S(2)}) async-start(bf16[8,432,1536]{2,1,0:T(8,128)(2,1)} %bitcast.398), calls=%async_computation.5 | async-start | bytes 21233664 | tf_op jit(solution)/shard_map/all_to_all | solution.py:322
  768.3 123.2 %all-to-all-start.7 = ((bf16[8,432,1536]{2,1,0:T(8,128)(2,1)}), bf16[8,432,1536]{2,1,0:T(8,128)(2,1)}, u32[]{:S(2)}, u32[]{:S(2)}) async-start(bf16[8,432,1536]{2,1,0:T(8,128)(2,1)} %bitcast.397), calls=%async_computation.7 | async-start | bytes 21233664 | tf_op jit(solution)/shard_map/all_to_all | solution.py:329
  773.7 20.4 %copy-start.7 = (f32[288,1536]{1,0:T(8,128)S(1)}, f32[288,1536]{1,0:T(8,128)}, u32[]{:S(2)}) copy-start(f32[288,1536]{1,0:T(8,128)} %convert_element_type.282) | copy-start | bytes 5308420
  773.7 20.4 %copy-start.34 = (f32[288,8]{1,0:T(8,128)S(1)}, f32[288,8]{1,0:T(8,128)}, u32[]{:S(2)}) copy-start(f32[288,8]{1,0:T(8,128)} %copy-done.33) | copy-start | bytes 27652
  802.8 117.1 %copy-start.61 = (f32[288,16]{0,1:T(8,128)}, f32[288,16]{0,1:T(8,128)S(1)}, u32[]{:S(2)}) copy-start(f32[288,16]{0,1:T(8,128)S(1)} %select_reduce_fusion) | copy-start | bytes 55300
  925.9 23.0 %all-to-all-start.8 = ((bf16[288,4,384]{2,0,1:T(8,128)(2,1)}), bf16[288,4,384]{2,0,1:T(8,128)(2,1)S(1)}, u32[]{:S(2)}, u32[]{:S(2)}) async-start(bf16[288,4,384]{2,0,1:T(8,128)(2,1)} %bitcast.389), calls=%async_computation.8 | async-start | bytes 1769472 | tf_op jit(solution)/shard_map/all_to_all | solution.py:360
  929.5 121.3 %reduce-scatter.32.cloned.1.call-start = ((), (), s32[]{:S(2)}) async-start(), calls=%async_computation.32 | async-start | bytes 294912 | tf_op jit(solution)/shard_map/reduce_scatter | solution.py:394
  972.5 12.4 copy-start.23
  972.5 12.4 copy-start.29
  984.9 12.4 copy-start.50
  984.9 14.2 copy-start.46
  1000.0 27.5 %slice-start = ((s8[18874368]{0:T(1024)(128)(4,1)}), s8[4194304]{0:T(1024)(128)(4,1)S(1)}, s32[]{:S(2)}) async-start(s8[18874368]{0:T(1024)(128)(4,1)} %bitcast.393), calls=%async_computation.46 | async-start | bytes 8388608
  1000.0 19.3 %copy-start.21 = (bf16[512,384]{0,1:T(8,128)(2,1)S(1)}, bf16[512,384]{0,1:T(8,128)(2,1)}, u32[]{:S(2)}) copy-start(bf16[512,384]{0,1:T(8,128)(2,1)} %copy-done.20) | copy-start | bytes 1179652
  1000.0 27.5 %slice-start.1 = ((s8[18874368]{0:T(1024)(128)(4,1)}), s8[4194304]{0:T(1024)(128)(4,1)S(1)}, s32[]{:S(2)}) async-start(s8[18874368]{0:T(1024)(128)(4,1)} %bitcast.393), calls=%async_computation.47 | async-start | bytes 8388608
  1000.0 27.5 %slice-start.2 = ((s8[18874368]{0:T(1024)(128)(4,1)}), s8[4194304]{0:T(1024)(128)(4,1)S(1)}, s32[]{:S(2)}) async-start(s8[18874368]{0:T(1024)(128)(4,1)} %bitcast.393), calls=%async_computation.48 | async-start | bytes 8388608
  1000.0 27.5 %slice-start.3 = ((s8[18874368]{0:T(1024)(128)(4,1)}), s8[4194304]{0:T(1024)(128)(4,1)S(1)}, s32[]{:S(2)}) async-start(s8[18874368]{0:T(1024)(128)(4,1)} %bitcast.393), calls=%async_computation.49 | async-start | bytes 8388608
  1000.0 27.5 %slice-start.4 = ((s8[18874368]{0:T(1024)(128)(4,1)}), s8[2097152]{0:T(1024)(128)(4,1)S(1)}, s32[]{:S(2)}) async-start(s8[18874368]{0:T(1024)(128)(4,1)} %bitcast.393), calls=%async_computation.50 | async-start | bytes 4194304
  1027.5 13.7 copy-start.19
  1052.3 12.1 all-to-all-start.11
  1055.9 40.5 %reduce-scatter.30.cloned.1.call-start = ((), (), s32[]{:S(2)}) async-start(), calls=%async_computation.31 | async-start | bytes 294912 | tf_op jit(solution)/shard_map/reduce_scatter | solution.py:391
  1059.1 123.2 %reduce-scatter.54.cloned.1.call-start = ((), (), s32[]{:S(2)}) async-start(), calls=%async_computation.43 | async-start | bytes 442368
  1060.6 180.3 %reduce-scatter.50.cloned.1.call-start = ((), (), s32[]{:S(2)}) async-start(), calls=%async_computation.41 | async-start | bytes 1966080
  1069.2 41.7 %copy-start.37 = (f32[288,32]{0,1:T(8,128)S(1)}, f32[288,32]{0,1:T(8,128)}, u32[]{:S(2)}) copy-start(f32[288,32]{0,1:T(8,128)} %copy-done.35) | copy-start | bytes 110596
  1069.2 41.7 %copy-start.52 = (f32[288,32]{0,1:T(8,128)S(1)}, f32[288,32]{0,1:T(8,128)}, u32[]{:S(2)}) copy-start(f32[288,32]{0,1:T(8,128)} %get-tuple-element.125) | copy-start | bytes 110596
  1069.3 173.9 %reduce-scatter.48.cloned.1.call-start = ((), (), s32[]{:S(2)}) async-start(), calls=%async_computation.40 | async-start | bytes 1966080
  1116.2 196.5 %reduce-scatter.40.cloned.1.call-start = ((), (), s32[]{:S(2)}) async-start(), calls=%async_computation.36 | async-start | bytes 5898240 | tf_op jit(solution)/shard_map/reduce_scatter | solution.py:427
  1120.6 255.4 %reduce-scatter.58.cloned.1.call-start = ((), (), s32[]{:S(2)}) async-start(), calls=%async_computation.45 | async-start | bytes 3932160
  1142.2 296.3 %reduce-scatter.44.cloned.1.call-start = ((), (), s32[]{:S(2)}) async-start(), calls=%async_computation.38 | async-start | bytes 3932160 | tf_op jit(solution)/shard_map/reduce_scatter | solution.py:465
  1153.4 347.8 %reduce-scatter.42.cloned.1.call-start = ((), (), s32[]{:S(2)}) async-start(), calls=%async_computation.37 | async-start | bytes 3932160 | tf_op jit(solution)/shard_map/reduce_scatter | solution.py:462
  1178.7 46.3 %all-to-all-start.9 = ((bf16[4,288,384]{2,1,0:T(8,128)(2,1)}), bf16[4,288,384]{2,1,0:T(8,128)(2,1)S(1)}, u32[]{:S(2)}, u32[]{:S(2)}) async-start(bf16[4,288,384]{2,1,0:T(8,128)(2,1)} %bitcast.102), calls=%async_computation.9 | async-start | bytes 1769472 | tf_op jit(solution)/shard_map/all_to_all | solution.py:403
  1182.3 340.2 %reduce-scatter.56.cloned.1.call-start = ((), (), s32[]{:S(2)}) async-start(), calls=%async_computation.44 | async-start | bytes 61440
  1182.8 45.5 %copy-start.38 = (f32[288,32]{0,1:T(8,128)S(1)}, f32[288,32]{0,1:T(8,128)}, u32[]{:S(2)}) copy-start(f32[288,32]{0,1:T(8,128)} %copy-done.35) | copy-start | bytes 110596
  1182.8 45.5 %copy-start.53 = (f32[288,32]{0,1:T(8,128)S(1)}, f32[288,32]{0,1:T(8,128)}, u32[]{:S(2)}) copy-start(f32[288,32]{0,1:T(8,128)} %get-tuple-element.125) | copy-start | bytes 110596
  1182.9 425.2 %reduce-scatter.46.cloned.1.call-start = ((), (), s32[]{:S(2)}) async-start(), calls=%async_computation.39 | async-start | bytes 5898240
  1240.8 405.2 %reduce-scatter.38.cloned.1.call-start = ((), (), s32[]{:S(2)}) async-start(), calls=%async_computation.35 | async-start | bytes 442368 | tf_op jit(solution)/shard_map/reduce_scatter | solution.py:445
  1242.8 439.4 %reduce-scatter.36.cloned.1.call-start = ((), (), s32[]{:S(2)}) async-start(), calls=%async_computation.34 | async-start | bytes 442368 | tf_op jit(solution)/shard_map/reduce_scatter | solution.py:442
  1245.2 476.9 %reduce-scatter.52.cloned.1.call-start = ((), (), s32[]{:S(2)}) async-start(), calls=%async_computation.42 | async-start | bytes 1327104
  1315.1 446.9 %reduce-scatter.34.cloned.1.call-start = ((), (), s32[]{:S(2)}) async-start(), calls=%async_computation.33 | async-start | bytes 1327104 | tf_op jit(solution)/shard_map/reduce_scatter | solution.py:439
  1379.3 144.6 %copy-start.42 = (bf16[288,24,64]{0,2,1:T(8,128)(2,1)S(1)}, bf16[288,24,64]{0,2,1:T(8,128)(2,1)}, u32[]{:S(2)}) copy-start(bf16[288,24,64]{0,2,1:T(8,128)(2,1)} %copy-done.41) | copy-start | bytes 2654212
  1613.6 28.4 %copy-start.87 = (f32[288]{0:T(512)S(1)}, f32[288]{0:T(512)}, u32[]{:S(2)}) copy-start(f32[288]{0:T(512)} %copy-done.86) | copy-start | bytes 3460
  1641.9 121.7 %copy-start.1 = (bf16[2,512,1536]{2,1,0:T(8,128)(2,1)S(1)}, bf16[2,512,1536]{2,1,0:T(8,128)(2,1)}, u32[]{:S(2)}) copy-start(bf16[2,512,1536]{2,1,0:T(8,128)(2,1)} %param.24) | copy-start | bytes 9437188
  (74 other events, 407.4 us)
Sparse Core Ops, SparseCore 0:
  23.9 24.1 all-gather.6
  50.0 25.5 all-gather.8
  77.5 38.9 all-gather.10
  118.2 39.8 all-gather.12
  1000.1 33.9 reduce-scatter.31
  1060.0 36.3 reduce-scatter.29
  1099.4 33.8 reduce-scatter.53
  1135.7 35.4 reduce-scatter.49
  1174.0 48.8 reduce-scatter.47
  1225.0 87.6 reduce-scatter.39
  1315.0 60.9 reduce-scatter.57
  1378.1 60.2 reduce-scatter.43
  1440.8 60.3 reduce-scatter.41
  1503.2 19.2 reduce-scatter.55
  1524.6 83.4 reduce-scatter.45
  1611.0 34.3 reduce-scatter.37
  1648.4 33.8 reduce-scatter.35
  1685.4 36.6 reduce-scatter.51
  1725.3 36.6 reduce-scatter.33
where the time goes:
time: 1780 us; the launch traced here: 1770 us
  waiting for transfers between devices  818 us (46%)
  matrix products  282 us (16%)
  blocking collectives  266 us (15%)
  local copies, waits for them, and re-layouts  213 us (12%)
  other arithmetic  122 us (7%)
  starting transfers between devices  51 us (3%)
  between operations  18.8 us (1%)
    unnamed x26, waiting for transfers between devices  196 us
    all_gather x1, blocking collectives, on_device(): lax.all_gather(router_weight, 'shard', axis=0, tiled=True)  108 us
    all_to_all x1, waiting for transfers between devices, on_device(): lax.all_to_all(slot_grads.reshape(shard_count, -1, model_width), 'shard',...  93.6 us
    all_to_all x1, waiting for transfers between devices, on_device(): lax.all_to_all(row_grad.reshape(shard_count, -1, model_width), 'shard', s...  88.7 us
    all_to_all x1, waiting for transfers between devices, on_device(): lax.all_to_all(expert_out.reshape(shard_count, -1, model_width), 'shard',...  81.9 us
    reduce_scatter x1, waiting for transfers between devices, on_device(): lax.psum_scatter(whole_out.astype(jnp.bfloat16), 'seq', scatter_dimension...  67.5 us
    reduce_scatter x1, waiting for transfers between devices, on_device(): lax.psum_scatter(grad_gate.astype(jnp.bfloat16), 'seq', scatter_dimension...  60.2 us
    reduce_scatter x1, waiting for transfers between devices, on_device(): lax.psum_scatter(grad_up.astype(jnp.bfloat16), 'seq', scatter_dimension=1...  58 us
  transfers between devices with their start and end apart: 30, of which 18 were waited for; matrix products, arithmetic and copies ran while one was open for 26% of the time, Pallas kernels for 0%

commit v1 on v0

v1 whole, which is shorter than its diff:
```python
import jax
import jax.numpy as jnp
from jax import lax
from jax.sharding import PartitionSpec as P

HEAD_DIMENSION = 64
CONT_LEN = 512
PROMPT_BLK = 128


norm_eps = 1e-05
negative = -1e30
rope_base = 10000.0
highest = lax.Precision.HIGHEST


def rms_norm(values, scaling):
    factor = lax.rsqrt(jnp.mean(values * values, axis=-1, keepdims=True) + norm_eps)
    return values * factor * scaling


def swiglu(gate_pre, up_pre):
    return jax.nn.silu(gate_pre) * up_pre


def softmax_last(values):
    return jax.nn.softmax(values, axis=-1)


def rotary_tables(places, head_size):
    half_size = head_size // 2
    frequency = jnp.exp(
        jnp.arange(half_size, dtype=jnp.float32) * (-2.0 * jnp.log(rope_base) / head_size)
    )
    angles = places.astype(jnp.float32)[:, None] * frequency[None, :]
    return (jnp.cos(angles)[:, None, :], jnp.sin(angles)[:, None, :])


def rotate(values, cosine, sine, head_size):
    total_row_count = values.shape[0]
    by_head = values.reshape(total_row_count, -1, head_size)
    half_size = head_size // 2
    first_half = by_head[..., :half_size]
    second_half = by_head[..., half_size:]
    turned = jnp.concatenate(
        [first_half * cosine - second_half * sine, second_half * cosine + first_half * sine],
        axis=-1,
    )
    return turned.reshape(total_row_count, -1)


def place_of(within, block_index, prompt_len):
    return jnp.where(
        within < PROMPT_BLK,
        block_index * PROMPT_BLK + within,
        prompt_len + (within - PROMPT_BLK) % CONT_LEN,
    )


def times_transposed(left_side, right_side, precision=None):
    return lax.dot_general(
        left_side,
        right_side,
        (((1,), (1,)), ((), ())),
        precision=precision,
        preferred_element_type=jnp.float32,
    )


def transposed_times(left_side, right_side, precision=None):
    return lax.dot_general(
        left_side,
        right_side,
        (((0,), (0,)), ((), ())),
        precision=precision,
        preferred_element_type=jnp.float32,
    )


def head_scores(query_matrix, key_matrix_rows, allowed, head_size):
    total_row_count = query_matrix.shape[0]
    kv_heads = key_matrix_rows.shape[1] // head_size
    grouped_heads = query_matrix.reshape(total_row_count, kv_heads, -1, head_size)
    key_head_split = key_matrix_rows.reshape(key_matrix_rows.shape[0], kv_heads, head_size)
    scores = jnp.einsum(
        "rhgd,khd->hgrk", grouped_heads, key_head_split, preferred_element_type=jnp.float32
    ) * head_size ** (-0.5)
    return jnp.where(allowed, scores, negative)


def attend_forward(query_matrix, key_matrix_rows, value_matrix_rows, allowed, head_size):
    scores = head_scores(query_matrix, key_matrix_rows, allowed, head_size)
    row_max = jnp.max(scores, axis=-1, keepdims=True)
    weights = jnp.exp(scores - row_max)
    row_total = jnp.sum(weights, axis=-1, keepdims=True)
    probs_low = (weights / row_total).astype(jnp.bfloat16)
    kv_heads = key_matrix_rows.shape[1] // head_size
    value_heads_split = value_matrix_rows.reshape(value_matrix_rows.shape[0], kv_heads, head_size)
    mixed_out = jnp.einsum(
        "hgrk,khd->rhgd", probs_low, value_heads_split, preferred_element_type=jnp.float32
    )
    return (mixed_out.reshape(query_matrix.shape[0], -1), row_max + jnp.log(row_total))


def attend_backward(
    query_matrix, key_matrix_rows, value_matrix_rows, allowed, log_total, mixed_grad, head_size
):
    total_row_count = query_matrix.shape[0]
    kv_heads = key_matrix_rows.shape[1] // head_size
    scores = head_scores(query_matrix, key_matrix_rows, allowed, head_size)
    probs = jnp.exp(scores - log_total)
    value_heads_split = value_matrix_rows.reshape(-1, kv_heads, head_size)
    key_head_split = key_matrix_rows.reshape(-1, kv_heads, head_size)
    grouped_heads = query_matrix.reshape(total_row_count, kv_heads, -1, head_size)
    grad_grouped = mixed_grad.reshape(total_row_count, kv_heads, -1, head_size)
    prob_grad = jnp.einsum(
        "rhgd,khd->hgrk", grad_grouped, value_heads_split, preferred_element_type=jnp.float32
    )
    inner_sum = jnp.sum(probs * prob_grad, axis=-1, keepdims=True)
    score_grad = (probs * (prob_grad - inner_sum)).astype(jnp.bfloat16)
    score_scale = head_size ** (-0.5)
    query_grad = (
        jnp.einsum("hgrk,khd->rhgd", score_grad, key_head_split, preferred_element_type=jnp.float32)
        * score_scale
    )
    key_grad = (
        jnp.einsum("hgrk,rhgd->khd", score_grad, grouped_heads, preferred_element_type=jnp.float32)
        * score_scale
    )
    value_grad = jnp.einsum(
        "hgrk,rhgd->khd",
        probs.astype(jnp.bfloat16),
        grad_grouped,
        preferred_element_type=jnp.float32,
    )
    return (
        query_grad.reshape(total_row_count, -1),
        key_grad.reshape(key_matrix_rows.shape[0], -1),
        value_grad.reshape(value_matrix_rows.shape[0], -1),
    )


def rms_parts(values):
    return lax.rsqrt(jnp.mean(values * values, axis=-1, keepdims=True) + norm_eps)


def rms_backward(values, factor, scaling, normed_grad):
    scaled = scaling * normed_grad
    inner = jnp.mean(scaled * values, axis=-1, keepdims=True)
    values_grad = factor * scaled - values * (factor * factor * factor) * inner
    gain_grad = jnp.sum(normed_grad * values * factor, axis=0)
    return values_grad, gain_grad


def matmul(left_side, right_side):
    return jnp.dot(left_side, right_side, preferred_element_type=jnp.float32)


def on_device(
    tokens,
    routes,
    w_query,
    key_projection,
    value_projection,
    w_out,
    gain_attn,
    gain_ffn,
    w_router,
    w_gate,
    w_up,
    w_down,
    out_grad,
):
    bf16 = jnp.bfloat16
    shard_count = lax.axis_size("shard")
    seq_count = lax.axis_size("seq")
    shard_index = lax.axis_index("shard")
    seq_index = lax.axis_index("seq")
    tok_count, model_width = tokens.shape
    top_count = routes.shape[1]
    experts_all = w_router.shape[1]
    local_experts = w_gate.shape[0]
    block_len = tok_count * seq_count
    prompt_len = PROMPT_BLK * shard_count
    query_width = w_query.shape[1]
    key_width = key_projection.shape[1]

    small = jnp.concatenate([w_router, gain_attn[:, None], gain_ffn[:, None]], axis=1)
    small = lax.all_gather(small, "seq", axis=0, tiled=True)
    small = lax.all_gather(small, "shard", axis=0, tiled=True)
    router_weight = small[:, :experts_all]
    first_gain = small[:, experts_all].astype(jnp.float32)
    second_gain = small[:, experts_all + 1].astype(jnp.float32)
    block_tokens = lax.all_gather(tokens, "seq", axis=0, tiled=True)
    qkv_weight = lax.all_gather(
        jnp.concatenate([w_query, key_projection, value_projection], axis=1),
        "shard",
        axis=0,
        tiled=True,
    )
    out_weight = lax.all_gather(w_out, "seq", axis=0, tiled=True)
    out_weight = lax.all_gather(out_weight, "shard", axis=1, tiled=True)
    plane_grads = lax.all_gather(out_grad, "shard", axis=0, tiled=True)

    block_rows = jnp.arange(block_len, dtype=jnp.int32)
    cos_table, sin_table = rotary_tables(
        place_of(block_rows, shard_index, prompt_len), HEAD_DIMENSION
    )
    inputs = block_tokens.astype(jnp.float32)
    first_factor = rms_parts(inputs)
    normed_low = (inputs * first_factor * first_gain).astype(bf16)
    lin = matmul(normed_low, qkv_weight)
    query_heads = rotate(lin[:, :query_width], cos_table, sin_table, HEAD_DIMENSION).astype(bf16)
    key_heads = rotate(
        lin[:, query_width : query_width + key_width], cos_table, sin_table, HEAD_DIMENSION
    ).astype(bf16)
    value_heads = lin[:, query_width + key_width :].astype(bf16)
    prompt_both = lax.all_gather(
        jnp.concatenate([key_heads[:PROMPT_BLK], value_heads[:PROMPT_BLK]], axis=1),
        "shard",
        axis=0,
        tiled=True,
    )
    prompt_keys = prompt_both[:, :key_width]
    prompt_values = prompt_both[:, key_width:]
    key_places = jnp.arange(prompt_len, dtype=jnp.int32)
    prompt_allowed = (
        key_places[None, :]
        <= shard_index * PROMPT_BLK + jnp.arange(PROMPT_BLK, dtype=jnp.int32)[:, None]
    )
    wide_places = jnp.arange(prompt_len + CONT_LEN, dtype=jnp.int32)
    cont_allowed = (wide_places[None, :] < prompt_len) | (
        wide_places[None, :] - prompt_len <= jnp.arange(CONT_LEN, dtype=jnp.int32)[:, None]
    )
    cont_count = (block_len - PROMPT_BLK) // CONT_LEN
    mixed_piece, prompt_level = attend_forward(
        query_heads[:PROMPT_BLK], prompt_keys, prompt_values, prompt_allowed, HEAD_DIMENSION
    )
    mixed_parts = [mixed_piece]
    cont_levels = []
    cont_keys = []
    cont_values = []
    for number in range(cont_count):
        first_row = PROMPT_BLK + number * CONT_LEN
        last_row = first_row + CONT_LEN
        keys_all = jnp.concatenate([prompt_keys, key_heads[first_row:last_row]], axis=0)
        values_all = jnp.concatenate([prompt_values, value_heads[first_row:last_row]], axis=0)
        mixed_piece, cont_level = attend_forward(
            query_heads[first_row:last_row], keys_all, values_all, cont_allowed, HEAD_DIMENSION
        )
        mixed_parts.append(mixed_piece)
        cont_levels.append(cont_level)
        cont_keys.append(keys_all)
        cont_values.append(values_all)
    mixed_heads = jnp.concatenate(mixed_parts, axis=0).astype(bf16)
    mixed_tokens = lax.all_to_all(mixed_heads, "seq", split_axis=0, concat_axis=1, tiled=True)

    own_inputs = tokens.astype(jnp.float32)
    upstream = out_grad.astype(jnp.float32)
    residual = own_inputs + matmul(mixed_tokens, out_weight)
    second_factor = rms_parts(residual)
    second_low = (residual * second_factor * second_gain).astype(bf16)
    logits = matmul(second_low, router_weight)
    chosen = routes[:, :, None] == jnp.arange(experts_all, dtype=jnp.int32)[None, None, :]
    named = jnp.any(chosen, axis=1)
    gate_dense = jax.nn.softmax(jnp.where(named, logits, negative), axis=-1)
    gate_dense = jnp.where(named, gate_dense, 0.0)

    plane_rows = lax.all_gather(second_low, "shard", axis=0, tiled=True)
    plane_gates = lax.all_gather(gate_dense, "shard", axis=0, tiled=True)
    local_gates = lax.dynamic_slice_in_dim(
        plane_gates, shard_index * local_experts, local_experts, axis=1
    )
    expert_gates = local_gates.T[:, :, None]
    gate_pre = jnp.einsum("td,edf->etf", plane_rows, w_gate, preferred_element_type=jnp.float32)
    up_pre = jnp.einsum("td,edf->etf", plane_rows, w_up, preferred_element_type=jnp.float32)
    down_grad = jnp.einsum("td,efd->etf", plane_grads, w_down, preferred_element_type=jnp.float32)
    sigmoid = jax.nn.sigmoid(gate_pre)
    silu = gate_pre * sigmoid
    hidden = silu * up_pre
    gate_grad = jnp.sum(hidden * down_grad, axis=-1)
    hidden_low = (expert_gates * hidden).astype(bf16)
    hidden_grad = expert_gates * down_grad
    gate_pre_low = (hidden_grad * up_pre * sigmoid * (1.0 + gate_pre * (1.0 - sigmoid))).astype(bf16)
    up_pre_low = (hidden_grad * silu).astype(bf16)
    grad_down = jnp.einsum(
        "td,etf->edf", plane_grads, hidden_low, preferred_element_type=jnp.float32
    ).astype(bf16)
    grad_gate = jnp.einsum(
        "td,etf->edf", plane_rows, gate_pre_low, preferred_element_type=jnp.float32
    ).astype(bf16)
    grad_up = jnp.einsum(
        "td,etf->edf", plane_rows, up_pre_low, preferred_element_type=jnp.float32
    ).astype(bf16)
    row_part = (
        jnp.einsum("etf,edf->td", gate_pre_low, w_gate, preferred_element_type=jnp.float32)
        + jnp.einsum("etf,edf->td", up_pre_low, w_up, preferred_element_type=jnp.float32)
    ).astype(bf16)
    out_part = jnp.einsum(
        "etf,efd->td", hidden_low, w_down, preferred_element_type=jnp.float32
    ).astype(bf16)
    row_grad = lax.psum_scatter(row_part, "shard", scatter_dimension=0, tiled=True)
    gate_back = lax.all_to_all(
        gate_grad.reshape(local_experts, shard_count, tok_count).transpose(1, 0, 2),
        "shard",
        split_axis=0,
        concat_axis=0,
        tiled=True,
    )
    expert_sum = lax.psum_scatter(out_part, "shard", scatter_dimension=0, tiled=True)
    output = (residual + expert_sum.astype(jnp.float32)).astype(bf16)
    gate_grad_dense = gate_back.reshape(experts_all, tok_count).T
    weighted = gate_dense * gate_grad_dense
    logit_grad = weighted - gate_dense * jnp.sum(weighted, axis=-1, keepdims=True)
    grad_router = transposed_times(second_low.astype(jnp.float32), logit_grad, highest)
    second_grad = row_grad.astype(jnp.float32) + times_transposed(
        logit_grad, router_weight.astype(jnp.float32), highest
    )
    residual_part, grad_gain_ffn = rms_backward(residual, second_factor, second_gain, second_grad)
    residual_grad = upstream + residual_part
    residual_low = residual_grad.astype(bf16)
    mixed_grad_tokens = times_transposed(residual_low, out_weight).astype(bf16)
    mixed_grad = lax.all_to_all(mixed_grad_tokens, "seq", split_axis=1, concat_axis=0, tiled=True)
    whole_out = transposed_times(residual_low, mixed_tokens).astype(bf16)
    grad_out = lax.psum_scatter(whole_out, "shard", scatter_dimension=0, tiled=True)
    grad_out = lax.psum_scatter(grad_out, "seq", scatter_dimension=1, tiled=True)
    grad_out = grad_out.T.astype(jnp.float32)

    query_piece, prompt_key_grad, prompt_value_grad = attend_backward(
        query_heads[:PROMPT_BLK],
        prompt_keys,
        prompt_values,
        prompt_allowed,
        prompt_level,
        mixed_grad[:PROMPT_BLK],
        HEAD_DIMENSION,
    )
    query_parts = [query_piece]
    self_key_grads = []
    self_value_grads = []
    for number in range(cont_count):
        first_row = PROMPT_BLK + number * CONT_LEN
        last_row = first_row + CONT_LEN
        query_piece, key_piece, value_piece = attend_backward(
            query_heads[first_row:last_row],
            cont_keys[number],
            cont_values[number],
            cont_allowed,
            cont_levels[number],
            mixed_grad[first_row:last_row],
            HEAD_DIMENSION,
        )
        query_parts.append(query_piece)
        prompt_key_grad = prompt_key_grad + key_piece[:prompt_len]
        prompt_value_grad = prompt_value_grad + value_piece[:prompt_len]
        self_key_grads.append(key_piece[prompt_len:])
        self_value_grads.append(value_piece[prompt_len:])
    own_prompt = lax.psum_scatter(
        jnp.concatenate([prompt_key_grad, prompt_value_grad], axis=1).astype(bf16),
        "shard",
        scatter_dimension=0,
        tiled=True,
    ).astype(jnp.float32)
    query_grad = jnp.concatenate(query_parts, axis=0)
    key_grad = jnp.concatenate([own_prompt[:, :key_width]] + self_key_grads, axis=0)
    value_low = jnp.concatenate([own_prompt[:, key_width:]] + self_value_grads, axis=0).astype(bf16)
    lin_query = rotate(query_grad, cos_table, -sin_table, HEAD_DIMENSION).astype(bf16)
    lin_key = rotate(key_grad, cos_table, -sin_table, HEAD_DIMENSION).astype(bf16)
    lin_all = jnp.concatenate([lin_query, lin_key, value_low], axis=1)
    normed_part = times_transposed(lin_all, qkv_weight)
    normed_grad = lax.psum_scatter(
        normed_part.astype(bf16), "seq", scatter_dimension=0, tiled=True
    ).astype(jnp.float32)
    grad_qkv = lax.psum_scatter(
        transposed_times(normed_low, lin_all).astype(bf16),
        "shard",
        scatter_dimension=0,
        tiled=True,
    ).astype(jnp.float32)
    grad_query = grad_qkv[:, :query_width]
    grad_key = grad_qkv[:, query_width : query_width + key_width]
    grad_value = grad_qkv[:, query_width + key_width :]
    gain_part = jnp.sum(normed_part * inputs * first_factor, axis=0)
    own_factor = rms_parts(own_inputs)
    input_part, _ = rms_backward(own_inputs, own_factor, first_gain, normed_grad)
    tokens_grad = residual_grad + input_part
    small_grad = jnp.concatenate(
        [grad_router, gain_part[:, None], grad_gain_ffn[:, None]], axis=1
    ).astype(bf16)
    small_grad = lax.psum_scatter(small_grad, "shard", scatter_dimension=0, tiled=True)
    small_grad = lax.psum_scatter(small_grad, "seq", scatter_dimension=0, tiled=True)
    small_grad = small_grad.astype(jnp.float32)
    grad_gate = lax.psum_scatter(grad_gate, "seq", scatter_dimension=1, tiled=True)
    grad_up = lax.psum_scatter(grad_up, "seq", scatter_dimension=1, tiled=True)
    grad_down = lax.psum_scatter(grad_down, "seq", scatter_dimension=1, tiled=True)
    return (
        output,
        tokens_grad,
        grad_query,
        grad_key,
        grad_value,
        grad_out,
        small_grad[:, experts_all],
        small_grad[:, experts_all + 1],
        small_grad[:, :experts_all],
        grad_gate.astype(jnp.float32),
        grad_up.astype(jnp.float32),
        grad_down.transpose(0, 2, 1).astype(jnp.float32),
    )


def solution(mesh):
    return jax.shard_map(
        on_device,
        mesh=mesh,
        in_specs=(
            P(("shard", "seq"), None),
            P(("shard", "seq"), None),
            P("shard", "seq"),
            P("shard", "seq"),
            P("shard", "seq"),
            P("seq", "shard"),
            P(("shard", "seq")),
            P(("shard", "seq")),
            P(("shard", "seq"), None),
            P("shard", None, None),
            P("shard", None, None),
            P("shard", None, None),
            P(("shard", "seq"), None),
        ),
        out_specs=(
            P(("shard", "seq"), None),
            P(("shard", "seq"), None),
            P("shard", "seq"),
            P("shard", "seq"),
            P("shard", "seq"),
            P("seq", "shard"),
            P(("shard", "seq")),
            P(("shard", "seq")),
            P(("shard", "seq"), None),
            P("shard", "seq", None),
            P("shard", "seq", None),
            P("shard", None, "seq"),
        ),
        check_vma=False,
    )
```

time: 1780 us -> 1140 us (0.64)
  waiting for transfers between devices: 818 us -> 605 us
  blocking collectives: 266 us -> 103 us
  local copies, waits for them, and re-layouts: 213 us -> 69.4 us
  starting transfers between devices: 51 us -> 5.49 us
  other arithmetic: 122 us -> 76.6 us
  matrix products: 282 us -> 256 us
    all_to_all x10 -> x0, waiting for transfers between devices: 321 us -> none  [the longest x1 93.6 us: on_device(): lax.all_to_all(slot_grads.reshape(shard_count, -1, model_width), 'shard',...]
    all_gather x8 -> x5, blocking collectives: 204 us -> 67.6 us  [the longest x1 24.3 us: on_device(): out_weight = lax.all_gather(w_out, 'seq', axis=0, tiled=True)]
    all_gather x4 -> x5, waiting for transfers between devices: 0.04 us -> 110 us  [the longest x1 34.8 us: on_device(): plane_rows = lax.all_gather(second_low, 'shard', axis=0, tiled=True)]
    gather x4 -> x0, local copies, waits for them, and re-layouts: 90.5 us -> none  [the longest x1 26.1 us: on_device(): jnp.concatenate([entry_grads, blank_row], axis=0)[entry_of_slot]]
    reduce_scatter x8 -> x5, waiting for transfers between devices: 283 us -> 229 us  [the longest x1 66.4 us: on_device(): lax.psum_scatter(normed_part.astype(bf16), 'seq', scatter_dimension=0, ti...]
    unnamed x26 -> x24, waiting for transfers between devices: 196 us -> 247 us
    unnamed x4 -> x0, blocking collectives: 48.1 us -> none
    all_to_all x10 -> x0, starting transfers between devices: 46.4 us -> none  [the longest x1 5.61 us: on_device(): lax.all_to_all(expert_out.reshape(shard_count, -1, model_width), 'shard',...]
  transfers between devices with their start and end apart: 30 -> 18, of which waited for: 18 -> 16; matrix products, arithmetic and copies ran while one was open for 26% -> 21% of each run, Pallas kernels for 0% -> 0%
where the time goes in v1:
time: 1140 us; the launch traced here: 1130 us
  waiting for transfers between devices  605 us (53%)
  matrix products  256 us (22%)
  blocking collectives  103 us (9%)
  other arithmetic  76.6 us (7%)
  local copies, waits for them, and re-layouts  69.4 us (6%)
  between operations  15.6 us (1%)
    unnamed x24, waiting for transfers between devices  247 us
    reduce_scatter x1, waiting for transfers between devices, on_device(): lax.psum_scatter(normed_part.astype(bf16), 'seq', scatter_dimension=0, ti...  66.4 us
    reduce_scatter x1, waiting for transfers between devices, on_device(): lax.psum_scatter(out_part, 'shard', scatter_dimension=0, tiled=True)  65.4 us
    unnamed x146, local copies, waits for them, and re-layouts  52.4 us
    reduce_scatter x1, waiting for transfers between devices, on_device(): lax.psum_scatter(row_part, 'shard', scatter_dimension=0, tiled=True)  45.8 us
    reduce_scatter x1, waiting for transfers between devices, on_device(): lax.psum_scatter(transposed_times(normed_low, lin_all).astype(bf16), 'sha...  39.6 us
    all_gather x1, waiting for transfers between devices, on_device(): plane_rows = lax.all_gather(second_low, 'shard', axis=0, tiled=True)  34.8 us
    convert_element_type x3, other arithmetic, attend_backward(): score_grad = (probs * (prob_grad - inner_sum)).astype(jnp.bfloat16)  27.8 us
  transfers between devices with their start and end apart: 18, of which 16 were waited for; matrix products, arithmetic and copies ran while one was open for 21% of the time, Pallas kernels for 0%

profile of v1, /device:TPU:0, one launch (start us, length us, event | category | flops | bytes accessed | tf_op | source)
XLA Modules:
  0.0 1130.8 jit_solution(790183203877107098)
XLA Ops:
  9.9 24.3 %all_gather.35 = bf16[1536,192]{0,1:T(8,128)(2,1)} all-gather(bf16[384,192]{0,1:T(8,128)(2,1)} %param.18), channel_id=1, replica_groups=mesh['shard'=8,'seq'=4] {'seq'}, dimensions={0}, use_global_device_ids=true | all-gather | bytes 737280 | tf_op jit(solution)/shard_map/all_gather | solution.py:201
  35.1 13.7 %all-gather = bf16[4,48,18]{1,2,0:T(8,128)(2,1)S(1)} all-gather(bf16[1,48,18]{1,2,0:T(8,128)(2,1)S(1)} %maximum_bitcast_fusion), channel_id=1, replica_groups=mesh['shard'=8,'seq'=4] {'seq'}, dimensions={0}, use_global_device_ids=true | all-gather | bytes 8640 | tf_op jit(solution)/shard_map/all_gather | solution.py:189
  48.9 9.0 all-gather.1
  62.5 23.4 %all-gather.9.cloned.1.call-done = bf16[1152,1536]{1,0:T(8,128)(2,1)} async-done(((bf16[288,1536]{1,0:T(8,128)(2,1)}), bf16[1152,1536]{1,0:T(8,128)(2,1)}) %all-gather.9.cloned.1.call-update) | async-done | bytes 3538960 | tf_op jit(solution)/shard_map/all_gather | solution.py:194
  85.9 2.8 fusion.27
  88.7 26.0 %all-gather.11.cloned.1.call-done = bf16[1536,640]{1,0:T(8,128)(2,1)} async-done(((bf16[192,640]{1,0:T(8,128)(2,1)}), bf16[1536,640]{1,0:T(8,128)(2,1)}) %all-gather.11.cloned.1.call-update) | async-done | bytes 1966096 | tf_op jit(solution)/shard_map/all_gather | solution.py:195
  114.7 5.7 fusion.134
  121.1 12.3 %all_gather.34 = bf16[1024,256]{0,1:T(8,128)(2,1)S(1)} all-gather(bf16[128,256]{0,1:T(8,128)(2,1)S(1)} %pad_maximum_fusion.17), channel_id=1, replica_groups=mesh['shard'=8,'seq'=4] {'shard'}, dimensions={0}, use_global_device_ids=true | all-gather | bytes 589824 | tf_op jit(solution)/shard_map/all_gather | solution.py:218
  138.0 8.3 fusion.135
  146.4 9.6 fusion.7
  156.0 3.2 fusion.106
  160.8 10.4 fusion.87
  173.2 9.5 fusion.136
  182.7 9.5 fusion.6
  192.2 8.9 fusion.88
  203.4 27.4 %all_to_all.40 = bf16[4,288,384]{2,1,0:T(8,128)(2,1)S(1)} all-to-all(bf16[4,288,384]{2,1,0:T(8,128)(2,1)S(1)} %bitcast.381), channel_id=1, replica_groups=mesh['shard'=8,'seq'=4] {'seq'}, dimensions={0} | all-to-all | bytes 1769472 | tf_op jit(solution)/shard_map/all_to_all | solution.py:256
  231.8 4.5 multiply_reduce_fusion.2
  241.0 8.2 all-gather.2
  251.0 34.8 %all-gather.15.cloned.1.call-done = bf16[2304,1536]{1,0:T(8,128)(2,1)} async-done(((bf16[288,1536]{1,0:T(8,128)(2,1)}), bf16[2304,1536]{1,0:T(8,128)(2,1)}) %all-gather.15.cloned.1.call-update) | async-done | bytes 7077904 | tf_op jit(solution)/shard_map/all_gather | solution.py:269
  285.8 14.2 %fusion.40 = f32[2304,2,512]{0,2,1:T(8,128)} fusion(bf16[2,1536,512]{2,1,0:T(8,128)(2,1)} %param.23, bf16[2304,1536]{1,0:T(8,128)(2,1)} %all-gather.15.cloned.1.call-done), kind=kOutput, calls=%fused_computation.65 | convolution fusion | flops 7247757312 | bytes 19660800 | tf_op jit(solution)/shard_map/td,edf->etf/dot_general | solution.py:276
  300.0 10.0 fusion.42
  310.0 26.3 %all-gather.17.cloned.1.call-done = bf16[2304,1536]{1,0:T(8,128)(2,1)} async-done(((bf16[288,1536]{1,0:T(8,128)(2,1)}), bf16[2304,1536]{1,0:T(8,128)(2,1)}) %all-gather.17.cloned.1.call-update) | async-done | bytes 7077904 | tf_op jit(solution)/shard_map/all_gather | solution.py:203
  336.3 20.3 %fusion.15 = (f32[2,2304]{1,0:T(2,128)S(1)}, bf16[2,2304,512]{1,2,0:T(8,128)(2,1)}, bf16[2,2304,512]{1,2,0:T(8,128)(2,1)}, bf16[2,2304,512]{1,2,0:T(8,128)(2,1)}) fusion(f32[2304,2,512]{0,2,1:T(8,128)} %fusion.40, f32[2304,2,512]{0,2,1:T(8,128)} %fusion.42, f32[2,2304]{1,0:T(2,128)S(1)} %dynamic-slice_bitcast_fusion, bf16[2,512,1536]{2,1,0:T(8,128)(2,1)S(1)} %copy-done, ...), kind=kOutput, calls=%fused_computation.32 | convolution fusion | flops 7292579328 | bytes 43290624 | tf_op jit(solution)/shard_map/td,efd->etf/dot_general | solution.py:277
  356.6 13.8 %fusion.139 = f32[2304,1536,1]{1,0,2:T(8,128)} fusion(bf16[2,2304,512]{1,2,0:T(8,128)(2,1)} %get-tuple-element.79, bf16[2,1536,512]{2,1,0:T(8,128)(2,1)} %param.22), kind=kOutput, calls=%fused_computation.231 | convolution fusion | flops 7247757312 | bytes 22020096 | tf_op jit(solution)/shard_map/etf,edf->td/dot_general | solution.py:296
  370.3 12.5 %fusion.10 = bf16[2304,1536]{1,0:T(8,128)(2,1)} fusion(f32[2304,1536,1]{1,0,2:T(8,128)} %fusion.139, bf16[2,2304,512]{1,2,0:T(8,128)(2,1)S(1)} %copy-done.60, bf16[2,1536,512]{2,1,0:T(8,128)(2,1)S(1)} %copy-done.59), kind=kOutput, calls=%fused_computation.23 | convolution fusion | flops 7254835200 | bytes 29097984 | tf_op jit(solution)/shard_map/etf,edf->td/dot_general | solution.py:297
  382.9 12.0 %bitcast_convert_fusion = bf16[2304,1536]{1,0:T(8,128)(2,1)} fusion(bf16[2,2304,512]{1,2,0:T(8,128)(2,1)} %get-tuple-element.80, bf16[2,512,1536]{2,1,0:T(8,128)(2,1)S(1)} %copy-done), kind=kOutput, calls=%fused_computation.24 | convolution fusion | flops 7251296256 | bytes 14942208 | tf_op jit(solution)/shard_map/etf,efd->td/dot_general | solution.py:299
  395.1 7.6 all_to_all.41
  402.7 45.8 %reduce-scatter.29.cloned.1.call-done = bf16[288,1536]{1,0:T(8,128)(2,1)} async-done(((bf16[2304,1536]{1,0:T(8,128)(2,1)}), bf16[288,1536]{1,0:T(8,128)(2,1)}) %reduce-scatter.29.cloned.1.call-update) | async-done | bytes 884752 | tf_op jit(solution)/shard_map/reduce_scatter | solution.py:302
  448.6 3.7 multiply_reduce_fusion
  452.2 65.4 %reduce-scatter.27.cloned.1.call-done = bf16[288,1536]{1,0:T(8,128)(2,1)} async-done(((bf16[2304,1536]{1,0:T(8,128)(2,1)}), bf16[288,1536]{1,0:T(8,128)(2,1)}) %reduce-scatter.27.cloned.1.call-update) | async-done | bytes 884752 | tf_op jit(solution)/shard_map/reduce_scatter | solution.py:310
  517.6 3.2 subtract_add_fusion
  520.8 4.5 convolution_convert_fusion.2
  526.4 4.6 all-to-all-start.2
  534.0 19.1 %all-to-all-done.2 = bf16[288,4,384]{2,0,1:T(8,128)(2,1)S(1)} async-done(((bf16[288,4,384]{2,0,1:T(8,128)(2,1)}), bf16[288,4,384]{2,0,1:T(8,128)(2,1)S(1)}, u32[]{:S(2)}, u32[]{:S(2)}) %all-to-all-start.2) | async-done | bytes 884768 | tf_op jit(solution)/shard_map/all_to_all | solution.py:323
  555.1 8.4 fusion.70
  564.1 8.1 fusion.67
  574.6 11.9 %fusion.3 = (f32[2,3,512]{2,1,0:T(4,128)S(1)}, f32[2,1536,512,3]{2,1,3,0:T(8,128)}) fusion(f32[2,3,512,1536]{2,3,1,0:T(8,128)} %get-tuple-element.126, f32[2,3,512]{2,1,0:T(4,128)S(1)} %copy-done.38, bf16[1536,2,64,1]{0,2,3,1:T(8,128)(2,1)S(1)} %bitcast.399, bf16[512,2,3,64]{0,3,2,1:T(8,128)(2,1)S(1)} %bitcast.378), kind=kOutput, calls=%fused_computation.7 | convolution fusion | flops 618132480 | bytes 38559744 | tf_op jit(solution)/shard_map/rhgd,khd->hgrk/dot_general | solution.py:116
  586.5 13.4 %fusion.5 = bf16[2,3,512,1536]{2,3,1,0:T(8,128)(2,1)S(1)} fusion(f32[2,1536,512,3]{2,1,3,0:T(8,128)} %get-tuple-element.139, f32[2,3,512,1536]{2,3,1,0:T(8,128)} %get-tuple-element.126, f32[2,3,512]{2,1,0:T(4,128)S(1)} %get-tuple-element.138, f32[2,3,512]{2,1,0:T(4,128)S(1)} %copy-done.38), kind=kLoop, calls=%fused_computation.9 | loop fusion | flops 18874368 | bytes 47210496 | tf_op jit(solution)/shard_map/convert_element_type | solution.py:120
  599.9 2.9 fusion.76
  602.9 2.6 convolution_multiply_fusion.1
  605.5 11.7 %fusion = (f32[2,3,512]{2,1,0:T(4,128)S(1)}, f32[2,1536,512,3]{2,1,3,0:T(8,128)}) fusion(f32[2,3,512,1536]{2,3,1,0:T(8,128)} %get-tuple-element.124, f32[2,3,512]{2,1,0:T(4,128)S(1)} %log_add_fusion, bf16[1536,2,64,1]{0,2,3,1:T(8,128)(2,1)S(1)} %bitcast.397, bf16[512,2,3,64]{0,3,2,1:T(8,128)(2,1)S(1)} %bitcast.376), kind=kOutput, calls=%fused_computation.2 | convolution fusion | flops 618132480 | bytes 38559744 | tf_op jit(solution)/shard_map/rhgd,khd->hgrk/dot_general | solution.py:116
  617.3 13.5 %fusion.2 = bf16[2,3,512,1536]{2,3,1,0:T(8,128)(2,1)S(1)} fusion(f32[2,1536,512,3]{2,1,3,0:T(8,128)} %get-tuple-element.137, f32[2,3,512,1536]{2,3,1,0:T(8,128)} %get-tuple-element.124, f32[2,3,512]{2,1,0:T(4,128)S(1)} %get-tuple-element.136, f32[2,3,512]{2,1,0:T(4,128)S(1)} %log_add_fusion), kind=kLoop, calls=%fused_computation.4 | loop fusion | flops 18874368 | bytes 47210496 | tf_op jit(solution)/shard_map/convert_element_type | solution.py:120
  630.8 2.9 fusion.74
  633.8 2.6 convolution_multiply_fusion
  642.4 29.5 %reduce-scatter.37.cloned.1.call-done = bf16[128,256]{1,0:T(8,128)(2,1)} async-done(((bf16[1024,256]{1,0:T(8,128)(2,1)}), bf16[128,256]{1,0:T(8,128)(2,1)}) %reduce-scatter.37.cloned.1.call-update) | async-done | bytes 65552
  673.2 8.4 fusion.31
  682.8 4.3 convolution_convert_fusion
  687.1 12.6 %fusion.53 = bf16[2,1536,512]{1,2,0:T(8,128)(2,1)} fusion(bf16[2,2304,512]{1,2,0:T(8,128)(2,1)} %get-tuple-element.80, bf16[2304,1536]{1,0:T(8,128)(2,1)} %all-gather.17.cloned.1.call-done), kind=kOutput, calls=%fused_computation.72 | convolution fusion | flops 7249330176 | bytes 14942208 | tf_op jit(solution)/shard_map/td,etf->edf/dot_general | solution.py:286
  699.7 7.1 copy.212
  709.5 12.3 %fusion.59 = bf16[2,1536,512]{1,2,0:T(8,128)(2,1)} fusion(bf16[2,2304,512]{1,2,0:T(8,128)(2,1)} %get-tuple-element.79, bf16[2304,1536]{1,0:T(8,128)(2,1)} %all-gather.15.cloned.1.call-done), kind=kOutput, calls=%fused_computation.74 | convolution fusion | flops 7249330176 | bytes 14942208 | tf_op jit(solution)/shard_map/td,etf->edf/dot_general | solution.py:289
  721.8 7.2 copy.208
  731.5 12.7 %fusion.56 = bf16[2,1536,512]{1,2,0:T(8,128)(2,1)} fusion(bf16[2,2304,512]{1,2,0:T(8,128)(2,1)} %get-tuple-element.81, bf16[2304,1536]{1,0:T(8,128)(2,1)} %all-gather.15.cloned.1.call-done), kind=kOutput, calls=%fused_computation.73 | convolution fusion | flops 7249330176 | bytes 14942208 | tf_op jit(solution)/shard_map/td,etf->edf/dot_general | solution.py:292
  744.3 7.1 copy.210
  754.8 7.2 convolution_convert_fusion.1
  762.1 11.8 %reduce-scatter.35.cloned.1.call-done = bf16[192,1536]{1,0:T(8,128)(2,1)} async-done(((bf16[1536,1536]{1,0:T(8,128)(2,1)}), bf16[192,1536]{1,0:T(8,128)(2,1)}) %reduce-scatter.35.cloned.1.call-update) | async-done | bytes 589840 | tf_op jit(solution)/shard_map/reduce_scatter | solution.py:325
  776.7 59.9 %reduce-scatter.49.cloned.1.call-done = bf16[384,1024]{1,0:T(8,128)(2,1)} async-done(((bf16[1536,1024]{1,0:T(8,128)(2,1)}), bf16[384,1024]{1,0:T(8,128)(2,1)}) %reduce-scatter.49.cloned.1.call-update) | async-done | bytes 786448
  836.6 2.6 reshape.439
  839.9 59.2 %reduce-scatter.45.cloned.1.call-done = bf16[384,1024]{1,0:T(8,128)(2,1)} async-done(((bf16[1536,1024]{1,0:T(8,128)(2,1)}), bf16[384,1024]{1,0:T(8,128)(2,1)}) %reduce-scatter.45.cloned.1.call-update) | async-done | bytes 786448
  902.4 59.4 %reduce-scatter.47.cloned.1.call-done = bf16[384,1024]{1,0:T(8,128)(2,1)} async-done(((bf16[1536,1024]{1,0:T(8,128)(2,1)}), bf16[384,1024]{1,0:T(8,128)(2,1)}) %reduce-scatter.47.cloned.1.call-update) | async-done | bytes 786448
  969.2 13.9 %reduce-scatter.43.cloned.1.call-done = bf16[48,18]{1,0:T(8,128)(2,1)} async-done(((bf16[192,18]{1,0:T(8,128)(2,1)}), bf16[48,18]{1,0:T(8,128)(2,1)}) %reduce-scatter.43.cloned.1.call-update) | async-done | bytes 1744
  985.0 39.6 %reduce-scatter.33.cloned.1.call-done = bf16[192,640]{1,0:T(8,128)(2,1)} async-done(((bf16[1536,640]{1,0:T(8,128)(2,1)}), bf16[192,640]{1,0:T(8,128)(2,1)}) %reduce-scatter.33.cloned.1.call-update) | async-done | bytes 245776 | tf_op jit(solution)/shard_map/reduce_scatter | solution.py:374
  1027.8 22.2 %reduce-scatter.39.cloned.1.call-done = bf16[384,192]{1,0:T(8,128)(2,1)} async-done(((bf16[1536,192]{1,0:T(8,128)(2,1)}), bf16[384,192]{1,0:T(8,128)(2,1)}) %reduce-scatter.39.cloned.1.call-update) | async-done | bytes 147472
  1051.8 66.4 %reduce-scatter.31.cloned.1.call-done = bf16[288,1536]{1,0:T(8,128)(2,1)} async-done(((bf16[1152,1536]{1,0:T(8,128)(2,1)}), bf16[288,1536]{1,0:T(8,128)(2,1)}) %reduce-scatter.31.cloned.1.call-update) | async-done | bytes 884752 | tf_op jit(solution)/shard_map/reduce_scatter | solution.py:371
  1120.1 3.7 fusion.81
  (268 shorter events, 75.4 us)
Async XLA Ops:
  7.2 329.1 %copy-start = (bf16[2,512,1536]{2,1,0:T(8,128)(2,1)S(1)}, bf16[2,512,1536]{2,1,0:T(8,128)(2,1)}, u32[]{:S(2)}) copy-start(bf16[2,512,1536]{2,1,0:T(8,128)(2,1)} %param.24) | copy-start | bytes 9437188
  7.2 78.7 %all-gather.9.cloned.1.call-start = ((), (), s32[]{:S(2)}) async-start(), calls=%async_computation.15 | async-start | bytes 4423680 | tf_op jit(solution)/shard_map/all_gather | solution.py:194
  7.9 106.8 %all-gather.11.cloned.1.call-start = ((), (), s32[]{:S(2)}) async-start(), calls=%async_computation.16 | async-start | bytes 2211840 | tf_op jit(solution)/shard_map/all_gather | solution.py:195
  9.8 222.0 %all-gather.13.cloned.1.call-start = ((), (), s32[]{:S(2)}) async-start(), calls=%async_computation.17 | async-start | bytes 5308416 | tf_op jit(solution)/shard_map/all_gather | solution.py:202
  34.2 251.6 %all-gather.15.cloned.1.call-start = ((), (), s32[]{:S(2)}) async-start(), calls=%async_computation.18 | async-start | bytes 7962624 | tf_op jit(solution)/shard_map/all_gather | solution.py:269
  58.7 61.7 %copy-start.45 = (f32[1536]{0:T(1024)}, f32[1536]{0:T(1024)S(1)}, u32[]{:S(2)}) copy-start(f32[1536]{0:T(1024)S(1)} %get-tuple-element.77) | copy-start | bytes 18436
  60.7 60.0 %copy-start.18 = (f32[1152,32]{0,1:T(8,128)}, f32[1152,32]{0,1:T(8,128)S(1)}, u32[]{:S(2)}) copy-start(f32[1152,32]{0,1:T(8,128)S(1)} %get-tuple-element.116) | copy-start | bytes 442372
  88.7 31.7 %copy-start.55 = (f32[1152]{0:T(1024)}, f32[1152]{0:T(1024)S(1)}, u32[]{:S(2)}) copy-start(f32[1152]{0:T(1024)S(1)} %add_rsqrt_fusion) | copy-start | bytes 13828
  120.7 12.8 %copy-start.35 = (pred[128,1024]{0,1:T(8,128)(4,1)S(1)}, pred[128,1024]{0,1:T(8,128)(4,1)}, u32[]{:S(2)}) copy-start(pred[128,1024]{0,1:T(8,128)(4,1)} %iota_compare_fusion.1) | copy-start | bytes 393220
  121.0 13.2 %copy-start.32 = (bf16[128,6,64]{0,2,1:T(8,128)(2,1)}, bf16[128,6,64]{0,2,1:T(8,128)(2,1)S(1)}, u32[]{:S(2)}) copy-start(bf16[128,6,64]{0,2,1:T(8,128)(2,1)S(1)} %pad_maximum_fusion.15) | copy-start | bytes 294916
  121.1 16.9 %copy-start.12 = (bf16[512,6,64]{0,2,1:T(8,128)(2,1)}, bf16[512,6,64]{0,2,1:T(8,128)(2,1)S(1)}, u32[]{:S(2)}) copy-start(bf16[512,6,64]{0,2,1:T(8,128)(2,1)S(1)} %get-tuple-element.97) | copy-start | bytes 1179652
  121.1 52.1 %copy-start.14 = (bf16[512,6,64]{0,2,1:T(8,128)(2,1)}, bf16[512,6,64]{0,2,1:T(8,128)(2,1)S(1)}, u32[]{:S(2)}) copy-start(bf16[512,6,64]{0,2,1:T(8,128)(2,1)S(1)} %get-tuple-element.96) | copy-start | bytes 1179652
  133.5 4.5 copy-start.16
  133.5 4.5 copy-start.25
  138.0 8.4 copy-start.22
  146.4 14.5 %copy-start.40 = (f32[2,3,512]{2,1,0:T(4,128)}, f32[2,3,512]{2,1,0:T(4,128)S(1)}, u32[]{:S(2)}) copy-start(f32[2,3,512]{2,1,0:T(4,128)S(1)} %get-tuple-element.123) | copy-start | bytes 36868
  182.7 9.5 copy-start.42
  182.7 9.5 copy-start.28
  231.8 5.8 copy-start.44
  238.7 97.6 %all-gather.17.cloned.1.call-start = ((), (), s32[]{:S(2)}) async-start(), calls=%async_computation.20 | async-start | bytes 7962624 | tf_op jit(solution)/shard_map/all_gather | solution.py:203
  239.3 209.2 %reduce-scatter.29.cloned.1.call-start = ((), (), s32[]{:S(2)}) async-start(), calls=%async_computation.21 | async-start | bytes 7962624 | tf_op jit(solution)/shard_map/reduce_scatter | solution.py:302
  285.8 14.2 %copy-start.57 = (bf16[2304,1536]{1,0:T(8,128)(2,1)S(1)}, bf16[2304,1536]{1,0:T(8,128)(2,1)}, u32[]{:S(2)}) copy-start(bf16[2304,1536]{1,0:T(8,128)(2,1)} %all-gather.15.cloned.1.call-done) | copy-start | bytes 21233668
  285.8 14.2 %copy-start.58 = (bf16[2,1536,512]{2,1,0:T(8,128)(2,1)S(1)}, bf16[2,1536,512]{2,1,0:T(8,128)(2,1)}, u32[]{:S(2)}) copy-start(bf16[2,1536,512]{2,1,0:T(8,128)(2,1)} %param.22) | copy-start | bytes 9437188
  356.6 13.8 %copy-start.59 = (bf16[2,1536,512]{2,1,0:T(8,128)(2,1)S(1)}, bf16[2,1536,512]{2,1,0:T(8,128)(2,1)}, u32[]{:S(2)}) copy-start(bf16[2,1536,512]{2,1,0:T(8,128)(2,1)} %param.23) | copy-start | bytes 9437188
  356.6 13.8 %copy-start.60 = (bf16[2,2304,512]{1,2,0:T(8,128)(2,1)S(1)}, bf16[2,2304,512]{1,2,0:T(8,128)(2,1)}, u32[]{:S(2)}) copy-start(bf16[2,2304,512]{1,2,0:T(8,128)(2,1)} %get-tuple-element.81) | copy-start | bytes 14155780
  382.9 134.7 %reduce-scatter.27.cloned.1.call-start = ((), (), s32[]{:S(2)}) async-start(), calls=%async_computation.19 | async-start | bytes 7962624 | tf_op jit(solution)/shard_map/reduce_scatter | solution.py:310
  394.9 53.6 %copy-start.6 = (f32[288,1536]{1,0:T(8,128)S(1)}, f32[288,1536]{1,0:T(8,128)}, u32[]{:S(2)}) copy-start(f32[288,1536]{1,0:T(8,128)} %copy-done.5) | copy-start | bytes 5308420
  394.9 122.7 %copy-start.21 = (bf16[288,1536]{1,0:T(8,128)(2,1)S(1)}, bf16[288,1536]{1,0:T(8,128)(2,1)}, u32[]{:S(2)}) copy-start(bf16[288,1536]{1,0:T(8,128)(2,1)} %param.25) | copy-start | bytes 2654212
  520.8 4.5 copy-start.8
  525.3 5.7 copy-start.51
  525.3 5.7 copy-start.53
  525.4 6.2 copy-start.41
  525.4 6.2 copy-start.47
  525.4 6.3 copy-start.43
  525.4 6.3 copy-start.48
  525.4 6.9 copy-start.7
  526.4 26.6 %all-to-all-start.2 = ((bf16[288,4,384]{2,0,1:T(8,128)(2,1)}), bf16[288,4,384]{2,0,1:T(8,128)(2,1)S(1)}, u32[]{:S(2)}, u32[]{:S(2)}) async-start(bf16[288,4,384]{2,0,1:T(8,128)(2,1)} %bitcast.361), calls=%async_computation.4 | async-start | bytes 1769472 | tf_op jit(solution)/shard_map/all_to_all | solution.py:323
  531.0 140.9 %reduce-scatter.37.cloned.1.call-start = ((), (), s32[]{:S(2)}) async-start(), calls=%async_computation.25 | async-start | bytes 589824
  555.0 9.1 copy-start.20
  555.1 9.1 copy-start.38
  564.1 8.8 copy-start.3
  564.1 8.8 copy-start.34
  564.1 8.8 copy-start.49
  586.5 13.4 %copy-start.15 = (bf16[512,6,64]{0,2,1:T(8,128)(2,1)S(1)}, bf16[512,6,64]{0,2,1:T(8,128)(2,1)}, u32[]{:S(2)}) copy-start(bf16[512,6,64]{0,2,1:T(8,128)(2,1)} %copy-done.14) | copy-start | bytes 1179652
  602.9 34.9 %copy-start.10 = (f32[1536,2,64]{0,2,1:T(8,128)}, f32[1536,2,64]{0,2,1:T(8,128)S(1)}, u32[]{:S(2)}) copy-start(f32[1536,2,64]{0,2,1:T(8,128)S(1)} %fusion.76) | copy-start | bytes 2359300
  617.3 13.6 %copy-start.13 = (bf16[512,6,64]{0,2,1:T(8,128)(2,1)S(1)}, bf16[512,6,64]{0,2,1:T(8,128)(2,1)}, u32[]{:S(2)}) copy-start(bf16[512,6,64]{0,2,1:T(8,128)(2,1)} %copy-done.12) | copy-start | bytes 1179652
  633.8 4.6 copy-start.11
  639.6 114.5 %reduce-scatter.41.cloned.1.call-start = ((), (), s32[]{:S(2)}) async-start(), calls=%async_computation.27 | async-start | bytes 442368
  639.6 33.4 %slice-start = ((f32[1536,2,64]{0,2,1:T(8,128)}), f32[512,2,64]{0,2,1:T(8,128)S(1)}, s32[]{:S(2)}) async-start(f32[1536,2,64]{0,2,1:T(8,128)} %copy-done.10), calls=%async_computation.32 | async-start | bytes 524288 | tf_op jit(solution)/shard_map/slice | solution.py:356
  639.6 33.4 %slice-start.1 = ((f32[1536,2,64]{0,2,1:T(8,128)}), f32[512,2,64]{0,2,1:T(8,128)S(1)}, s32[]{:S(2)}) async-start(f32[1536,2,64]{0,2,1:T(8,128)} %copy-done.11), calls=%async_computation.33 | async-start | bytes 524288 | tf_op jit(solution)/shard_map/slice | solution.py:356
  641.2 32.0 %copy-start.56 = (f32[1152]{0:T(1024)S(1)}, f32[1152]{0:T(1024)}, u32[]{:S(2)}) copy-start(f32[1152]{0:T(1024)} %copy-done.55) | copy-start | bytes 13828
  673.2 8.5 copy-start.39
  673.2 8.5 copy-start.52
  673.2 9.5 copy-start.9
  673.2 9.5 copy-start.31
  682.7 91.2 %reduce-scatter.35.cloned.1.call-start = ((), (), s32[]{:S(2)}) async-start(), calls=%async_computation.24 | async-start | bytes 5308416 | tf_op jit(solution)/shard_map/reduce_scatter | solution.py:325
  687.1 149.5 %reduce-scatter.49.cloned.1.call-start = ((), (), s32[]{:S(2)}) async-start(), calls=%async_computation.31 | async-start | bytes 3932160
  709.5 189.6 %reduce-scatter.45.cloned.1.call-start = ((), (), s32[]{:S(2)}) async-start(), calls=%async_computation.29 | async-start | bytes 3932160
  731.5 230.3 %reduce-scatter.47.cloned.1.call-start = ((), (), s32[]{:S(2)}) async-start(), calls=%async_computation.30 | async-start | bytes 3932160
  753.9 229.2 %reduce-scatter.43.cloned.1.call-start = ((), (), s32[]{:S(2)}) async-start(), calls=%async_computation.28 | async-start | bytes 61440
  754.5 270.1 %reduce-scatter.33.cloned.1.call-start = ((), (), s32[]{:S(2)}) async-start(), calls=%async_computation.23 | async-start | bytes 2211840 | tf_op jit(solution)/shard_map/reduce_scatter | solution.py:374
  762.1 287.9 %reduce-scatter.39.cloned.1.call-start = ((), (), s32[]{:S(2)}) async-start(), calls=%async_computation.26 | async-start | bytes 983040
  776.1 342.1 %reduce-scatter.31.cloned.1.call-start = ((), (), s32[]{:S(2)}) async-start(), calls=%async_computation.22 | async-start | bytes 4423680 | tf_op jit(solution)/shard_map/reduce_scatter | solution.py:371
  1051.1 72.8 %copy-start.1 = (bf16[2,512,1536]{2,1,0:T(8,128)(2,1)S(1)}, bf16[2,512,1536]{2,1,0:T(8,128)(2,1)}, u32[]{:S(2)}) copy-start(bf16[2,512,1536]{2,1,0:T(8,128)(2,1)} %param.24) | copy-start | bytes 9437188
  (17 other events, 39.3 us)
Sparse Core Ops, SparseCore 0:
  9.6 76.3 all-gather.8
  88.4 26.2 all-gather.10
  116.6 40.1 all-gather.12
  238.9 46.8 all-gather.14
  287.5 48.7 all-gather.16
  383.0 65.4 reduce-scatter.28
  452.1 65.4 reduce-scatter.26
  639.7 32.2 reduce-scatter.36
  682.8 33.9 reduce-scatter.40
  720.1 53.7 reduce-scatter.34
  776.2 60.3 reduce-scatter.48
  838.8 60.2 reduce-scatter.44
  901.4 60.3 reduce-scatter.46
  963.8 19.2 reduce-scatter.42
  986.3 38.2 reduce-scatter.32
  1026.8 23.1 reduce-scatter.38
  1052.2 65.9 reduce-scatter.30

commit v2 on v1

--- a/solution.py
+++ b/solution.py
@@ -1,6 +1,10 @@
+from functools import partial
+
 import jax
 import jax.numpy as jnp
 from jax import lax
+from jax.experimental import pallas as pl
+from jax.experimental.pallas import tpu as pltpu
 from jax.sharding import PartitionSpec as P
 
 HEAD_DIMENSION = 64
@@ -154,6 +158,245 @@
 
 def matmul(left_side, right_side):
     return jnp.dot(left_side, right_side, preferred_element_type=jnp.float32)
+
+
+LANES = 128
+
+
+def exchange(values, axis_name, bit):
+    count = lax.axis_size(axis_name)
+    return lax.ppermute(values, axis_name, [(i, i ^ bit) for i in range(count)])
+
+
+def bits_of(number):
+    return [1 << k for k in range(number.bit_length()) if number >> k & 1]
+
+
+def gather_blocks(own, axis_name):
+    count = lax.axis_size(axis_name)
+    half = own.shape[0] // 2
+    blocks = {0: own}
+    even = sorted(range(2, count, 2), key=lambda j: (len(bits_of(j)), j))
+    if count > 1:
+        blocks[1] = exchange(own, axis_name, 1)
+    for j in even:
+        bits = bits_of(j)
+        if len(bits) == 1:
+            blocks[j] = exchange(own, axis_name, j)
+        else:
+            low_bit, high_bit = bits[0], bits[-1]
+            top = exchange(blocks[j ^ low_bit][:half], axis_name, low_bit)
+            bottom = exchange(blocks[j ^ high_bit][half:], axis_name, high_bit)
+            blocks[j] = jnp.concatenate([top, bottom], axis=0)
+        blocks[j + 1] = exchange(blocks[j], axis_name, 1)
+    return [blocks[j] for j in range(count)]
+
+
+def add_rounded(left_side, right_side):
+    return (left_side.astype(jnp.float32) + right_side.astype(jnp.float32)).astype(jnp.bfloat16)
+
+
+def reduce_blocks(blocks, axis_name):
+    count = lax.axis_size(axis_name)
+    half = blocks[0].shape[0] // 2
+    sums = {}
+    for j in sorted(range(0, count, 2), key=lambda j: (-len(bits_of(j)), j)):
+        arrived = exchange(blocks[j + 1], axis_name, 1)
+        sums[j] = [
+            add_rounded(blocks[j][:half], arrived[:half]),
+            add_rounded(blocks[j][half:], arrived[half:]),
+        ]
+    extra = [[], []]
+    for j in sorted(range(2, count, 2), key=lambda j: (-len(bits_of(j)), j)):
+        bits = bits_of(j)
+        if len(bits) > 1:
+            low_bit, high_bit = bits[0], bits[-1]
+            top = exchange(sums[j][0], axis_name, low_bit)
+            bottom = exchange(sums[j][1], axis_name, high_bit)
+            sums[j ^ low_bit][0] = add_rounded(sums[j ^ low_bit][0], top)
+            sums[j ^ high_bit][1] = add_rounded(sums[j ^ high_bit][1], bottom)
+        else:
+            extra[0].append(exchange(sums[j][0], axis_name, j))
+            extra[1].append(exchange(sums[j][1], axis_name, j))
+    halves = []
+    for part in range(2):
+        total = sums[0][part].astype(jnp.float32)
+        for piece in extra[part]:
+            total = total + piece.astype(jnp.float32)
+        halves.append(total)
+    return jnp.concatenate(halves, axis=0)
+
+
+def in_order(blocks, index):
+    stacked = jnp.stack(blocks)
+    return jnp.concatenate(
+        [lax.dynamic_index_in_dim(stacked, j ^ index, 0, keepdims=True) for j in range(len(blocks))],
+        axis=0,
+    )
+
+
+def relative_blocks(values, index, count):
+    rows = values.shape[0] // count
+    return [
+        lax.dynamic_slice_in_dim(values, (index ^ j) * rows, rows, axis=0) for j in range(count)
+    ]
+
+
+def scatter_direct(pieces, axis_name):
+    count = lax.axis_size(axis_name)
+    index = lax.axis_index(axis_name)
+    total = lax.dynamic_index_in_dim(pieces, index, 0, keepdims=False).astype(jnp.float32)
+    for step in range(1, count):
+        piece = lax.dynamic_index_in_dim(pieces, (index + step) % count, 0, keepdims=False)
+        arrived = lax.ppermute(piece, axis_name, [(i, (i + step) % count) for i in range(count)])
+        total = total + arrived.astype(jnp.float32)
+    return total
+
+
+def expert_body(
+    experts_all, index_ref, x_even, x_odd, og_even, og_odd, gate_w, up_w, down_w, *rest
+):
+    (x_all, og_all, pre_all, hid_all, row_even, row_odd, out_even, out_odd) = rest[-12:-4]
+    (row_acc, out_acc, back_acc, _) = rest[-4:]
+    expert = pl.program_id(0)
+    last = pl.num_programs(0) - 1
+    rows = x_even.shape[0]
+    width = x_all.shape[1]
+    hidden_units = gate_w.shape[2]
+    nt_dims = (((1,), (1,)), ((), ()))
+
+    @pl.when(expert == 0)
+    def _():
+        x_all[:rows, :] = x_even[:, :width]
+        x_all[rows:, :] = x_odd[:, :width]
+        og_all[:rows, :] = og_even[...]
+        og_all[rows:, :] = og_odd[...]
+
+    column = index_ref[0] + expert
+    lane = lax.broadcasted_iota(jnp.int32, (2 * rows, LANES), 1)
+    coded = jnp.concatenate([x_even[:, width:], x_odd[:, width:]], axis=0).astype(jnp.float32)
+    gate = jnp.sum(
+        jnp.where((lane == column) | (lane == column + experts_all), coded, 0.0),
+        axis=1,
+        keepdims=True,
+    )
+    x_rows = x_all[...]
+    og_rows = og_all[...]
+    gate_pre = jnp.dot(x_rows, gate_w[0], preferred_element_type=jnp.float32)
+    up_pre = jnp.dot(x_rows, up_w[0], preferred_element_type=jnp.float32)
+    down_grad = lax.dot_general(og_rows, down_w[0], nt_dims, preferred_element_type=jnp.float32)
+    sigmoid = 1.0 / (1.0 + jnp.exp(-gate_pre))
+    silu = gate_pre * sigmoid
+    hidden = silu * up_pre
+    gate_back = jnp.sum(hidden * down_grad, axis=1, keepdims=True)
+    hidden_low = (gate * hidden).astype(jnp.bfloat16)
+    hidden_grad = gate * down_grad
+    gate_pre_low = (
+        hidden_grad * up_pre * sigmoid * (1.0 + gate_pre * (1.0 - sigmoid))
+    ).astype(jnp.bfloat16)
+    up_pre_low = (hidden_grad * silu).astype(jnp.bfloat16)
+    hid_all[...] = hidden_low
+    pre_all[0, :, :hidden_units] = gate_pre_low
+    pre_all[0, :, hidden_units:] = up_pre_low
+    row = lax.dot_general(
+        gate_pre_low, gate_w[0], nt_dims, preferred_element_type=jnp.float32
+    ) + lax.dot_general(up_pre_low, up_w[0], nt_dims, preferred_element_type=jnp.float32)
+    out = jnp.dot(hidden_low, down_w[0], preferred_element_type=jnp.float32)
+    high = gate_back.astype(jnp.bfloat16).astype(jnp.float32)
+    back = jnp.where(lane == column, high, 0.0) + jnp.where(
+        lane == column + experts_all, gate_back - high, 0.0
+    )
+
+    @pl.when(expert == 0)
+    def _():
+        row_acc[...] = row
+        out_acc[...] = out
+        back_acc[...] = back
+
+    @pl.when(expert > 0)
+    def _():
+        row_acc[...] += row
+        out_acc[...] += out
+        back_acc[...] += back
+
+    @pl.when(expert == last)
+    def _():
+        for ref, first in ((row_even, 0), (row_odd, rows)):
+            ref[:, :width] = row_acc[first : first + rows, :].astype(jnp.bfloat16)
+            ref[:, width:] = back_acc[first : first + rows, :].astype(jnp.bfloat16)
+        out_even[...] = out_acc[:rows, :].astype(jnp.bfloat16)
+        out_odd[...] = out_acc[rows:, :].astype(jnp.bfloat16)
+
+
+def expert_pair(position, pairs, first_expert, experts_all, x_pair, og_pair, weights, carried):
+    w_gate, w_up, w_down = weights
+    rows, coded_width = x_pair[0].shape
+    width = coded_width - LANES
+    local_experts, _, hidden_units = w_gate.shape
+    bf16 = jnp.bfloat16
+    whole = 2 * rows
+    fixed = lambda e, i: (0, 0)
+    once = pl.Buffered(1)
+    in_specs = (
+        [pl.BlockSpec((rows, coded_width), fixed, pipeline_mode=once)] * 2
+        + [pl.BlockSpec((rows, width), fixed, pipeline_mode=once)] * 2
+        + [pl.BlockSpec((1, width, hidden_units), lambda e, i: (e, 0, 0))] * 2
+        + [pl.BlockSpec((1, hidden_units, width), lambda e, i: (e, 0, 0))]
+    )
+    operands = [*x_pair, *og_pair, w_gate, w_up, w_down]
+    aliases = {}
+    if carried is not None:
+        in_specs = in_specs + [pl.BlockSpec(memory_space=pl.ANY)] * 4
+        aliases = {1 + len(operands) + k: k for k in range(4)}
+        operands = operands + list(carried)
+    out_shape = [
+        jax.ShapeDtypeStruct((pairs * whole, width), bf16),
+        jax.ShapeDtypeStruct((pairs * whole, width), bf16),
+        jax.ShapeDtypeStruct((local_experts, pairs * whole, 2 * hidden_units), bf16),
+        jax.ShapeDtypeStruct((pairs * whole, local_experts * hidden_units), bf16),
+        jax.ShapeDtypeStruct((rows, coded_width), bf16),
+        jax.ShapeDtypeStruct((rows, coded_width), bf16),
+        jax.ShapeDtypeStruct((rows, width), bf16),
+        jax.ShapeDtypeStruct((rows, width), bf16),
+    ]
+    out_specs = [
+        pl.BlockSpec((whole, width), lambda e, i: (position, 0)),
+        pl.BlockSpec((whole, width), lambda e, i: (position, 0)),
+        pl.BlockSpec((1, whole, 2 * hidden_units), lambda e, i: (e, position, 0)),
+        pl.BlockSpec((whole, hidden_units), lambda e, i: (position, e)),
+        pl.BlockSpec((rows, coded_width), fixed),
+        pl.BlockSpec((rows, coded_width), fixed),
+        pl.BlockSpec((rows, width), fixed),
+        pl.BlockSpec((rows, width), fixed),
+    ]
+    products = 2 * whole * width * hidden_units * local_experts
+    results = pl.pallas_call(
+        partial(expert_body, experts_all),
+        out_shape=out_shape,
+        grid_spec=pltpu.PrefetchScalarGridSpec(
+            num_scalar_prefetch=1,
+            grid=(local_experts,),
+            in_specs=in_specs,
+            out_specs=out_specs,
+            scratch_shapes=[
+                pltpu.VMEM((whole, width), jnp.float32),
+                pltpu.VMEM((whole, width), jnp.float32),
+                pltpu.VMEM((whole, LANES), jnp.float32),
+                pltpu.VMEM((8, LANES), jnp.float32),
+            ],
+        ),
+        input_output_aliases=aliases,
+        compiler_params=pltpu.CompilerParams(
+            dimension_semantics=("arbitrary",), vmem_limit_bytes=60 * 1024 * 1024
+        ),
+        cost_estimate=pl.CostEstimate(
+            flops=6 * products,
+            bytes_accessed=3 * 2 * local_experts * width * hidden_units + 20 * whole * width,
+            transcendentals=whole * hidden_units * local_experts,
+        ),
+        name="experts",
+    )(first_expert, *operands)
+    return results[:4], results[4:]
 
 
 def on_device(
@@ -192,15 +435,13 @@
     first_gain = small[:, experts_all].astype(jnp.float32)
     second_gain = small[:, experts_all + 1].astype(jnp.float32)
     block_tokens = lax.all_gather(tokens, "seq", axis=0, tiled=True)
-    qkv_weight = lax.all_gather(
-        jnp.concatenate([w_query, key_projection, value_projection], axis=1),
-        "shard",
-        axis=0,
-        tiled=True,
-    )
+    qkv_blocks = gather_blocks(
+        jnp.concatenate([w_query, key_projection, value_projection], axis=1), "shard"
+    )
+    qkv_weight = in_order(qkv_blocks, shard_index).reshape(model_width, -1)
     out_weight = lax.all_gather(w_out, "seq", axis=0, tiled=True)
     out_weight = lax.all_gather(out_weight, "shard", axis=1, tiled=True)
-    plane_grads = lax.all_gather(out_grad, "shard", axis=0, tiled=True)
+    grad_blocks = gather_blocks(lax.optimization_barrier((out_grad, qkv_weight))[0], "shard")
 
     block_rows = jnp.arange(block_len, dtype=jnp.int32)
     cos_table, sin_table = rotary_tables(
@@ -266,54 +507,48 @@
     gate_dense = jax.nn.softmax(jnp.where(named, logits, negative), axis=-1)
     gate_dense = jnp.where(named, gate_dense, 0.0)
 
-    plane_rows = lax.all_gather(second_low, "shard", axis=0, tiled=True)
-    plane_gates = lax.all_gather(gate_dense, "shard", axis=0, tiled=True)
-    local_gates = lax.dynamic_slice_in_dim(
-        plane_gates, shard_index * local_experts, local_experts, axis=1
-    )
-    expert_gates = local_gates.T[:, :, None]
-    gate_pre = jnp.einsum("td,edf->etf", plane_rows, w_gate, preferred_element_type=jnp.float32)
-    up_pre = jnp.einsum("td,edf->etf", plane_rows, w_up, preferred_element_type=jnp.float32)
-    down_grad = jnp.einsum("td,efd->etf", plane_grads, w_down, preferred_element_type=jnp.float32)
-    sigmoid = jax.nn.sigmoid(gate_pre)
-    silu = gate_pre * sigmoid
-    hidden = silu * up_pre
-    gate_grad = jnp.sum(hidden * down_grad, axis=-1)
-    hidden_low = (expert_gates * hidden).astype(bf16)
-    hidden_grad = expert_gates * down_grad
-    gate_pre_low = (hidden_grad * up_pre * sigmoid * (1.0 + gate_pre * (1.0 - sigmoid))).astype(bf16)
-    up_pre_low = (hidden_grad * silu).astype(bf16)
-    grad_down = jnp.einsum(
-        "td,etf->edf", plane_grads, hidden_low, preferred_element_type=jnp.float32
-    ).astype(bf16)
-    grad_gate = jnp.einsum(
-        "td,etf->edf", plane_rows, gate_pre_low, preferred_element_type=jnp.float32
-    ).astype(bf16)
-    grad_up = jnp.einsum(
-        "td,etf->edf", plane_rows, up_pre_low, preferred_element_type=jnp.float32
-    ).astype(bf16)
-    row_part = (
-        jnp.einsum("etf,edf->td", gate_pre_low, w_gate, preferred_element_type=jnp.float32)
-        + jnp.einsum("etf,edf->td", up_pre_low, w_up, preferred_element_type=jnp.float32)
-    ).astype(bf16)
-    out_part = jnp.einsum(
-        "etf,efd->td", hidden_low, w_down, preferred_element_type=jnp.float32
-    ).astype(bf16)
-    row_grad = lax.psum_scatter(row_part, "shard", scatter_dimension=0, tiled=True)
-    gate_back = lax.all_to_all(
-        gate_grad.reshape(local_experts, shard_count, tok_count).transpose(1, 0, 2),
-        "shard",
-        split_axis=0,
-        concat_axis=0,
-        tiled=True,
-    )
-    expert_sum = lax.psum_scatter(out_part, "shard", scatter_dimension=0, tiled=True)
-    output = (residual + expert_sum.astype(jnp.float32)).astype(bf16)
-    gate_grad_dense = gate_back.reshape(experts_all, tok_count).T
+    gate_high = lax.reduce_precision(gate_dense, 8, 7)
+    coded = jnp.concatenate(
+        [
+            second_low,
+            gate_high.astype(bf16),
+            (gate_dense - gate_high).astype(bf16),
+            jnp.zeros((tok_count, LANES - 2 * experts_all), bf16),
+        ],
+        axis=1,
+    )
+    row_blocks = gather_blocks(coded, "shard")
+    order = sorted(range(0, shard_count, 2), key=lambda j: (len(bits_of(j)), j))
+    first_expert = (shard_index * local_experts).astype(jnp.int32).reshape(1)
+    carried = None
+    row_parts = [None] * shard_count
+    out_parts = [None] * shard_count
+    for position, j in enumerate(order):
+        carried, pieces = expert_pair(
+            position,
+            len(order),
+            first_expert,
+            experts_all,
+            row_blocks[j : j + 2],
+            grad_blocks[j : j + 2],
+            (w_gate, w_up, w_down),
+            carried,
+        )
+        row_parts[j], row_parts[j + 1], out_parts[j], out_parts[j + 1] = pieces
+    all_rows, all_grads, all_pre, all_hidden = carried
+    down_sum = transposed_times(all_grads, all_hidden).astype(bf16)
+    pre_sums = [transposed_times(all_rows, all_pre[e]).astype(bf16) for e in range(local_experts)]
+    row_total = reduce_blocks(row_parts, "shard")
+    row_total = lax.optimization_barrier((row_total, down_sum, *pre_sums))[0]
+    row_grad = row_total[:, :model_width]
+    gate_grad_dense = (
+        row_total[:, model_width : model_width + experts_all]
+        + row_total[:, model_width + experts_all : model_width + 2 * experts_all]
+    )
     weighted = gate_dense * gate_grad_dense
     logit_grad = weighted - gate_dense * jnp.sum(weighted, axis=-1, keepdims=True)
     grad_router = transposed_times(second_low.astype(jnp.float32), logit_grad, highest)
-    second_grad = row_grad.astype(jnp.float32) + times_transposed(
+    second_grad = row_grad + times_transposed(
         logit_grad, router_weight.astype(jnp.float32), highest
     )
     residual_part, grad_gain_ffn = rms_backward(residual, second_factor, second_gain, second_grad)
@@ -321,10 +556,22 @@
     residual_low = residual_grad.astype(bf16)
     mixed_grad_tokens = times_transposed(residual_low, out_weight).astype(bf16)
     mixed_grad = lax.all_to_all(mixed_grad_tokens, "seq", split_axis=1, concat_axis=0, tiled=True)
-    whole_out = transposed_times(residual_low, mixed_tokens).astype(bf16)
-    grad_out = lax.psum_scatter(whole_out, "shard", scatter_dimension=0, tiled=True)
-    grad_out = lax.psum_scatter(grad_out, "seq", scatter_dimension=1, tiled=True)
-    grad_out = grad_out.T.astype(jnp.float32)
+    out_parts = lax.optimization_barrier((out_parts, mixed_grad_tokens))[0]
+    expert_sum = reduce_blocks(out_parts, "shard")
+    output = (residual + expert_sum).astype(bf16)
+    columns = [
+        lax.dynamic_slice_in_dim(
+            residual_low,
+            (shard_index ^ j) * (model_width // shard_count),
+            model_width // shard_count,
+            axis=1,
+        )
+        for j in range(shard_count)
+    ]
+    whole_out = [transposed_times(part, mixed_tokens).astype(bf16) for part in columns]
+    grad_out = reduce_blocks(whole_out, "shard").astype(bf16)
+    grad_out = grad_out.reshape(grad_out.shape[0], seq_count, -1).transpose(1, 0, 2)
+    grad_out = scatter_direct(grad_out, "seq").T
 
     query_piece, prompt_key_grad, prompt_value_grad = attend_backward(
         query_heads[:PROMPT_BLK],
@@ -355,12 +602,14 @@
         prompt_value_grad = prompt_value_grad + value_piece[:prompt_len]
         self_key_grads.append(key_piece[prompt_len:])
         self_value_grads.append(value_piece[prompt_len:])
-    own_prompt = lax.psum_scatter(
-        jnp.concatenate([prompt_key_grad, prompt_value_grad], axis=1).astype(bf16),
+    own_prompt = reduce_blocks(
+        relative_blocks(
+            jnp.concatenate([prompt_key_grad, prompt_value_grad], axis=1).astype(bf16),
+            shard_index,
+            shard_count,
+        ),
         "shard",
-        scatter_dimension=0,
-        tiled=True,
-    ).astype(jnp.float32)
+    )
     query_grad = jnp.concatenate(query_parts, axis=0)
     key_grad = jnp.concatenate([own_prompt[:, :key_width]] + self_key_grads, axis=0)
     value_low = jnp.concatenate([own_prompt[:, key_width:]] + self_value_grads, axis=0).astype(bf16)
@@ -371,28 +620,32 @@
     normed_grad = lax.psum_scatter(
         normed_part.astype(bf16), "seq", scatter_dimension=0, tiled=True
     ).astype(jnp.float32)
-    grad_qkv = lax.psum_scatter(
-        transposed_times(normed_low, lin_all).astype(bf16),
-        "shard",
-        scatter_dimension=0,
-        tiled=True,
-    ).astype(jnp.float32)
+    gain_part = jnp.sum(normed_part * inputs * first_factor, axis=0)
+    small_grad = jnp.concatenate(
+        [grad_router, gain_part[:, None], grad_gain_ffn[:, None]], axis=1
+    )
+    grad_qkv = jnp.concatenate([transposed_times(normed_low, lin_all), small_grad], axis=1)
+    grad_qkv = reduce_blocks(
+        relative_blocks(grad_qkv.astype(bf16), shard_index, shard_count), "shard"
+    )
     grad_query = grad_qkv[:, :query_width]
     grad_key = grad_qkv[:, query_width : query_width + key_width]
-    grad_value = grad_qkv[:, query_width + key_width :]
-    gain_part = jnp.sum(normed_part * inputs * first_factor, axis=0)
+    grad_value = grad_qkv[:, query_width + key_width : query_width + 2 * key_width]
+    small_grad = grad_qkv[:, query_width + 2 * key_width :].astype(bf16)
+    small_grad = scatter_direct(
+        small_grad.reshape(seq_count, -1, small_grad.shape[1]), "seq"
+    )
     own_factor = rms_parts(own_inputs)
     input_part, _ = rms_backward(own_inputs, own_factor, first_gain, normed_grad)
     tokens_grad = residual_grad + input_part
-    small_grad = jnp.concatenate(
-        [grad_router, gain_part[:, None], grad_gain_ffn[:, None]], axis=1
-    ).astype(bf16)
-    small_grad = lax.psum_scatter(small_grad, "shard", scatter_dimension=0, tiled=True)
-    small_grad = lax.psum_scatter(small_grad, "seq", scatter_dimension=0, tiled=True)
-    small_grad = small_grad.astype(jnp.float32)
-    grad_gate = lax.psum_scatter(grad_gate, "seq", scatter_dimension=1, tiled=True)
-    grad_up = lax.psum_scatter(grad_up, "seq", scatter_dimension=1, tiled=True)
-    grad_down = lax.psum_scatter(grad_down, "seq", scatter_dimension=1, tiled=True)
+    grad_down = lax.psum_scatter(down_sum, "seq", scatter_dimension=0, tiled=True)
+    pre_grads = [
+        lax.psum_scatter(part, "seq", scatter_dimension=0, tiled=True) for part in pre_sums
+    ]
+    hidden_units = w_gate.shape[2]
+    grad_down = grad_down.T.reshape(local_experts, hidden_units, -1)
+    grad_gate = jnp.stack([part[:, :hidden_units] for part in pre_grads])
+    grad_up = jnp.stack([part[:, hidden_units:] for part in pre_grads])
     return (
         output,
         tokens_grad,
@@ -405,7 +658,7 @@
         small_grad[:, :experts_all],
         grad_gate.astype(jnp.float32),
         grad_up.astype(jnp.float32),
-        grad_down.transpose(0, 2, 1).astype(jnp.float32),
+        grad_down.astype(jnp.float32),
     )
 
 

time: 1140 us -> 728 us (0.64)
  waiting for transfers between devices: 605 us -> 183 us
  Pallas kernels: 0 us -> 86.5 us
  matrix products: 256 us -> 172 us
  starting transfers between devices: 5.49 us -> 63.8 us
  blocking collectives: 103 us -> 59 us
  local copies, waits for them, and re-layouts: 69.4 us -> 36.7 us
  other arithmetic: 76.6 us -> 102 us
    unnamed x24 -> x6, waiting for transfers between devices: 247 us -> 0.76 us
    reduce_scatter x4 -> x3, waiting for transfers between devices: 163 us -> 0.02 us  [the longest x2 0.02 us: on_device(): lax.psum_scatter(part, 'seq', scatter_dimension=0, tiled=True)]
    ppermute x0 -> x80, waiting for transfers between devices: none -> 135 us  [the longest x74 115 us: exchange(): return lax.ppermute(values, axis_name, [(i, i ^ bit) for i in range(count)])]
    dot_general x9 -> x0, matrix products: 120 us -> none  [the longest x1 20.3 us: on_device(): jnp.einsum('td,efd->etf', plane_grads, w_down, preferred_element_type=jnp...]
    all_gather x3 -> x0, waiting for transfers between devices: 87.1 us -> none  [the longest x1 34.8 us: on_device(): plane_rows = lax.all_gather(second_low, 'shard', axis=0, tiled=True)]
    pallas_call x0 -> x4, Pallas kernels: none -> 86.5 us  [expert_pair(): pl.pallas_call(partial(expert_body, experts_all), out_shape=out_shape, gr...]
    reduce_scatter x1, waiting for transfers between devices: 66.4 us -> 0.01 us  [on_device(): lax.psum_scatter(normed_part.astype(bf16), 'seq', scatter_dimension=0, ti...]
    ppermute x0 -> x80, starting transfers between devices: none -> 55.6 us  [the longest x74 50.6 us: exchange(): return lax.ppermute(values, axis_name, [(i, i ^ bit) for i in range(count)])]
  transfers between devices with their start and end apart: 18 -> 88, of which waited for: 16 -> 27; matrix products, arithmetic and copies ran while one was open for 21% -> 40% of each run, Pallas kernels for 0% -> 9%
where the time goes in v2:
time: 728 us; the launch traced here: 720 us
  waiting for transfers between devices  183 us (25%)
  matrix products  172 us (24%)
  other arithmetic  102 us (14%)
  Pallas kernels  86.5 us (12%)
  starting transfers between devices  63.8 us (9%)
  blocking collectives  59 us (8%)
  local copies, waits for them, and re-layouts  36.7 us (5%)
  between operations  16.6 us (2%)
    ppermute x74, waiting for transfers between devices, exchange(): return lax.ppermute(values, axis_name, [(i, i ^ bit) for i in range(count)])  115 us
    pallas_call x4, Pallas kernels, expert_pair(): pl.pallas_call(partial(expert_body, experts_all), out_shape=out_shape, gr...  86.5 us
    dot_general x13, matrix products, transposed_times(): lax.dot_general(left_side, right_side, (((0,), (0,)), ((), ())), precisio...  51.9 us
    ppermute x74, starting transfers between devices, exchange(): return lax.ppermute(values, axis_name, [(i, i ^ bit) for i in range(count)])  50.6 us
    all_to_all x1, waiting for transfers between devices, on_device(): lax.all_to_all(mixed_grad_tokens, 'seq', split_axis=1, concat_axis=0, til...  34.6 us
    convert_element_type x3, other arithmetic, attend_backward(): score_grad = (probs * (prob_grad - inner_sum)).astype(jnp.bfloat16)  33.7 us
    dot_general x3, matrix products, attend_backward(): jnp.einsum('rhgd,khd->hgrk', grad_grouped, value_heads_split, preferred_e...  25.2 us
    all_gather x1, blocking collectives, on_device(): out_weight = lax.all_gather(w_out, 'seq', axis=0, tiled=True)  25 us
  transfers between devices with their start and end apart: 88, of which 27 were waited for; matrix products, arithmetic and copies ran while one was open for 40% of the time, Pallas kernels for 9%

profile of v2, /device:TPU:0, one launch (start us, length us, event | category | flops | bytes accessed | tf_op | source)
XLA Modules:
  0.0 720.0 jit_solution(14243185819520893433)
XLA Ops:
  10.5 3.1 collective-permute-start.3
  15.1 25.0 %all_gather.22 = bf16[1536,192]{0,1:T(8,128)(2,1)} all-gather(bf16[384,192]{0,1:T(8,128)(2,1)} %param.18), channel_id=1, replica_groups=mesh['shard'=8,'seq'=4] {'seq'}, dimensions={0}, use_global_device_ids=true | all-gather | bytes 737280 | tf_op jit(solution)/shard_map/all_gather | solution.py:442
  40.9 14.4 %all-gather = bf16[4,48,18]{1,2,0:T(8,128)(2,1)S(1)} all-gather(bf16[1,48,18]{1,2,0:T(8,128)(2,1)S(1)} %maximum_bitcast_fusion), channel_id=1, replica_groups=mesh['shard'=8,'seq'=4] {'seq'}, dimensions={0}, use_global_device_ids=true | all-gather | bytes 8640 | tf_op jit(solution)/shard_map/all_gather | solution.py:432
  55.4 7.8 %all-gather.1 = bf16[8,192,18]{1,2,0:T(8,128)(2,1)S(1)} all-gather(bf16[1,192,18]{1,2,0:T(8,128)(2,1)S(1)} %reshape.428), channel_id=1, replica_groups=mesh['shard'=8,'seq'=4] {'shard'}, dimensions={0}, use_global_device_ids=true | all-gather | bytes 62208 | tf_op jit(solution)/shard_map/all_gather | solution.py:433
  65.3 1.8 fusion.38
  67.8 2.0 collective-permute-start.5
  70.6 3.1 collective-permute-done.5
  77.3 12.1 %all-gather.5.cloned.1.call-done = bf16[1152,1536]{1,0:T(8,128)(2,1)} async-done(((bf16[288,1536]{1,0:T(8,128)(2,1)}), bf16[1152,1536]{1,0:T(8,128)(2,1)}) %all-gather.5.cloned.1.call-update) | async-done | bytes 3538960 | tf_op jit(solution)/shard_map/all_gather | solution.py:437
  89.4 2.9 fusion.18
  92.5 3.1 fusion.140
  96.4 11.9 %all_gather.21 = bf16[1024,256]{0,1:T(8,128)(2,1)S(1)} all-gather(bf16[128,256]{0,1:T(8,128)(2,1)S(1)} %pad_maximum_fusion.17), channel_id=1, replica_groups=mesh['shard'=8,'seq'=4] {'shard'}, dimensions={0}, use_global_device_ids=true | all-gather | bytes 589824 | tf_op jit(solution)/shard_map/all_gather | solution.py:459
  111.2 8.2 %fusion.141 = (f32[2,3,512]{2,1,0:T(4,128)S(1)}, f32[2,3,512,1536]{2,3,1,0:T(8,128)}) fusion(bf16[1536,2,64,1]{0,2,3,1:T(8,128)(2,1)S(1)} %bitcast.333, bf16[512,2,3,64]{0,3,2,1:T(8,128)(2,1)S(1)} %bitcast.320, pred[512,1536]{0,1:T(8,128)(4,1)S(1)} %copy-done.2), kind=kOutput, calls=%fused_computation.373 | convolution fusion | flops 618132480 | bytes 20459520 | tf_op jit(solution)/shard_map/rhgd,khd->hgrk/dot_general | solution.py:89
  119.4 9.6 %fusion.7 = f32[2,3,512]{2,1,0:T(4,128)} fusion(f32[2,3,512,1536]{2,3,1,0:T(8,128)} %get-tuple-element.281, f32[2,3,512]{2,1,0:T(4,128)S(1)} %get-tuple-element.280), kind=kLoop, calls=%fused_computation.19 | loop fusion | flops 9434112 | bytes 18898944 | tf_op jit(solution)/shard_map/reduce_sum | solution.py:99
  129.0 2.3 fusion.80
  132.3 9.8 %fusion.61 = bf16[2,64,3,512]{3,1,2,0:T(8,128)(2,1)S(1)} fusion(bf16[1536,2,64,1]{0,2,3,1:T(8,128)(2,1)} %bitcast.346, f32[2,3,512,1536]{2,3,1,0:T(8,128)} %get-tuple-element.281, f32[2,3,512]{2,1,0:T(4,128)} %fusion.7, f32[2,3,512]{2,1,0:T(4,128)S(1)} %get-tuple-element.280), kind=kOutput, calls=%fused_computation.105 | convolution fusion | flops 618332160 | bytes 19685376 | tf_op jit(solution)/shard_map/hgrk,khd->rhgd/dot_general | solution.py:103
  142.3 8.5 %fusion.142 = (f32[2,3,512]{2,1,0:T(4,128)S(1)}, f32[2,3,512,1536]{2,3,1,0:T(8,128)}) fusion(bf16[1536,2,64,1]{0,2,3,1:T(8,128)(2,1)S(1)} %bitcast.335, bf16[512,2,3,64]{0,3,2,1:T(8,128)(2,1)S(1)} %bitcast.322, pred[512,1536]{0,1:T(8,128)(4,1)S(1)} %copy-done.3), kind=kOutput, calls=%fused_computation.374 | convolution fusion | flops 618132480 | bytes 20459520 | tf_op jit(solution)/shard_map/rhgd,khd->hgrk/dot_general | solution.py:89
  150.8 8.9 %fusion.6 = f32[2,3,512]{2,1,0:T(4,128)S(1)} fusion(f32[2,3,512,1536]{2,3,1,0:T(8,128)} %get-tuple-element.283, f32[2,3,512]{2,1,0:T(4,128)S(1)} %get-tuple-element.282), kind=kLoop, calls=%fused_computation.18 | loop fusion | flops 9434112 | bytes 18898944 | tf_op jit(solution)/shard_map/reduce_sum | solution.py:99
  159.8 8.2 %fusion.62 = bf16[2,64,3,512]{3,1,2,0:T(8,128)(2,1)S(1)} fusion(bf16[1536,2,64,1]{0,2,3,1:T(8,128)(2,1)S(1)} %bitcast.348, f32[2,3,512,1536]{2,3,1,0:T(8,128)} %get-tuple-element.283, f32[2,3,512]{2,1,0:T(4,128)S(1)} %fusion.6, f32[2,3,512]{2,1,0:T(4,128)S(1)} %get-tuple-element.282), kind=kOutput, calls=%fused_computation.106 | convolution fusion | flops 618332160 | bytes 19685376 | tf_op jit(solution)/shard_map/hgrk,khd->rhgd/dot_general | solution.py:103
  169.2 3.5 all-to-all-start
  176.1 18.9 %collective-permute-done.16.og_even = bf16[288,1536]{1,0:T(8,128)(2,1)S(1)} collective-permute-done((bf16[288,1536]{1,0:T(8,128)(2,1)}, bf16[288,1536]{1,0:T(8,128)(2,1)S(1)}, u32[]{:S(2)}, u32[]{:S(2)}) %collective-permute-start.16) | collective-permute-done | bytes 884768 | tf_op jit(solution)/shard_map/ppermute | solution.py:168
  197.4 4.0 multiply_reduce_fusion.2
  205.7 1.9 concatenate.120.x_even
  214.4 25.4 %collective-permute-done.22 = bf16[144,1536]{1,0:T(8,128)(2,1)} collective-permute-done((bf16[144,1536]{1,0:T(8,128)(2,1)}, bf16[144,1536]{1,0:T(8,128)(2,1)}, u32[]{:S(2)}, u32[]{:S(2)}) %collective-permute-start.22) | collective-permute-done | bytes 442400 | tf_op jit(solution)/shard_map/ppermute | solution.py:168
  242.1 1.8 slice.613
  244.7 1.8 slice.614
  247.9 21.4 %experts.4 = (bf16[2304,1536]{1,0:T(8,128)(2,1)}, bf16[2304,1536]{1,0:T(8,128)(2,1)}, bf16[2,2304,1024]{2,1,0:T(8,128)(2,1)}, bf16[2304,1024]{1,0:T(8,128)(2,1)}...) custom-call(s32[1]{0:T(128)} %bitcast.49.index_ref, ...), custom_call_target="tpu_custom_call" | custom-call | flops 10871635968 | bytes 27131904 | tf_op jit(solution)/shard_map/experts/pallas_call | solution.py:373
  269.9 1.8 constant_dynamic-update-slice_fusion.6
  273.0 21.6 %experts.5 = (bf16[2304,1536]{1,0:T(8,128)(2,1)}, bf16[2304,1536]{1,0:T(8,128)(2,1)}, bf16[2,2304,1024]{2,1,0:T(8,128)(2,1)}, bf16[2304,1024]{1,0:T(8,128)(2,1)}...) custom-call(s32[1]{0:T(128)} %bitcast.49.index_ref, ...), custom_call_target="tpu_custom_call", output_to_operand_aliasing={{0}: (8, {}), {1}: (9, {}), {2}: (10, {}), {3}: (11, {})} | custom-call | flops 10871635968 | bytes 27131904 | tf_op jit(solution)/shard_map/experts/pallas_call | solution.py:373
  294.7 21.6 %experts.6 = (bf16[2304,1536]{1,0:T(8,128)(2,1)}, bf16[2304,1536]{1,0:T(8,128)(2,1)}, bf16[2,2304,1024]{2,1,0:T(8,128)(2,1)}, bf16[2304,1024]{1,0:T(8,128)(2,1)}...) custom-call(s32[1]{0:T(128)} %bitcast.49.index_ref, ...), custom_call_target="tpu_custom_call", output_to_operand_aliasing={{0}: (8, {}), {1}: (9, {}), {2}: (10, {}), {3}: (11, {})} | custom-call | flops 10871635968 | bytes 27131904 | tf_op jit(solution)/shard_map/experts/pallas_call | solution.py:373
  316.3 21.9 %experts.7 = (bf16[2304,1536]{1,0:T(8,128)(2,1)}, bf16[2304,1536]{1,0:T(8,128)(2,1)}, bf16[2,2304,1024]{2,1,0:T(8,128)(2,1)}, bf16[2304,1024]{1,0:T(8,128)(2,1)}...) custom-call(s32[1]{0:T(128)} %bitcast.49.index_ref, ...), custom_call_target="tpu_custom_call", output_to_operand_aliasing={{0}: (8, {}), {1}: (9, {}), {2}: (10, {}), {3}: (11, {})} | custom-call | flops 10871635968 | bytes 27131904 | tf_op jit(solution)/shard_map/experts/pallas_call | solution.py:373
  338.2 12.4 %convolution_convert_fusion = bf16[1536,1024]{1,0:T(8,128)(2,1)} fusion(bf16[2304,1536]{1,0:T(8,128)(2,1)} %get-tuple-element.83, bf16[2304,1024]{1,0:T(8,128)(2,1)} %get-tuple-element.84), kind=kOutput, calls=%fused_computation.44 | convolution fusion | flops 7249330176 | bytes 14942208 | tf_op jit(solution)/shard_map/dot_general | solution.py:75
  350.7 12.7 %fusion.29 = bf16[1536,1024]{1,0:T(8,128)(2,1)} fusion(bf16[2304,1536]{1,0:T(8,128)(2,1)} %get-tuple-element.85, bf16[2,2304,1024]{2,1,0:T(8,128)(2,1)} %get-tuple-element.86), kind=kOutput, calls=%fused_computation.42 | convolution fusion | flops 7249330176 | bytes 14942208 | tf_op jit(solution)/shard_map/dot_general | solution.py:75
  364.0 2.4 collective-permute-done.28
  374.3 7.0 collective-permute-done.29
  384.5 2.6 collective-permute-done.31
  390.4 13.0 %fusion.32 = bf16[1536,1024]{1,0:T(8,128)(2,1)} fusion(bf16[2304,1536]{1,0:T(8,128)(2,1)} %get-tuple-element.85, bf16[2,2304,1024]{2,1,0:T(8,128)(2,1)} %get-tuple-element.86), kind=kOutput, calls=%fused_computation.43 | convolution fusion | flops 7249330176 | bytes 14942208 | tf_op jit(solution)/shard_map/dot_general | solution.py:75
  403.4 3.4 collective-permute-done.33
  406.8 3.3 collective-permute-done.32
  410.1 2.5 convert_add_fusion.2
  415.3 3.0 fusion.136
  434.8 4.5 all-to-all-start.1
  440.3 2.4 add_convert_fusion.24
  442.7 6.2 collective-permute-done.69
  448.9 2.2 add_convert_fusion.23
  452.3 34.6 %all-to-all-done.1 = bf16[288,4,384]{2,0,1:T(8,128)(2,1)S(1)} async-done(((bf16[288,4,384]{2,0,1:T(8,128)(2,1)}), bf16[288,4,384]{2,0,1:T(8,128)(2,1)S(1)}, u32[]{:S(2)}, u32[]{:S(2)}) %all-to-all-start.1) | async-done | bytes 884768 | tf_op jit(solution)/shard_map/all_to_all | solution.py:558
  487.9 9.3 %fusion.40 = f32[1536,2,64]{0,2,1:T(8,128)S(1)} fusion(bf16[512,2,3,64]{0,3,2,1:T(8,128)(2,1)S(1)} %bitcast.326, f32[2,3,512,1536]{2,3,1,0:T(8,128)} %get-tuple-element.283, f32[2,3,512]{2,1,0:T(4,128)} %log_add_fusion.1), kind=kOutput, calls=%fused_computation.72 | convolution fusion | flops 613416960 | bytes 20066304 | tf_op jit(solution)/shard_map/hgrk,rhgd->khd/dot_general | solution.py:134
  497.3 12.5 %fusion.3 = (f32[2,3,512]{2,1,0:T(4,128)S(1)}, f32[2,1536,512,3]{2,1,3,0:T(8,128)}) fusion(f32[2,3,512,1536]{2,3,1,0:T(8,128)} %get-tuple-element.283, f32[2,3,512]{2,1,0:T(4,128)S(1)} %copy-done.46, bf16[1536,2,64,1]{0,2,3,1:T(8,128)(2,1)S(1)} %bitcast.349, bf16[512,2,3,64]{0,3,2,1:T(8,128)(2,1)S(1)} %bitcast.327), kind=kOutput, calls=%fused_computation.7 | convolution fusion | flops 618132480 | bytes 38559744 | tf_op jit(solution)/shard_map/rhgd,khd->hgrk/dot_general | solution.py:120
  510.9 9.0 %fusion.43 = f32[1536,2,64]{0,2,1:T(8,128)} fusion(bf16[512,2,3,64]{0,3,2,1:T(8,128)(2,1)S(1)} %bitcast.328, f32[2,3,512,1536]{2,3,1,0:T(8,128)} %get-tuple-element.281, f32[2,3,512]{2,1,0:T(4,128)S(1)} %log_add_fusion), kind=kOutput, calls=%fused_computation.73 | convolution fusion | flops 613416960 | bytes 20066304 | tf_op jit(solution)/shard_map/hgrk,rhgd->khd/dot_general | solution.py:134
  519.9 12.0 %fusion = (f32[2,3,512]{2,1,0:T(4,128)S(1)}, f32[2,1536,512,3]{2,1,3,0:T(8,128)}) fusion(f32[2,3,512,1536]{2,3,1,0:T(8,128)} %get-tuple-element.281, f32[2,3,512]{2,1,0:T(4,128)S(1)} %log_add_fusion, bf16[1536,2,64,1]{0,2,3,1:T(8,128)(2,1)S(1)} %bitcast.347, bf16[512,2,3,64]{0,3,2,1:T(8,128)(2,1)S(1)} %bitcast.329), kind=kOutput, calls=%fused_computation.2 | convolution fusion | flops 618132480 | bytes 38559744 | tf_op jit(solution)/shard_map/rhgd,khd->hgrk/dot_general | solution.py:120
  532.2 19.3 %fusion.5 = bf16[2,3,512,1536]{2,3,1,0:T(8,128)(2,1)} fusion(f32[2,1536,512,3]{2,1,3,0:T(8,128)} %get-tuple-element.296, f32[2,3,512,1536]{2,3,1,0:T(8,128)} %get-tuple-element.283, f32[2,3,512]{2,1,0:T(4,128)S(1)} %get-tuple-element.295, f32[2,3,512]{2,1,0:T(4,128)S(1)} %copy-done.46), kind=kLoop, calls=%fused_computation.9 | loop fusion | flops 18874368 | bytes 47210496 | tf_op jit(solution)/shard_map/convert_element_type | solution.py:124
  551.4 7.4 %fusion.49 = f32[1536,2,64]{0,2,1:T(8,128)S(1)} fusion(bf16[512,2,3,64]{0,3,2,1:T(8,128)(2,1)S(1)} %bitcast.323, bf16[2,3,512,1536]{2,3,1,0:T(8,128)(2,1)} %fusion.5), kind=kOutput, calls=%fused_computation.79 | convolution fusion | flops 604176384 | bytes 10616832 | tf_op jit(solution)/shard_map/hgrk,rhgd->khd/dot_general | solution.py:131
  558.9 13.8 %fusion.2 = bf16[2,3,512,1536]{2,3,1,0:T(8,128)(2,1)} fusion(f32[2,1536,512,3]{2,1,3,0:T(8,128)} %get-tuple-element.294, f32[2,3,512,1536]{2,3,1,0:T(8,128)S(1)} %bitcast.305, f32[2,3,512]{2,1,0:T(4,128)S(1)} %get-tuple-element.293, f32[2,3,512]{2,1,0:T(4,128)S(1)} %log_add_fusion), kind=kLoop, calls=%fused_computation.4 | loop fusion | flops 18874368 | bytes 47210496 | tf_op jit(solution)/shard_map/convert_element_type | solution.py:124
  572.7 6.8 fusion.47
  602.8 9.3 %fusion.22 = (bf16[1536]{0:T(1024)(128)(2,1)S(1)}, bf16[1152,1536]{1,0:T(8,128)(2,1)}) fusion(bf16[1152,1536]{1,0:T(8,128)(2,1)S(1)} %copy-done.18, f32[1152]{0:T(1024)S(1)} %copy-done.75, bf16[1536,640]{1,0:T(8,128)(2,1)S(1)} %bitcast.375, bf16[512,128]{0,1:T(8,128)(2,1)S(1)} %bitcast.368, bf16[512,128]{0,1:T(8,128)(2,1)S(1)} %bitcast.370, ...), kind=kOutput, calls=%fused_computation.35 | convolution fusion | flops 2281142784 | bytes 10526208 | tf_op jit(solution)/shard_map/dot_general | solution.py:65
  618.7 8.2 %collective-permute-done.39 = bf16[144,1536]{1,0:T(8,128)(2,1)S(1)} collective-permute-done((bf16[144,1536]{1,0:T(8,128)(2,1)}, bf16[144,1536]{1,0:T(8,128)(2,1)S(1)}, u32[]{:S(2)}, u32[]{:S(2)}) %collective-permute-start.39) | collective-permute-done | bytes 442400 | tf_op jit(solution)/shard_map/ppermute | solution.py:168
  627.0 2.6 collective-permute-start.76
  630.0 2.9 convolution_convert_fusion.1
  634.6 4.2 collective-permute-done.76
  639.5 14.6 %collective-permute-done.75 = bf16[192,384]{1,0:T(8,128)(2,1)S(1)} collective-permute-done((bf16[192,384]{1,0:T(8,128)(2,1)S(1)}, bf16[192,384]{1,0:T(8,128)(2,1)S(1)}, u32[]{:S(2)}, u32[]{:S(2)}) %collective-permute-start.75) | collective-permute-done | bytes 147488 | tf_op jit(solution)/shard_map/ppermute | solution.py:251
  657.9 9.3 %collective-permute-done.36 = bf16[144,1536]{1,0:T(8,128)(2,1)S(1)} collective-permute-done((bf16[144,1536]{1,0:T(8,128)(2,1)S(1)}, bf16[144,1536]{1,0:T(8,128)(2,1)S(1)}, u32[]{:S(2)}, u32[]{:S(2)}) %collective-permute-start.36) | collective-permute-done | bytes 442400 | tf_op jit(solution)/shard_map/ppermute | solution.py:168
  667.8 8.2 %collective-permute-done.42 = bf16[144,1536]{1,0:T(8,128)(2,1)S(1)} collective-permute-done((bf16[144,1536]{1,0:T(8,128)(2,1)S(1)}, bf16[144,1536]{1,0:T(8,128)(2,1)S(1)}, u32[]{:S(2)}, u32[]{:S(2)}) %collective-permute-start.42) | collective-permute-done | bytes 442400 | tf_op jit(solution)/shard_map/ppermute | solution.py:168
  676.8 4.9 collective-permute-done.59
  684.2 2.0 collective-permute-start.63
  710.1 2.9 fusion.54
  (504 shorter events, 143.6 us)
Async XLA Ops:
  7.2 82.2 %all-gather.5.cloned.1.call-start = ((), (), s32[]{:S(2)}) async-start(), calls=%async_computation.6 | async-start | bytes 4423680 | tf_op jit(solution)/shard_map/all_gather | solution.py:437
  7.9 189.4 %all-gather.7.cloned.1.call-start = ((), (), s32[]{:S(2)}) async-start(), calls=%async_computation.7 | async-start | bytes 5308416 | tf_op jit(solution)/shard_map/all_gather | solution.py:443
  10.5 57.3 %collective-permute-start.3 = (bf16[192,640]{1,0:T(8,128)(2,1)S(1)}, bf16[192,640]{1,0:T(8,128)(2,1)S(1)}, u32[]{:S(2)}, u32[]{:S(2)}) collective-permute-start(bf16[192,640]{1,0:T(8,128)(2,1)S(1)} %constant_dynamic-update-slice_fusion), channel_id=1, source_target_pairs={{0,16},{4,20},{8,24},{12,28},{16,0},{20,4},{24,8},{28,12},{1,17},{... | collective-permute-start | bytes 737288 | tf_op jit(solution)/shard_map/ppermute | solution.py:168
  13.6 56.3 %collective-permute-start.1 = (bf16[192,640]{1,0:T(8,128)(2,1)S(1)}, bf16[192,640]{1,0:T(8,128)(2,1)S(1)}, u32[]{:S(2)}, u32[]{:S(2)}) collective-permute-start(bf16[192,640]{1,0:T(8,128)(2,1)S(1)} %constant_dynamic-update-slice_fusion), channel_id=1, source_target_pairs={{0,8},{4,12},{8,0},{12,4},{16,24},{20,28},{24,16},{28,20},{1,9},{5... | collective-permute-start | bytes 737288 | tf_op jit(solution)/shard_map/ppermute | solution.py:168
  15.1 55.5 %collective-permute-start = (bf16[192,640]{1,0:T(8,128)(2,1)S(1)}, bf16[192,640]{1,0:T(8,128)(2,1)S(1)}, u32[]{:S(2)}, u32[]{:S(2)}) collective-permute-start(bf16[192,640]{1,0:T(8,128)(2,1)S(1)} %constant_dynamic-update-slice_fusion), channel_id=1, source_target_pairs={{0,4},{4,0},{8,12},{12,8},{16,20},{20,16},{24,28},{28,24},{1,5},{5... | collective-permute-start | bytes 737288 | tf_op jit(solution)/shard_map/ppermute | solution.py:168
  169.2 28.0 %all-to-all-start = ((bf16[4,288,384]{2,1,0:T(8,128)(2,1)}), bf16[4,288,384]{2,1,0:T(8,128)(2,1)S(1)}, u32[]{:S(2)}, u32[]{:S(2)}) async-start(bf16[4,288,384]{2,1,0:T(8,128)(2,1)} %bitcast.47), calls=%async_computation | async-start | bytes 1769472 | tf_op jit(solution)/shard_map/all_to_all | solution.py:497
  172.7 527.8 %reduce-scatter.11.cloned.1.call-start = ((), (), s32[]{:S(2)}) async-start(), calls=%async_computation.11 | async-start | bytes 3932160 | tf_op jit(solution)/shard_map/reduce_scatter | solution.py:641
  172.8 22.3 %collective-permute-start.16 = (bf16[288,1536]{1,0:T(8,128)(2,1)}, bf16[288,1536]{1,0:T(8,128)(2,1)S(1)}, u32[]{:S(2)}, u32[]{:S(2)}) collective-permute-start(bf16[288,1536]{1,0:T(8,128)(2,1)} %og_even), channel_id=1, source_target_pairs={{0,16},{4,20},{8,24},{12,28},{16,0},{20,4},{24,8},{28,12},{1,17},{... | collective-permute-start | bytes 2654216 | tf_op jit(solution)/shard_map/ppermute | solution.py:168
  175.0 34.6 %collective-permute-start.12 = (bf16[288,1536]{1,0:T(8,128)(2,1)}, bf16[288,1536]{1,0:T(8,128)(2,1)}, u32[]{:S(2)}, u32[]{:S(2)}) collective-permute-start(bf16[288,1536]{1,0:T(8,128)(2,1)} %og_even), channel_id=1, source_target_pairs={{0,8},{4,12},{8,0},{12,4},{16,24},{20,28},{24,16},{28,20},{1,9},{5... | collective-permute-start | bytes 2654216 | tf_op jit(solution)/shard_map/ppermute | solution.py:168
  195.9 16.0 %collective-permute-start.21 = (bf16[144,1536]{1,0:T(8,128)(2,1)}, bf16[144,1536]{1,0:T(8,128)(2,1)}, u32[]{:S(2)}, u32[]{:S(2)}) collective-permute-start(bf16[144,1536]{1,0:T(8,128)(2,1)} %slice.615), channel_id=1, source_target_pairs={{0,8},{4,12},{8,0},{12,4},{16,24},{20,28},{24,16},{28,20},{1,9},{5... | collective-permute-start | bytes 1327112 | tf_op jit(solution)/shard_map/ppermute | solution.py:168
  207.5 34.1 %collective-permute-start.14 = (bf16[288,1664]{1,0:T(8,128)(2,1)}, bf16[288,1664]{1,0:T(8,128)(2,1)}, u32[]{:S(2)}, u32[]{:S(2)}) collective-permute-start(bf16[288,1664]{1,0:T(8,128)(2,1)} %concatenate.120.x_even), channel_id=1, source_target_pairs={{0,16},{4,20},{8,24},{12,28},{16,0},{20,4},{24,8},{28,12},{1,17},{... | collective-permute-start | bytes 2875400 | tf_op jit(solution)/shard_map/ppermute | solution.py:168
  208.7 35.3 %collective-permute-start.10 = (bf16[288,1664]{1,0:T(8,128)(2,1)}, bf16[288,1664]{1,0:T(8,128)(2,1)}, u32[]{:S(2)}, u32[]{:S(2)}) collective-permute-start(bf16[288,1664]{1,0:T(8,128)(2,1)} %concatenate.120.x_even), channel_id=1, source_target_pairs={{0,8},{4,12},{8,0},{12,4},{16,24},{20,28},{24,16},{28,20},{1,9},{5... | collective-permute-start | bytes 2875400 | tf_op jit(solution)/shard_map/ppermute | solution.py:168
  209.6 38.3 %collective-permute-start.8 = (bf16[288,1664]{1,0:T(8,128)(2,1)}, bf16[288,1664]{1,0:T(8,128)(2,1)}, u32[]{:S(2)}, u32[]{:S(2)}) collective-permute-start(bf16[288,1664]{1,0:T(8,128)(2,1)} %concatenate.120.x_even), channel_id=1, source_target_pairs={{0,4},{4,0},{8,12},{12,8},{16,20},{20,16},{24,28},{28,24},{1,5},{5... | collective-permute-start | bytes 2875400 | tf_op jit(solution)/shard_map/ppermute | solution.py:168
  209.6 37.0 %collective-permute-start.9 = (bf16[288,1536]{1,0:T(8,128)(2,1)}, bf16[288,1536]{1,0:T(8,128)(2,1)}, u32[]{:S(2)}, u32[]{:S(2)}) collective-permute-start(bf16[288,1536]{1,0:T(8,128)(2,1)} %og_even), channel_id=1, source_target_pairs={{0,4},{4,0},{8,12},{12,8},{16,20},{20,16},{24,28},{28,24},{1,5},{5... | collective-permute-start | bytes 2654216 | tf_op jit(solution)/shard_map/ppermute | solution.py:168
  211.9 27.9 %collective-permute-start.22 = (bf16[144,1536]{1,0:T(8,128)(2,1)}, bf16[144,1536]{1,0:T(8,128)(2,1)}, u32[]{:S(2)}, u32[]{:S(2)}) collective-permute-start(bf16[144,1536]{1,0:T(8,128)(2,1)} %slice.616), channel_id=1, source_target_pairs={{0,16},{4,20},{8,24},{12,28},{16,0},{20,4},{24,8},{28,12},{1,17},{... | collective-permute-start | bytes 1327112 | tf_op jit(solution)/shard_map/ppermute | solution.py:168
  239.8 54.8 %collective-permute-start.17 = (bf16[288,1536]{1,0:T(8,128)(2,1)}, bf16[288,1536]{1,0:T(8,128)(2,1)}, u32[]{:S(2)}, u32[]{:S(2)}) collective-permute-start(bf16[288,1536]{1,0:T(8,128)(2,1)} %copy-done.28), channel_id=1, source_target_pairs={{0,4},{4,0},{8,12},{12,8},{16,20},{20,16},{24,28},{28,24},{1,5},{5... | collective-permute-start | bytes 2654216 | tf_op jit(solution)/shard_map/ppermute | solution.py:168
  241.6 30.9 %collective-permute-start.13 = (bf16[288,1536]{1,0:T(8,128)(2,1)}, bf16[288,1536]{1,0:T(8,128)(2,1)}, u32[]{:S(2)}, u32[]{:S(2)}) collective-permute-start(bf16[288,1536]{1,0:T(8,128)(2,1)} %collective-permute-done.12.og_even), channel_id=1, source_target_pairs={{0,4},{4,0},{8,12},{12,8},{16,20},{20,16},{24,28},{28,24},{1,5},{5... | collective-permute-start | bytes 2654216 | tf_op jit(solution)/shard_map/ppermute | solution.py:168
  244.0 25.3 %collective-permute-start.18 = (bf16[144,1664]{1,0:T(8,128)(2,1)}, bf16[144,1664]{1,0:T(8,128)(2,1)}, u32[]{:S(2)}, u32[]{:S(2)}) collective-permute-start(bf16[144,1664]{1,0:T(8,128)(2,1)} %slice.613), channel_id=1, source_target_pairs={{0,8},{4,12},{8,0},{12,4},{16,24},{20,28},{24,16},{28,20},{1,9},{5... | collective-permute-start | bytes 1437704 | tf_op jit(solution)/shard_map/ppermute | solution.py:168
  246.6 25.1 %collective-permute-start.19 = (bf16[144,1664]{1,0:T(8,128)(2,1)}, bf16[144,1664]{1,0:T(8,128)(2,1)S(1)}, u32[]{:S(2)}, u32[]{:S(2)}) collective-permute-start(bf16[144,1664]{1,0:T(8,128)(2,1)} %slice.614), channel_id=1, source_target_pairs={{0,16},{4,20},{8,24},{12,28},{16,0},{20,4},{24,8},{28,12},{1,17},{... | collective-permute-start | bytes 1437704 | tf_op jit(solution)/shard_map/ppermute | solution.py:168
  247.9 25.2 %collective-permute-start.11 = (bf16[288,1664]{1,0:T(8,128)(2,1)}, bf16[288,1664]{1,0:T(8,128)(2,1)}, u32[]{:S(2)}, u32[]{:S(2)}) collective-permute-start(bf16[288,1664]{1,0:T(8,128)(2,1)} %collective-permute-done.10.x_even), channel_id=1, source_target_pairs={{0,4},{4,0},{8,12},{12,8},{16,20},{20,16},{24,28},{28,24},{1,5},{5... | collective-permute-start | bytes 2875400 | tf_op jit(solution)/shard_map/ppermute | solution.py:168
  269.3 46.9 %collective-permute-start.23 = (bf16[288,1536]{1,0:T(8,128)(2,1)}, bf16[288,1536]{1,0:T(8,128)(2,1)}, u32[]{:S(2)}, u32[]{:S(2)}) collective-permute-start(bf16[288,1536]{1,0:T(8,128)(2,1)} %constant_dynamic-update-slice_fusion.7.og_even), channel_id=1, source_target_pairs={{0,4},{4,0},{8,12},{12,8},{16,20},{20,16},{24,28},{28,24},{1,5},{5... | collective-permute-start | bytes 2654216 | tf_op jit(solution)/shard_map/ppermute | solution.py:168
  271.7 23.0 %collective-permute-start.15 = (bf16[288,1664]{1,0:T(8,128)(2,1)}, bf16[288,1664]{1,0:T(8,128)(2,1)}, u32[]{:S(2)}, u32[]{:S(2)}) collective-permute-start(bf16[288,1664]{1,0:T(8,128)(2,1)} %collective-permute-done.14.x_even), channel_id=1, source_target_pairs={{0,4},{4,0},{8,12},{12,8},{16,20},{20,16},{24,28},{28,24},{1,5},{5... | collective-permute-start | bytes 2875400 | tf_op jit(solution)/shard_map/ppermute | solution.py:168
  272.5 43.7 %collective-permute-start.20 = (bf16[288,1664]{1,0:T(8,128)(2,1)}, bf16[288,1664]{1,0:T(8,128)(2,1)}, u32[]{:S(2)}, u32[]{:S(2)}) collective-permute-start(bf16[288,1664]{1,0:T(8,128)(2,1)} %constant_dynamic-update-slice_fusion.5.x_even), channel_id=1, source_target_pairs={{0,4},{4,0},{8,12},{12,8},{16,20},{20,16},{24,28},{28,24},{1,5},{5... | collective-permute-start | bytes 2875400 | tf_op jit(solution)/shard_map/ppermute | solution.py:168
  350.6 352.8 %reduce-scatter.7.cloned.1.call-start = ((), (), s32[]{:S(2)}) async-start(), calls=%async_computation.9 | async-start | bytes 3932160 | tf_op jit(solution)/shard_map/reduce_scatter | solution.py:643
  363.4 341.3 %reduce-scatter.9.cloned.1.call-start = ((), (), s32[]{:S(2)}) async-start(), calls=%async_computation.10 | async-start | bytes 3932160 | tf_op jit(solution)/shard_map/reduce_scatter | solution.py:643
  363.7 10.5 %collective-permute-start.27 = (bf16[288,1664]{1,0:T(8,128)(2,1)}, bf16[288,1664]{1,0:T(8,128)(2,1)S(1)}, u32[]{:S(2)}, u32[]{:S(2)}) collective-permute-start(bf16[288,1664]{1,0:T(8,128)(2,1)} %get-tuple-element.80), channel_id=1, source_target_pairs={{0,4},{4,0},{8,12},{12,8},{16,20},{20,16},{24,28},{28,24},{1,5},{5... | collective-permute-start | bytes 2875400 | tf_op jit(solution)/shard_map/ppermute | solution.py:168
  368.2 13.1 %collective-permute-start.29 = (bf16[144,1664]{1,0:T(8,128)(2,1)S(1)}, bf16[144,1664]{1,0:T(8,128)(2,1)S(1)}, u32[]{:S(2)}, u32[]{:S(2)}) collective-permute-start(bf16[144,1664]{1,0:T(8,128)(2,1)S(1)} %get-tuple-element.204), channel_id=1, source_target_pairs={{0,8},{4,12},{8,0},{12,4},{16,24},{20,28},{24,16},{28,20},{1,9},{5... | collective-permute-start | bytes 1437704 | tf_op jit(solution)/shard_map/ppermute | solution.py:168
  370.1 14.5 %collective-permute-start.25 = (bf16[288,1664]{1,0:T(8,128)(2,1)}, bf16[288,1664]{1,0:T(8,128)(2,1)S(1)}, u32[]{:S(2)}, u32[]{:S(2)}) collective-permute-start(bf16[288,1664]{1,0:T(8,128)(2,1)} %get-tuple-element.78), channel_id=1, source_target_pairs={{0,4},{4,0},{8,12},{12,8},{16,20},{20,16},{24,28},{28,24},{1,5},{5... | collective-permute-start | bytes 2875400 | tf_op jit(solution)/shard_map/ppermute | solution.py:168
  372.8 30.6 %collective-permute-start.24 = (bf16[288,1664]{1,0:T(8,128)(2,1)}, bf16[288,1664]{1,0:T(8,128)(2,1)}, u32[]{:S(2)}, u32[]{:S(2)}) collective-permute-start(bf16[288,1664]{1,0:T(8,128)(2,1)} %get-tuple-element.76), channel_id=1, source_target_pairs={{0,4},{4,0},{8,12},{12,8},{16,20},{20,16},{24,28},{28,24},{1,5},{5... | collective-permute-start | bytes 2875400 | tf_op jit(solution)/shard_map/ppermute | solution.py:168
  373.3 13.8 %collective-permute-start.31 = (bf16[144,1664]{1,0:T(8,128)(2,1)S(1)}, bf16[144,1664]{1,0:T(8,128)(2,1)S(1)}, u32[]{:S(2)}, u32[]{:S(2)}) collective-permute-start(bf16[144,1664]{1,0:T(8,128)(2,1)S(1)} %get-tuple-element.205), channel_id=1, source_target_pairs={{0,16},{4,20},{8,24},{12,28},{16,0},{20,4},{24,8},{28,12},{1,17},{... | collective-permute-start | bytes 1437704 | tf_op jit(solution)/shard_map/ppermute | solution.py:168
  382.5 20.9 %collective-permute-start.30 = (bf16[144,1664]{1,0:T(8,128)(2,1)}, bf16[144,1664]{1,0:T(8,128)(2,1)}, u32[]{:S(2)}, u32[]{:S(2)}) collective-permute-start(bf16[144,1664]{1,0:T(8,128)(2,1)} %get-tuple-element.202), channel_id=1, source_target_pairs={{0,16},{4,20},{8,24},{12,28},{16,0},{20,4},{24,8},{28,12},{1,17},{... | collective-permute-start | bytes 1437704 | tf_op jit(solution)/shard_map/ppermute | solution.py:168
  383.2 23.6 %collective-permute-start.33 = (bf16[144,1664]{1,0:T(8,128)(2,1)}, bf16[144,1664]{1,0:T(8,128)(2,1)}, u32[]{:S(2)}, u32[]{:S(2)}) collective-permute-start(bf16[144,1664]{1,0:T(8,128)(2,1)} %get-tuple-element.203), channel_id=1, source_target_pairs={{0,16},{4,20},{8,24},{12,28},{16,0},{20,4},{24,8},{28,12},{1,17},{... | collective-permute-start | bytes 1437704 | tf_op jit(solution)/shard_map/ppermute | solution.py:168
  388.4 18.5 %collective-permute-start.26 = (bf16[144,1664]{1,0:T(8,128)(2,1)}, bf16[144,1664]{1,0:T(8,128)(2,1)}, u32[]{:S(2)}, u32[]{:S(2)}) collective-permute-start(bf16[144,1664]{1,0:T(8,128)(2,1)} %get-tuple-element.200), channel_id=1, source_target_pairs={{0,8},{4,12},{8,0},{12,4},{16,24},{20,28},{24,16},{28,20},{1,9},{5... | collective-permute-start | bytes 1437704 | tf_op jit(solution)/shard_map/ppermute | solution.py:168
  389.3 20.8 %collective-permute-start.32 = (bf16[144,1664]{1,0:T(8,128)(2,1)}, bf16[144,1664]{1,0:T(8,128)(2,1)}, u32[]{:S(2)}, u32[]{:S(2)}) collective-permute-start(bf16[144,1664]{1,0:T(8,128)(2,1)} %get-tuple-element.201), channel_id=1, source_target_pairs={{0,8},{4,12},{8,0},{12,4},{16,24},{20,28},{24,16},{28,20},{1,9},{5... | collective-permute-start | bytes 1437704 | tf_op jit(solution)/shard_map/ppermute | solution.py:168
  426.5 13.8 %collective-permute-start.65 = (bf16[192,1536]{1,0:T(8,128)(2,1)}, bf16[192,1536]{1,0:T(8,128)(2,1)}, u32[]{:S(2)}, u32[]{:S(2)}) collective-permute-start(bf16[192,1536]{1,0:T(8,128)(2,1)} %convolution_convert_fusion.7), channel_id=1, source_target_pairs={{0,4},{4,0},{8,12},{12,8},{16,20},{20,16},{24,28},{28,24},{1,5},{5... | collective-permute-start | bytes 1769480 | tf_op jit(solution)/shard_map/ppermute | solution.py:168
  429.5 10.8 %collective-permute-start.71 = (bf16[96,1536]{1,0:T(8,128)(2,1)}, bf16[96,1536]{1,0:T(8,128)(2,1)}, u32[]{:S(2)}, u32[]{:S(2)}) collective-permute-start(bf16[96,1536]{1,0:T(8,128)(2,1)} %get-tuple-element.220), channel_id=1, source_target_pairs={{0,16},{4,20},{8,24},{12,28},{16,0},{20,4},{24,8},{28,12},{1,17},{... | collective-permute-start | bytes 884744 | tf_op jit(solution)/shard_map/ppermute | solution.py:168
  431.9 10.8 %collective-permute-start.67 = (bf16[192,1536]{1,0:T(8,128)(2,1)}, bf16[192,1536]{1,0:T(8,128)(2,1)}, u32[]{:S(2)}, u32[]{:S(2)}) collective-permute-start(bf16[192,1536]{1,0:T(8,128)(2,1)} %convolution_convert_fusion.5), channel_id=1, source_target_pairs={{0,4},{4,0},{8,12},{12,8},{16,20},{20,16},{24,28},{28,24},{1,5},{5... | collective-permute-start | bytes 1769480 | tf_op jit(solution)/shard_map/ppermute | solution.py:168
  434.8 52.1 %all-to-all-start.1 = ((bf16[288,4,384]{2,0,1:T(8,128)(2,1)}), bf16[288,4,384]{2,0,1:T(8,128)(2,1)S(1)}, u32[]{:S(2)}, u32[]{:S(2)}) async-start(bf16[288,4,384]{2,0,1:T(8,128)(2,1)} %bitcast.300), calls=%async_computation.1 | async-start | bytes 1769472 | tf_op jit(solution)/shard_map/all_to_all | solution.py:558
  439.3 269.2 %reduce-scatter.5.cloned.1.call-start = ((), (), s32[]{:S(2)}) async-start(), calls=%async_computation.8 | async-start | bytes 4423680 | tf_op jit(solution)/shard_map/reduce_scatter | solution.py:620
  439.3 11.9 %collective-permute-start.38 = (bf16[288,1536]{1,0:T(8,128)(2,1)}, bf16[288,1536]{1,0:T(8,128)(2,1)S(1)}, u32[]{:S(2)}, u32[]{:S(2)}) collective-permute-start(bf16[288,1536]{1,0:T(8,128)(2,1)} %get-tuple-element.95), channel_id=1, source_target_pairs={{0,4},{4,0},{8,12},{12,8},{16,20},{20,16},{24,28},{28,24},{1,5},{5... | collective-permute-start | bytes 2654216 | tf_op jit(solution)/shard_map/ppermute | solution.py:168
  439.5 9.4 %collective-permute-start.69 = (bf16[96,1536]{1,0:T(8,128)(2,1)}, bf16[96,1536]{1,0:T(8,128)(2,1)S(1)}, u32[]{:S(2)}, u32[]{:S(2)}) collective-permute-start(bf16[96,1536]{1,0:T(8,128)(2,1)} %get-tuple-element.221), channel_id=1, source_target_pairs={{0,8},{4,12},{8,0},{12,4},{16,24},{20,28},{24,16},{28,20},{1,9},{5... | collective-permute-start | bytes 884744 | tf_op jit(solution)/shard_map/ppermute | solution.py:168
  583.7 14.3 %collective-permute-start.44 = (bf16[128,256]{0,1:T(8,128)(2,1)S(1)}, bf16[128,256]{0,1:T(8,128)(2,1)S(1)}, u32[]{:S(2)}, u32[]{:S(2)}) collective-permute-start(bf16[128,256]{0,1:T(8,128)(2,1)S(1)} %get-tuple-element.242), channel_id=1, source_target_pairs={{0,4},{4,0},{8,12},{12,8},{16,20},{20,16},{24,28},{28,24},{1,5},{5... | collective-permute-start | bytes 196616 | tf_op jit(solution)/shard_map/ppermute | solution.py:168
  584.3 11.2 %collective-permute-start.47 = (bf16[128,256]{0,1:T(8,128)(2,1)S(1)}, bf16[128,256]{0,1:T(8,128)(2,1)S(1)}, u32[]{:S(2)}, u32[]{:S(2)}) collective-permute-start(bf16[128,256]{0,1:T(8,128)(2,1)S(1)} %get-tuple-element.246), channel_id=1, source_target_pairs={{0,4},{4,0},{8,12},{12,8},{16,20},{20,16},{24,28},{28,24},{1,5},{5... | collective-permute-start | bytes 196616 | tf_op jit(solution)/shard_map/ppermute | solution.py:168
  598.1 14.1 %collective-permute-start.64 = (bf16[192,1536]{1,0:T(8,128)(2,1)}, bf16[192,1536]{1,0:T(8,128)(2,1)S(1)}, u32[]{:S(2)}, u32[]{:S(2)}) collective-permute-start(bf16[192,1536]{1,0:T(8,128)(2,1)} %convolution_convert_fusion.9), channel_id=1, source_target_pairs={{0,4},{4,0},{8,12},{12,8},{16,20},{20,16},{24,28},{28,24},{1,5},{5... | collective-permute-start | bytes 1769480 | tf_op jit(solution)/shard_map/ppermute | solution.py:168
  598.2 14.1 %collective-permute-start.72 = (bf16[96,1536]{1,0:T(8,128)(2,1)}, bf16[96,1536]{1,0:T(8,128)(2,1)S(1)}, u32[]{:S(2)}, u32[]{:S(2)}) collective-permute-start(bf16[96,1536]{1,0:T(8,128)(2,1)} %get-tuple-element.218), channel_id=1, source_target_pairs={{0,8},{4,12},{8,0},{12,4},{16,24},{20,28},{24,16},{28,20},{1,9},{5... | collective-permute-start | bytes 884744 | tf_op jit(solution)/shard_map/ppermute | solution.py:168
  599.0 15.2 %collective-permute-start.66 = (bf16[96,1536]{1,0:T(8,128)(2,1)}, bf16[96,1536]{1,0:T(8,128)(2,1)}, u32[]{:S(2)}, u32[]{:S(2)}) collective-permute-start(bf16[96,1536]{1,0:T(8,128)(2,1)} %get-tuple-element.219), channel_id=1, source_target_pairs={{0,8},{4,12},{8,0},{12,4},{16,24},{20,28},{24,16},{28,20},{1,9},{5... | collective-permute-start | bytes 884744 | tf_op jit(solution)/shard_map/ppermute | solution.py:168
  600.3 13.9 %collective-permute-start.73 = (bf16[96,1536]{1,0:T(8,128)(2,1)}, bf16[96,1536]{1,0:T(8,128)(2,1)}, u32[]{:S(2)}, u32[]{:S(2)}) collective-permute-start(bf16[96,1536]{1,0:T(8,128)(2,1)} %get-tuple-element.222), channel_id=1, source_target_pairs={{0,16},{4,20},{8,24},{12,28},{16,0},{20,4},{24,8},{28,12},{1,17},{... | collective-permute-start | bytes 884744 | tf_op jit(solution)/shard_map/ppermute | solution.py:168
  601.3 14.4 %collective-permute-start.70 = (bf16[96,1536]{1,0:T(8,128)(2,1)}, bf16[96,1536]{1,0:T(8,128)(2,1)}, u32[]{:S(2)}, u32[]{:S(2)}) collective-permute-start(bf16[96,1536]{1,0:T(8,128)(2,1)} %get-tuple-element.223), channel_id=1, source_target_pairs={{0,16},{4,20},{8,24},{12,28},{16,0},{20,4},{24,8},{28,12},{1,17},{... | collective-permute-start | bytes 884744 | tf_op jit(solution)/shard_map/ppermute | solution.py:168
  612.1 45.0 %collective-permute-start.34 = (bf16[288,1536]{1,0:T(8,128)(2,1)}, bf16[288,1536]{1,0:T(8,128)(2,1)S(1)}, u32[]{:S(2)}, u32[]{:S(2)}) collective-permute-start(bf16[288,1536]{1,0:T(8,128)(2,1)} %get-tuple-element.89), channel_id=1, source_target_pairs={{0,4},{4,0},{8,12},{12,8},{16,20},{20,16},{24,28},{28,24},{1,5},{5... | collective-permute-start | bytes 2654216 | tf_op jit(solution)/shard_map/ppermute | solution.py:168
  612.2 21.5 %collective-permute-start.35 = (bf16[288,1536]{1,0:T(8,128)(2,1)}, bf16[288,1536]{1,0:T(8,128)(2,1)S(1)}, u32[]{:S(2)}, u32[]{:S(2)}) collective-permute-start(bf16[288,1536]{1,0:T(8,128)(2,1)} %get-tuple-element.91), channel_id=1, source_target_pairs={{0,4},{4,0},{8,12},{12,8},{16,20},{20,16},{24,28},{28,24},{1,5},{5... | collective-permute-start | bytes 2654216 | tf_op jit(solution)/shard_map/ppermute | solution.py:168
  614.2 12.8 %collective-permute-start.39 = (bf16[144,1536]{1,0:T(8,128)(2,1)}, bf16[144,1536]{1,0:T(8,128)(2,1)S(1)}, u32[]{:S(2)}, u32[]{:S(2)}) collective-permute-start(bf16[144,1536]{1,0:T(8,128)(2,1)} %get-tuple-element.212), channel_id=1, source_target_pairs={{0,8},{4,12},{8,0},{12,4},{16,24},{20,28},{24,16},{28,20},{1,9},{5... | collective-permute-start | bytes 1327112 | tf_op jit(solution)/shard_map/ppermute | solution.py:168
  615.7 18.2 %collective-permute-start.41 = (bf16[144,1536]{1,0:T(8,128)(2,1)}, bf16[144,1536]{1,0:T(8,128)(2,1)S(1)}, u32[]{:S(2)}, u32[]{:S(2)}) collective-permute-start(bf16[144,1536]{1,0:T(8,128)(2,1)} %get-tuple-element.213), channel_id=1, source_target_pairs={{0,16},{4,20},{8,24},{12,28},{16,0},{20,4},{24,8},{28,12},{1,17},{... | collective-permute-start | bytes 1327112 | tf_op jit(solution)/shard_map/ppermute | solution.py:168
  618.5 15.9 %collective-permute-start.74 = (bf16[192,384]{1,0:T(8,128)(2,1)S(1)}, bf16[192,384]{1,0:T(8,128)(2,1)S(1)}, u32[]{:S(2)}, u32[]{:S(2)}) collective-permute-start(bf16[192,384]{1,0:T(8,128)(2,1)S(1)} %get-tuple-element.238), channel_id=1, source_target_pairs={{0,1},{1,2},{2,3},{3,0},{4,5},{5,6},{6,7},{7,4},{8,9},{9,10},{10,1... | collective-permute-start | bytes 442376 | tf_op jit(solution)/shard_map/ppermute | solution.py:251
  627.0 11.7 %collective-permute-start.76 = (bf16[192,384]{1,0:T(8,128)(2,1)S(1)}, bf16[192,384]{1,0:T(8,128)(2,1)S(1)}, u32[]{:S(2)}, u32[]{:S(2)}) collective-permute-start(bf16[192,384]{1,0:T(8,128)(2,1)S(1)} %get-tuple-element.239), channel_id=1, source_target_pairs={{0,3},{1,0},{2,1},{3,2},{4,7},{5,4},{6,5},{7,6},{8,11},{9,8},{10,9... | collective-permute-start | bytes 442376 | tf_op jit(solution)/shard_map/ppermute | solution.py:251
  633.7 20.4 %collective-permute-start.75 = (bf16[192,384]{1,0:T(8,128)(2,1)S(1)}, bf16[192,384]{1,0:T(8,128)(2,1)S(1)}, u32[]{:S(2)}, u32[]{:S(2)}) collective-permute-start(bf16[192,384]{1,0:T(8,128)(2,1)S(1)} %get-tuple-element.240), channel_id=1, source_target_pairs={{0,2},{1,3},{2,0},{3,1},{4,6},{5,7},{6,4},{7,5},{8,10},{9,11},{10,... | collective-permute-start | bytes 442376 | tf_op jit(solution)/shard_map/ppermute | solution.py:251
  633.8 21.0 %collective-permute-start.58 = (bf16[192,658]{0,1:T(8,128)(2,1)S(1)}, bf16[192,658]{0,1:T(8,128)(2,1)S(1)}, u32[]{:S(2)}, u32[]{:S(2)}) collective-permute-start(bf16[192,658]{0,1:T(8,128)(2,1)S(1)} %get-tuple-element.195), channel_id=1, source_target_pairs={{0,4},{4,0},{8,12},{12,8},{16,20},{20,16},{24,28},{28,24},{1,5},{5... | collective-permute-start | bytes 758024 | tf_op jit(solution)/shard_map/ppermute | solution.py:168
  634.4 22.9 %collective-permute-start.40 = (bf16[144,1536]{1,0:T(8,128)(2,1)S(1)}, bf16[144,1536]{1,0:T(8,128)(2,1)S(1)}, u32[]{:S(2)}, u32[]{:S(2)}) collective-permute-start(bf16[144,1536]{1,0:T(8,128)(2,1)S(1)} %get-tuple-element.210), channel_id=1, source_target_pairs={{0,16},{4,20},{8,24},{12,28},{16,0},{20,4},{24,8},{28,12},{1,17},{... | collective-permute-start | bytes 1327112 | tf_op jit(solution)/shard_map/ppermute | solution.py:168
  638.7 19.0 %collective-permute-start.43 = (bf16[144,1536]{1,0:T(8,128)(2,1)S(1)}, bf16[144,1536]{1,0:T(8,128)(2,1)S(1)}, u32[]{:S(2)}, u32[]{:S(2)}) collective-permute-start(bf16[144,1536]{1,0:T(8,128)(2,1)S(1)} %get-tuple-element.211), channel_id=1, source_target_pairs={{0,16},{4,20},{8,24},{12,28},{16,0},{20,4},{24,8},{28,12},{1,17},{... | collective-permute-start | bytes 1327112 | tf_op jit(solution)/shard_map/ppermute | solution.py:168
  654.1 13.0 %collective-permute-start.36 = (bf16[144,1536]{1,0:T(8,128)(2,1)S(1)}, bf16[144,1536]{1,0:T(8,128)(2,1)S(1)}, u32[]{:S(2)}, u32[]{:S(2)}) collective-permute-start(bf16[144,1536]{1,0:T(8,128)(2,1)S(1)} %get-tuple-element.208), channel_id=1, source_target_pairs={{0,8},{4,12},{8,0},{12,4},{16,24},{20,28},{24,16},{28,20},{1,9},{5... | collective-permute-start | bytes 1327112 | tf_op jit(solution)/shard_map/ppermute | solution.py:168
  654.9 21.0 %collective-permute-start.42 = (bf16[144,1536]{1,0:T(8,128)(2,1)S(1)}, bf16[144,1536]{1,0:T(8,128)(2,1)S(1)}, u32[]{:S(2)}, u32[]{:S(2)}) collective-permute-start(bf16[144,1536]{1,0:T(8,128)(2,1)S(1)} %get-tuple-element.209), channel_id=1, source_target_pairs={{0,8},{4,12},{8,0},{12,4},{16,24},{20,28},{24,16},{28,20},{1,9},{5... | collective-permute-start | bytes 1327112 | tf_op jit(solution)/shard_map/ppermute | solution.py:168
  657.2 30.2 %collective-permute-start.54 = (bf16[192,658]{0,1:T(8,128)(2,1)S(1)}, bf16[192,658]{0,1:T(8,128)(2,1)S(1)}, u32[]{:S(2)}, u32[]{:S(2)}) collective-permute-start(bf16[192,658]{0,1:T(8,128)(2,1)S(1)} %get-tuple-element.194), channel_id=1, source_target_pairs={{0,4},{4,0},{8,12},{12,8},{16,20},{20,16},{24,28},{28,24},{1,5},{5... | collective-permute-start | bytes 758024 | tf_op jit(solution)/shard_map/ppermute | solution.py:168
  657.3 19.5 %collective-permute-start.57 = (bf16[192,658]{0,1:T(8,128)(2,1)S(1)}, bf16[192,658]{0,1:T(8,128)(2,1)S(1)}, u32[]{:S(2)}, u32[]{:S(2)}) collective-permute-start(bf16[192,658]{0,1:T(8,128)(2,1)S(1)} %get-tuple-element.196), channel_id=1, source_target_pairs={{0,4},{4,0},{8,12},{12,8},{16,20},{20,16},{24,28},{28,24},{1,5},{5... | collective-permute-start | bytes 758024 | tf_op jit(solution)/shard_map/ppermute | solution.py:168
  657.8 19.0 %collective-permute-start.55 = (bf16[192,658]{0,1:T(8,128)(2,1)S(1)}, bf16[192,658]{0,1:T(8,128)(2,1)S(1)}, u32[]{:S(2)}, u32[]{:S(2)}) collective-permute-start(bf16[192,658]{0,1:T(8,128)(2,1)S(1)} %get-tuple-element.197), channel_id=1, source_target_pairs={{0,4},{4,0},{8,12},{12,8},{16,20},{20,16},{24,28},{28,24},{1,5},{5... | collective-permute-start | bytes 758024 | tf_op jit(solution)/shard_map/ppermute | solution.py:168
  667.2 9.6 %collective-permute-start.61 = (bf16[96,658]{0,1:T(8,128)(2,1)S(1)}, bf16[96,658]{0,1:T(8,128)(2,1)S(1)}, u32[]{:S(2)}, u32[]{:S(2)}) collective-permute-start(bf16[96,658]{0,1:T(8,128)(2,1)S(1)} %get-tuple-element.184), channel_id=1, source_target_pairs={{0,16},{4,20},{8,24},{12,28},{16,0},{20,4},{24,8},{28,12},{1,17},{... | collective-permute-start | bytes 379016 | tf_op jit(solution)/shard_map/ppermute | solution.py:168
  (113 other events, 1025.1 us)
Sparse Core Ops, SparseCore 0:
  9.6 79.8 all-gather.4
  91.3 37.9 all-gather.6
  350.7 60.1 reduce-scatter.10
  413.1 74.3 reduce-scatter.6
  489.7 63.8 reduce-scatter.8
  612.2 74.2 reduce-scatter.4

commit v3 on v2

--- a/solution.py
+++ b/solution.py
@@ -25,10 +25,6 @@
 
 def swiglu(gate_pre, up_pre):
     return jax.nn.silu(gate_pre) * up_pre
-
-
-def softmax_last(values):
-    return jax.nn.softmax(values, axis=-1)
 
 
 def rotary_tables(places, head_size):
@@ -81,69 +77,6 @@
     )
 
 
-def head_scores(query_matrix, key_matrix_rows, allowed, head_size):
-    total_row_count = query_matrix.shape[0]
-    kv_heads = key_matrix_rows.shape[1] // head_size
-    grouped_heads = query_matrix.reshape(total_row_count, kv_heads, -1, head_size)
-    key_head_split = key_matrix_rows.reshape(key_matrix_rows.shape[0], kv_heads, head_size)
-    scores = jnp.einsum(
-        "rhgd,khd->hgrk", grouped_heads, key_head_split, preferred_element_type=jnp.float32
-    ) * head_size ** (-0.5)
-    return jnp.where(allowed, scores, negative)
-
-
-def attend_forward(query_matrix, key_matrix_rows, value_matrix_rows, allowed, head_size):
-    scores = head_scores(query_matrix, key_matrix_rows, allowed, head_size)
-    row_max = jnp.max(scores, axis=-1, keepdims=True)
-    weights = jnp.exp(scores - row_max)
-    row_total = jnp.sum(weights, axis=-1, keepdims=True)
-    probs_low = (weights / row_total).astype(jnp.bfloat16)
-    kv_heads = key_matrix_rows.shape[1] // head_size
-    value_heads_split = value_matrix_rows.reshape(value_matrix_rows.shape[0], kv_heads, head_size)
-    mixed_out = jnp.einsum(
-        "hgrk,khd->rhgd", probs_low, value_heads_split, preferred_element_type=jnp.float32
-    )
-    return (mixed_out.reshape(query_matrix.shape[0], -1), row_max + jnp.log(row_total))
-
-
-def attend_backward(
-    query_matrix, key_matrix_rows, value_matrix_rows, allowed, log_total, mixed_grad, head_size
-):
-    total_row_count = query_matrix.shape[0]
-    kv_heads = key_matrix_rows.shape[1] // head_size
-    scores = head_scores(query_matrix, key_matrix_rows, allowed, head_size)
-    probs = jnp.exp(scores - log_total)
-    value_heads_split = value_matrix_rows.reshape(-1, kv_heads, head_size)
-    key_head_split = key_matrix_rows.reshape(-1, kv_heads, head_size)
-    grouped_heads = query_matrix.reshape(total_row_count, kv_heads, -1, head_size)
-    grad_grouped = mixed_grad.reshape(total_row_count, kv_heads, -1, head_size)
-    prob_grad = jnp.einsum(
-        "rhgd,khd->hgrk", grad_grouped, value_heads_split, preferred_element_type=jnp.float32
-    )
-    inner_sum = jnp.sum(probs * prob_grad, axis=-1, keepdims=True)
-    score_grad = (probs * (prob_grad - inner_sum)).astype(jnp.bfloat16)
-    score_scale = head_size ** (-0.5)
-    query_grad = (
-        jnp.einsum("hgrk,khd->rhgd", score_grad, key_head_split, preferred_element_type=jnp.float32)
-        * score_scale
-    )
-    key_grad = (
-        jnp.einsum("hgrk,rhgd->khd", score_grad, grouped_heads, preferred_element_type=jnp.float32)
-        * score_scale
-    )
-    value_grad = jnp.einsum(
-        "hgrk,rhgd->khd",
-        probs.astype(jnp.bfloat16),
-        grad_grouped,
-        preferred_element_type=jnp.float32,
-    )
-    return (
-        query_grad.reshape(total_row_count, -1),
-        key_grad.reshape(key_matrix_rows.shape[0], -1),
-        value_grad.reshape(value_matrix_rows.shape[0], -1),
-    )
-
-
 def rms_parts(values):
     return lax.rsqrt(jnp.mean(values * values, axis=-1, keepdims=True) + norm_eps)
 
@@ -161,6 +94,336 @@
 
 
 LANES = 128
+
+
+def relane(values, source, target):
+    lane = lax.broadcasted_iota(jnp.int32, values.shape, 1)
+    swapped = jnp.where(source != target, pltpu.roll(values, HEAD_DIMENSION, 1), values)
+    return jnp.where(lane // HEAD_DIMENSION == target, swapped, 0.0)
+
+
+def head_rows(ref, first, count, source, target):
+    values = ref[pl.ds(first, count), :].astype(jnp.float32)
+    return relane(values, source, target).astype(jnp.bfloat16)
+
+
+def nt_dot(left_side, right_side):
+    return lax.dot_general(
+        left_side, right_side, (((1,), (1,)), ((), ())), preferred_element_type=jnp.float32
+    )
+
+
+def nn_dot(left_side, right_side):
+    return jnp.dot(left_side, right_side, preferred_element_type=jnp.float32)
+
+
+def below_diagonal(scores):
+    key_row = lax.broadcasted_iota(jnp.int32, scores.shape, 0)
+    query_column = lax.broadcasted_iota(jnp.int32, scores.shape, 1)
+    return jnp.where(key_row <= query_column, scores, negative)
+
+
+def seen_prompt(scores, first_key, shard_index):
+    key_row = lax.broadcasted_iota(jnp.int32, scores.shape, 0) + first_key
+    query_column = lax.broadcasted_iota(jnp.int32, scores.shape, 1) % PROMPT_BLK
+    return jnp.where(key_row <= query_column + shard_index * PROMPT_BLK, scores, negative)
+
+
+def transposed(values):
+    return values.astype(jnp.float32).T
+
+
+QUERY_CHUNK = 512
+KEY_CHUNK = 1024
+FORWARD_CHUNK = 256
+
+
+def attend_forward_body(
+    group, kv_heads, index_ref, q_ref, kp_ref, vp_ref, ko_ref, vo_ref, mixed_ref, level_ref, vt_all, acc
+):
+    pair = pl.program_id(0)
+    prompt_len = kp_ref.shape[0]
+    block_len = ko_ref.shape[0]
+    conts = (block_len - PROMPT_BLK) // CONT_LEN
+    shard_index = index_ref[0]
+
+    @pl.when(pair == 0)
+    def _():
+        vt_all[:, :prompt_len] = transposed(vp_ref[...]).astype(jnp.bfloat16)
+        vt_all[:, prompt_len:] = transposed(vo_ref[...]).astype(jnp.bfloat16)
+
+    acc[...] = jnp.zeros_like(acc)
+    size = min(FORWARD_CHUNK, prompt_len)
+    prompt_keys = [slice(first, first + size) for first in range(0, prompt_len, size)]
+
+    def kv_half(side):
+        return jnp.minimum((2 * pair + side) // group, kv_heads - 1)
+
+    def finish(scores, value_columns):
+        level = jnp.max(scores[0], axis=0, keepdims=True)
+        for part in scores[1:]:
+            level = jnp.maximum(level, jnp.max(part, axis=0, keepdims=True))
+        total = None
+        mixed = None
+        for part, columns in zip(scores, value_columns):
+            weights = jnp.exp(part - level)
+            part_total = jnp.sum(weights, axis=0, keepdims=True)
+            part_mixed = nn_dot(columns, weights.astype(jnp.bfloat16))
+            total = part_total if total is None else total + part_total
+            mixed = part_mixed if mixed is None else mixed + part_mixed
+        return mixed / total, level + jnp.log(total)
+
+    both = jnp.concatenate(
+        [head_rows(q_ref, 0, PROMPT_BLK, side, kv_half(side)) for side in range(2)], axis=0
+    )
+    mixed, level = finish(
+        [
+            seen_prompt(nt_dot(kp_ref[keys, :], both), keys.start, shard_index)
+            for keys in prompt_keys
+        ],
+        [vt_all[:, keys] for keys in prompt_keys],
+    )
+    mixed = mixed.T
+    for side in range(2):
+        rows = slice(side * PROMPT_BLK, (side + 1) * PROMPT_BLK)
+        acc[:PROMPT_BLK, :] += relane(mixed[rows], kv_half(side), side)
+        level_ref[side, :, :PROMPT_BLK] = level[:, rows]
+
+    def step(turn, _):
+        side = turn // conts
+        number = turn % conts
+        half = kv_half(side)
+        first_own = PROMPT_BLK + number * CONT_LEN
+        for chunk in range(CONT_LEN // QUERY_CHUNK):
+            before = chunk * QUERY_CHUNK
+            first_row = pl.multiple_of(first_own + before, PROMPT_BLK)
+            queries = head_rows(q_ref, first_row, QUERY_CHUNK, side, half)
+            scores = [nt_dot(kp_ref[keys, :], queries) for keys in prompt_keys]
+            columns = [vt_all[:, keys] for keys in prompt_keys]
+            if before:
+                start = pl.multiple_of(first_own, PROMPT_BLK)
+                scores.append(nt_dot(ko_ref[pl.ds(start, before), :], queries))
+                columns.append(
+                    vt_all[:, pl.ds(pl.multiple_of(prompt_len + start, PROMPT_BLK), before)]
+                )
+            scores.append(below_diagonal(nt_dot(ko_ref[pl.ds(first_row, QUERY_CHUNK), :], queries)))
+            columns.append(
+                vt_all[:, pl.ds(pl.multiple_of(prompt_len + first_row, PROMPT_BLK), QUERY_CHUNK)]
+            )
+            mixed, level = finish(scores, columns)
+            acc[pl.ds(first_row, QUERY_CHUNK), :] += relane(mixed.T, half, side)
+            level_ref[side, :, pl.ds(first_row, QUERY_CHUNK)] = level
+        return 0
+
+    lax.fori_loop(0, 2 * conts, step, 0)
+    mixed_ref[...] = acc[...].astype(jnp.bfloat16)
+
+
+def attend_backward_body(
+    group,
+    kv_heads,
+    index_ref,
+    q_ref,
+    grad_ref,
+    mixed_ref,
+    level_ref,
+    kp_ref,
+    vp_ref,
+    ko_ref,
+    vo_ref,
+    dq_ref,
+    dprompt_ref,
+    down_ref,
+    kt_all,
+    acc,
+    prompt_acc,
+):
+    pair = pl.program_id(0)
+    last = pl.num_programs(0) - 1
+    prompt_len = kp_ref.shape[0]
+    block_len = ko_ref.shape[0]
+    conts = (block_len - PROMPT_BLK) // CONT_LEN
+    shard_index = index_ref[0]
+    bf16 = jnp.bfloat16
+
+    @pl.when(pair == 0)
+    def _():
+        kt_all[:, :prompt_len] = transposed(kp_ref[...]).astype(bf16)
+        kt_all[:, prompt_len:] = transposed(ko_ref[...]).astype(bf16)
+        prompt_acc[...] = jnp.zeros_like(prompt_acc)
+        down_ref[...] = jnp.zeros_like(down_ref)
+
+    acc[...] = jnp.zeros_like(acc)
+
+    def kv_half(side):
+        return jnp.minimum((2 * pair + side) // group, kv_heads - 1)
+
+    def inner_sums(first_row, count, side):
+        rows = pl.ds(first_row, count)
+        product = mixed_ref[rows, :].astype(jnp.float32) * grad_ref[rows, :].astype(jnp.float32)
+        return jnp.sum(relane(product, side, side).T, axis=0, keepdims=True)
+
+    def part(keys, values, key_columns, queries, grads, level, inner, mask, sums, first_key):
+        scores = nt_dot(keys, queries)
+        if mask is not None:
+            scores = mask(scores)
+        probs = jnp.exp(scores - level)
+        score_grad = (probs * (nt_dot(values, grads) - inner)).astype(bf16)
+        rows = pl.ds(first_key, keys.shape[0])
+        sums[rows, :LANES] += nn_dot(score_grad, queries)
+        sums[rows, LANES:] += nn_dot(probs.astype(bf16), grads)
+        return nn_dot(key_columns, score_grad)
+
+    def prompt_parts(queries, grads, level, inner, masked):
+        total = None
+        size = min(KEY_CHUNK, prompt_len)
+        for first_key in range(0, prompt_len, size):
+            rows = slice(first_key, first_key + size)
+            mask = (lambda s, f=first_key: seen_prompt(s, f, shard_index)) if masked else None
+            piece = part(
+                kp_ref[rows, :], vp_ref[rows, :], kt_all[:, rows], queries, grads, level, inner,
+                mask, prompt_acc, first_key,
+            )
+            total = piece if total is None else total + piece
+        return total
+
+    both_q, both_g, both_level, both_inner = [], [], [], []
+    for side in range(2):
+        both_q.append(head_rows(q_ref, 0, PROMPT_BLK, side, kv_half(side)))
+        both_g.append(head_rows(grad_ref, 0, PROMPT_BLK, side, kv_half(side)))
+        both_level.append(level_ref[side, :, :PROMPT_BLK])
+        both_inner.append(inner_sums(0, PROMPT_BLK, side))
+    grad_q = prompt_parts(
+        jnp.concatenate(both_q, axis=0),
+        jnp.concatenate(both_g, axis=0),
+        jnp.concatenate(both_level, axis=1),
+        jnp.concatenate(both_inner, axis=1),
+        True,
+    ).T
+    for side in range(2):
+        rows = slice(side * PROMPT_BLK, (side + 1) * PROMPT_BLK)
+        acc[:PROMPT_BLK, :] += relane(grad_q[rows], kv_half(side), side)
+
+    def step(turn, _):
+        side = turn // conts
+        number = turn % conts
+        half = kv_half(side)
+        first_own = PROMPT_BLK + number * CONT_LEN
+        for chunk in range(CONT_LEN // QUERY_CHUNK):
+            before = chunk * QUERY_CHUNK
+            first_row = pl.multiple_of(first_own + before, PROMPT_BLK)
+            queries = head_rows(q_ref, first_row, QUERY_CHUNK, side, half)
+            grads = head_rows(grad_ref, first_row, QUERY_CHUNK, side, half)
+            level = level_ref[side, :, pl.ds(first_row, QUERY_CHUNK)]
+            inner = inner_sums(first_row, QUERY_CHUNK, side)
+            grad_q = prompt_parts(queries, grads, level, inner, False)
+            own = [(first_row, QUERY_CHUNK, below_diagonal)]
+            if before:
+                own.append((pl.multiple_of(first_own, PROMPT_BLK), before, None))
+            for start, size, mask in own:
+                rows = pl.ds(start, size)
+                columns = pl.ds(pl.multiple_of(prompt_len + start, PROMPT_BLK), size)
+                grad_q += part(
+                    ko_ref[rows, :], vo_ref[rows, :], kt_all[:, columns], queries, grads, level,
+                    inner, mask, down_ref, start,
+                )
+            acc[pl.ds(first_row, QUERY_CHUNK), :] += relane(grad_q.T, half, side)
+        return 0
+
+    lax.fori_loop(0, 2 * conts, step, 0)
+    dq_ref[...] = acc[...] * HEAD_DIMENSION ** (-0.5)
+
+    @pl.when(pair == last)
+    def _():
+        dprompt_ref[...] = prompt_acc[...].astype(bf16)
+
+
+def pair_specs(block_len, prompt_len):
+    by_pair = pl.BlockSpec((block_len, LANES), lambda b, i: (0, b))
+    levels = pl.BlockSpec((2, 1, block_len), lambda b, i: (b, 0, 0))
+    sources = [
+        pl.BlockSpec((prompt_len, LANES), lambda b, i: (0, 0)),
+        pl.BlockSpec((prompt_len, LANES), lambda b, i: (0, 1)),
+        pl.BlockSpec((block_len, LANES), lambda b, i: (0, 0)),
+        pl.BlockSpec((block_len, LANES), lambda b, i: (0, 1)),
+    ]
+    return by_pair, levels, sources
+
+
+def attention_cost(block_len, prompt_len, width, products):
+    pairs = (block_len * prompt_len + block_len * CONT_LEN // 2) * (width // HEAD_DIMENSION)
+    return pl.CostEstimate(
+        flops=products * 2 * pairs * 2 * LANES,
+        bytes_accessed=8 * block_len * width,
+        transcendentals=pairs,
+    )
+
+
+def attend_forward(index, queries, kv_prompt, kv_own, group, kv_heads):
+    block_len, width = queries.shape
+    prompt_len = kv_prompt.shape[0]
+    by_pair, levels, sources = pair_specs(block_len, prompt_len)
+    return pl.pallas_call(
+        partial(attend_forward_body, group, kv_heads),
+        out_shape=[
+            jax.ShapeDtypeStruct((block_len, width), jnp.bfloat16),
+            jax.ShapeDtypeStruct((width // HEAD_DIMENSION, 1, block_len), jnp.float32),
+        ],
+        grid_spec=pltpu.PrefetchScalarGridSpec(
+            num_scalar_prefetch=1,
+            grid=(width // LANES,),
+            in_specs=[by_pair] + sources,
+            out_specs=[by_pair, levels],
+            scratch_shapes=[
+                pltpu.VMEM((LANES, prompt_len + block_len), jnp.bfloat16),
+                pltpu.VMEM((block_len, LANES), jnp.float32),
+            ],
+        ),
+        compiler_params=pltpu.CompilerParams(
+            dimension_semantics=("arbitrary",), vmem_limit_bytes=56 * 1024 * 1024
+        ),
+        cost_estimate=attention_cost(block_len, prompt_len, width, 2),
+        name="attend_forward",
+    )(index, queries, kv_prompt, kv_prompt, kv_own, kv_own)
+
+
+def attend_backward(index, queries, grads, mixed, level, kv_prompt, kv_own, group, kv_heads):
+    block_len, width = queries.shape
+    prompt_len = kv_prompt.shape[0]
+    by_pair, levels, sources = pair_specs(block_len, prompt_len)
+    return pl.pallas_call(
+        partial(attend_backward_body, group, kv_heads),
+        out_shape=[
+            jax.ShapeDtypeStruct((block_len, width), jnp.float32),
+            jax.ShapeDtypeStruct((prompt_len, 2 * LANES), jnp.bfloat16),
+            jax.ShapeDtypeStruct((block_len, 2 * LANES), jnp.float32),
+        ],
+        grid_spec=pltpu.PrefetchScalarGridSpec(
+            num_scalar_prefetch=1,
+            grid=(width // LANES,),
+            in_specs=[by_pair, by_pair, by_pair, levels] + sources,
+            out_specs=[
+                by_pair,
+                pl.BlockSpec((prompt_len, 2 * LANES), lambda b, i: (0, 0)),
+                pl.BlockSpec((block_len, 2 * LANES), lambda b, i: (0, 0)),
+            ],
+            scratch_shapes=[
+                pltpu.VMEM((LANES, prompt_len + block_len), jnp.bfloat16),
+                pltpu.VMEM((block_len, LANES), jnp.float32),
+                pltpu.VMEM((prompt_len, 2 * LANES), jnp.float32),
+            ],
+        ),
+        compiler_params=pltpu.CompilerParams(
+            dimension_semantics=("arbitrary",), vmem_limit_bytes=56 * 1024 * 1024
+        ),
+        cost_estimate=attention_cost(block_len, prompt_len, width, 5),
+        name="attend_backward",
+    )(index, queries, grads, mixed, level, kv_prompt, kv_prompt, kv_own, kv_own)
+
+
+def to_lanes(values):
+    extra = -values.shape[1] % LANES
+    return jnp.pad(values, ((0, 0), (0, extra))) if extra else values
 
 
 def exchange(values, axis_name, bit):
@@ -451,49 +714,19 @@
     first_factor = rms_parts(inputs)
     normed_low = (inputs * first_factor * first_gain).astype(bf16)
     lin = matmul(normed_low, qkv_weight)
-    query_heads = rotate(lin[:, :query_width], cos_table, sin_table, HEAD_DIMENSION).astype(bf16)
+    kv_heads = key_width // HEAD_DIMENSION
+    group = query_width // key_width
+    queries = rotate(lin[:, :query_width], cos_table, sin_table, HEAD_DIMENSION)
+    queries = to_lanes((queries * HEAD_DIMENSION ** (-0.5)).astype(bf16))
     key_heads = rotate(
         lin[:, query_width : query_width + key_width], cos_table, sin_table, HEAD_DIMENSION
     ).astype(bf16)
     value_heads = lin[:, query_width + key_width :].astype(bf16)
-    prompt_both = lax.all_gather(
-        jnp.concatenate([key_heads[:PROMPT_BLK], value_heads[:PROMPT_BLK]], axis=1),
-        "shard",
-        axis=0,
-        tiled=True,
-    )
-    prompt_keys = prompt_both[:, :key_width]
-    prompt_values = prompt_both[:, key_width:]
-    key_places = jnp.arange(prompt_len, dtype=jnp.int32)
-    prompt_allowed = (
-        key_places[None, :]
-        <= shard_index * PROMPT_BLK + jnp.arange(PROMPT_BLK, dtype=jnp.int32)[:, None]
-    )
-    wide_places = jnp.arange(prompt_len + CONT_LEN, dtype=jnp.int32)
-    cont_allowed = (wide_places[None, :] < prompt_len) | (
-        wide_places[None, :] - prompt_len <= jnp.arange(CONT_LEN, dtype=jnp.int32)[:, None]
-    )
-    cont_count = (block_len - PROMPT_BLK) // CONT_LEN
-    mixed_piece, prompt_level = attend_forward(
-        query_heads[:PROMPT_BLK], prompt_keys, prompt_values, prompt_allowed, HEAD_DIMENSION
-    )
-    mixed_parts = [mixed_piece]
-    cont_levels = []
-    cont_keys = []
-    cont_values = []
-    for number in range(cont_count):
-        first_row = PROMPT_BLK + number * CONT_LEN
-        last_row = first_row + CONT_LEN
-        keys_all = jnp.concatenate([prompt_keys, key_heads[first_row:last_row]], axis=0)
-        values_all = jnp.concatenate([prompt_values, value_heads[first_row:last_row]], axis=0)
-        mixed_piece, cont_level = attend_forward(
-            query_heads[first_row:last_row], keys_all, values_all, cont_allowed, HEAD_DIMENSION
-        )
-        mixed_parts.append(mixed_piece)
-        cont_levels.append(cont_level)
-        cont_keys.append(keys_all)
-        cont_values.append(values_all)
-    mixed_heads = jnp.concatenate(mixed_parts, axis=0).astype(bf16)
+    kv_own = jnp.concatenate([to_lanes(key_heads), to_lanes(value_heads)], axis=1)
+    kv_prompt = lax.all_gather(kv_own[:PROMPT_BLK], "shard", axis=0, tiled=True)
+    block_number = shard_index.astype(jnp.int32).reshape(1)
+    mixed_own, levels = attend_forward(block_number, queries, kv_prompt, kv_own, group, kv_heads)
+    mixed_heads = mixed_own[:, :query_width]
     mixed_tokens = lax.all_to_all(mixed_heads, "seq", split_axis=0, concat_axis=1, tiled=True)
 
     own_inputs = tokens.astype(jnp.float32)
@@ -573,46 +806,26 @@
     grad_out = grad_out.reshape(grad_out.shape[0], seq_count, -1).transpose(1, 0, 2)
     grad_out = scatter_direct(grad_out, "seq").T
 
-    query_piece, prompt_key_grad, prompt_value_grad = attend_backward(
-        query_heads[:PROMPT_BLK],
-        prompt_keys,
-        prompt_values,
-        prompt_allowed,
-        prompt_level,
-        mixed_grad[:PROMPT_BLK],
-        HEAD_DIMENSION,
-    )
-    query_parts = [query_piece]
-    self_key_grads = []
-    self_value_grads = []
-    for number in range(cont_count):
-        first_row = PROMPT_BLK + number * CONT_LEN
-        last_row = first_row + CONT_LEN
-        query_piece, key_piece, value_piece = attend_backward(
-            query_heads[first_row:last_row],
-            cont_keys[number],
-            cont_values[number],
-            cont_allowed,
-            cont_levels[number],
-            mixed_grad[first_row:last_row],
-            HEAD_DIMENSION,
-        )
-        query_parts.append(query_piece)
-        prompt_key_grad = prompt_key_grad + key_piece[:prompt_len]
-        prompt_value_grad = prompt_value_grad + value_piece[:prompt_len]
-        self_key_grads.append(key_piece[prompt_len:])
-        self_value_grads.append(value_piece[prompt_len:])
-    own_prompt = reduce_blocks(
-        relative_blocks(
-            jnp.concatenate([prompt_key_grad, prompt_value_grad], axis=1).astype(bf16),
-            shard_index,
-            shard_count,
-        ),
-        "shard",
-    )
-    query_grad = jnp.concatenate(query_parts, axis=0)
-    key_grad = jnp.concatenate([own_prompt[:, :key_width]] + self_key_grads, axis=0)
-    value_low = jnp.concatenate([own_prompt[:, key_width:]] + self_value_grads, axis=0).astype(bf16)
+    query_grad, prompt_grad, self_grad = attend_backward(
+        block_number,
+        queries,
+        to_lanes(mixed_grad),
+        mixed_own,
+        levels,
+        kv_prompt,
+        kv_own,
+        group,
+        kv_heads,
+    )
+    query_grad = query_grad[:, :query_width]
+    own_prompt = reduce_blocks(relative_blocks(prompt_grad, shard_index, shard_count), "shard")
+    key_grad = jnp.concatenate(
+        [own_prompt[:, :key_width], self_grad[PROMPT_BLK:, :key_width]], axis=0
+    )
+    value_low = jnp.concatenate(
+        [own_prompt[:, LANES : LANES + key_width], self_grad[PROMPT_BLK:, LANES : LANES + key_width]],
+        axis=0,
+    ).astype(bf16)
     lin_query = rotate(query_grad, cos_table, -sin_table, HEAD_DIMENSION).astype(bf16)
     lin_key = rotate(key_grad, cos_table, -sin_table, HEAD_DIMENSION).astype(bf16)
     lin_all = jnp.concatenate([lin_query, lin_key, value_low], axis=1)

time: 728 us -> 627 us (0.86)
  matrix products: 172 us -> 76.4 us
  Pallas kernels: 86.5 us -> 146 us
  other arithmetic: 102 us -> 43.5 us
  waiting for transfers between devices: 183 us -> 165 us
  local copies, waits for them, and re-layouts: 36.7 us -> 47 us
    dot_general x18 -> x0, matrix products: 100 us -> none  [the longest x3 25.2 us: attend_backward(): jnp.einsum('rhgd,khd->hgrk', grad_grouped, value_heads_split, preferred_e...]
    pallas_call x0 -> x2, Pallas kernels: none -> 59.7 us  [the longest x1 34.8 us: attend_backward(): pl.pallas_call(partial(attend_backward_body, group, kv_heads), out_shape=...]
    convert_element_type x4 -> x1, other arithmetic: 35 us -> 0.15 us  [on_device(): queries = to_lanes((queries * HEAD_DIMENSION ** (-0.5)).astype(bf16))]
    reduce_sum x3 -> x0, other arithmetic: 19.5 us -> none  [attend_forward(): row_total = jnp.sum(weights, axis=-1, keepdims=True)]
    unnamed x207 -> x144, local copies, waits for them, and re-layouts: 13.5 us -> 19.9 us
  transfers between devices with their start and end apart: 88 -> 88, of which waited for: 27 -> 26; matrix products, arithmetic and copies ran while one was open for 40% -> 23% of each run, Pallas kernels for 9% -> 20%
where the time goes in v3:
time: 627 us; the launch traced here: 617 us
  waiting for transfers between devices  165 us (26%)
  Pallas kernels  146 us (23%)
  matrix products  76.4 us (12%)
  starting transfers between devices  66.7 us (11%)
  blocking collectives  57 us (9%)
  local copies, waits for them, and re-layouts  47 us (7%)
  other arithmetic  43.5 us (7%)
  between operations  15.6 us (2%)
    ppermute x74, waiting for transfers between devices, exchange(): return lax.ppermute(values, axis_name, [(i, i ^ bit) for i in range(count)])  111 us
    pallas_call x4, Pallas kernels, expert_pair(): pl.pallas_call(partial(expert_body, experts_all), out_shape=out_shape, gr...  86.2 us
    dot_general x13, matrix products, transposed_times(): lax.dot_general(left_side, right_side, (((0,), (0,)), ((), ())), precisio...  55.1 us
    ppermute x74, starting transfers between devices, exchange(): return lax.ppermute(values, axis_name, [(i, i ^ bit) for i in range(count)])  48.3 us
    pallas_call x1, Pallas kernels, attend_backward(): pl.pallas_call(partial(attend_backward_body, group, kv_heads), out_shape=...  34.8 us
    all_to_all x1, waiting for transfers between devices, on_device(): lax.all_to_all(mixed_grad_tokens, 'seq', split_axis=1, concat_axis=0, til...  27.6 us
    pallas_call x1, Pallas kernels, attend_forward(): pl.pallas_call(partial(attend_forward_body, group, kv_heads), out_shape=[...  25 us
    all_gather x1, blocking collectives, on_device(): out_weight = lax.all_gather(w_out, 'seq', axis=0, tiled=True)  24.9 us
  transfers between devices with their start and end apart: 88, of which 26 were waited for; matrix products, arithmetic and copies ran while one was open for 23% of the time, Pallas kernels for 20%

profile of v3, /device:TPU:0, one launch (start us, length us, event | category | flops | bytes accessed | tf_op | source)
XLA Modules:
  0.0 616.9 jit_solution(10493464065102927961)
XLA Ops:
  11.1 2.6 collective-permute-start.1
  15.2 24.9 %all_gather.22 = bf16[1536,192]{0,1:T(8,128)(2,1)} all-gather(bf16[384,192]{0,1:T(8,128)(2,1)} %param.18), channel_id=1, replica_groups=mesh['shard'=8,'seq'=4] {'seq'}, dimensions={0}, use_global_device_ids=true | all-gather | bytes 737280 | tf_op jit(solution)/shard_map/all_gather | solution.py:705
  40.2 13.7 %all-gather = bf16[4,48,18]{1,2,0:T(8,128)(2,1)S(1)} all-gather(bf16[1,48,18]{1,2,0:T(8,128)(2,1)S(1)} %maximum_bitcast_fusion), channel_id=1, replica_groups=mesh['shard'=8,'seq'=4] {'seq'}, dimensions={0}, use_global_device_ids=true | all-gather | bytes 8640 | tf_op jit(solution)/shard_map/all_gather | solution.py:695
  54.0 8.1 %all-gather.1 = bf16[8,192,18]{1,2,0:T(8,128)(2,1)S(1)} all-gather(bf16[1,192,18]{1,2,0:T(8,128)(2,1)S(1)} %reshape.259), channel_id=1, replica_groups=mesh['shard'=8,'seq'=4] {'shard'}, dimensions={0}, use_global_device_ids=true | all-gather | bytes 62208 | tf_op jit(solution)/shard_map/all_gather | solution.py:696
  66.5 2.9 collective-permute-done.5
  78.2 10.7 %all-gather.5.cloned.1.call-done = bf16[1152,1536]{1,0:T(8,128)(2,1)} async-done(((bf16[288,1536]{1,0:T(8,128)(2,1)}), bf16[1152,1536]{1,0:T(8,128)(2,1)}) %all-gather.5.cloned.1.call-update) | async-done | bytes 3538960 | tf_op jit(solution)/shard_map/all_gather | solution.py:700
  88.9 2.9 fusion
  92.0 4.5 fusion.25
  101.5 10.2 %all_gather.21.kp_ref.vp_ref = bf16[1024,256]{1,0:T(8,128)(2,1)} all-gather(bf16[128,256]{1,0:T(8,128)(2,1)S(1)} %fusion.45), channel_id=1, replica_groups=mesh['shard'=8,'seq'=4] {'shard'}, dimensions={0}, use_global_device_ids=true | all-gather | bytes 589824 | tf_op jit(solution)/shard_map/all_gather | solution.py:726
  112.6 25.0 %attend_forward.1 = (bf16[1152,384]{1,0:T(8,128)(2,1)}, f32[6,1,1152]{2,1,0:T(1,128)}) custom-call(s32[1]{0:T(128)} %bitcast.index_ref, bf16[1152,384]{1,0:T(8,128)(2,1)} %copy.148.q_ref, bf16[1024,256]{1,0:T(8,128)(2,1)} %all_gather.21.kp_ref.vp_ref, bf16[1024,256]{1,0:T(8,128)(2,1)} %all_gather.21.kp_ref.vp_ref, ...), custom_call_target="tpu_custom_call" | custom-call | flops 9059696640 | bytes 3538944 | tf_op jit(solution)/shard_map/attend_forward/pallas_call | solution.py:366
  137.5 4.0 all-to-all-start
  144.5 19.2 %collective-permute-done.16.og_even = bf16[288,1536]{1,0:T(8,128)(2,1)S(1)} collective-permute-done((bf16[288,1536]{1,0:T(8,128)(2,1)}, bf16[288,1536]{1,0:T(8,128)(2,1)S(1)}, u32[]{:S(2)}, u32[]{:S(2)}) %collective-permute-start.16) | collective-permute-done | bytes 884768 | tf_op jit(solution)/shard_map/ppermute | solution.py:431
  165.8 4.0 multiply_reduce_fusion.2
  174.2 1.9 concatenate.81.x_even
  178.6 1.8 slice.505
  181.2 1.8 constant_dynamic-update-slice_fusion.8
  183.0 25.0 %collective-permute-done.22 = bf16[144,1536]{1,0:T(8,128)(2,1)} collective-permute-done((bf16[144,1536]{1,0:T(8,128)(2,1)}, bf16[144,1536]{1,0:T(8,128)(2,1)}, u32[]{:S(2)}, u32[]{:S(2)}) %collective-permute-start.22) | collective-permute-done | bytes 442400 | tf_op jit(solution)/shard_map/ppermute | solution.py:431
  208.0 1.8 constant_dynamic-update-slice_fusion.7.og_even
  210.3 1.8 slice.502
  213.0 1.9 slice.503
  216.1 21.4 %experts.4 = (bf16[2304,1536]{1,0:T(8,128)(2,1)}, bf16[2304,1536]{1,0:T(8,128)(2,1)}, bf16[2,2304,1024]{2,1,0:T(8,128)(2,1)}, bf16[2304,1024]{1,0:T(8,128)(2,1)}...) custom-call(s32[1]{0:T(128)} %bitcast.19.index_ref, ...), custom_call_target="tpu_custom_call" | custom-call | flops 10871635968 | bytes 27131904 | tf_op jit(solution)/shard_map/experts/pallas_call | solution.py:636
  238.1 1.8 constant_dynamic-update-slice_fusion.6
  241.2 21.8 %experts.5 = (bf16[2304,1536]{1,0:T(8,128)(2,1)}, bf16[2304,1536]{1,0:T(8,128)(2,1)}, bf16[2,2304,1024]{2,1,0:T(8,128)(2,1)}, bf16[2304,1024]{1,0:T(8,128)(2,1)}...) custom-call(s32[1]{0:T(128)} %bitcast.19.index_ref, ...), custom_call_target="tpu_custom_call", output_to_operand_aliasing={{0}: (8, {}), {1}: (9, {}), {2}: (10, {}), {3}: (11, {})} | custom-call | flops 10871635968 | bytes 27131904 | tf_op jit(solution)/shard_map/experts/pallas_call | solution.py:636
  263.1 21.4 %experts.6 = (bf16[2304,1536]{1,0:T(8,128)(2,1)}, bf16[2304,1536]{1,0:T(8,128)(2,1)}, bf16[2,2304,1024]{2,1,0:T(8,128)(2,1)}, bf16[2304,1024]{1,0:T(8,128)(2,1)}...) custom-call(s32[1]{0:T(128)} %bitcast.19.index_ref, ...), custom_call_target="tpu_custom_call", output_to_operand_aliasing={{0}: (8, {}), {1}: (9, {}), {2}: (10, {}), {3}: (11, {})} | custom-call | flops 10871635968 | bytes 27131904 | tf_op jit(solution)/shard_map/experts/pallas_call | solution.py:636
  284.5 21.6 %experts.7 = (bf16[2304,1536]{1,0:T(8,128)(2,1)}, bf16[2304,1536]{1,0:T(8,128)(2,1)}, bf16[2,2304,1024]{2,1,0:T(8,128)(2,1)}, bf16[2304,1024]{1,0:T(8,128)(2,1)}...) custom-call(s32[1]{0:T(128)} %bitcast.19.index_ref, ...), custom_call_target="tpu_custom_call", output_to_operand_aliasing={{0}: (8, {}), {1}: (9, {}), {2}: (10, {}), {3}: (11, {})} | custom-call | flops 10871635968 | bytes 27131904 | tf_op jit(solution)/shard_map/experts/pallas_call | solution.py:636
  306.1 12.6 %convolution_convert_fusion = bf16[1536,1024]{1,0:T(8,128)(2,1)} fusion(bf16[2304,1536]{1,0:T(8,128)(2,1)} %get-tuple-element.89, bf16[2304,1024]{1,0:T(8,128)(2,1)} %get-tuple-element.90), kind=kOutput, calls=%fused_computation.16 | convolution fusion | flops 7249330176 | bytes 14942208 | tf_op jit(solution)/shard_map/dot_general | solution.py:71
  318.7 12.8 %fusion.14 = bf16[1536,1024]{1,0:T(8,128)(2,1)} fusion(bf16[2304,1536]{1,0:T(8,128)(2,1)} %get-tuple-element.91, bf16[2,2304,1024]{2,1,0:T(8,128)(2,1)} %get-tuple-element.92), kind=kOutput, calls=%fused_computation.15 | convolution fusion | flops 7249330176 | bytes 14942208 | tf_op jit(solution)/shard_map/dot_general | solution.py:71
  332.2 2.2 collective-permute-done.28
  334.4 2.4 add_convert_fusion.6
  339.3 10.8 %collective-permute-done.31 = bf16[144,1664]{1,0:T(8,128)(2,1)} collective-permute-done((bf16[144,1664]{1,0:T(8,128)(2,1)}, bf16[144,1664]{1,0:T(8,128)(2,1)}, u32[]{:S(2)}, u32[]{:S(2)}) %collective-permute-start.31) | collective-permute-done | bytes 479264 | tf_op jit(solution)/shard_map/ppermute | solution.py:431
  350.1 2.9 add_convert_fusion.8
  355.0 2.5 add_convert_fusion.5
  359.5 13.1 %fusion.11 = bf16[1536,1024]{1,0:T(8,128)(2,1)} fusion(bf16[2304,1536]{1,0:T(8,128)(2,1)} %get-tuple-element.91, bf16[2,2304,1024]{2,1,0:T(8,128)(2,1)} %get-tuple-element.92), kind=kOutput, calls=%fused_computation.14 | convolution fusion | flops 7249330176 | bytes 14942208 | tf_op jit(solution)/shard_map/dot_general | solution.py:71
  372.7 3.0 collective-permute-done.32
  375.7 3.9 collective-permute-done.33
  379.6 2.5 convert_add_fusion.2
  383.2 1.9 multiply_reduce_fusion
  385.2 3.0 fusion.74
  395.0 4.6 all-to-all-start.1
  407.8 2.3 convolution_convert_fusion.11
  413.0 3.5 collective-permute-done.71
  418.7 27.6 %all-to-all-done.1 = bf16[288,4,384]{2,0,1:T(8,128)(2,1)} async-done(((bf16[288,4,384]{2,0,1:T(8,128)(2,1)}), bf16[288,4,384]{2,0,1:T(8,128)(2,1)}, u32[]{:S(2)}, u32[]{:S(2)}) %all-to-all-start.1) | async-done | bytes 884768 | tf_op jit(solution)/shard_map/all_to_all | solution.py:791
  446.2 34.8 %attend_backward.1 = (f32[1152,384]{1,0:T(8,128)}, bf16[1024,256]{1,0:T(8,128)(2,1)}, f32[1152,256]{1,0:T(8,128)}) custom-call(s32[1]{0:T(128)} %bitcast.index_ref, bf16[1152,384]{1,0:T(8,128)(2,1)} %copy.148.q_ref, bf16[1152,384]{1,0:T(8,128)(2,1)} %bitcast.23.grad_ref, bf16[1152,384]{1,0:T(8,128)(2,1)} %get-tuple-element.59.mixed_ref, ...), custom_call_target="tpu_custom_call" | custom-call | flops 22649241600 | bytes 3538944 | tf_op jit(solution)/shard_map/attend_backward/pallas_call | solution.py:394
  483.6 2.9 copy.155
  488.9 1.8 subtract_convert_fusion
  495.0 2.0 collective-permute-start.53
  500.3 2.0 collective-permute-start.73
  505.2 8.7 %fusion.4 = (bf16[1536]{0:T(1024)(128)(2,1)}, bf16[1152,1536]{1,0:T(8,128)(2,1)}) fusion(bf16[1152,1536]{1,0:T(8,128)(2,1)} %all-gather.5.cloned.1.call-done, f32[1152]{0:T(1024)S(1)} %copy-done.48, bf16[1536,640]{1,0:T(8,128)(2,1)} %bitcast.12, bf16[1152,128]{0,1:T(8,128)(2,1)S(1)} %copy.157, bf16[1152,128]{0,1:T(8,128)(2,1)S(1)} %bitcast.148, ...), kind=kOutput, calls=%fused_computation.7 | convolution fusion | flops 2278193664 | bytes 10526208 | tf_op jit(solution)/shard_map/dot_general | solution.py:61
  518.8 8.3 %collective-permute-done.41 = bf16[144,1536]{1,0:T(8,128)(2,1)S(1)} collective-permute-done((bf16[144,1536]{1,0:T(8,128)(2,1)S(1)}, bf16[144,1536]{1,0:T(8,128)(2,1)S(1)}, u32[]{:S(2)}, u32[]{:S(2)}) %collective-permute-start.41) | collective-permute-done | bytes 442400 | tf_op jit(solution)/shard_map/ppermute | solution.py:431
  527.5 2.8 convolution_convert_fusion.1
  531.1 2.3 collective-permute-start.76
  534.7 7.2 %collective-permute-done.75 = bf16[192,384]{1,0:T(8,128)(2,1)S(1)} collective-permute-done((bf16[192,384]{1,0:T(8,128)(2,1)S(1)}, bf16[192,384]{1,0:T(8,128)(2,1)S(1)}, u32[]{:S(2)}, u32[]{:S(2)}) %collective-permute-start.75) | collective-permute-done | bytes 147488 | tf_op jit(solution)/shard_map/ppermute | solution.py:514
  541.9 7.9 %collective-permute-done.76 = bf16[192,384]{1,0:T(8,128)(2,1)S(1)} collective-permute-done((bf16[192,384]{1,0:T(8,128)(2,1)S(1)}, bf16[192,384]{1,0:T(8,128)(2,1)S(1)}, u32[]{:S(2)}, u32[]{:S(2)}) %collective-permute-start.76) | collective-permute-done | bytes 147488 | tf_op jit(solution)/shard_map/ppermute | solution.py:514
  549.8 2.0 collective-permute-start.43
  553.4 2.4 collective-permute-done.42
  555.9 7.0 %collective-permute-done.40 = bf16[144,1536]{1,0:T(8,128)(2,1)S(1)} collective-permute-done((bf16[144,1536]{1,0:T(8,128)(2,1)S(1)}, bf16[144,1536]{1,0:T(8,128)(2,1)S(1)}, u32[]{:S(2)}, u32[]{:S(2)}) %collective-permute-start.40) | collective-permute-done | bytes 442400 | tf_op jit(solution)/shard_map/ppermute | solution.py:431
  563.4 8.1 %collective-permute-done.43 = bf16[144,1536]{1,0:T(8,128)(2,1)S(1)} collective-permute-done((bf16[144,1536]{1,0:T(8,128)(2,1)S(1)}, bf16[144,1536]{1,0:T(8,128)(2,1)S(1)}, u32[]{:S(2)}, u32[]{:S(2)}) %collective-permute-start.43) | collective-permute-done | bytes 442400 | tf_op jit(solution)/shard_map/ppermute | solution.py:431
  572.3 5.0 collective-permute-done.61
  578.5 1.9 collective-permute-start.62
  587.1 4.6 collective-permute-start.77
  591.7 2.4 collective-permute-start.79
  603.3 1.9 maximum_convert_fusion
  605.1 1.8 fusion.17
  606.9 2.9 fusion.20
  (396 shorter events, 112.4 us)
Async XLA Ops:
  7.2 81.7 %all-gather.5.cloned.1.call-start = ((), (), s32[]{:S(2)}) async-start(), calls=%async_computation.6 | async-start | bytes 4423680 | tf_op jit(solution)/shard_map/all_gather | solution.py:700
  7.9 157.9 %all-gather.7.cloned.1.call-start = ((), (), s32[]{:S(2)}) async-start(), calls=%async_computation.7 | async-start | bytes 5308416 | tf_op jit(solution)/shard_map/all_gather | solution.py:706
  10.6 55.9 %collective-permute-start = (bf16[192,640]{1,0:T(8,128)(2,1)S(1)}, bf16[192,640]{1,0:T(8,128)(2,1)S(1)}, u32[]{:S(2)}, u32[]{:S(2)}) collective-permute-start(bf16[192,640]{1,0:T(8,128)(2,1)S(1)} %constant_dynamic-update-slice_fusion), channel_id=1, source_target_pairs={{0,4},{4,0},{8,12},{12,8},{16,20},{20,16},{24,28},{28,24},{1,5},{5... | collective-permute-start | bytes 737288 | tf_op jit(solution)/shard_map/ppermute | solution.py:431
  11.1 54.3 %collective-permute-start.1 = (bf16[192,640]{1,0:T(8,128)(2,1)S(1)}, bf16[192,640]{1,0:T(8,128)(2,1)S(1)}, u32[]{:S(2)}, u32[]{:S(2)}) collective-permute-start(bf16[192,640]{1,0:T(8,128)(2,1)S(1)} %constant_dynamic-update-slice_fusion), channel_id=1, source_target_pairs={{0,8},{4,12},{8,0},{12,4},{16,24},{20,28},{24,16},{28,20},{1,9},{5... | collective-permute-start | bytes 737288 | tf_op jit(solution)/shard_map/ppermute | solution.py:431
  13.7 50.0 %collective-permute-start.3 = (bf16[192,640]{1,0:T(8,128)(2,1)S(1)}, bf16[192,640]{1,0:T(8,128)(2,1)S(1)}, u32[]{:S(2)}, u32[]{:S(2)}) collective-permute-start(bf16[192,640]{1,0:T(8,128)(2,1)S(1)} %constant_dynamic-update-slice_fusion), channel_id=1, source_target_pairs={{0,16},{4,20},{8,24},{12,28},{16,0},{20,4},{24,8},{28,12},{1,17},{... | collective-permute-start | bytes 737288 | tf_op jit(solution)/shard_map/ppermute | solution.py:431
  137.5 28.2 %all-to-all-start = ((bf16[4,288,384]{2,1,0:T(8,128)(2,1)}), bf16[4,288,384]{2,1,0:T(8,128)(2,1)S(1)}, u32[]{:S(2)}, u32[]{:S(2)}) async-start(bf16[4,288,384]{2,1,0:T(8,128)(2,1)} %bitcast.144), calls=%async_computation | async-start | bytes 1769472 | tf_op jit(solution)/shard_map/all_to_all | solution.py:730
  141.5 456.4 %reduce-scatter.11.cloned.1.call-start = ((), (), s32[]{:S(2)}) async-start(), calls=%async_computation.11 | async-start | bytes 3932160 | tf_op jit(solution)/shard_map/reduce_scatter | solution.py:854
  141.7 21.9 %collective-permute-start.16 = (bf16[288,1536]{1,0:T(8,128)(2,1)}, bf16[288,1536]{1,0:T(8,128)(2,1)S(1)}, u32[]{:S(2)}, u32[]{:S(2)}) collective-permute-start(bf16[288,1536]{1,0:T(8,128)(2,1)} %og_even), channel_id=1, source_target_pairs={{0,16},{4,20},{8,24},{12,28},{16,0},{20,4},{24,8},{28,12},{1,17},{... | collective-permute-start | bytes 2654216 | tf_op jit(solution)/shard_map/ppermute | solution.py:431
  143.8 34.3 %collective-permute-start.12 = (bf16[288,1536]{1,0:T(8,128)(2,1)}, bf16[288,1536]{1,0:T(8,128)(2,1)}, u32[]{:S(2)}, u32[]{:S(2)}) collective-permute-start(bf16[288,1536]{1,0:T(8,128)(2,1)} %og_even), channel_id=1, source_target_pairs={{0,8},{4,12},{8,0},{12,4},{16,24},{20,28},{24,16},{28,20},{1,9},{5... | collective-permute-start | bytes 2654216 | tf_op jit(solution)/shard_map/ppermute | solution.py:431
  164.5 15.9 %collective-permute-start.21 = (bf16[144,1536]{1,0:T(8,128)(2,1)}, bf16[144,1536]{1,0:T(8,128)(2,1)}, u32[]{:S(2)}, u32[]{:S(2)}) collective-permute-start(bf16[144,1536]{1,0:T(8,128)(2,1)} %slice.504), channel_id=1, source_target_pairs={{0,8},{4,12},{8,0},{12,4},{16,24},{20,28},{24,16},{28,20},{1,9},{5... | collective-permute-start | bytes 1327112 | tf_op jit(solution)/shard_map/ppermute | solution.py:431
  176.0 33.8 %collective-permute-start.14 = (bf16[288,1664]{1,0:T(8,128)(2,1)}, bf16[288,1664]{1,0:T(8,128)(2,1)}, u32[]{:S(2)}, u32[]{:S(2)}) collective-permute-start(bf16[288,1664]{1,0:T(8,128)(2,1)} %concatenate.81.x_even), channel_id=1, source_target_pairs={{0,16},{4,20},{8,24},{12,28},{16,0},{20,4},{24,8},{28,12},{1,17},{... | collective-permute-start | bytes 2875400 | tf_op jit(solution)/shard_map/ppermute | solution.py:431
  177.0 35.2 %collective-permute-start.10 = (bf16[288,1664]{1,0:T(8,128)(2,1)}, bf16[288,1664]{1,0:T(8,128)(2,1)}, u32[]{:S(2)}, u32[]{:S(2)}) collective-permute-start(bf16[288,1664]{1,0:T(8,128)(2,1)} %concatenate.81.x_even), channel_id=1, source_target_pairs={{0,8},{4,12},{8,0},{12,4},{16,24},{20,28},{24,16},{28,20},{1,9},{5... | collective-permute-start | bytes 2875400 | tf_op jit(solution)/shard_map/ppermute | solution.py:431
  178.1 38.0 %collective-permute-start.8 = (bf16[288,1664]{1,0:T(8,128)(2,1)}, bf16[288,1664]{1,0:T(8,128)(2,1)}, u32[]{:S(2)}, u32[]{:S(2)}) collective-permute-start(bf16[288,1664]{1,0:T(8,128)(2,1)} %concatenate.81.x_even), channel_id=1, source_target_pairs={{0,4},{4,0},{8,12},{12,8},{16,20},{20,16},{24,28},{28,24},{1,5},{5... | collective-permute-start | bytes 2875400 | tf_op jit(solution)/shard_map/ppermute | solution.py:431
  178.1 36.8 %collective-permute-start.9 = (bf16[288,1536]{1,0:T(8,128)(2,1)}, bf16[288,1536]{1,0:T(8,128)(2,1)}, u32[]{:S(2)}, u32[]{:S(2)}) collective-permute-start(bf16[288,1536]{1,0:T(8,128)(2,1)} %og_even), channel_id=1, source_target_pairs={{0,4},{4,0},{8,12},{12,8},{16,20},{20,16},{24,28},{28,24},{1,5},{5... | collective-permute-start | bytes 2654216 | tf_op jit(solution)/shard_map/ppermute | solution.py:431
  180.4 27.6 %collective-permute-start.22 = (bf16[144,1536]{1,0:T(8,128)(2,1)}, bf16[144,1536]{1,0:T(8,128)(2,1)}, u32[]{:S(2)}, u32[]{:S(2)}) collective-permute-start(bf16[144,1536]{1,0:T(8,128)(2,1)} %slice.505), channel_id=1, source_target_pairs={{0,16},{4,20},{8,24},{12,28},{16,0},{20,4},{24,8},{28,12},{1,17},{... | collective-permute-start | bytes 1327112 | tf_op jit(solution)/shard_map/ppermute | solution.py:431
  208.0 32.7 %collective-permute-start.13 = (bf16[288,1536]{1,0:T(8,128)(2,1)}, bf16[288,1536]{1,0:T(8,128)(2,1)}, u32[]{:S(2)}, u32[]{:S(2)}) collective-permute-start(bf16[288,1536]{1,0:T(8,128)(2,1)} %collective-permute-done.12.og_even), channel_id=1, source_target_pairs={{0,4},{4,0},{8,12},{12,8},{16,20},{20,16},{24,28},{28,24},{1,5},{5... | collective-permute-start | bytes 2654216 | tf_op jit(solution)/shard_map/ppermute | solution.py:431
  209.8 53.3 %collective-permute-start.17 = (bf16[288,1536]{1,0:T(8,128)(2,1)}, bf16[288,1536]{1,0:T(8,128)(2,1)}, u32[]{:S(2)}, u32[]{:S(2)}) collective-permute-start(bf16[288,1536]{1,0:T(8,128)(2,1)} %copy-done.18), channel_id=1, source_target_pairs={{0,4},{4,0},{8,12},{12,8},{16,20},{20,16},{24,28},{28,24},{1,5},{5... | collective-permute-start | bytes 2654216 | tf_op jit(solution)/shard_map/ppermute | solution.py:431
  212.2 25.3 %collective-permute-start.18 = (bf16[144,1664]{1,0:T(8,128)(2,1)}, bf16[144,1664]{1,0:T(8,128)(2,1)}, u32[]{:S(2)}, u32[]{:S(2)}) collective-permute-start(bf16[144,1664]{1,0:T(8,128)(2,1)} %slice.502), channel_id=1, source_target_pairs={{0,8},{4,12},{8,0},{12,4},{16,24},{20,28},{24,16},{28,20},{1,9},{5... | collective-permute-start | bytes 1437704 | tf_op jit(solution)/shard_map/ppermute | solution.py:431
  214.9 25.0 %collective-permute-start.19 = (bf16[144,1664]{1,0:T(8,128)(2,1)}, bf16[144,1664]{1,0:T(8,128)(2,1)S(1)}, u32[]{:S(2)}, u32[]{:S(2)}) collective-permute-start(bf16[144,1664]{1,0:T(8,128)(2,1)} %slice.503), channel_id=1, source_target_pairs={{0,16},{4,20},{8,24},{12,28},{16,0},{20,4},{24,8},{28,12},{1,17},{... | collective-permute-start | bytes 1437704 | tf_op jit(solution)/shard_map/ppermute | solution.py:431
  216.1 25.2 %collective-permute-start.11 = (bf16[288,1664]{1,0:T(8,128)(2,1)}, bf16[288,1664]{1,0:T(8,128)(2,1)}, u32[]{:S(2)}, u32[]{:S(2)}) collective-permute-start(bf16[288,1664]{1,0:T(8,128)(2,1)} %collective-permute-done.10.x_even), channel_id=1, source_target_pairs={{0,4},{4,0},{8,12},{12,8},{16,20},{20,16},{24,28},{28,24},{1,5},{5... | collective-permute-start | bytes 2875400 | tf_op jit(solution)/shard_map/ppermute | solution.py:431
  237.5 47.0 %collective-permute-start.23 = (bf16[288,1536]{1,0:T(8,128)(2,1)}, bf16[288,1536]{1,0:T(8,128)(2,1)}, u32[]{:S(2)}, u32[]{:S(2)}) collective-permute-start(bf16[288,1536]{1,0:T(8,128)(2,1)} %constant_dynamic-update-slice_fusion.7.og_even), channel_id=1, source_target_pairs={{0,4},{4,0},{8,12},{12,8},{16,20},{20,16},{24,28},{28,24},{1,5},{5... | collective-permute-start | bytes 2654216 | tf_op jit(solution)/shard_map/ppermute | solution.py:431
  239.9 23.2 %collective-permute-start.15 = (bf16[288,1664]{1,0:T(8,128)(2,1)}, bf16[288,1664]{1,0:T(8,128)(2,1)}, u32[]{:S(2)}, u32[]{:S(2)}) collective-permute-start(bf16[288,1664]{1,0:T(8,128)(2,1)} %collective-permute-done.14.x_even), channel_id=1, source_target_pairs={{0,4},{4,0},{8,12},{12,8},{16,20},{20,16},{24,28},{28,24},{1,5},{5... | collective-permute-start | bytes 2875400 | tf_op jit(solution)/shard_map/ppermute | solution.py:431
  240.7 43.8 %collective-permute-start.20 = (bf16[288,1664]{1,0:T(8,128)(2,1)}, bf16[288,1664]{1,0:T(8,128)(2,1)}, u32[]{:S(2)}, u32[]{:S(2)}) collective-permute-start(bf16[288,1664]{1,0:T(8,128)(2,1)} %constant_dynamic-update-slice_fusion.5.x_even), channel_id=1, source_target_pairs={{0,4},{4,0},{8,12},{12,8},{16,20},{20,16},{24,28},{28,24},{1,5},{5... | collective-permute-start | bytes 2875400 | tf_op jit(solution)/shard_map/ppermute | solution.py:431
  318.7 282.2 %reduce-scatter.9.cloned.1.call-start = ((), (), s32[]{:S(2)}) async-start(), calls=%async_computation.10 | async-start | bytes 3932160 | tf_op jit(solution)/shard_map/reduce_scatter | solution.py:856
  331.5 270.5 %reduce-scatter.7.cloned.1.call-start = ((), (), s32[]{:S(2)}) async-start(), calls=%async_computation.9 | async-start | bytes 3932160 | tf_op jit(solution)/shard_map/reduce_scatter | solution.py:856
  336.8 13.3 %collective-permute-start.31 = (bf16[144,1664]{1,0:T(8,128)(2,1)}, bf16[144,1664]{1,0:T(8,128)(2,1)}, u32[]{:S(2)}, u32[]{:S(2)}) collective-permute-start(bf16[144,1664]{1,0:T(8,128)(2,1)} %get-tuple-element.215), channel_id=1, source_target_pairs={{0,16},{4,20},{8,24},{12,28},{16,0},{20,4},{24,8},{28,12},{1,17},{... | collective-permute-start | bytes 1437704 | tf_op jit(solution)/shard_map/ppermute | solution.py:431
  337.6 17.4 %collective-permute-start.27 = (bf16[288,1664]{1,0:T(8,128)(2,1)}, bf16[288,1664]{1,0:T(8,128)(2,1)}, u32[]{:S(2)}, u32[]{:S(2)}) collective-permute-start(bf16[288,1664]{1,0:T(8,128)(2,1)} %get-tuple-element.86), channel_id=1, source_target_pairs={{0,4},{4,0},{8,12},{12,8},{16,20},{20,16},{24,28},{28,24},{1,5},{5... | collective-permute-start | bytes 2875400 | tf_op jit(solution)/shard_map/ppermute | solution.py:431
  337.6 35.0 %collective-permute-start.24 = (bf16[288,1664]{1,0:T(8,128)(2,1)}, bf16[288,1664]{1,0:T(8,128)(2,1)}, u32[]{:S(2)}, u32[]{:S(2)}) collective-permute-start(bf16[288,1664]{1,0:T(8,128)(2,1)} %get-tuple-element.82), channel_id=1, source_target_pairs={{0,4},{4,0},{8,12},{12,8},{16,20},{20,16},{24,28},{28,24},{1,5},{5... | collective-permute-start | bytes 2875400 | tf_op jit(solution)/shard_map/ppermute | solution.py:431
  338.1 16.9 %collective-permute-start.29 = (bf16[144,1664]{1,0:T(8,128)(2,1)}, bf16[144,1664]{1,0:T(8,128)(2,1)S(1)}, u32[]{:S(2)}, u32[]{:S(2)}) collective-permute-start(bf16[144,1664]{1,0:T(8,128)(2,1)} %get-tuple-element.214), channel_id=1, source_target_pairs={{0,8},{4,12},{8,0},{12,4},{16,24},{20,28},{24,16},{28,20},{1,9},{5... | collective-permute-start | bytes 1437704 | tf_op jit(solution)/shard_map/ppermute | solution.py:431
  353.0 19.7 %collective-permute-start.26 = (bf16[144,1664]{1,0:T(8,128)(2,1)}, bf16[144,1664]{1,0:T(8,128)(2,1)}, u32[]{:S(2)}, u32[]{:S(2)}) collective-permute-start(bf16[144,1664]{1,0:T(8,128)(2,1)} %get-tuple-element.210), channel_id=1, source_target_pairs={{0,8},{4,12},{8,0},{12,4},{16,24},{20,28},{24,16},{28,20},{1,9},{5... | collective-permute-start | bytes 1437704 | tf_op jit(solution)/shard_map/ppermute | solution.py:431
  354.2 21.5 %collective-permute-start.32 = (bf16[144,1664]{1,0:T(8,128)(2,1)}, bf16[144,1664]{1,0:T(8,128)(2,1)}, u32[]{:S(2)}, u32[]{:S(2)}) collective-permute-start(bf16[144,1664]{1,0:T(8,128)(2,1)} %get-tuple-element.211), channel_id=1, source_target_pairs={{0,8},{4,12},{8,0},{12,4},{16,24},{20,28},{24,16},{28,20},{1,9},{5... | collective-permute-start | bytes 1437704 | tf_op jit(solution)/shard_map/ppermute | solution.py:431
  357.5 18.2 %collective-permute-start.30 = (bf16[144,1664]{1,0:T(8,128)(2,1)}, bf16[144,1664]{1,0:T(8,128)(2,1)}, u32[]{:S(2)}, u32[]{:S(2)}) collective-permute-start(bf16[144,1664]{1,0:T(8,128)(2,1)} %get-tuple-element.212), channel_id=1, source_target_pairs={{0,16},{4,20},{8,24},{12,28},{16,0},{20,4},{24,8},{28,12},{1,17},{... | collective-permute-start | bytes 1437704 | tf_op jit(solution)/shard_map/ppermute | solution.py:431
  358.3 21.3 %collective-permute-start.33 = (bf16[144,1664]{1,0:T(8,128)(2,1)}, bf16[144,1664]{1,0:T(8,128)(2,1)}, u32[]{:S(2)}, u32[]{:S(2)}) collective-permute-start(bf16[144,1664]{1,0:T(8,128)(2,1)} %get-tuple-element.213), channel_id=1, source_target_pairs={{0,16},{4,20},{8,24},{12,28},{16,0},{20,4},{24,8},{28,12},{1,17},{... | collective-permute-start | bytes 1437704 | tf_op jit(solution)/shard_map/ppermute | solution.py:431
  395.0 51.2 %all-to-all-start.1 = ((bf16[288,4,384]{2,0,1:T(8,128)(2,1)}), bf16[288,4,384]{2,0,1:T(8,128)(2,1)}, u32[]{:S(2)}, u32[]{:S(2)}) async-start(bf16[288,4,384]{2,0,1:T(8,128)(2,1)} %bitcast.135), calls=%async_computation.1 | async-start | bytes 1769472 | tf_op jit(solution)/shard_map/all_to_all | solution.py:791
  399.6 205.6 %reduce-scatter.5.cloned.1.call-start = ((), (), s32[]{:S(2)}) async-start(), calls=%async_computation.8 | async-start | bytes 4423680 | tf_op jit(solution)/shard_map/reduce_scatter | solution.py:833
  402.8 10.2 %collective-permute-start.65 = (bf16[192,1536]{1,0:T(8,128)(2,1)S(1)}, bf16[192,1536]{1,0:T(8,128)(2,1)S(1)}, u32[]{:S(2)}, u32[]{:S(2)}) collective-permute-start(bf16[192,1536]{1,0:T(8,128)(2,1)S(1)} %convolution_convert_fusion.7), channel_id=1, source_target_pairs={{0,4},{4,0},{8,12},{12,8},{16,20},{20,16},{24,28},{28,24},{1,5},{5... | collective-permute-start | bytes 1769480 | tf_op jit(solution)/shard_map/ppermute | solution.py:431
  403.4 14.1 %collective-permute-start.38 = (bf16[288,1536]{1,0:T(8,128)(2,1)S(1)}, bf16[288,1536]{1,0:T(8,128)(2,1)S(1)}, u32[]{:S(2)}, u32[]{:S(2)}) collective-permute-start(bf16[288,1536]{1,0:T(8,128)(2,1)S(1)} %copy-done.54), channel_id=1, source_target_pairs={{0,4},{4,0},{8,12},{12,8},{16,20},{20,16},{24,28},{28,24},{1,5},{5... | collective-permute-start | bytes 2654216 | tf_op jit(solution)/shard_map/ppermute | solution.py:431
  407.1 9.3 %collective-permute-start.71 = (bf16[96,1536]{1,0:T(8,128)(2,1)S(1)}, bf16[96,1536]{1,0:T(8,128)(2,1)S(1)}, u32[]{:S(2)}, u32[]{:S(2)}) collective-permute-start(bf16[96,1536]{1,0:T(8,128)(2,1)S(1)} %get-tuple-element.228), channel_id=1, source_target_pairs={{0,16},{4,20},{8,24},{12,28},{16,0},{20,4},{24,8},{28,12},{1,17},{... | collective-permute-start | bytes 884744 | tf_op jit(solution)/shard_map/ppermute | solution.py:431
  410.1 72.5 %collective-permute-start.67 = (bf16[192,1536]{1,0:T(8,128)(2,1)}, bf16[192,1536]{1,0:T(8,128)(2,1)S(1)}, u32[]{:S(2)}, u32[]{:S(2)}) collective-permute-start(bf16[192,1536]{1,0:T(8,128)(2,1)} %convolution_convert_fusion.5), channel_id=1, source_target_pairs={{0,4},{4,0},{8,12},{12,8},{16,20},{20,16},{24,28},{28,24},{1,5},{5... | collective-permute-start | bytes 1769480 | tf_op jit(solution)/shard_map/ppermute | solution.py:431
  411.7 70.9 %collective-permute-start.69 = (bf16[96,1536]{1,0:T(8,128)(2,1)}, bf16[96,1536]{1,0:T(8,128)(2,1)S(1)}, u32[]{:S(2)}, u32[]{:S(2)}) collective-permute-start(bf16[96,1536]{1,0:T(8,128)(2,1)} %get-tuple-element.229), channel_id=1, source_target_pairs={{0,8},{4,12},{8,0},{12,4},{16,24},{20,28},{24,16},{28,20},{1,9},{5... | collective-permute-start | bytes 884744 | tf_op jit(solution)/shard_map/ppermute | solution.py:431
  487.0 11.0 %collective-permute-start.44 = (bf16[128,256]{1,0:T(8,128)(2,1)}, bf16[128,256]{1,0:T(8,128)(2,1)S(1)}, u32[]{:S(2)}, u32[]{:S(2)}) collective-permute-start(bf16[128,256]{1,0:T(8,128)(2,1)} %get-tuple-element.255), channel_id=1, source_target_pairs={{0,4},{4,0},{8,12},{12,8},{16,20},{20,16},{24,28},{28,24},{1,5},{5... | collective-permute-start | bytes 196616 | tf_op jit(solution)/shard_map/ppermute | solution.py:431
  498.1 15.8 %collective-permute-start.64 = (bf16[192,1536]{1,0:T(8,128)(2,1)}, bf16[192,1536]{1,0:T(8,128)(2,1)}, u32[]{:S(2)}, u32[]{:S(2)}) collective-permute-start(bf16[192,1536]{1,0:T(8,128)(2,1)} %convolution_convert_fusion.9), channel_id=1, source_target_pairs={{0,4},{4,0},{8,12},{12,8},{16,20},{20,16},{24,28},{28,24},{1,5},{5... | collective-permute-start | bytes 1769480 | tf_op jit(solution)/shard_map/ppermute | solution.py:431
  498.2 15.8 %collective-permute-start.66 = (bf16[96,1536]{1,0:T(8,128)(2,1)}, bf16[96,1536]{1,0:T(8,128)(2,1)}, u32[]{:S(2)}, u32[]{:S(2)}) collective-permute-start(bf16[96,1536]{1,0:T(8,128)(2,1)} %get-tuple-element.227), channel_id=1, source_target_pairs={{0,8},{4,12},{8,0},{12,4},{16,24},{20,28},{24,16},{28,20},{1,9},{5... | collective-permute-start | bytes 884744 | tf_op jit(solution)/shard_map/ppermute | solution.py:431
  499.0 15.5 %collective-permute-start.72 = (bf16[96,1536]{1,0:T(8,128)(2,1)}, bf16[96,1536]{1,0:T(8,128)(2,1)}, u32[]{:S(2)}, u32[]{:S(2)}) collective-permute-start(bf16[96,1536]{1,0:T(8,128)(2,1)} %get-tuple-element.226), channel_id=1, source_target_pairs={{0,8},{4,12},{8,0},{12,4},{16,24},{20,28},{24,16},{28,20},{1,9},{5... | collective-permute-start | bytes 884744 | tf_op jit(solution)/shard_map/ppermute | solution.py:431
  500.3 14.3 %collective-permute-start.70 = (bf16[96,1536]{1,0:T(8,128)(2,1)}, bf16[96,1536]{1,0:T(8,128)(2,1)}, u32[]{:S(2)}, u32[]{:S(2)}) collective-permute-start(bf16[96,1536]{1,0:T(8,128)(2,1)} %get-tuple-element.231), channel_id=1, source_target_pairs={{0,16},{4,20},{8,24},{12,28},{16,0},{20,4},{24,8},{28,12},{1,17},{... | collective-permute-start | bytes 884744 | tf_op jit(solution)/shard_map/ppermute | solution.py:431
  500.3 15.4 %collective-permute-start.73 = (bf16[96,1536]{1,0:T(8,128)(2,1)}, bf16[96,1536]{1,0:T(8,128)(2,1)}, u32[]{:S(2)}, u32[]{:S(2)}) collective-permute-start(bf16[96,1536]{1,0:T(8,128)(2,1)} %get-tuple-element.230), channel_id=1, source_target_pairs={{0,16},{4,20},{8,24},{12,28},{16,0},{20,4},{24,8},{28,12},{1,17},{... | collective-permute-start | bytes 884744 | tf_op jit(solution)/shard_map/ppermute | solution.py:431
  514.0 17.1 %collective-permute-start.37 = (bf16[288,1536]{1,0:T(8,128)(2,1)}, bf16[288,1536]{1,0:T(8,128)(2,1)S(1)}, u32[]{:S(2)}, u32[]{:S(2)}) collective-permute-start(bf16[288,1536]{1,0:T(8,128)(2,1)} %get-tuple-element.99), channel_id=1, source_target_pairs={{0,4},{4,0},{8,12},{12,8},{16,20},{20,16},{24,28},{28,24},{1,5},{5... | collective-permute-start | bytes 2654216 | tf_op jit(solution)/shard_map/ppermute | solution.py:431
  514.5 38.3 %collective-permute-start.34 = (bf16[288,1536]{1,0:T(8,128)(2,1)}, bf16[288,1536]{1,0:T(8,128)(2,1)S(1)}, u32[]{:S(2)}, u32[]{:S(2)}) collective-permute-start(bf16[288,1536]{1,0:T(8,128)(2,1)} %get-tuple-element.95), channel_id=1, source_target_pairs={{0,4},{4,0},{8,12},{12,8},{16,20},{20,16},{24,28},{28,24},{1,5},{5... | collective-permute-start | bytes 2654216 | tf_op jit(solution)/shard_map/ppermute | solution.py:431
  514.9 12.2 %collective-permute-start.41 = (bf16[144,1536]{1,0:T(8,128)(2,1)S(1)}, bf16[144,1536]{1,0:T(8,128)(2,1)S(1)}, u32[]{:S(2)}, u32[]{:S(2)}) collective-permute-start(bf16[144,1536]{1,0:T(8,128)(2,1)S(1)} %copy-done.32), channel_id=1, source_target_pairs={{0,16},{4,20},{8,24},{12,28},{16,0},{20,4},{24,8},{28,12},{1,17},{... | collective-permute-start | bytes 1327112 | tf_op jit(solution)/shard_map/ppermute | solution.py:431
  515.7 17.7 %collective-permute-start.39 = (bf16[144,1536]{1,0:T(8,128)(2,1)S(1)}, bf16[144,1536]{1,0:T(8,128)(2,1)S(1)}, u32[]{:S(2)}, u32[]{:S(2)}) collective-permute-start(bf16[144,1536]{1,0:T(8,128)(2,1)S(1)} %copy-done.31), channel_id=1, source_target_pairs={{0,8},{4,12},{8,0},{12,4},{16,24},{20,28},{24,16},{28,20},{1,9},{5... | collective-permute-start | bytes 1327112 | tf_op jit(solution)/shard_map/ppermute | solution.py:431
  518.5 15.2 %collective-permute-start.74 = (bf16[192,384]{1,0:T(8,128)(2,1)S(1)}, bf16[192,384]{1,0:T(8,128)(2,1)S(1)}, u32[]{:S(2)}, u32[]{:S(2)}) collective-permute-start(bf16[192,384]{1,0:T(8,128)(2,1)S(1)} %get-tuple-element.242), channel_id=1, source_target_pairs={{0,1},{1,2},{2,3},{3,0},{4,5},{5,6},{6,7},{7,4},{8,9},{9,10},{10,1... | collective-permute-start | bytes 442376 | tf_op jit(solution)/shard_map/ppermute | solution.py:514
  527.1 14.8 %collective-permute-start.75 = (bf16[192,384]{1,0:T(8,128)(2,1)S(1)}, bf16[192,384]{1,0:T(8,128)(2,1)S(1)}, u32[]{:S(2)}, u32[]{:S(2)}) collective-permute-start(bf16[192,384]{1,0:T(8,128)(2,1)S(1)} %get-tuple-element.244), channel_id=1, source_target_pairs={{0,2},{1,3},{2,0},{3,1},{4,6},{5,7},{6,4},{7,5},{8,10},{9,11},{10,... | collective-permute-start | bytes 442376 | tf_op jit(solution)/shard_map/ppermute | solution.py:514
  531.1 18.6 %collective-permute-start.76 = (bf16[192,384]{1,0:T(8,128)(2,1)S(1)}, bf16[192,384]{1,0:T(8,128)(2,1)S(1)}, u32[]{:S(2)}, u32[]{:S(2)}) collective-permute-start(bf16[192,384]{1,0:T(8,128)(2,1)S(1)} %get-tuple-element.243), channel_id=1, source_target_pairs={{0,3},{1,0},{2,1},{3,2},{4,7},{5,4},{6,5},{7,6},{8,11},{9,8},{10,9... | collective-permute-start | bytes 442376 | tf_op jit(solution)/shard_map/ppermute | solution.py:514
  533.4 16.4 %collective-permute-start.58 = (bf16[192,658]{0,1:T(8,128)(2,1)S(1)}, bf16[192,658]{0,1:T(8,128)(2,1)S(1)}, u32[]{:S(2)}, u32[]{:S(2)}) collective-permute-start(bf16[192,658]{0,1:T(8,128)(2,1)S(1)} %get-tuple-element.205), channel_id=1, source_target_pairs={{0,4},{4,0},{8,12},{12,8},{16,20},{20,16},{24,28},{28,24},{1,5},{5... | collective-permute-start | bytes 758024 | tf_op jit(solution)/shard_map/ppermute | solution.py:431
  533.7 19.2 %collective-permute-start.36 = (bf16[144,1536]{1,0:T(8,128)(2,1)S(1)}, bf16[144,1536]{1,0:T(8,128)(2,1)S(1)}, u32[]{:S(2)}, u32[]{:S(2)}) collective-permute-start(bf16[144,1536]{1,0:T(8,128)(2,1)S(1)} %get-tuple-element.218), channel_id=1, source_target_pairs={{0,8},{4,12},{8,0},{12,4},{16,24},{20,28},{24,16},{28,20},{1,9},{5... | collective-permute-start | bytes 1327112 | tf_op jit(solution)/shard_map/ppermute | solution.py:431
  541.9 13.9 %collective-permute-start.42 = (bf16[144,1536]{1,0:T(8,128)(2,1)S(1)}, bf16[144,1536]{1,0:T(8,128)(2,1)S(1)}, u32[]{:S(2)}, u32[]{:S(2)}) collective-permute-start(bf16[144,1536]{1,0:T(8,128)(2,1)S(1)} %get-tuple-element.219), channel_id=1, source_target_pairs={{0,8},{4,12},{8,0},{12,4},{16,24},{20,28},{24,16},{28,20},{1,9},{5... | collective-permute-start | bytes 1327112 | tf_op jit(solution)/shard_map/ppermute | solution.py:431
  549.8 13.0 %collective-permute-start.40 = (bf16[144,1536]{1,0:T(8,128)(2,1)S(1)}, bf16[144,1536]{1,0:T(8,128)(2,1)S(1)}, u32[]{:S(2)}, u32[]{:S(2)}) collective-permute-start(bf16[144,1536]{1,0:T(8,128)(2,1)S(1)} %get-tuple-element.220), channel_id=1, source_target_pairs={{0,16},{4,20},{8,24},{12,28},{16,0},{20,4},{24,8},{28,12},{1,17},{... | collective-permute-start | bytes 1327112 | tf_op jit(solution)/shard_map/ppermute | solution.py:431
  549.8 21.8 %collective-permute-start.43 = (bf16[144,1536]{1,0:T(8,128)(2,1)S(1)}, bf16[144,1536]{1,0:T(8,128)(2,1)S(1)}, u32[]{:S(2)}, u32[]{:S(2)}) collective-permute-start(bf16[144,1536]{1,0:T(8,128)(2,1)S(1)} %get-tuple-element.221), channel_id=1, source_target_pairs={{0,16},{4,20},{8,24},{12,28},{16,0},{20,4},{24,8},{28,12},{1,17},{... | collective-permute-start | bytes 1327112 | tf_op jit(solution)/shard_map/ppermute | solution.py:431
  552.8 19.4 %collective-permute-start.55 = (bf16[192,658]{0,1:T(8,128)(2,1)S(1)}, bf16[192,658]{0,1:T(8,128)(2,1)S(1)}, u32[]{:S(2)}, u32[]{:S(2)}) collective-permute-start(bf16[192,658]{0,1:T(8,128)(2,1)S(1)} %get-tuple-element.207), channel_id=1, source_target_pairs={{0,4},{4,0},{8,12},{12,8},{16,20},{20,16},{24,28},{28,24},{1,5},{5... | collective-permute-start | bytes 758024 | tf_op jit(solution)/shard_map/ppermute | solution.py:431
  552.9 19.4 %collective-permute-start.57 = (bf16[192,658]{0,1:T(8,128)(2,1)S(1)}, bf16[192,658]{0,1:T(8,128)(2,1)S(1)}, u32[]{:S(2)}, u32[]{:S(2)}) collective-permute-start(bf16[192,658]{0,1:T(8,128)(2,1)S(1)} %get-tuple-element.206), channel_id=1, source_target_pairs={{0,4},{4,0},{8,12},{12,8},{16,20},{20,16},{24,28},{28,24},{1,5},{5... | collective-permute-start | bytes 758024 | tf_op jit(solution)/shard_map/ppermute | solution.py:431
  555.9 27.2 %collective-permute-start.54 = (bf16[192,658]{0,1:T(8,128)(2,1)S(1)}, bf16[192,658]{0,1:T(8,128)(2,1)S(1)}, u32[]{:S(2)}, u32[]{:S(2)}) collective-permute-start(bf16[192,658]{0,1:T(8,128)(2,1)S(1)} %get-tuple-element.204), channel_id=1, source_target_pairs={{0,4},{4,0},{8,12},{12,8},{16,20},{20,16},{24,28},{28,24},{1,5},{5... | collective-permute-start | bytes 758024 | tf_op jit(solution)/shard_map/ppermute | solution.py:431
  562.8 9.5 %collective-permute-start.59 = (bf16[96,658]{0,1:T(8,128)(2,1)S(1)}, bf16[96,658]{0,1:T(8,128)(2,1)S(1)}, u32[]{:S(2)}, u32[]{:S(2)}) collective-permute-start(bf16[96,658]{0,1:T(8,128)(2,1)S(1)} %get-tuple-element.195), channel_id=1, source_target_pairs={{0,8},{4,12},{8,0},{12,4},{16,24},{20,28},{24,16},{28,20},{1,9},{5... | collective-permute-start | bytes 379016 | tf_op jit(solution)/shard_map/ppermute | solution.py:431
  578.5 8.0 %collective-permute-start.62 = (bf16[96,658]{0,1:T(8,128)(2,1)S(1)}, bf16[96,658]{0,1:T(8,128)(2,1)S(1)}, u32[]{:S(2)}, u32[]{:S(2)}) collective-permute-start(bf16[96,658]{0,1:T(8,128)(2,1)S(1)} %get-tuple-element.192), channel_id=1, source_target_pairs={{0,8},{4,12},{8,0},{12,4},{16,24},{20,28},{24,16},{28,20},{1,9},{5... | collective-permute-start | bytes 379016 | tf_op jit(solution)/shard_map/ppermute | solution.py:431
  587.1 9.7 %collective-permute-start.77 = (bf16[48,18]{0,1:T(8,128)(2,1)S(1)}, bf16[48,18]{0,1:T(8,128)(2,1)S(1)}, u32[]{:S(2)}, u32[]{:S(2)}) collective-permute-start(bf16[48,18]{0,1:T(8,128)(2,1)S(1)} %bitcast.150), channel_id=1, source_target_pairs={{0,1},{1,2},{2,3},{3,0},{4,5},{5,6},{6,7},{7,4},{8,9},{9,10},{10,1... | collective-permute-start | bytes 5192 | tf_op jit(solution)/shard_map/ppermute | solution.py:514
  (82 other events, 637.1 us)
Sparse Core Ops, SparseCore 0:
  9.6 79.3 all-gather.4
  90.8 37.0 all-gather.6
  318.8 60.3 reduce-scatter.10
  381.3 74.3 reduce-scatter.8
  457.9 63.7 reduce-scatter.6
  523.8 72.6 reduce-scatter.4

commit v4 on v3

--- a/solution.py
+++ b/solution.py
@@ -435,18 +435,19 @@
     return [1 << k for k in range(number.bit_length()) if number >> k & 1]
 
 
-def gather_blocks(own, axis_name):
+def gather_blocks(own, axis_name, after_first=None):
     count = lax.axis_size(axis_name)
     half = own.shape[0] // 2
-    blocks = {0: own}
+    blocks = {0: own, 1: exchange(own, axis_name, 1)}
     even = sorted(range(2, count, 2), key=lambda j: (len(bits_of(j)), j))
-    if count > 1:
-        blocks[1] = exchange(own, axis_name, 1)
+    singles = [j for j in even if len(bits_of(j)) == 1]
+    for j in singles:
+        blocks[j] = exchange(own, axis_name, j)
+    if after_first is not None:
+        blocks.update(zip(singles, after_first([blocks[j] for j in singles])))
     for j in even:
         bits = bits_of(j)
-        if len(bits) == 1:
-            blocks[j] = exchange(own, axis_name, j)
-        else:
+        if len(bits) > 1:
             low_bit, high_bit = bits[0], bits[-1]
             top = exchange(blocks[j ^ low_bit][:half], axis_name, low_bit)
             bottom = exchange(blocks[j ^ high_bit][half:], axis_name, high_bit)
@@ -455,37 +456,74 @@
     return [blocks[j] for j in range(count)]
 
 
+def pass_on(values, axis_name, step, way):
+    count = lax.axis_size(axis_name)
+    if way > 0:
+        pairs = [(i, i + 1) for i in range(step - 1, count - 1)]
+    else:
+        pairs = [(i, i - 1) for i in range(1, count - step + 1)]
+    return lax.ppermute(values, axis_name, pairs)
+
+
+def gather_line(own, rising, falling, axis_name):
+    count = lax.axis_size(axis_name)
+    index = lax.axis_index(axis_name)
+    rows = own.shape[0]
+    buffer = jnp.zeros(((count + 1) * rows, own.shape[1]), own.dtype)
+    buffer = lax.dynamic_update_slice_in_dim(buffer, own, index * rows, axis=0)
+    for step in range(1, count):
+        if step > 1:
+            rising = pass_on(rising, axis_name, step, 1)
+            falling = pass_on(falling, axis_name, step, -1)
+        slot = jnp.where(index >= step, index - step, count)
+        buffer = lax.dynamic_update_slice_in_dim(buffer, rising, slot * rows, axis=0)
+        slot = jnp.where(index + step < count, index + step, count)
+        buffer = lax.dynamic_update_slice_in_dim(buffer, falling, slot * rows, axis=0)
+    return buffer[: count * rows]
+
+
 def add_rounded(left_side, right_side):
     return (left_side.astype(jnp.float32) + right_side.astype(jnp.float32)).astype(jnp.bfloat16)
 
 
+def fold(even, odd, axis_name):
+    arrived = exchange(odd, axis_name, 1)
+    half = even.shape[0] // 2
+    return [add_rounded(even[:half], arrived[:half]), add_rounded(even[half:], arrived[half:])]
+
+
 def reduce_blocks(blocks, axis_name):
-    count = lax.axis_size(axis_name)
-    half = blocks[0].shape[0] // 2
+    count = len(blocks)
     sums = {}
     for j in sorted(range(0, count, 2), key=lambda j: (-len(bits_of(j)), j)):
-        arrived = exchange(blocks[j + 1], axis_name, 1)
-        sums[j] = [
-            add_rounded(blocks[j][:half], arrived[:half]),
-            add_rounded(blocks[j][half:], arrived[half:]),
-        ]
-    extra = [[], []]
-    for j in sorted(range(2, count, 2), key=lambda j: (-len(bits_of(j)), j)):
-        bits = bits_of(j)
-        if len(bits) > 1:
-            low_bit, high_bit = bits[0], bits[-1]
-            top = exchange(sums[j][0], axis_name, low_bit)
-            bottom = exchange(sums[j][1], axis_name, high_bit)
-            sums[j ^ low_bit][0] = add_rounded(sums[j ^ low_bit][0], top)
-            sums[j ^ high_bit][1] = add_rounded(sums[j ^ high_bit][1], bottom)
-        else:
-            extra[0].append(exchange(sums[j][0], axis_name, j))
-            extra[1].append(exchange(sums[j][1], axis_name, j))
+        sums[j] = fold(blocks[j], blocks[j + 1], axis_name)
+    return reduce_singles(sums, reduce_several(sums, axis_name), axis_name)
+
+
+def reduce_several(sums, axis_name):
+    sums = {j: list(halves) for j, halves in sums.items()}
+    pending = []
+    for j in sorted((j for j in sums if len(bits_of(j)) > 1), key=lambda j: (-len(bits_of(j)), j)):
+        low_bit, high_bit = bits_of(j)[0], bits_of(j)[-1]
+        for part, bit in ((0, low_bit), (1, high_bit)):
+            piece = exchange(sums[j][part], axis_name, bit)
+            if len(bits_of(j ^ bit)) > 1:
+                sums[j ^ bit][part] = add_rounded(sums[j ^ bit][part], piece)
+            else:
+                pending.append((j ^ bit, part, piece))
+    return pending
+
+
+def reduce_singles(sums, pending, axis_name):
+    sums = {j: list(halves) for j, halves in sums.items()}
+    for j, part, piece in pending:
+        sums[j][part] = add_rounded(sums[j][part], piece)
     halves = []
     for part in range(2):
         total = sums[0][part].astype(jnp.float32)
-        for piece in extra[part]:
-            total = total + piece.astype(jnp.float32)
+        for j in sums:
+            if len(bits_of(j)) == 1:
+                total = total + exchange(sums[j][part], axis_name, j).astype(jnp.float32)
         halves.append(total)
     return jnp.concatenate(halves, axis=0)
 
@@ -691,20 +729,26 @@
     query_width = w_query.shape[1]
     key_width = key_projection.shape[1]
 
+    line = [pass_on(tokens, "seq", 1, 1), pass_on(tokens, "seq", 1, -1)]
     small = jnp.concatenate([w_router, gain_attn[:, None], gain_ffn[:, None]], axis=1)
-    small = lax.all_gather(small, "seq", axis=0, tiled=True)
-    small = lax.all_gather(small, "shard", axis=0, tiled=True)
+    small = lax.all_gather(small, ("shard", "seq"), axis=0, tiled=True)
     router_weight = small[:, :experts_all]
     first_gain = small[:, experts_all].astype(jnp.float32)
     second_gain = small[:, experts_all + 1].astype(jnp.float32)
-    block_tokens = lax.all_gather(tokens, "seq", axis=0, tiled=True)
-    qkv_blocks = gather_blocks(
-        jnp.concatenate([w_query, key_projection, value_projection], axis=1), "shard"
-    )
-    qkv_weight = in_order(qkv_blocks, shard_index).reshape(model_width, -1)
-    out_weight = lax.all_gather(w_out, "seq", axis=0, tiled=True)
-    out_weight = lax.all_gather(out_weight, "shard", axis=1, tiled=True)
-    grad_blocks = gather_blocks(lax.optimization_barrier((out_grad, qkv_weight))[0], "shard")
+    own_weight = jnp.concatenate([w_query, key_projection, value_projection], axis=1)
+
+    def after_tokens(blocks):
+        blocks, line[:] = lax.optimization_barrier((blocks, line))
+        return blocks
+
+    qkv_weight = in_order(gather_blocks(own_weight, "shard", after_tokens), shard_index)
+    block_tokens = gather_line(tokens, line[0], line[1], "seq")
+    qkv_weight = qkv_weight.reshape(model_width, -1)
+    out_weight = lax.all_gather(w_out, ("shard", "seq"), axis=0, tiled=False)
+    out_weight = out_weight.reshape(shard_count, seq_count, *w_out.shape)
+    out_weight = out_weight.transpose(1, 2, 0, 3).reshape(model_width, model_width)
+    out_grad_late, qkv_weight = lax.optimization_barrier((out_grad, qkv_weight))
+    grad_blocks = gather_blocks(out_grad_late, "shard")
 
     block_rows = jnp.arange(block_len, dtype=jnp.int32)
     cos_table, sin_table = rotary_tables(
@@ -725,9 +769,22 @@
     kv_own = jnp.concatenate([to_lanes(key_heads), to_lanes(value_heads)], axis=1)
     kv_prompt = lax.all_gather(kv_own[:PROMPT_BLK], "shard", axis=0, tiled=True)
     block_number = shard_index.astype(jnp.int32).reshape(1)
+    singles = [1 << k for k in range(1, (shard_count - 1).bit_length())]
+    queries, grad_blocks[::2] = lax.optimization_barrier((queries, grad_blocks[::2]))
     mixed_own, levels = attend_forward(block_number, queries, kv_prompt, kv_own, group, kv_heads)
+    mixed_own, grad_blocks = lax.optimization_barrier((mixed_own, grad_blocks))
     mixed_heads = mixed_own[:, :query_width]
     mixed_tokens = lax.all_to_all(mixed_heads, "seq", split_axis=0, concat_axis=1, tiled=True)
+
+    half_features = model_width // 2
+    core_bit = shard_index % 2
+    half_weight, mixed_tokens = lax.optimization_barrier(
+        (
+            lax.dynamic_slice_in_dim(qkv_weight, core_bit * half_features, half_features, axis=0),
+            mixed_tokens,
+        )
+    )
+    wide_half = lax.all_gather(half_weight, "seq", axis=0, tiled=False)
 
     own_inputs = tokens.astype(jnp.float32)
     upstream = out_grad.astype(jnp.float32)
@@ -750,29 +807,56 @@
         ],
         axis=1,
     )
-    row_blocks = gather_blocks(coded, "shard")
-    order = sorted(range(0, shard_count, 2), key=lambda j: (len(bits_of(j)), j))
+    row_blocks = {0: coded, 1: exchange(coded, "shard", 1)}
+    for bit in singles:
+        row_blocks[bit] = exchange(coded, "shard", bit)
+    several = sorted(
+        (j for j in range(0, shard_count, 2) if len(bits_of(j)) > 1),
+        key=lambda j: (len(bits_of(j)), j),
+    )
+    order = [0] + singles[:-1] + several + singles[-1:]
     first_expert = (shard_index * local_experts).astype(jnp.int32).reshape(1)
     carried = None
-    row_parts = [None] * shard_count
+    row_sums = {}
     out_parts = [None] * shard_count
     for position, j in enumerate(order):
+        row_pair = [row_blocks[j], row_blocks[j + 1]]
+        if j == order[-1]:
+            row_pair, row_sums = lax.optimization_barrier((row_pair, row_sums))
+            pending = reduce_several(row_sums, "shard")
         carried, pieces = expert_pair(
             position,
             len(order),
             first_expert,
             experts_all,
-            row_blocks[j : j + 2],
+            row_pair,
             grad_blocks[j : j + 2],
             (w_gate, w_up, w_down),
             carried,
         )
-        row_parts[j], row_parts[j + 1], out_parts[j], out_parts[j + 1] = pieces
+        pieces = list(pieces)
+        if j == 0:
+            arrived, pieces[2] = lax.optimization_barrier(
+                ([row_blocks[bit] for bit in singles], pieces[2])
+            )
+            row_blocks.update(zip(singles, arrived))
+            half = tok_count // 2
+            for k in singles + several:
+                if k in several:
+                    low_bit, high_bit = bits_of(k)[0], bits_of(k)[-1]
+                    top = exchange(row_blocks[k ^ low_bit][:half], "shard", low_bit)
+                    bottom = exchange(row_blocks[k ^ high_bit][half:], "shard", high_bit)
+                    row_blocks[k] = jnp.concatenate([top, bottom], axis=0)
+                row_blocks[k + 1] = exchange(row_blocks[k], "shard", 1)
+        row_sums[j] = fold(pieces[0], pieces[1], "shard")
+        out_parts[j], out_parts[j + 1] = pieces[2], pieces[3]
     all_rows, all_grads, all_pre, all_hidden = carried
+    arrived = [piece for _, _, piece in pending]
+    row_sums, all_grads, arrived = lax.optimization_barrier((row_sums, all_grads, arrived))
+    pending = [(j, part, piece) for (j, part, _), piece in zip(pending, arrived)]
     down_sum = transposed_times(all_grads, all_hidden).astype(bf16)
-    pre_sums = [transposed_times(all_rows, all_pre[e]).astype(bf16) for e in range(local_experts)]
-    row_total = reduce_blocks(row_parts, "shard")
-    row_total = lax.optimization_barrier((row_total, down_sum, *pre_sums))[0]
+    row_total = reduce_singles(row_sums, pending, "shard")
+    row_total, down_sum = lax.optimization_barrier((row_total, down_sum))
     row_grad = row_total[:, :model_width]
     gate_grad_dense = (
         row_total[:, model_width : model_width + experts_all]
@@ -788,8 +872,13 @@
     residual_grad = upstream + residual_part
     residual_low = residual_grad.astype(bf16)
     mixed_grad_tokens = times_transposed(residual_low, out_weight).astype(bf16)
+    other_half = exchange(wide_half, "shard", 1)
+    mixed_grad_tokens, out_parts, all_rows, other_half, mixed_late = lax.optimization_barrier(
+        (mixed_grad_tokens, out_parts, all_rows, other_half, mixed_tokens)
+    )
     mixed_grad = lax.all_to_all(mixed_grad_tokens, "seq", split_axis=1, concat_axis=0, tiled=True)
-    out_parts = lax.optimization_barrier((out_parts, mixed_grad_tokens))[0]
+    pre_sums = [transposed_times(all_rows, all_pre[e]).astype(bf16) for e in range(local_experts)]
+    mixed_grad, pre_sums = lax.optimization_barrier((mixed_grad, pre_sums))
     expert_sum = reduce_blocks(out_parts, "shard")
     output = (residual + expert_sum).astype(bf16)
     columns = [
@@ -801,7 +890,7 @@
         )
         for j in range(shard_count)
     ]
-    whole_out = [transposed_times(part, mixed_tokens).astype(bf16) for part in columns]
+    whole_out = [transposed_times(part, mixed_late).astype(bf16) for part in columns]
     grad_out = reduce_blocks(whole_out, "shard").astype(bf16)
     grad_out = grad_out.reshape(grad_out.shape[0], seq_count, -1).transpose(1, 0, 2)
     grad_out = scatter_direct(grad_out, "seq").T
@@ -828,23 +917,50 @@
     ).astype(bf16)
     lin_query = rotate(query_grad, cos_table, -sin_table, HEAD_DIMENSION).astype(bf16)
     lin_key = rotate(key_grad, cos_table, -sin_table, HEAD_DIMENSION).astype(bf16)
-    lin_all = jnp.concatenate([lin_query, lin_key, value_low], axis=1)
-    normed_part = times_transposed(lin_all, qkv_weight)
-    normed_grad = lax.psum_scatter(
-        normed_part.astype(bf16), "seq", scatter_dimension=0, tiled=True
-    ).astype(jnp.float32)
-    gain_part = jnp.sum(normed_part * inputs * first_factor, axis=0)
-    small_grad = jnp.concatenate(
-        [grad_router, gain_part[:, None], grad_gain_ffn[:, None]], axis=1
-    )
-    grad_qkv = jnp.concatenate([transposed_times(normed_low, lin_all), small_grad], axis=1)
+    lin_both = jnp.concatenate([lin_key, value_low], axis=1)
+    query_tokens = lax.all_to_all(lin_query, "seq", split_axis=0, concat_axis=1, tiled=True)
+    lin_both, query_tokens = lax.optimization_barrier((lin_both, query_tokens))
+    both_tokens = lax.all_to_all(lin_both, "seq", split_axis=0, concat_axis=1, tiled=True)
+    parts = [0.0, 0.0]
+    for lin, first, last in (
+        (query_tokens, 0, query_width),
+        (both_tokens, query_width, query_width + 2 * key_width),
+    ):
+        for k, weight in enumerate((wide_half, other_half)):
+            for group_index in range(seq_count):
+                columns = slice(group_index * (last - first), (group_index + 1) * (last - first))
+                parts[k] = parts[k] + times_transposed(
+                    lin[:, columns], weight[group_index, :, first:last]
+                )
+    normed_grad = jnp.concatenate(
+        [
+            jnp.where(core_bit == 0, parts[0], parts[1]),
+            jnp.where(core_bit == 0, parts[1], parts[0]),
+        ],
+        axis=1,
+    )
+    small_grad = jnp.concatenate([grad_router, grad_gain_ffn[:, None]], axis=1)
+    grad_qkv = jnp.concatenate(
+        [
+            transposed_times(normed_low, lin_query),
+            transposed_times(normed_low, lin_both),
+            small_grad,
+        ],
+        axis=1,
+    )
     grad_qkv = reduce_blocks(
         relative_blocks(grad_qkv.astype(bf16), shard_index, shard_count), "shard"
+    )
+    own_features = own_weight.shape[0]
+    gain_own = lax.dynamic_slice_in_dim(first_gain, shard_index * own_features, own_features)
+    all_columns = own_weight.shape[1]
+    gain_part = (
+        jnp.sum(own_weight.astype(jnp.float32) * grad_qkv[:, :all_columns], axis=1) / gain_own
     )
     grad_query = grad_qkv[:, :query_width]
     grad_key = grad_qkv[:, query_width : query_width + key_width]
     grad_value = grad_qkv[:, query_width + key_width : query_width + 2 * key_width]
-    small_grad = grad_qkv[:, query_width + 2 * key_width :].astype(bf16)
+    small_grad = jnp.concatenate([grad_qkv[:, all_columns:], gain_part[:, None]], axis=1).astype(bf16)
     small_grad = scatter_direct(
         small_grad.reshape(seq_count, -1, small_grad.shape[1]), "seq"
     )
@@ -866,8 +982,8 @@
         grad_key,
         grad_value,
         grad_out,
+        small_grad[:, experts_all + 1],
         small_grad[:, experts_all],
-        small_grad[:, experts_all + 1],
         small_grad[:, :experts_all],
         grad_gate.astype(jnp.float32),
         grad_up.astype(jnp.float32),

time: 627 us -> 765 us (1.22)
  local copies, waits for them, and re-layouts: 47 us -> 97.8 us
  blocking collectives: 57 us -> 81.8 us
  starting transfers between devices: 66.7 us -> 90 us
  other arithmetic: 43.5 us -> 63.3 us
  matrix products: 76.4 us -> 94.8 us
    ppermute x74 -> x75, waiting for transfers between devices: 111 us -> 76.4 us  [exchange(): return lax.ppermute(values, axis_name, [(i, i ^ bit) for i in range(count)])]
    ppermute x0 -> x6, waiting for transfers between devices: none -> 25.1 us  [pass_on(): return lax.ppermute(values, axis_name, pairs)]
    all_gather x3 -> x1, blocking collectives: 46.7 us -> 71.4 us  [on_device(): small = lax.all_gather(small, ('shard', 'seq'), axis=0, tiled=True)]
    all_to_all x1, waiting for transfers between devices: 0.01 us -> 19.9 us  [on_device(): lax.all_to_all(mixed_heads, 'seq', split_axis=0, concat_axis=1, tiled=True)]
    all_to_all x1, waiting for transfers between devices: 27.6 us -> 8.73 us  [on_device(): lax.all_to_all(mixed_grad_tokens, 'seq', split_axis=1, concat_axis=0, til...]
    ppermute x6, waiting for transfers between devices: 15.1 us -> 33.1 us  [scatter_direct(): lax.ppermute(piece, axis_name, [(i, (i + step) % count) for i in range(co...]
    dot_general x3 -> x18, matrix products: 12.2 us -> 29.6 us  [times_transposed(): lax.dot_general(left_side, right_side, (((1,), (1,)), ((), ())), precisio...]
    unnamed x144 -> x123, local copies, waits for them, and re-layouts: 19.9 us -> 33.2 us
  transfers between devices with their start and end apart: 88 -> 96, of which waited for: 26 -> 30; matrix products, arithmetic and copies ran while one was open for 23% -> 30% of each run, Pallas kernels for 20% -> 19%
where the time goes in v4:
time: 765 us; the launch traced here: 755 us
  waiting for transfers between devices  163 us (21%)
  Pallas kernels  146 us (19%)
  local copies, waits for them, and re-layouts  97.8 us (13%)
  matrix products  94.8 us (12%)
  starting transfers between devices  90 us (12%)
  blocking collectives  81.8 us (11%)
  other arithmetic  63.3 us (8%)
  between operations  17.3 us (2%)
    pallas_call x4, Pallas kernels, expert_pair(): pl.pallas_call(partial(expert_body, experts_all), out_shape=out_shape, gr...  86.4 us
    ppermute x75, waiting for transfers between devices, exchange(): return lax.ppermute(values, axis_name, [(i, i ^ bit) for i in range(count)])  76.4 us
    all_gather x1, blocking collectives, on_device(): small = lax.all_gather(small, ('shard', 'seq'), axis=0, tiled=True)  71.4 us
    dot_general x14, matrix products, transposed_times(): lax.dot_general(left_side, right_side, (((0,), (0,)), ((), ())), precisio...  58 us
    ppermute x75, starting transfers between devices, exchange(): return lax.ppermute(values, axis_name, [(i, i ^ bit) for i in range(count)])  48.2 us
    pallas_call x1, Pallas kernels, attend_backward(): pl.pallas_call(partial(attend_backward_body, group, kv_heads), out_shape=...  34.8 us
    unnamed x123, local copies, waits for them, and re-layouts  33.2 us
    ppermute x6, waiting for transfers between devices, scatter_direct(): lax.ppermute(piece, axis_name, [(i, (i + step) % count) for i in range(co...  33.1 us
  transfers between devices with their start and end apart: 96, of which 30 were waited for; matrix products, arithmetic and copies ran while one was open for 30% of the time, Pallas kernels for 19%

profile of v4, /device:TPU:0, one launch (start us, length us, event | category | flops | bytes accessed | tf_op | source)
XLA Modules:
  0.0 754.6 jit_solution(710587287655420235)
XLA Ops:
  11.6 2.6 collective-permute-start.1
  15.7 4.5 collective-permute-start.3
  25.0 16.3 %collective-permute-done.3 = bf16[288,1536]{1,0:T(8,128)(2,1)} collective-permute-done((bf16[288,1536]{1,0:T(8,128)(2,1)}, bf16[288,1536]{1,0:T(8,128)(2,1)}, u32[]{:S(2)}, u32[]{:S(2)}) %collective-permute-start.3) | collective-permute-done | bytes 884768 | tf_op jit(solution)/shard_map/ppermute | solution.py:465
  41.3 5.2 collective-permute-done.4
  50.7 4.3 collective-permute-done.8
  71.4 4.3 copy.142
  77.2 2.3 broadcast_in_dim.18
  81.0 71.4 %all-gather.2 = bf16[32,48,18]{1,2,0:T(8,128)(2,1)S(1)} all-gather(bf16[1,48,18]{1,2,0:T(8,128)(2,1)S(1)} %maximum_bitcast_fusion), channel_id=1, replica_groups=mesh['shard'=8,'seq'=4] {'shard','seq'}, dimensions={0}, use_global_device_ids=true | all-gather | bytes 57024 | tf_op jit(solution)/shard_map/all_gather | solution.py:734
  152.8 2.1 constant_dynamic-update-slice_fusion.9
  159.1 2.1 constant_dynamic-update-slice_fusion.7
  162.9 2.1 constant_dynamic-update-slice_fusion.6
  165.0 6.6 collective-permute-done.16
  172.5 2.5 collective-permute-done.17
  177.2 3.6 collective-permute-done.13
  181.8 2.8 fusion
  184.6 5.1 fusion.129
  194.4 10.4 %all_gather.19.kp_ref.vp_ref = bf16[1024,256]{1,0:T(8,128)(2,1)} all-gather(bf16[128,256]{1,0:T(8,128)(2,1)S(1)} %fusion.91), channel_id=1, replica_groups=mesh['shard'=8,'seq'=4] {'shard'}, dimensions={0}, use_global_device_ids=true | all-gather | bytes 589824 | tf_op jit(solution)/shard_map/all_gather | solution.py:770
  206.1 24.9 %attend_forward.1 = (bf16[1152,384]{1,0:T(8,128)(2,1)}, f32[6,1,1152]{2,1,0:T(1,128)}) custom-call(s32[1]{0:T(128)} %bitcast.9.index_ref, bf16[1152,384]{1,0:T(8,128)(2,1)} %copy.146.q_ref, bf16[1024,256]{1,0:T(8,128)(2,1)} %all_gather.19.kp_ref.vp_ref, bf16[1024,256]{1,0:T(8,128)(2,1)} %all_gather.19.kp_ref.vp_ref, ...), custom_call_target="tpu_custom_call" | custom-call | flops 9059696640 | bytes 3538944 | tf_op jit(solution)/shard_map/attend_forward/pallas_call | solution.py:366
  231.1 3.5 all-to-all-start
  235.5 2.2 constant_dynamic-slice_fusion.9
  237.7 19.9 %all-to-all-done = bf16[4,288,384]{2,1,0:T(8,128)(2,1)S(1)} async-done(((bf16[4,288,384]{2,1,0:T(8,128)(2,1)}), bf16[4,288,384]{2,1,0:T(8,128)(2,1)S(1)}, u32[]{:S(2)}, u32[]{:S(2)}) %all-to-all-start) | async-done | bytes 884768 | tf_op jit(solution)/shard_map/all_to_all | solution.py:777
  257.7 8.1 %reshape.265 = bf16[8,4,384,192]{2,1,0,3:T(4,128)(2,1)} reshape(bf16[12288,192]{0,1:T(8,128)(2,1)} %all-gather.6.cloned.1.call-done) | data formatting | bytes 9437184 | tf_op jit(solution)/shard_map/reshape | solution.py:748
  265.9 4.0 copy.148
  282.0 21.5 %experts.4 = (bf16[2304,1536]{1,0:T(8,128)(2,1)}, bf16[2304,1536]{1,0:T(8,128)(2,1)}, bf16[2,2304,1024]{2,1,0:T(8,128)(2,1)}, bf16[2304,1024]{1,0:T(8,128)(2,1)}...) custom-call(s32[1]{0:T(128)} %bitcast.20.index_ref, ...), custom_call_target="tpu_custom_call" | custom-call | flops 10871635968 | bytes 27131904 | tf_op jit(solution)/shard_map/experts/pallas_call | solution.py:674
  310.6 9.2 %collective-permute-done.29 = bf16[144,1664]{1,0:T(8,128)(2,1)} collective-permute-done((bf16[144,1664]{1,0:T(8,128)(2,1)}, bf16[144,1664]{1,0:T(8,128)(2,1)}, u32[]{:S(2)}, u32[]{:S(2)}) %collective-permute-start.29) | collective-permute-done | bytes 479264 | tf_op jit(solution)/shard_map/ppermute | solution.py:431
  323.9 21.6 %experts.5 = (bf16[2304,1536]{1,0:T(8,128)(2,1)}, bf16[2304,1536]{1,0:T(8,128)(2,1)}, bf16[2,2304,1024]{2,1,0:T(8,128)(2,1)}, bf16[2304,1024]{1,0:T(8,128)(2,1)}...) custom-call(s32[1]{0:T(128)} %bitcast.20.index_ref, ...), custom_call_target="tpu_custom_call", output_to_operand_aliasing={{0}: (8, {}), {1}: (9, {}), {2}: (10, {}), {3}: (11, {})} | custom-call | flops 10871635968 | bytes 27131904 | tf_op jit(solution)/shard_map/experts/pallas_call | solution.py:674
  346.1 21.8 %experts.6 = (bf16[2304,1536]{1,0:T(8,128)(2,1)}, bf16[2304,1536]{1,0:T(8,128)(2,1)}, bf16[2,2304,1024]{2,1,0:T(8,128)(2,1)}, bf16[2304,1024]{1,0:T(8,128)(2,1)}...) custom-call(s32[1]{0:T(128)} %bitcast.20.index_ref, ...), custom_call_target="tpu_custom_call", output_to_operand_aliasing={{0}: (8, {}), {1}: (9, {}), {2}: (10, {}), {3}: (11, {})} | custom-call | flops 10871635968 | bytes 27131904 | tf_op jit(solution)/shard_map/experts/pallas_call | solution.py:674
  368.1 2.8 add_convert_fusion.8
  370.9 2.4 add_convert_fusion.6
  374.5 21.5 %experts.7 = (bf16[2304,1536]{1,0:T(8,128)(2,1)}, bf16[2304,1536]{1,0:T(8,128)(2,1)}, bf16[2,2304,1024]{2,1,0:T(8,128)(2,1)}, bf16[2304,1024]{1,0:T(8,128)(2,1)}...) custom-call(s32[1]{0:T(128)} %bitcast.20.index_ref, ...), custom_call_target="tpu_custom_call", output_to_operand_aliasing={{0}: (8, {}), {1}: (9, {}), {2}: (10, {}), {3}: (11, {})} | custom-call | flops 10871635968 | bytes 27131904 | tf_op jit(solution)/shard_map/experts/pallas_call | solution.py:674
  400.0 2.6 add_convert_fusion.2
  402.6 8.8 %collective-permute-done.34 = bf16[144,1664]{1,0:T(8,128)(2,1)S(1)} collective-permute-done((bf16[144,1664]{1,0:T(8,128)(2,1)}, bf16[144,1664]{1,0:T(8,128)(2,1)S(1)}, u32[]{:S(2)}, u32[]{:S(2)}) %collective-permute-start.34) | collective-permute-done | bytes 479264 | tf_op jit(solution)/shard_map/ppermute | solution.py:431
  418.2 11.2 %convolution_convert_fusion = bf16[1536,1024]{1,0:T(8,128)(2,1)} fusion(bf16[2304,1536]{1,0:T(8,128)(2,1)} %get-tuple-element.172, bf16[2304,1024]{1,0:T(8,128)(2,1)S(1)} %copy-done), kind=kOutput, calls=%fused_computation.13 | convolution fusion | flops 7249330176 | bytes 14942208 | tf_op jit(solution)/shard_map/dot_general | solution.py:71
  431.0 4.0 collective-permute-done.37
  438.6 3.1 multiply_reduce_fusion
  443.0 2.3 convolution_convert_fusion.12
  445.3 3.9 fusion.131
  449.3 3.9 convolution_convert_fusion.2
  454.2 4.2 all-to-all-start.1
  463.2 12.7 %fusion.9 = bf16[1536,1024]{1,0:T(8,128)(2,1)} fusion(bf16[2304,1536]{1,0:T(8,128)(2,1)} %get-tuple-element.194, bf16[2,2304,1024]{2,1,0:T(8,128)(2,1)} %get-tuple-element.195), kind=kOutput, calls=%fused_computation.11 | convolution fusion | flops 7249330176 | bytes 14942208 | tf_op jit(solution)/shard_map/dot_general | solution.py:71
  475.9 12.8 %fusion.12 = bf16[1536,1024]{1,0:T(8,128)(2,1)} fusion(bf16[2304,1536]{1,0:T(8,128)(2,1)} %get-tuple-element.194, bf16[2,2304,1024]{2,1,0:T(8,128)(2,1)} %get-tuple-element.195), kind=kOutput, calls=%fused_computation.12 | convolution fusion | flops 7249330176 | bytes 14942208 | tf_op jit(solution)/shard_map/dot_general | solution.py:71
  492.9 2.0 add_convert_fusion.23
  497.4 8.7 %all-to-all-done.1 = bf16[288,4,384]{2,0,1:T(8,128)(2,1)} async-done(((bf16[288,4,384]{2,0,1:T(8,128)(2,1)}), bf16[288,4,384]{2,0,1:T(8,128)(2,1)}, u32[]{:S(2)}, u32[]{:S(2)}) %all-to-all-start.1) | async-done | bytes 884768 | tf_op jit(solution)/shard_map/all_to_all | solution.py:879
  510.6 6.5 collective-permute-done.78
  521.3 2.3 add_convert_fusion.16
  524.1 4.1 collective-permute-done.79
  530.1 4.5 collective-permute-done.73
  538.1 34.8 %attend_backward.1 = (f32[1152,384]{1,0:T(8,128)}, bf16[1024,256]{1,0:T(8,128)(2,1)}, f32[1152,256]{1,0:T(8,128)}) custom-call(s32[1]{0:T(128)} %bitcast.9.index_ref, bf16[1152,384]{1,0:T(8,128)(2,1)} %copy.146.q_ref, bf16[1152,384]{1,0:T(8,128)(2,1)} %bitcast.23.grad_ref, bf16[1152,384]{1,0:T(8,128)(2,1)} %get-tuple-element.122.mixed_ref, ...), custom_call_target="tpu_custom_call" | custom-call | flops 22649241600 | bytes 3538944 | tf_op jit(solution)/shard_map/attend_backward/pallas_call | solution.py:394
  572.9 2.1 copy.156
  577.2 2.8 convert_element_type.842
  582.0 3.5 all-to-all-start.2
  585.5 5.1 convolution_convert_fusion.1
  592.3 2.7 add_convert_fusion.15
  595.6 2.8 add_convert_fusion.18
  598.4 2.8 collective-permute-start.82
  606.7 33.1 %collective-permute-done.82 = bf16[192,384]{1,0:T(8,128)(2,1)S(1)} collective-permute-done((bf16[192,384]{1,0:T(8,128)(2,1)S(1)}, bf16[192,384]{1,0:T(8,128)(2,1)S(1)}, u32[]{:S(2)}, u32[]{:S(2)}) %collective-permute-start.82) | collective-permute-done | bytes 147488 | tf_op jit(solution)/shard_map/ppermute | solution.py:552
  642.6 2.0 collective-permute-start.47
  653.4 2.7 collective-permute-done.47
  658.0 7.2 collective-permute-done.50
  666.9 2.4 convert_add_fusion.4
  670.5 3.5 convolution_convert_fusion.3
  674.0 8.5 %all-to-all-start.3 = ((bf16[4,288,256]{2,1,0:T(8,128)(2,1)}), bf16[4,288,256]{2,1,0:T(8,128)(2,1)}, u32[]{:S(2)}, u32[]{:S(2)}) async-start(bf16[4,288,256]{2,1,0:T(8,128)(2,1)} %bitcast.34), calls=%async_computation.3 | async-start | bytes 1179648 | tf_op jit(solution)/shard_map/all_to_all | solution.py:923
  706.1 2.1 collective-permute-done.67
  709.4 3.8 collective-permute-start.86
  (429 shorter events, 206.4 us)
Async XLA Ops:
  8.0 249.7 %all-gather.6.cloned.1.call-start = ((), (), s32[]{:S(2)}) async-start(), calls=%async_computation.10 | async-start | bytes 4866048 | tf_op jit(solution)/shard_map/all_gather | solution.py:747
  11.0 13.2 %collective-permute-start = (bf16[192,640]{0,1:T(8,128)(2,1)S(1)}, bf16[192,640]{0,1:T(8,128)(2,1)S(1)}, u32[]{:S(2)}, u32[]{:S(2)}) collective-permute-start(bf16[192,640]{0,1:T(8,128)(2,1)S(1)} %pad_maximum_fusion.5), channel_id=1, source_target_pairs={{0,4},{4,0},{8,12},{12,8},{16,20},{20,16},{24,28},{28,24},{1,5},{5... | collective-permute-start | bytes 737288 | tf_op jit(solution)/shard_map/ppermute | solution.py:431
  11.6 13.4 %collective-permute-start.1 = (bf16[192,640]{0,1:T(8,128)(2,1)S(1)}, bf16[192,640]{0,1:T(8,128)(2,1)S(1)}, u32[]{:S(2)}, u32[]{:S(2)}) collective-permute-start(bf16[192,640]{0,1:T(8,128)(2,1)S(1)} %pad_maximum_fusion.5), channel_id=1, source_target_pairs={{0,8},{4,12},{8,0},{12,4},{16,24},{20,28},{24,16},{28,20},{1,9},{5... | collective-permute-start | bytes 737288 | tf_op jit(solution)/shard_map/ppermute | solution.py:431
  15.7 25.6 %collective-permute-start.3 = (bf16[288,1536]{1,0:T(8,128)(2,1)}, bf16[288,1536]{1,0:T(8,128)(2,1)}, u32[]{:S(2)}, u32[]{:S(2)}) collective-permute-start(bf16[288,1536]{1,0:T(8,128)(2,1)} %param.13), channel_id=1, source_target_pairs={{0,1},{1,2},{2,3},{4,5},{5,6},{6,7},{8,9},{9,10},{10,11},{12,13},{... | collective-permute-start | bytes 2654216 | tf_op jit(solution)/shard_map/ppermute | solution.py:465
  20.1 26.4 %collective-permute-start.4 = (bf16[288,1536]{1,0:T(8,128)(2,1)}, bf16[288,1536]{1,0:T(8,128)(2,1)S(1)}, u32[]{:S(2)}, u32[]{:S(2)}) collective-permute-start(bf16[288,1536]{1,0:T(8,128)(2,1)} %param.13), channel_id=1, source_target_pairs={{1,0},{2,1},{3,2},{5,4},{6,5},{7,6},{9,8},{10,9},{11,10},{13,12},{... | collective-permute-start | bytes 2654216 | tf_op jit(solution)/shard_map/ppermute | solution.py:465
  46.7 12.3 %collective-permute-start.6 = (bf16[192,640]{0,1:T(8,128)(2,1)S(1)}, bf16[192,640]{0,1:T(8,128)(2,1)S(1)}, u32[]{:S(2)}, u32[]{:S(2)}) collective-permute-start(bf16[192,640]{0,1:T(8,128)(2,1)S(1)} %collective-permute-done.2), channel_id=1, source_target_pairs={{0,4},{4,0},{8,12},{12,8},{16,20},{20,16},{24,28},{28,24},{1,5},{5... | collective-permute-start | bytes 737288 | tf_op jit(solution)/shard_map/ppermute | solution.py:431
  48.4 107.6 %collective-permute-start.10 = (bf16[288,1536]{1,0:T(8,128)(2,1)}, bf16[288,1536]{1,0:T(8,128)(2,1)}, u32[]{:S(2)}, u32[]{:S(2)}) collective-permute-start(bf16[288,1536]{1,0:T(8,128)(2,1)} %collective-permute-done.3), channel_id=1, source_target_pairs={{1,2},{2,3},{5,6},{6,7},{9,10},{10,11},{13,14},{14,15},{17,18},{18... | collective-permute-start | bytes 2654216 | tf_op jit(solution)/shard_map/ppermute | solution.py:465
  55.0 101.7 %collective-permute-start.11 = (bf16[288,1536]{1,0:T(8,128)(2,1)S(1)}, bf16[288,1536]{1,0:T(8,128)(2,1)}, u32[]{:S(2)}, u32[]{:S(2)}) collective-permute-start(bf16[288,1536]{1,0:T(8,128)(2,1)S(1)} %collective-permute-done.4), channel_id=1, source_target_pairs={{1,0},{2,1},{5,4},{6,5},{9,8},{10,9},{13,12},{14,13},{17,16},{18,1... | collective-permute-start | bytes 2654216 | tf_op jit(solution)/shard_map/ppermute | solution.py:465
  75.7 82.3 %collective-permute-start.15 = (bf16[288,1536]{1,0:T(8,128)(2,1)}, bf16[288,1536]{1,0:T(8,128)(2,1)}, u32[]{:S(2)}, u32[]{:S(2)}) collective-permute-start(bf16[288,1536]{1,0:T(8,128)(2,1)} %og_even), channel_id=1, source_target_pairs={{0,16},{4,20},{8,24},{12,28},{16,0},{20,4},{24,8},{28,12},{1,17},{... | collective-permute-start | bytes 2654216 | tf_op jit(solution)/shard_map/ppermute | solution.py:431
  80.5 80.8 %collective-permute-start.14 = (bf16[288,1536]{1,0:T(8,128)(2,1)}, bf16[288,1536]{1,0:T(8,128)(2,1)}, u32[]{:S(2)}, u32[]{:S(2)}) collective-permute-start(bf16[288,1536]{1,0:T(8,128)(2,1)} %og_even), channel_id=1, source_target_pairs={{0,8},{4,12},{8,0},{12,4},{16,24},{20,28},{24,16},{28,20},{1,9},{5... | collective-permute-start | bytes 2654216 | tf_op jit(solution)/shard_map/ppermute | solution.py:431
  155.9 75.1 %collective-permute-start.18 = (bf16[288,1536]{1,0:T(8,128)(2,1)}, bf16[288,1536]{1,0:T(8,128)(2,1)}, u32[]{:S(2)}, u32[]{:S(2)}) collective-permute-start(bf16[288,1536]{1,0:T(8,128)(2,1)} %og_even), channel_id=1, source_target_pairs={{0,4},{4,0},{8,12},{12,8},{16,20},{20,16},{24,28},{28,24},{1,5},{5... | collective-permute-start | bytes 2654216 | tf_op jit(solution)/shard_map/ppermute | solution.py:431
  155.9 19.8 %collective-permute-start.12 = (bf16[288,1536]{1,0:T(8,128)(2,1)}, bf16[288,1536]{1,0:T(8,128)(2,1)S(1)}, u32[]{:S(2)}, u32[]{:S(2)}) collective-permute-start(bf16[288,1536]{1,0:T(8,128)(2,1)} %collective-permute-done.10), channel_id=1, source_target_pairs={{2,3},{6,7},{10,11},{14,15},{18,19},{22,23},{26,27},{30,31}} | collective-permute-start | bytes 2654216 | tf_op jit(solution)/shard_map/ppermute | solution.py:465
  156.7 24.2 %collective-permute-start.13 = (bf16[288,1536]{1,0:T(8,128)(2,1)}, bf16[288,1536]{1,0:T(8,128)(2,1)S(1)}, u32[]{:S(2)}, u32[]{:S(2)}) collective-permute-start(bf16[288,1536]{1,0:T(8,128)(2,1)} %collective-permute-done.11), channel_id=1, source_target_pairs={{1,0},{5,4},{9,8},{13,12},{17,16},{21,20},{25,24},{29,28}} | collective-permute-start | bytes 2654216 | tf_op jit(solution)/shard_map/ppermute | solution.py:465
  159.0 12.6 %collective-permute-start.16 = (bf16[144,1536]{1,0:T(8,128)(2,1)S(1)}, bf16[144,1536]{1,0:T(8,128)(2,1)S(1)}, u32[]{:S(2)}, u32[]{:S(2)}) collective-permute-start(bf16[144,1536]{1,0:T(8,128)(2,1)S(1)} %slice.605), channel_id=1, source_target_pairs={{0,8},{4,12},{8,0},{12,4},{16,24},{20,28},{24,16},{28,20},{1,9},{5... | collective-permute-start | bytes 1327112 | tf_op jit(solution)/shard_map/ppermute | solution.py:431
  162.3 12.6 %collective-permute-start.17 = (bf16[144,1536]{1,0:T(8,128)(2,1)S(1)}, bf16[144,1536]{1,0:T(8,128)(2,1)S(1)}, u32[]{:S(2)}, u32[]{:S(2)}) collective-permute-start(bf16[144,1536]{1,0:T(8,128)(2,1)S(1)} %slice.606), channel_id=1, source_target_pairs={{0,16},{4,20},{8,24},{12,28},{16,0},{20,4},{24,8},{28,12},{1,17},{... | collective-permute-start | bytes 1327112 | tf_op jit(solution)/shard_map/ppermute | solution.py:431
  171.7 59.4 %collective-permute-start.19 = (bf16[288,1536]{1,0:T(8,128)(2,1)}, bf16[288,1536]{1,0:T(8,128)(2,1)}, u32[]{:S(2)}, u32[]{:S(2)}) collective-permute-start(bf16[288,1536]{1,0:T(8,128)(2,1)} %collective-permute-done.14.og_even), channel_id=1, source_target_pairs={{0,4},{4,0},{8,12},{12,8},{16,20},{20,16},{24,28},{28,24},{1,5},{5... | collective-permute-start | bytes 2654216 | tf_op jit(solution)/shard_map/ppermute | solution.py:431
  174.9 56.1 %collective-permute-start.20 = (bf16[288,1536]{1,0:T(8,128)(2,1)}, bf16[288,1536]{1,0:T(8,128)(2,1)}, u32[]{:S(2)}, u32[]{:S(2)}) collective-permute-start(bf16[288,1536]{1,0:T(8,128)(2,1)} %collective-permute-done.15.og_even), channel_id=1, source_target_pairs={{0,4},{4,0},{8,12},{12,8},{16,20},{20,16},{24,28},{28,24},{1,5},{5... | collective-permute-start | bytes 2654216 | tf_op jit(solution)/shard_map/ppermute | solution.py:431
  175.7 55.3 %collective-permute-start.21 = (bf16[288,1536]{1,0:T(8,128)(2,1)}, bf16[288,1536]{1,0:T(8,128)(2,1)}, u32[]{:S(2)}, u32[]{:S(2)}) collective-permute-start(bf16[288,1536]{1,0:T(8,128)(2,1)} %constant_dynamic-update-slice_fusion.og_even), channel_id=1, source_target_pairs={{0,4},{4,0},{8,12},{12,8},{16,20},{20,16},{24,28},{28,24},{1,5},{5... | collective-permute-start | bytes 2654216 | tf_op jit(solution)/shard_map/ppermute | solution.py:431
  231.1 26.5 %all-to-all-start = ((bf16[4,288,384]{2,1,0:T(8,128)(2,1)}), bf16[4,288,384]{2,1,0:T(8,128)(2,1)S(1)}, u32[]{:S(2)}, u32[]{:S(2)}) async-start(bf16[4,288,384]{2,1,0:T(8,128)(2,1)} %bitcast.242), calls=%async_computation | async-start | bytes 1769472 | tf_op jit(solution)/shard_map/all_to_all | solution.py:777
  234.6 163.1 %all-gather.8.cloned.1.call-start = ((), (), s32[]{:S(2)}) async-start(), calls=%async_computation.11 | async-start | bytes 4915200 | tf_op jit(solution)/shard_map/all_gather | solution.py:787
  279.1 24.3 %collective-permute-start.22 = (bf16[288,1664]{1,0:T(8,128)(2,1)}, bf16[288,1664]{1,0:T(8,128)(2,1)}, u32[]{:S(2)}, u32[]{:S(2)}) collective-permute-start(bf16[288,1664]{1,0:T(8,128)(2,1)} %concatenate.93.x_even), channel_id=1, source_target_pairs={{0,8},{4,12},{8,0},{12,4},{16,24},{20,28},{24,16},{28,20},{1,9},{5... | collective-permute-start | bytes 2875400 | tf_op jit(solution)/shard_map/ppermute | solution.py:431
  280.5 23.7 %collective-permute-start.23 = (bf16[288,1664]{1,0:T(8,128)(2,1)}, bf16[288,1664]{1,0:T(8,128)(2,1)}, u32[]{:S(2)}, u32[]{:S(2)}) collective-permute-start(bf16[288,1664]{1,0:T(8,128)(2,1)} %concatenate.93.x_even), channel_id=1, source_target_pairs={{0,16},{4,20},{8,24},{12,28},{16,0},{20,4},{24,8},{28,12},{1,17},{... | collective-permute-start | bytes 2875400 | tf_op jit(solution)/shard_map/ppermute | solution.py:431
  304.2 19.7 %collective-permute-start.27 = (bf16[288,1664]{1,0:T(8,128)(2,1)}, bf16[288,1664]{1,0:T(8,128)(2,1)}, u32[]{:S(2)}, u32[]{:S(2)}) collective-permute-start(bf16[288,1664]{1,0:T(8,128)(2,1)} %collective-permute-done.22.x_even), channel_id=1, source_target_pairs={{0,4},{4,0},{8,12},{12,8},{16,20},{20,16},{24,28},{28,24},{1,5},{5... | collective-permute-start | bytes 2875400 | tf_op jit(solution)/shard_map/ppermute | solution.py:431
  306.1 13.7 %collective-permute-start.29 = (bf16[144,1664]{1,0:T(8,128)(2,1)}, bf16[144,1664]{1,0:T(8,128)(2,1)}, u32[]{:S(2)}, u32[]{:S(2)}) collective-permute-start(bf16[144,1664]{1,0:T(8,128)(2,1)} %slice.477), channel_id=1, source_target_pairs={{0,8},{4,12},{8,0},{12,4},{16,24},{20,28},{24,16},{28,20},{1,9},{5... | collective-permute-start | bytes 1437704 | tf_op jit(solution)/shard_map/ppermute | solution.py:431
  308.8 13.3 %collective-permute-start.30 = (bf16[144,1664]{1,0:T(8,128)(2,1)}, bf16[144,1664]{1,0:T(8,128)(2,1)}, u32[]{:S(2)}, u32[]{:S(2)}) collective-permute-start(bf16[144,1664]{1,0:T(8,128)(2,1)} %slice.478), channel_id=1, source_target_pairs={{0,16},{4,20},{8,24},{12,28},{16,0},{20,4},{24,8},{28,12},{1,17},{... | collective-permute-start | bytes 1437704 | tf_op jit(solution)/shard_map/ppermute | solution.py:431
  310.0 429.6 %reduce-scatter.8.cloned.1.call-start = ((), (), s32[]{:S(2)}) async-start(), calls=%async_computation.9 | async-start | bytes 3932160 | tf_op jit(solution)/shard_map/reduce_scatter | solution.py:970
  310.0 64.5 %collective-permute-start.25 = (bf16[288,1664]{1,0:T(8,128)(2,1)}, bf16[288,1664]{1,0:T(8,128)(2,1)}, u32[]{:S(2)}, u32[]{:S(2)}) collective-permute-start(bf16[288,1664]{1,0:T(8,128)(2,1)} %collective-permute-done.23.x_even), channel_id=1, source_target_pairs={{0,4},{4,0},{8,12},{12,8},{16,20},{20,16},{24,28},{28,24},{1,5},{5... | collective-permute-start | bytes 2875400 | tf_op jit(solution)/shard_map/ppermute | solution.py:431
  310.1 58.0 %collective-permute-start.26 = (bf16[288,1664]{1,0:T(8,128)(2,1)}, bf16[288,1664]{1,0:T(8,128)(2,1)}, u32[]{:S(2)}, u32[]{:S(2)}) collective-permute-start(bf16[288,1664]{1,0:T(8,128)(2,1)} %get-tuple-element.129), channel_id=1, source_target_pairs={{0,4},{4,0},{8,12},{12,8},{16,20},{20,16},{24,28},{28,24},{1,5},{5... | collective-permute-start | bytes 2875400 | tf_op jit(solution)/shard_map/ppermute | solution.py:431
  323.9 22.2 %collective-permute-start.31 = (bf16[288,1664]{1,0:T(8,128)(2,1)}, bf16[288,1664]{1,0:T(8,128)(2,1)}, u32[]{:S(2)}, u32[]{:S(2)}) collective-permute-start(bf16[288,1664]{1,0:T(8,128)(2,1)} %constant_dynamic-update-slice_fusion.2.x_even), channel_id=1, source_target_pairs={{0,4},{4,0},{8,12},{12,8},{16,20},{20,16},{24,28},{28,24},{1,5},{5... | collective-permute-start | bytes 2875400 | tf_op jit(solution)/shard_map/ppermute | solution.py:431
  345.5 25.4 %collective-permute-start.28 = (bf16[288,1664]{1,0:T(8,128)(2,1)}, bf16[288,1664]{1,0:T(8,128)(2,1)}, u32[]{:S(2)}, u32[]{:S(2)}) collective-permute-start(bf16[288,1664]{1,0:T(8,128)(2,1)} %get-tuple-element.138), channel_id=1, source_target_pairs={{0,4},{4,0},{8,12},{12,8},{16,20},{20,16},{24,28},{28,24},{1,5},{5... | collective-permute-start | bytes 2875400 | tf_op jit(solution)/shard_map/ppermute | solution.py:431
  397.8 55.4 %collective-permute-start.40 = (bf16[4,768,640]{2,1,0:T(8,128)(2,1)}, bf16[4,768,640]{2,1,0:T(8,128)(2,1)}, u32[]{:S(2)}, u32[]{:S(2)}) collective-permute-start(bf16[4,768,640]{2,1,0:T(8,128)(2,1)} %bitcast.221), channel_id=1, source_target_pairs={{0,4},{4,0},{8,12},{12,8},{16,20},{20,16},{24,28},{28,24},{1,5},{5... | collective-permute-start | bytes 11796488 | tf_op jit(solution)/shard_map/ppermute | solution.py:431
  398.0 13.4 %collective-permute-start.34 = (bf16[144,1664]{1,0:T(8,128)(2,1)}, bf16[144,1664]{1,0:T(8,128)(2,1)S(1)}, u32[]{:S(2)}, u32[]{:S(2)}) collective-permute-start(bf16[144,1664]{1,0:T(8,128)(2,1)} %get-tuple-element.161), channel_id=1, source_target_pairs={{0,8},{4,12},{8,0},{12,4},{16,24},{20,28},{24,16},{28,20},{1,9},{5... | collective-permute-start | bytes 1437704 | tf_op jit(solution)/shard_map/ppermute | solution.py:431
  399.2 13.1 %collective-permute-start.35 = (bf16[144,1664]{1,0:T(8,128)(2,1)}, bf16[144,1664]{1,0:T(8,128)(2,1)S(1)}, u32[]{:S(2)}, u32[]{:S(2)}) collective-permute-start(bf16[144,1664]{1,0:T(8,128)(2,1)} %get-tuple-element.162), channel_id=1, source_target_pairs={{0,16},{4,20},{8,24},{12,28},{16,0},{20,4},{24,8},{28,12},{1,17},{... | collective-permute-start | bytes 1437704 | tf_op jit(solution)/shard_map/ppermute | solution.py:431
  412.4 17.1 %collective-permute-start.39 = (bf16[144,1664]{1,0:T(8,128)(2,1)}, bf16[144,1664]{1,0:T(8,128)(2,1)}, u32[]{:S(2)}, u32[]{:S(2)}) collective-permute-start(bf16[144,1664]{1,0:T(8,128)(2,1)} %get-tuple-element.171), channel_id=1, source_target_pairs={{0,16},{4,20},{8,24},{12,28},{16,0},{20,4},{24,8},{28,12},{1,17},{... | collective-permute-start | bytes 1437704 | tf_op jit(solution)/shard_map/ppermute | solution.py:431
  414.0 15.5 %collective-permute-start.38 = (bf16[144,1664]{1,0:T(8,128)(2,1)}, bf16[144,1664]{1,0:T(8,128)(2,1)}, u32[]{:S(2)}, u32[]{:S(2)}) collective-permute-start(bf16[144,1664]{1,0:T(8,128)(2,1)} %add_convert_fusion), channel_id=1, source_target_pairs={{0,8},{4,12},{8,0},{12,4},{16,24},{20,28},{24,16},{28,20},{1,9},{5... | collective-permute-start | bytes 1437704 | tf_op jit(solution)/shard_map/ppermute | solution.py:431
  416.2 18.8 %collective-permute-start.37 = (bf16[144,1664]{1,0:T(8,128)(2,1)}, bf16[144,1664]{1,0:T(8,128)(2,1)}, u32[]{:S(2)}, u32[]{:S(2)}) collective-permute-start(bf16[144,1664]{1,0:T(8,128)(2,1)} %add_convert_fusion.1), channel_id=1, source_target_pairs={{0,16},{4,20},{8,24},{12,28},{16,0},{20,4},{24,8},{28,12},{1,17},{... | collective-permute-start | bytes 1437704 | tf_op jit(solution)/shard_map/ppermute | solution.py:431
  416.9 19.4 %collective-permute-start.36 = (bf16[144,1664]{1,0:T(8,128)(2,1)}, bf16[144,1664]{1,0:T(8,128)(2,1)}, u32[]{:S(2)}, u32[]{:S(2)}) collective-permute-start(bf16[144,1664]{1,0:T(8,128)(2,1)} %get-tuple-element.165), channel_id=1, source_target_pairs={{0,8},{4,12},{8,0},{12,4},{16,24},{20,28},{24,16},{28,20},{1,9},{5... | collective-permute-start | bytes 1437704 | tf_op jit(solution)/shard_map/ppermute | solution.py:431
  453.2 66.2 %collective-permute-start.45 = (bf16[288,1536]{1,0:T(8,128)(2,1)}, bf16[288,1536]{1,0:T(8,128)(2,1)}, u32[]{:S(2)}, u32[]{:S(2)}) collective-permute-start(bf16[288,1536]{1,0:T(8,128)(2,1)} %get-tuple-element.192), channel_id=1, source_target_pairs={{0,4},{4,0},{8,12},{12,8},{16,20},{20,16},{24,28},{28,24},{1,5},{5... | collective-permute-start | bytes 2654216 | tf_op jit(solution)/shard_map/ppermute | solution.py:431
  454.2 51.9 %all-to-all-start.1 = ((bf16[288,4,384]{2,0,1:T(8,128)(2,1)}), bf16[288,4,384]{2,0,1:T(8,128)(2,1)}, u32[]{:S(2)}, u32[]{:S(2)}) async-start(bf16[288,4,384]{2,0,1:T(8,128)(2,1)} %bitcast.231), calls=%async_computation.1 | async-start | bytes 1769472 | tf_op jit(solution)/shard_map/all_to_all | solution.py:879
  458.5 284.1 %reduce-scatter.6.cloned.1.call-start = ((), (), s32[]{:S(2)}) async-start(), calls=%async_computation.8 | async-start | bytes 3932160 | tf_op jit(solution)/shard_map/reduce_scatter | solution.py:972
  459.9 33.0 %collective-permute-start.75 = (bf16[192,1536]{1,0:T(8,128)(2,1)}, bf16[192,1536]{1,0:T(8,128)(2,1)}, u32[]{:S(2)}, u32[]{:S(2)}) collective-permute-start(bf16[192,1536]{1,0:T(8,128)(2,1)} %convolution_convert_fusion.4), channel_id=1, source_target_pairs={{0,4},{4,0},{8,12},{12,8},{16,20},{20,16},{24,28},{28,24},{1,5},{5... | collective-permute-start | bytes 1769480 | tf_op jit(solution)/shard_map/ppermute | solution.py:431
  490.1 16.8 %collective-permute-start.74 = (bf16[192,1536]{1,0:T(8,128)(2,1)}, bf16[192,1536]{1,0:T(8,128)(2,1)}, u32[]{:S(2)}, u32[]{:S(2)}) collective-permute-start(bf16[192,1536]{1,0:T(8,128)(2,1)} %convolution_convert_fusion.6), channel_id=1, source_target_pairs={{0,4},{4,0},{8,12},{12,8},{16,20},{20,16},{24,28},{28,24},{1,5},{5... | collective-permute-start | bytes 1769480 | tf_op jit(solution)/shard_map/ppermute | solution.py:431
  494.9 13.0 %collective-permute-start.76 = (bf16[96,1536]{1,0:T(8,128)(2,1)}, bf16[96,1536]{1,0:T(8,128)(2,1)}, u32[]{:S(2)}, u32[]{:S(2)}) collective-permute-start(bf16[96,1536]{1,0:T(8,128)(2,1)} %get-tuple-element.319), channel_id=1, source_target_pairs={{0,8},{4,12},{8,0},{12,4},{16,24},{20,28},{24,16},{28,20},{1,9},{5... | collective-permute-start | bytes 884744 | tf_op jit(solution)/shard_map/ppermute | solution.py:431
  497.2 13.3 %collective-permute-start.72 = (bf16[192,1536]{1,0:T(8,128)(2,1)}, bf16[192,1536]{1,0:T(8,128)(2,1)}, u32[]{:S(2)}, u32[]{:S(2)}) collective-permute-start(bf16[192,1536]{1,0:T(8,128)(2,1)} %convolution_convert_fusion.8), channel_id=1, source_target_pairs={{0,4},{4,0},{8,12},{12,8},{16,20},{20,16},{24,28},{28,24},{1,5},{5... | collective-permute-start | bytes 1769480 | tf_op jit(solution)/shard_map/ppermute | solution.py:431
  506.8 16.8 %collective-permute-start.71 = (bf16[192,1536]{1,0:T(8,128)(2,1)S(1)}, bf16[192,1536]{1,0:T(8,128)(2,1)S(1)}, u32[]{:S(2)}, u32[]{:S(2)}) collective-permute-start(bf16[192,1536]{1,0:T(8,128)(2,1)S(1)} %convolution_convert_fusion.10), channel_id=1, source_target_pairs={{0,4},{4,0},{8,12},{12,8},{16,20},{20,16},{24,28},{28,24},{1,5},{5... | collective-permute-start | bytes 1769480 | tf_op jit(solution)/shard_map/ppermute | solution.py:431
  509.4 14.2 %collective-permute-start.80 = (bf16[96,1536]{1,0:T(8,128)(2,1)S(1)}, bf16[96,1536]{1,0:T(8,128)(2,1)S(1)}, u32[]{:S(2)}, u32[]{:S(2)}) collective-permute-start(bf16[96,1536]{1,0:T(8,128)(2,1)S(1)} %get-tuple-element.320), channel_id=1, source_target_pairs={{0,16},{4,20},{8,24},{12,28},{16,0},{20,4},{24,8},{28,12},{1,17},{... | collective-permute-start | bytes 884744 | tf_op jit(solution)/shard_map/ppermute | solution.py:431
  519.4 15.2 %collective-permute-start.73 = (bf16[96,1536]{1,0:T(8,128)(2,1)S(1)}, bf16[96,1536]{1,0:T(8,128)(2,1)S(1)}, u32[]{:S(2)}, u32[]{:S(2)}) collective-permute-start(bf16[96,1536]{1,0:T(8,128)(2,1)S(1)} %get-tuple-element.317), channel_id=1, source_target_pairs={{0,8},{4,12},{8,0},{12,4},{16,24},{20,28},{24,16},{28,20},{1,9},{5... | collective-permute-start | bytes 884744 | tf_op jit(solution)/shard_map/ppermute | solution.py:431
  523.6 68.1 %collective-permute-start.44 = (bf16[288,1536]{1,0:T(8,128)(2,1)}, bf16[288,1536]{1,0:T(8,128)(2,1)}, u32[]{:S(2)}, u32[]{:S(2)}) collective-permute-start(bf16[288,1536]{1,0:T(8,128)(2,1)} %get-tuple-element.190), channel_id=1, source_target_pairs={{0,4},{4,0},{8,12},{12,8},{16,20},{20,16},{24,28},{28,24},{1,5},{5... | collective-permute-start | bytes 2654216 | tf_op jit(solution)/shard_map/ppermute | solution.py:431
  523.6 71.6 %collective-permute-start.42 = (bf16[288,1536]{1,0:T(8,128)(2,1)}, bf16[288,1536]{1,0:T(8,128)(2,1)}, u32[]{:S(2)}, u32[]{:S(2)}) collective-permute-start(bf16[288,1536]{1,0:T(8,128)(2,1)} %get-tuple-element.188), channel_id=1, source_target_pairs={{0,4},{4,0},{8,12},{12,8},{16,20},{20,16},{24,28},{28,24},{1,5},{5... | collective-permute-start | bytes 2654216 | tf_op jit(solution)/shard_map/ppermute | solution.py:431
  528.2 63.6 %collective-permute-start.46 = (bf16[144,1536]{1,0:T(8,128)(2,1)}, bf16[144,1536]{1,0:T(8,128)(2,1)}, u32[]{:S(2)}, u32[]{:S(2)}) collective-permute-start(bf16[144,1536]{1,0:T(8,128)(2,1)} %get-tuple-element.312), channel_id=1, source_target_pairs={{0,8},{4,12},{8,0},{12,4},{16,24},{20,28},{24,16},{28,20},{1,9},{5... | collective-permute-start | bytes 1327112 | tf_op jit(solution)/shard_map/ppermute | solution.py:431
  529.2 66.1 %collective-permute-start.48 = (bf16[144,1536]{1,0:T(8,128)(2,1)}, bf16[144,1536]{1,0:T(8,128)(2,1)}, u32[]{:S(2)}, u32[]{:S(2)}) collective-permute-start(bf16[144,1536]{1,0:T(8,128)(2,1)} %get-tuple-element.313), channel_id=1, source_target_pairs={{0,16},{4,20},{8,24},{12,28},{16,0},{20,4},{24,8},{28,12},{1,17},{... | collective-permute-start | bytes 1327112 | tf_op jit(solution)/shard_map/ppermute | solution.py:431
  536.6 68.4 %collective-permute-start.83 = (bf16[192,384]{1,0:T(8,128)(2,1)}, bf16[192,384]{1,0:T(8,128)(2,1)}, u32[]{:S(2)}, u32[]{:S(2)}) collective-permute-start(bf16[192,384]{1,0:T(8,128)(2,1)} %get-tuple-element.333), channel_id=1, source_target_pairs={{0,3},{1,0},{2,1},{3,2},{4,7},{5,4},{6,5},{7,6},{8,11},{9,8},{10,9... | collective-permute-start | bytes 442376 | tf_op jit(solution)/shard_map/ppermute | solution.py:552
  582.0 88.4 %all-to-all-start.2 = ((bf16[4,288,384]{2,1,0:T(8,128)(2,1)}), bf16[4,288,384]{2,1,0:T(8,128)(2,1)S(1)}, u32[]{:S(2)}, u32[]{:S(2)}) async-start(bf16[4,288,384]{2,1,0:T(8,128)(2,1)} %copy.157), calls=%async_computation.2 | async-start | bytes 1769472 | tf_op jit(solution)/shard_map/all_to_all | solution.py:921
  585.5 158.2 %reduce-scatter.4.cloned.1.call-start = ((), (), s32[]{:S(2)}) async-start(), calls=%async_computation.7 | async-start | bytes 3932160 | tf_op jit(solution)/shard_map/reduce_scatter | solution.py:972
  598.4 41.4 %collective-permute-start.82 = (bf16[192,384]{1,0:T(8,128)(2,1)S(1)}, bf16[192,384]{1,0:T(8,128)(2,1)S(1)}, u32[]{:S(2)}, u32[]{:S(2)}) collective-permute-start(bf16[192,384]{1,0:T(8,128)(2,1)S(1)} %copy-done.41), channel_id=1, source_target_pairs={{0,2},{1,3},{2,0},{3,1},{4,6},{5,7},{6,4},{7,5},{8,10},{9,11},{10,... | collective-permute-start | bytes 442376 | tf_op jit(solution)/shard_map/ppermute | solution.py:552
  601.2 38.6 %collective-permute-start.81 = (bf16[192,384]{1,0:T(8,128)(2,1)S(1)}, bf16[192,384]{1,0:T(8,128)(2,1)S(1)}, u32[]{:S(2)}, u32[]{:S(2)}) collective-permute-start(bf16[192,384]{1,0:T(8,128)(2,1)S(1)} %copy-done.40), channel_id=1, source_target_pairs={{0,1},{1,2},{2,3},{3,0},{4,5},{5,6},{6,7},{7,4},{8,9},{9,10},{10,1... | collective-permute-start | bytes 442376 | tf_op jit(solution)/shard_map/ppermute | solution.py:552
  603.1 39.5 %collective-permute-start.51 = (bf16[128,256]{1,0:T(8,128)(2,1)S(1)}, bf16[128,256]{1,0:T(8,128)(2,1)S(1)}, u32[]{:S(2)}, u32[]{:S(2)}) collective-permute-start(bf16[128,256]{1,0:T(8,128)(2,1)S(1)} %get-tuple-element.345), channel_id=1, source_target_pairs={{0,4},{4,0},{8,12},{12,8},{16,20},{20,16},{24,28},{28,24},{1,5},{5... | collective-permute-start | bytes 196616 | tf_op jit(solution)/shard_map/ppermute | solution.py:431
  603.2 39.5 %collective-permute-start.57 = (bf16[64,256]{1,0:T(8,128)(2,1)S(1)}, bf16[64,256]{1,0:T(8,128)(2,1)S(1)}, u32[]{:S(2)}, u32[]{:S(2)}) collective-permute-start(bf16[64,256]{1,0:T(8,128)(2,1)S(1)} %get-tuple-element.344), channel_id=1, source_target_pairs={{0,16},{4,20},{8,24},{12,28},{16,0},{20,4},{24,8},{28,12},{1,17},{... | collective-permute-start | bytes 98312 | tf_op jit(solution)/shard_map/ppermute | solution.py:431
  605.0 39.7 %collective-permute-start.53 = (bf16[64,256]{1,0:T(8,128)(2,1)S(1)}, bf16[64,256]{1,0:T(8,128)(2,1)S(1)}, u32[]{:S(2)}, u32[]{:S(2)}) collective-permute-start(bf16[64,256]{1,0:T(8,128)(2,1)S(1)} %get-tuple-element.337), channel_id=1, source_target_pairs={{0,8},{4,12},{8,0},{12,4},{16,24},{20,28},{24,16},{28,20},{1,9},{5... | collective-permute-start | bytes 98312 | tf_op jit(solution)/shard_map/ppermute | solution.py:431
  642.6 13.4 %collective-permute-start.47 = (bf16[144,1536]{1,0:T(8,128)(2,1)}, bf16[144,1536]{1,0:T(8,128)(2,1)}, u32[]{:S(2)}, u32[]{:S(2)}) collective-permute-start(bf16[144,1536]{1,0:T(8,128)(2,1)} %get-tuple-element.310), channel_id=1, source_target_pairs={{0,16},{4,20},{8,24},{12,28},{16,0},{20,4},{24,8},{28,12},{1,17},{... | collective-permute-start | bytes 1327112 | tf_op jit(solution)/shard_map/ppermute | solution.py:431
  644.7 13.4 %collective-permute-start.43 = (bf16[144,1536]{1,0:T(8,128)(2,1)}, bf16[144,1536]{1,0:T(8,128)(2,1)}, u32[]{:S(2)}, u32[]{:S(2)}) collective-permute-start(bf16[144,1536]{1,0:T(8,128)(2,1)} %get-tuple-element.308), channel_id=1, source_target_pairs={{0,8},{4,12},{8,0},{12,4},{16,24},{20,28},{24,16},{28,20},{1,9},{5... | collective-permute-start | bytes 1327112 | tf_op jit(solution)/shard_map/ppermute | solution.py:431
  646.6 18.6 %collective-permute-start.50 = (bf16[144,1536]{1,0:T(8,128)(2,1)}, bf16[144,1536]{1,0:T(8,128)(2,1)}, u32[]{:S(2)}, u32[]{:S(2)}) collective-permute-start(bf16[144,1536]{1,0:T(8,128)(2,1)} %get-tuple-element.311), channel_id=1, source_target_pairs={{0,16},{4,20},{8,24},{12,28},{16,0},{20,4},{24,8},{28,12},{1,17},{... | collective-permute-start | bytes 1327112 | tf_op jit(solution)/shard_map/ppermute | solution.py:431
  646.7 20.2 %collective-permute-start.49 = (bf16[144,1536]{1,0:T(8,128)(2,1)}, bf16[144,1536]{1,0:T(8,128)(2,1)}, u32[]{:S(2)}, u32[]{:S(2)}) collective-permute-start(bf16[144,1536]{1,0:T(8,128)(2,1)} %get-tuple-element.309), channel_id=1, source_target_pairs={{0,8},{4,12},{8,0},{12,4},{16,24},{20,28},{24,16},{28,20},{1,9},{5... | collective-permute-start | bytes 1327112 | tf_op jit(solution)/shard_map/ppermute | solution.py:431
  674.0 47.6 %all-to-all-start.3 = ((bf16[4,288,256]{2,1,0:T(8,128)(2,1)}), bf16[4,288,256]{2,1,0:T(8,128)(2,1)}, u32[]{:S(2)}, u32[]{:S(2)}) async-start(bf16[4,288,256]{2,1,0:T(8,128)(2,1)} %bitcast.34), calls=%async_computation.3 | async-start | bytes 1179648 | tf_op jit(solution)/shard_map/all_to_all | solution.py:923
  (82 other events, 917.5 us)
Sparse Core Ops, SparseCore 0:
  21.6 73.0 all-gather.5
Sparse Core Ops, SparseCore 1:
  310.0 74.4 all-gather.7
  442.4 72.6 reduce-scatter.7
  517.3 66.7 reduce-scatter.5
  590.7 70.1 reduce-scatter.3

commit v5 on v4

--- a/solution.py
+++ b/solution.py
@@ -435,23 +435,24 @@
     return [1 << k for k in range(number.bit_length()) if number >> k & 1]
 
 
+def even_blocks(count):
+    even = sorted(range(2, count, 2), key=lambda j: (len(bits_of(j)), j))
+    singles = [j for j in even if len(bits_of(j)) == 1]
+    return singles, even[len(singles) :]
+
+
 def gather_blocks(own, axis_name, after_first=None):
     count = lax.axis_size(axis_name)
-    half = own.shape[0] // 2
+    singles, several = even_blocks(count)
     blocks = {0: own, 1: exchange(own, axis_name, 1)}
-    even = sorted(range(2, count, 2), key=lambda j: (len(bits_of(j)), j))
-    singles = [j for j in even if len(bits_of(j)) == 1]
     for j in singles:
         blocks[j] = exchange(own, axis_name, j)
     if after_first is not None:
         blocks.update(zip(singles, after_first([blocks[j] for j in singles])))
-    for j in even:
-        bits = bits_of(j)
-        if len(bits) > 1:
-            low_bit, high_bit = bits[0], bits[-1]
-            top = exchange(blocks[j ^ low_bit][:half], axis_name, low_bit)
-            bottom = exchange(blocks[j ^ high_bit][half:], axis_name, high_bit)
-            blocks[j] = jnp.concatenate([top, bottom], axis=0)
+    for j in several:
+        low_bit = bits_of(j)[0]
+        blocks[j] = exchange(blocks[j ^ low_bit], axis_name, low_bit)
+    for j in singles + several:
         blocks[j + 1] = exchange(blocks[j], axis_name, 1)
     return [blocks[j] for j in range(count)]
 
@@ -465,67 +466,71 @@
     return lax.ppermute(values, axis_name, pairs)
 
 
-def gather_line(own, rising, falling, axis_name):
+def gather_line(owns, axis_name, after_first, after_last):
     count = lax.axis_size(axis_name)
     index = lax.axis_index(axis_name)
-    rows = own.shape[0]
-    buffer = jnp.zeros(((count + 1) * rows, own.shape[1]), own.dtype)
-    buffer = lax.dynamic_update_slice_in_dim(buffer, own, index * rows, axis=0)
+    rising, falling = list(owns), list(owns)
+    arrived = []
     for step in range(1, count):
-        if step > 1:
-            rising = pass_on(rising, axis_name, step, 1)
-            falling = pass_on(falling, axis_name, step, -1)
-        slot = jnp.where(index >= step, index - step, count)
-        buffer = lax.dynamic_update_slice_in_dim(buffer, rising, slot * rows, axis=0)
-        slot = jnp.where(index + step < count, index + step, count)
-        buffer = lax.dynamic_update_slice_in_dim(buffer, falling, slot * rows, axis=0)
-    return buffer[: count * rows]
+        rising = [pass_on(own, axis_name, step, 1) for own in rising]
+        falling = [pass_on(own, axis_name, step, -1) for own in falling]
+        if step == 1:
+            rising, falling = after_first((rising, falling))
+        if step == count - 1:
+            rising, falling = after_last((rising, falling))
+        arrived.append((rising, falling))
+    results = []
+    for k, own in enumerate(owns):
+        rows = own.shape[0]
+        buffer = jnp.zeros(((count + 1) * rows, own.shape[1]), own.dtype)
+        buffer = lax.dynamic_update_slice_in_dim(buffer, own, index * rows, axis=0)
+        for step, (rising, falling) in enumerate(arrived, 1):
+            slot = jnp.where(index >= step, index - step, count)
+            buffer = lax.dynamic_update_slice_in_dim(buffer, rising[k], slot * rows, axis=0)
+            slot = jnp.where(index + step < count, index + step, count)
+            buffer = lax.dynamic_update_slice_in_dim(buffer, falling[k], slot * rows, axis=0)
+        results.append(buffer[: count * rows])
+    return results
 
 
 def add_rounded(left_side, right_side):
     return (left_side.astype(jnp.float32) + right_side.astype(jnp.float32)).astype(jnp.bfloat16)
 
 
-def fold(even, odd, axis_name):
-    arrived = exchange(odd, axis_name, 1)
-    half = even.shape[0] // 2
-    return [add_rounded(even[:half], arrived[:half]), add_rounded(even[half:], arrived[half:])]
-
-
-def reduce_blocks(blocks, axis_name):
-    count = len(blocks)
-    sums = {}
-    for j in sorted(range(0, count, 2), key=lambda j: (-len(bits_of(j)), j)):
-        sums[j] = fold(blocks[j], blocks[j + 1], axis_name)
-    return reduce_singles(sums, reduce_several(sums, axis_name), axis_name)
-
-
 def reduce_several(sums, axis_name):
-    sums = {j: list(halves) for j, halves in sums.items()}
+    sums = dict(sums)
     pending = []
     for j in sorted((j for j in sums if len(bits_of(j)) > 1), key=lambda j: (-len(bits_of(j)), j)):
-        low_bit, high_bit = bits_of(j)[0], bits_of(j)[-1]
-        for part, bit in ((0, low_bit), (1, high_bit)):
-            piece = exchange(sums[j][part], axis_name, bit)
-            if len(bits_of(j ^ bit)) > 1:
-                sums[j ^ bit][part] = add_rounded(sums[j ^ bit][part], piece)
-            else:
-                pending.append((j ^ bit, part, piece))
+        bit = bits_of(j)[-1]
+        piece = exchange(sums[j], axis_name, bit)
+        if len(bits_of(j ^ bit)) > 1:
+            sums[j ^ bit] = add_rounded(sums[j ^ bit], piece)
+        else:
+            pending.append((j ^ bit, piece))
     return pending
 
 
 def reduce_singles(sums, pending, axis_name):
-    sums = {j: list(halves) for j, halves in sums.items()}
-    for j, part, piece in pending:
-        sums[j][part] = add_rounded(sums[j][part], piece)
-    halves = []
-    for part in range(2):
-        total = sums[0][part].astype(jnp.float32)
-        for j in sums:
-            if len(bits_of(j)) == 1:
-                total = total + exchange(sums[j][part], axis_name, j).astype(jnp.float32)
-        halves.append(total)
-    return jnp.concatenate(halves, axis=0)
+    sums = dict(sums)
+    for j, piece in pending:
+        sums[j] = add_rounded(sums[j], piece)
+    return [sums[0]] + [exchange(sums[j], axis_name, j) for j in sums if len(bits_of(j)) == 1]
+
+
+def add_all(pieces):
+    total = pieces[0].astype(jnp.float32)
+    for piece in pieces[1:]:
+        total = total + piece.astype(jnp.float32)
+    return total
+
+
+def reduce_blocks(blocks, axis_name):
+    singles, several = even_blocks(len(blocks))
+    sums = {
+        j: add_rounded(blocks[j], exchange(blocks[j + 1], axis_name, 1))
+        for j in several[::-1] + singles + [0]
+    }
+    return add_all(reduce_singles(sums, reduce_several(sums, axis_name), axis_name))
 
 
 def in_order(blocks, index):
@@ -729,26 +734,40 @@
     query_width = w_query.shape[1]
     key_width = key_projection.shape[1]
 
-    line = [pass_on(tokens, "seq", 1, 1), pass_on(tokens, "seq", 1, -1)]
-    small = jnp.concatenate([w_router, gain_attn[:, None], gain_ffn[:, None]], axis=1)
-    small = lax.all_gather(small, ("shard", "seq"), axis=0, tiled=True)
+    singles, several = even_blocks(shard_count)
+    own_weight = jnp.concatenate([w_query, key_projection, value_projection], axis=1)
+    held = {}
+
+    def after_first(line):
+        small = jnp.concatenate([w_router, gain_attn[:, None], gain_ffn[:, None]], axis=1)
+        small = lax.all_gather(small, "seq", axis=0, tiled=True)
+        small = lax.all_gather(small, "shard", axis=0, tiled=True)
+
+        def tie(blocks):
+            blocks, held["line"], held["small"] = lax.optimization_barrier((blocks, line, small))
+            return blocks
+
+        blocks = gather_blocks(own_weight, "shard", tie)
+        late = lax.optimization_barrier(([blocks[k] for k in several], out_grad))[1]
+        held["weights"] = blocks
+        held["grads"] = gather_blocks(late, "shard")
+        return held["line"]
+
+    def after_last(line):
+        near = [held["grads"][k] for k in singles]
+        line, near = lax.optimization_barrier((line, near))
+        for k, block in zip(singles, near):
+            held["grads"][k] = block
+        return line
+
+    block_tokens, out_weight = gather_line([tokens, w_out], "seq", after_first, after_last)
+    out_weight = lax.all_gather(out_weight, "shard", axis=1, tiled=True)
+    small = held["small"]
     router_weight = small[:, :experts_all]
     first_gain = small[:, experts_all].astype(jnp.float32)
     second_gain = small[:, experts_all + 1].astype(jnp.float32)
-    own_weight = jnp.concatenate([w_query, key_projection, value_projection], axis=1)
-
-    def after_tokens(blocks):
-        blocks, line[:] = lax.optimization_barrier((blocks, line))
-        return blocks
-
-    qkv_weight = in_order(gather_blocks(own_weight, "shard", after_tokens), shard_index)
-    block_tokens = gather_line(tokens, line[0], line[1], "seq")
-    qkv_weight = qkv_weight.reshape(model_width, -1)
-    out_weight = lax.all_gather(w_out, ("shard", "seq"), axis=0, tiled=False)
-    out_weight = out_weight.reshape(shard_count, seq_count, *w_out.shape)
-    out_weight = out_weight.transpose(1, 2, 0, 3).reshape(model_width, model_width)
-    out_grad_late, qkv_weight = lax.optimization_barrier((out_grad, qkv_weight))
-    grad_blocks = gather_blocks(out_grad_late, "shard")
+    qkv_weight = in_order(held["weights"], shard_index).reshape(model_width, -1)
+    grad_blocks = held["grads"]
 
     block_rows = jnp.arange(block_len, dtype=jnp.int32)
     cos_table, sin_table = rotary_tables(
@@ -769,10 +788,13 @@
     kv_own = jnp.concatenate([to_lanes(key_heads), to_lanes(value_heads)], axis=1)
     kv_prompt = lax.all_gather(kv_own[:PROMPT_BLK], "shard", axis=0, tiled=True)
     block_number = shard_index.astype(jnp.int32).reshape(1)
-    singles = [1 << k for k in range(1, (shard_count - 1).bit_length())]
-    queries, grad_blocks[::2] = lax.optimization_barrier((queries, grad_blocks[::2]))
     mixed_own, levels = attend_forward(block_number, queries, kv_prompt, kv_own, group, kv_heads)
-    mixed_own, grad_blocks = lax.optimization_barrier((mixed_own, grad_blocks))
+    sooner = [j for j in range(1, shard_count) if j - 1 not in several]
+    mixed_own, held_blocks = lax.optimization_barrier((mixed_own, [grad_blocks[j] for j in sooner]))
+    for j, block in zip(sooner, held_blocks):
+        grad_blocks[j] = block
+    for j in several:
+        grad_blocks[j + 1] = exchange(grad_blocks[j], "shard", 1)
     mixed_heads = mixed_own[:, :query_width]
     mixed_tokens = lax.all_to_all(mixed_heads, "seq", split_axis=0, concat_axis=1, tiled=True)
 
@@ -810,13 +832,10 @@
     row_blocks = {0: coded, 1: exchange(coded, "shard", 1)}
     for bit in singles:
         row_blocks[bit] = exchange(coded, "shard", bit)
-    several = sorted(
-        (j for j in range(0, shard_count, 2) if len(bits_of(j)) > 1),
-        key=lambda j: (len(bits_of(j)), j),
-    )
     order = [0] + singles[:-1] + several + singles[-1:]
     first_expert = (shard_index * local_experts).astype(jnp.int32).reshape(1)
     carried = None
+    pending = []
     row_sums = {}
     out_parts = [None] * shard_count
     for position, j in enumerate(order):
@@ -834,29 +853,33 @@
             (w_gate, w_up, w_down),
             carried,
         )
-        pieces = list(pieces)
-        if j == 0:
-            arrived, pieces[2] = lax.optimization_barrier(
-                ([row_blocks[bit] for bit in singles], pieces[2])
+        if position == 0:
+            arrived, pieces = lax.optimization_barrier(
+                ([row_blocks[bit] for bit in singles], pieces)
             )
             row_blocks.update(zip(singles, arrived))
-            half = tok_count // 2
-            for k in singles + several:
-                if k in several:
-                    low_bit, high_bit = bits_of(k)[0], bits_of(k)[-1]
-                    top = exchange(row_blocks[k ^ low_bit][:half], "shard", low_bit)
-                    bottom = exchange(row_blocks[k ^ high_bit][half:], "shard", high_bit)
-                    row_blocks[k] = jnp.concatenate([top, bottom], axis=0)
+            for bit in singles:
+                row_blocks[bit + 1] = exchange(row_blocks[bit], "shard", 1)
+            for k in several:
+                low_bit = bits_of(k)[0]
+                row_blocks[k] = exchange(row_blocks[k ^ low_bit], "shard", low_bit)
+        elif position == 1:
+            arrived, pieces = lax.optimization_barrier(([row_blocks[k] for k in several], pieces))
+            row_blocks.update(zip(several, arrived))
+            for k in several:
                 row_blocks[k + 1] = exchange(row_blocks[k], "shard", 1)
-        row_sums[j] = fold(pieces[0], pieces[1], "shard")
+        elif j == order[-1]:
+            arrived, pieces = lax.optimization_barrier(([piece for _, piece in pending], pieces))
+            pending = [(k, piece) for (k, _), piece in zip(pending, arrived)]
+        row_sums[j] = add_rounded(pieces[0], exchange(pieces[1], "shard", 1))
         out_parts[j], out_parts[j + 1] = pieces[2], pieces[3]
     all_rows, all_grads, all_pre, all_hidden = carried
-    arrived = [piece for _, _, piece in pending]
-    row_sums, all_grads, arrived = lax.optimization_barrier((row_sums, all_grads, arrived))
-    pending = [(j, part, piece) for (j, part, _), piece in zip(pending, arrived)]
+    row_sums, all_grads = lax.optimization_barrier((row_sums, all_grads))
     down_sum = transposed_times(all_grads, all_hidden).astype(bf16)
-    row_total = reduce_singles(row_sums, pending, "shard")
-    row_total, down_sum = lax.optimization_barrier((row_total, down_sum))
+    grad_down = lax.psum_scatter(down_sum, "seq", scatter_dimension=0, tiled=True)
+    row_pieces = reduce_singles(row_sums, pending, "shard")
+    row_pieces, down_sum = lax.optimization_barrier((row_pieces, down_sum))
+    row_total = add_all(row_pieces)
     row_grad = row_total[:, :model_width]
     gate_grad_dense = (
         row_total[:, model_width : model_width + experts_all]
@@ -877,10 +900,17 @@
         (mixed_grad_tokens, out_parts, all_rows, other_half, mixed_tokens)
     )
     mixed_grad = lax.all_to_all(mixed_grad_tokens, "seq", split_axis=1, concat_axis=0, tiled=True)
-    pre_sums = [transposed_times(all_rows, all_pre[e]).astype(bf16) for e in range(local_experts)]
-    mixed_grad, pre_sums = lax.optimization_barrier((mixed_grad, pre_sums))
-    expert_sum = reduce_blocks(out_parts, "shard")
-    output = (residual + expert_sum).astype(bf16)
+    odd = [exchange(out_parts[j + 1], "shard", 1) for j in order]
+    pre_sums = [transposed_times(all_rows, all_pre[0]).astype(bf16)]
+    odd, pre_sums[0], all_rows = lax.optimization_barrier((odd, pre_sums[0], all_rows))
+    out_sums = {j: add_rounded(out_parts[j], piece) for j, piece in zip(order, odd)}
+    out_pending = reduce_several(out_sums, "shard")
+    pre_sums += [
+        transposed_times(all_rows, all_pre[e]).astype(bf16) for e in range(1, local_experts)
+    ]
+    arrived, pre_sums = lax.optimization_barrier(([piece for _, piece in out_pending], pre_sums))
+    out_pending = [(j, piece) for (j, _), piece in zip(out_pending, arrived)]
+    out_pieces = reduce_singles(out_sums, out_pending, "shard")
     columns = [
         lax.dynamic_slice_in_dim(
             residual_low,
@@ -891,9 +921,11 @@
         for j in range(shard_count)
     ]
     whole_out = [transposed_times(part, mixed_late).astype(bf16) for part in columns]
-    grad_out = reduce_blocks(whole_out, "shard").astype(bf16)
-    grad_out = grad_out.reshape(grad_out.shape[0], seq_count, -1).transpose(1, 0, 2)
-    grad_out = scatter_direct(grad_out, "seq").T
+    first_odd = [exchange(whole_out[j + 1], "shard", 1) for j in order[:2]]
+    mixed_grad, pre_sums, whole_out, first_odd = lax.optimization_barrier(
+        (mixed_grad, pre_sums, whole_out, first_odd)
+    )
+    whole_odd = first_odd + [exchange(whole_out[j + 1], "shard", 1) for j in order[2:]]
 
     query_grad, prompt_grad, self_grad = attend_backward(
         block_number,
@@ -906,6 +938,9 @@
         group,
         kv_heads,
     )
+    query_grad, prompt_grad, self_grad, out_pieces, whole_odd = lax.optimization_barrier(
+        (query_grad, prompt_grad, self_grad, out_pieces, whole_odd)
+    )
     query_grad = query_grad[:, :query_width]
     own_prompt = reduce_blocks(relative_blocks(prompt_grad, shard_index, shard_count), "shard")
     key_grad = jnp.concatenate(
@@ -921,6 +956,16 @@
     query_tokens = lax.all_to_all(lin_query, "seq", split_axis=0, concat_axis=1, tiled=True)
     lin_both, query_tokens = lax.optimization_barrier((lin_both, query_tokens))
     both_tokens = lax.all_to_all(lin_both, "seq", split_axis=0, concat_axis=1, tiled=True)
+    whole_sums = {j: add_rounded(whole_out[j], piece) for j, piece in zip(order, whole_odd)}
+    grad_out = add_all(
+        reduce_singles(whole_sums, reduce_several(whole_sums, "shard"), "shard")
+    ).astype(bf16)
+    grad_out, output_sum, both_tokens = lax.optimization_barrier(
+        (grad_out, add_all(out_pieces), both_tokens)
+    )
+    output = (residual + output_sum).astype(bf16)
+    grad_out = grad_out.reshape(grad_out.shape[0], seq_count, -1).transpose(1, 0, 2)
+    grad_out = scatter_direct(grad_out, "seq").T
     parts = [0.0, 0.0]
     for lin, first, last in (
         (query_tokens, 0, query_width),
@@ -967,7 +1012,6 @@
     own_factor = rms_parts(own_inputs)
     input_part, _ = rms_backward(own_inputs, own_factor, first_gain, normed_grad)
     tokens_grad = residual_grad + input_part
-    grad_down = lax.psum_scatter(down_sum, "seq", scatter_dimension=0, tiled=True)
     pre_grads = [
         lax.psum_scatter(part, "seq", scatter_dimension=0, tiled=True) for part in pre_sums
     ]

time: 765 us -> 680 us (0.89)
  waiting for transfers between devices: 163 us -> 107 us
  blocking collectives: 81.8 us -> 42.3 us
  matrix products: 94.8 us -> 112 us
  starting transfers between devices: 90 us -> 78.7 us
    all_gather x1 -> x2, blocking collectives: 71.4 us -> 23.4 us  [the longest x1 14.2 us: after_first(): small = lax.all_gather(small, 'seq', axis=0, tiled=True)]
    ppermute x6, waiting for transfers between devices: 33.1 us -> 0.02 us  [scatter_direct(): lax.ppermute(piece, axis_name, [(i, (i + step) % count) for i in range(co...]
    ppermute x75 -> x57, waiting for transfers between devices: 76.4 us -> 47.3 us  [exchange(): return lax.ppermute(values, axis_name, [(i, i ^ bit) for i in range(count)])]
    ppermute x75 -> x57, starting transfers between devices: 48.2 us -> 31.3 us  [exchange(): return lax.ppermute(values, axis_name, [(i, i ^ bit) for i in range(count)])]
    dot_general x14, matrix products: 58 us -> 73.8 us  [transposed_times(): lax.dot_general(left_side, right_side, (((0,), (0,)), ((), ())), precisio...]
    reshape x2 -> x1, local copies, waits for them, and re-layouts: 12.1 us -> 1.59 us  [on_device(): grad_out.reshape(grad_out.shape[0], seq_count, -1).transpose(1, 0, 2)]
    ppermute x6 -> x12, starting transfers between devices: 10.6 us -> 20.2 us  [pass_on(): return lax.ppermute(values, axis_name, pairs)]
    all_to_all x1, waiting for transfers between devices: 8.73 us -> 0.01 us  [on_device(): lax.all_to_all(mixed_grad_tokens, 'seq', split_axis=1, concat_axis=0, til...]
  transfers between devices with their start and end apart: 96 -> 84, of which waited for: 30 -> 20; matrix products, arithmetic and copies ran while one was open for 30% -> 38% of each run, Pallas kernels for 19% -> 22%
where the time goes in v5:
time: 680 us; the launch traced here: 668 us
  Pallas kernels  147 us (22%)
  matrix products  112 us (16%)
  waiting for transfers between devices  107 us (16%)
  local copies, waits for them, and re-layouts  96.7 us (14%)
  starting transfers between devices  78.7 us (12%)
  other arithmetic  68.1 us (10%)
  blocking collectives  42.3 us (6%)
  between operations  17.6 us (3%)
    pallas_call x4, Pallas kernels, expert_pair(): pl.pallas_call(partial(expert_body, experts_all), out_shape=out_shape, gr...  86.8 us
    dot_general x14, matrix products, transposed_times(): lax.dot_general(left_side, right_side, (((0,), (0,)), ((), ())), precisio...  73.8 us
    ppermute x57, waiting for transfers between devices, exchange(): return lax.ppermute(values, axis_name, [(i, i ^ bit) for i in range(count)])  47.3 us
    unnamed x173, local copies, waits for them, and re-layouts  39 us
    pallas_call x1, Pallas kernels, attend_backward(): pl.pallas_call(partial(attend_backward_body, group, kv_heads), out_shape=...  34.9 us
    ppermute x12, waiting for transfers between devices, pass_on(): return lax.ppermute(values, axis_name, pairs)  32.8 us
    ppermute x57, starting transfers between devices, exchange(): return lax.ppermute(values, axis_name, [(i, i ^ bit) for i in range(count)])  31.3 us
    convert_element_type x16, other arithmetic, add_rounded(): (left_side.astype(jnp.float32) + right_side.astype(jnp.float32)).astype(j...  30.5 us
  transfers between devices with their start and end apart: 84, of which 20 were waited for; matrix products, arithmetic and copies ran while one was open for 38% of the time, Pallas kernels for 22%

profile of v5, /device:TPU:0, one launch (start us, length us, event | category | flops | bytes accessed | tf_op | source)
XLA Modules:
  0.0 668.2 jit_solution(13743317467711046657)
XLA Ops:
  8.1 5.0 collective-permute-start.3
  14.4 4.6 collective-permute-start.4
  26.8 2.4 broadcast_in_dim.22
  30.1 5.3 collective-permute-done.4
  36.9 14.2 %all-gather.1 = bf16[4,48,18]{1,2,0:T(8,128)(2,1)S(1)} all-gather(bf16[1,48,18]{1,2,0:T(8,128)(2,1)S(1)} %maximum_bitcast_fusion), channel_id=1, replica_groups=mesh['shard'=8,'seq'=4] {'seq'}, dimensions={0}, use_global_device_ids=true | all-gather | bytes 8640 | tf_op jit(solution)/shard_map/all_gather | solution.py:743
  51.9 9.2 %all-gather.2 = bf16[8,192,18]{1,2,0:T(8,128)(2,1)S(1)} all-gather(bf16[1,192,18]{1,2,0:T(8,128)(2,1)S(1)} %reshape.268), channel_id=1, replica_groups=mesh['shard'=8,'seq'=4] {'shard'}, dimensions={0}, use_global_device_ids=true | all-gather | bytes 62208 | tf_op jit(solution)/shard_map/all_gather | solution.py:744
  76.2 3.1 collective-permute-done.9
  82.1 8.2 %collective-permute-done.12 = bf16[288,1536]{1,0:T(8,128)(2,1)} collective-permute-done((bf16[288,1536]{1,0:T(8,128)(2,1)}, bf16[288,1536]{1,0:T(8,128)(2,1)}, u32[]{:S(2)}, u32[]{:S(2)}) %collective-permute-start.12) | collective-permute-done | bytes 884768 | tf_op jit(solution)/shard_map/ppermute | solution.py:466
  98.2 18.1 %collective-permute-done.18 = bf16[384,192]{0,1:T(8,128)(2,1)S(1)} collective-permute-done((bf16[384,192]{0,1:T(8,128)(2,1)S(1)}, bf16[384,192]{0,1:T(8,128)(2,1)S(1)}, u32[]{:S(2)}, u32[]{:S(2)}) %collective-permute-start.18) | collective-permute-done | bytes 147488 | tf_op jit(solution)/shard_map/ppermute | solution.py:466
  137.8 3.0 copy.177
  140.9 2.9 constant_dynamic-update-slice_fusion.10
  143.8 2.3 constant_dynamic-update-slice_fusion.9
  149.1 2.8 fusion
  151.9 5.1 fusion.122
  165.6 18.9 %all_gather.20.kp_ref.vp_ref = bf16[1024,256]{1,0:T(8,128)(2,1)} all-gather(bf16[128,256]{1,0:T(8,128)(2,1)S(1)} %fusion.87), channel_id=1, replica_groups=mesh['shard'=8,'seq'=4] {'shard'}, dimensions={0}, use_global_device_ids=true | all-gather | bytes 589824 | tf_op jit(solution)/shard_map/all_gather | solution.py:789
  185.8 25.1 %attend_forward.1 = (bf16[1152,384]{1,0:T(8,128)(2,1)}, f32[6,1,1152]{2,1,0:T(1,128)}) custom-call(s32[1]{0:T(128)} %bitcast.12.index_ref, bf16[1152,384]{1,0:T(8,128)(2,1)} %copy.180.q_ref, bf16[1024,256]{1,0:T(8,128)(2,1)} %all_gather.20.kp_ref.vp_ref, bf16[1024,256]{1,0:T(8,128)(2,1)} %all_gather.20.kp_ref.vp_ref, ...), custom_call_target="tpu_custom_call" | custom-call | flops 9059696640 | bytes 3538944 | tf_op jit(solution)/shard_map/attend_forward/pallas_call | solution.py:366
  210.9 4.6 all-to-all-start
  217.3 21.0 %all-to-all-done = bf16[4,288,384]{2,1,0:T(8,128)(2,1)} async-done(((bf16[4,288,384]{2,1,0:T(8,128)(2,1)}), bf16[4,288,384]{2,1,0:T(8,128)(2,1)}, u32[]{:S(2)}, u32[]{:S(2)}) %all-to-all-start) | async-done | bytes 884768 | tf_op jit(solution)/shard_map/all_to_all | solution.py:799
  239.6 4.0 multiply_reduce_fusion.2
  252.7 21.4 %experts.4 = (bf16[2304,1536]{1,0:T(8,128)(2,1)}, bf16[2304,1536]{1,0:T(8,128)(2,1)}, bf16[2,2304,1024]{2,1,0:T(8,128)(2,1)}, bf16[2304,1024]{1,0:T(8,128)(2,1)}...) custom-call(s32[1]{0:T(128)} %bitcast.19.index_ref, ...), custom_call_target="tpu_custom_call" | custom-call | flops 10871635968 | bytes 27131904 | tf_op jit(solution)/shard_map/experts/pallas_call | solution.py:679
  277.1 22.0 %experts.5 = (bf16[2304,1536]{1,0:T(8,128)(2,1)}, bf16[2304,1536]{1,0:T(8,128)(2,1)}, bf16[2,2304,1024]{2,1,0:T(8,128)(2,1)}, bf16[2304,1024]{1,0:T(8,128)(2,1)}...) custom-call(s32[1]{0:T(128)} %bitcast.19.index_ref, ...), custom_call_target="tpu_custom_call", output_to_operand_aliasing={{0}: (8, {}), {1}: (9, {}), {2}: (10, {}), {3}: (11, {})} | custom-call | flops 10871635968 | bytes 27131904 | tf_op jit(solution)/shard_map/experts/pallas_call | solution.py:679
  300.3 3.0 collective-permute-done.34.og_odd
  303.3 21.6 %experts.6 = (bf16[2304,1536]{1,0:T(8,128)(2,1)}, bf16[2304,1536]{1,0:T(8,128)(2,1)}, bf16[2,2304,1024]{2,1,0:T(8,128)(2,1)}, bf16[2304,1024]{1,0:T(8,128)(2,1)}...) custom-call(s32[1]{0:T(128)} %bitcast.19.index_ref, ...), custom_call_target="tpu_custom_call", output_to_operand_aliasing={{0}: (8, {}), {1}: (9, {}), {2}: (10, {}), {3}: (11, {})} | custom-call | flops 10871635968 | bytes 27131904 | tf_op jit(solution)/shard_map/experts/pallas_call | solution.py:679
  325.2 2.8 add_convert_fusion.4
  328.0 2.4 add_convert_fusion.3
  332.9 21.7 %experts.7 = (bf16[2304,1536]{1,0:T(8,128)(2,1)}, bf16[2304,1536]{1,0:T(8,128)(2,1)}, bf16[2,2304,1024]{2,1,0:T(8,128)(2,1)}, bf16[2304,1024]{1,0:T(8,128)(2,1)}...) custom-call(s32[1]{0:T(128)} %bitcast.19.index_ref, ...), custom_call_target="tpu_custom_call", output_to_operand_aliasing={{0}: (8, {}), {1}: (9, {}), {2}: (10, {}), {3}: (11, {})} | custom-call | flops 10871635968 | bytes 27131904 | tf_op jit(solution)/shard_map/experts/pallas_call | solution.py:679
  356.0 2.4 collective-permute-done.37
  358.4 2.6 add_convert_fusion.1
  361.0 2.4 add_convert_fusion
  365.0 21.7 %convolution_convert_fusion = bf16[1536,1024]{1,0:T(8,128)(2,1)} fusion(bf16[2304,1536]{1,0:T(8,128)(2,1)} %get-tuple-element.215, bf16[2304,1024]{1,0:T(8,128)(2,1)S(1)} %copy-done), kind=kOutput, calls=%fused_computation.13 | convolution fusion | flops 7249330176 | bytes 14942208 | tf_op jit(solution)/shard_map/dot_general | solution.py:71
  392.4 3.0 fusion.124
  397.9 4.2 all-to-all-start.1
  403.3 2.3 convolution_convert_fusion.11
  405.6 2.3 convolution_convert_fusion.10
  412.3 12.7 %fusion.9 = bf16[1536,1024]{1,0:T(8,128)(2,1)} fusion(bf16[2304,1536]{1,0:T(8,128)(2,1)} %get-tuple-element.240, bf16[2,2304,1024]{2,1,0:T(8,128)(2,1)} %get-tuple-element.237), kind=kOutput, calls=%fused_computation.11 | convolution fusion | flops 7249330176 | bytes 14942208 | tf_op jit(solution)/shard_map/dot_general | solution.py:71
  424.9 2.4 convolution_convert_fusion.6
  427.4 2.3 convolution_convert_fusion.5
  429.7 2.3 convolution_convert_fusion.4
  432.5 2.3 add_convert_fusion.10
  435.3 12.7 %fusion.12 = bf16[1536,1024]{1,0:T(8,128)(2,1)} fusion(bf16[2304,1536]{1,0:T(8,128)(2,1)} %get-tuple-element.240, bf16[2,2304,1024]{2,1,0:T(8,128)(2,1)} %get-tuple-element.237), kind=kOutput, calls=%fused_computation.12 | convolution fusion | flops 7249330176 | bytes 14942208 | tf_op jit(solution)/shard_map/dot_general | solution.py:71
  448.0 8.7 %collective-permute-done.45 = bf16[288,1536]{1,0:T(8,128)(2,1)} collective-permute-done((bf16[288,1536]{1,0:T(8,128)(2,1)}, bf16[288,1536]{1,0:T(8,128)(2,1)}, u32[]{:S(2)}, u32[]{:S(2)}) %collective-permute-start.45) | collective-permute-done | bytes 884768 | tf_op jit(solution)/shard_map/ppermute | solution.py:431
  458.5 2.3 convolution_convert_fusion.12
  460.8 2.6 add_convert_fusion.6
  464.0 2.4 add_convert_fusion.9
  466.4 2.7 add_convert_fusion.7
  471.0 34.9 %attend_backward.1 = (f32[1152,384]{1,0:T(8,128)}, bf16[1024,256]{1,0:T(8,128)(2,1)}, f32[1152,256]{1,0:T(8,128)}) custom-call(s32[1]{0:T(128)} %bitcast.12.index_ref, bf16[1152,384]{1,0:T(8,128)(2,1)} %copy.180.q_ref, bf16[1152,384]{1,0:T(8,128)(2,1)} %bitcast.22.grad_ref, bf16[1152,384]{1,0:T(8,128)(2,1)} %get-tuple-element.160.mixed_ref, ...), custom_call_target="tpu_custom_call" | custom-call | flops 22649241600 | bytes 3538944 | tf_op jit(solution)/shard_map/attend_backward/pallas_call | solution.py:394
  514.3 2.8 copy.189
  521.0 3.2 copy.190
  524.2 5.0 all-to-all-start.2
  531.1 3.3 convert_add_fusion.2
  534.5 4.1 collective-permute-done.58
  542.0 5.0 convolution_convert_fusion.1
  551.5 2.5 add_convert_fusion.13
  559.1 9.1 %collective-permute-done.53 = bf16[192,1536]{1,0:T(8,128)(2,1)} collective-permute-done((bf16[192,1536]{1,0:T(8,128)(2,1)}, bf16[192,1536]{1,0:T(8,128)(2,1)}, u32[]{:S(2)}, u32[]{:S(2)}) %collective-permute-start.53) | collective-permute-done | bytes 589856 | tf_op jit(solution)/shard_map/ppermute | solution.py:431
  568.2 2.5 add_convert_fusion.11
  570.7 5.3 all-to-all-done.2
  576.1 3.5 convolution_convert_fusion.3
  579.6 4.3 all-to-all-start.3
  587.0 2.4 convolution_add_fusion.5
  595.5 7.5 %collective-permute-done.65 = bf16[192,657]{0,1:T(8,128)(2,1)S(1)} collective-permute-done((bf16[192,657]{0,1:T(8,128)(2,1)S(1)}, bf16[192,657]{0,1:T(8,128)(2,1)S(1)}, u32[]{:S(2)}, u32[]{:S(2)}) %collective-permute-start.65) | collective-permute-done | bytes 252320 | tf_op jit(solution)/shard_map/ppermute | solution.py:431
  605.8 2.4 convolution_add_fusion.2
  608.2 4.6 collective-permute-done.68
  614.1 3.7 collective-permute-start.74
  630.7 2.6 collective-permute-start.71
  (453 shorter events, 192.8 us)
Async XLA Ops:
  8.0 231.6 %all-gather.6.cloned.1.call-start = ((), (), s32[]{:S(2)}) async-start(), calls=%async_computation.7 | async-start | bytes 5308416 | tf_op jit(solution)/shard_map/all_gather | solution.py:764
  8.1 54.6 %collective-permute-start.3 = (bf16[288,1536]{1,0:T(8,128)(2,1)}, bf16[288,1536]{1,0:T(8,128)(2,1)S(1)}, u32[]{:S(2)}, u32[]{:S(2)}) collective-permute-start(bf16[288,1536]{1,0:T(8,128)(2,1)} %param.13), channel_id=1, source_target_pairs={{0,1},{1,2},{2,3},{4,5},{5,6},{6,7},{8,9},{9,10},{10,11},{12,13},{... | collective-permute-start | bytes 2654216 | tf_op jit(solution)/shard_map/ppermute | solution.py:466
  13.1 51.2 %collective-permute-start.5 = (bf16[288,1536]{1,0:T(8,128)(2,1)}, bf16[288,1536]{1,0:T(8,128)(2,1)}, u32[]{:S(2)}, u32[]{:S(2)}) collective-permute-start(bf16[288,1536]{1,0:T(8,128)(2,1)} %param.13), channel_id=1, source_target_pairs={{1,0},{2,1},{3,2},{5,4},{6,5},{7,6},{9,8},{10,9},{11,10},{13,12},{... | collective-permute-start | bytes 2654216 | tf_op jit(solution)/shard_map/ppermute | solution.py:466
  14.4 21.0 %collective-permute-start.4 = (bf16[384,192]{0,1:T(8,128)(2,1)}, bf16[384,192]{0,1:T(8,128)(2,1)S(1)}, u32[]{:S(2)}, u32[]{:S(2)}) collective-permute-start(bf16[384,192]{0,1:T(8,128)(2,1)} %param.18), channel_id=1, source_target_pairs={{0,1},{1,2},{2,3},{4,5},{5,6},{6,7},{8,9},{9,10},{10,11},{12,13},{... | collective-permute-start | bytes 442376 | tf_op jit(solution)/shard_map/ppermute | solution.py:466
  18.9 32.3 %collective-permute-start.6 = (bf16[384,192]{0,1:T(8,128)(2,1)}, bf16[384,192]{0,1:T(8,128)(2,1)S(1)}, u32[]{:S(2)}, u32[]{:S(2)}) collective-permute-start(bf16[384,192]{0,1:T(8,128)(2,1)} %param.18), channel_id=1, source_target_pairs={{1,0},{2,1},{3,2},{5,4},{6,5},{7,6},{9,8},{10,9},{11,10},{13,12},{... | collective-permute-start | bytes 442376 | tf_op jit(solution)/shard_map/ppermute | solution.py:466
  24.0 38.7 %collective-permute-start.1 = (bf16[192,640]{0,1:T(8,128)(2,1)}, bf16[192,640]{0,1:T(8,128)(2,1)S(1)}, u32[]{:S(2)}, u32[]{:S(2)}) collective-permute-start(bf16[192,640]{0,1:T(8,128)(2,1)} %pad_maximum_fusion.3), channel_id=1, source_target_pairs={{0,8},{4,12},{8,0},{12,4},{16,24},{20,28},{24,16},{28,20},{1,9},{5... | collective-permute-start | bytes 737288 | tf_op jit(solution)/shard_map/ppermute | solution.py:431
  35.4 27.3 %collective-permute-start.2 = (bf16[192,640]{0,1:T(8,128)(2,1)}, bf16[192,640]{0,1:T(8,128)(2,1)S(1)}, u32[]{:S(2)}, u32[]{:S(2)}) collective-permute-start(bf16[192,640]{0,1:T(8,128)(2,1)} %pad_maximum_fusion.3), channel_id=1, source_target_pairs={{0,16},{4,20},{8,24},{12,28},{16,0},{20,4},{24,8},{28,12},{1,17},{... | collective-permute-start | bytes 737288 | tf_op jit(solution)/shard_map/ppermute | solution.py:431
  51.2 16.4 %collective-permute-start = (bf16[192,640]{0,1:T(8,128)(2,1)}, bf16[192,640]{0,1:T(8,128)(2,1)}, u32[]{:S(2)}, u32[]{:S(2)}) collective-permute-start(bf16[192,640]{0,1:T(8,128)(2,1)} %pad_maximum_fusion.3), channel_id=1, source_target_pairs={{0,4},{4,0},{8,12},{12,8},{16,20},{20,16},{24,28},{28,24},{1,5},{5... | collective-permute-start | bytes 737288 | tf_op jit(solution)/shard_map/ppermute | solution.py:431
  64.3 17.0 %collective-permute-start.11 = (bf16[288,1536]{1,0:T(8,128)(2,1)}, bf16[288,1536]{1,0:T(8,128)(2,1)S(1)}, u32[]{:S(2)}, u32[]{:S(2)}) collective-permute-start(bf16[288,1536]{1,0:T(8,128)(2,1)} %copy-done.37), channel_id=1, source_target_pairs={{1,2},{2,3},{5,6},{6,7},{9,10},{10,11},{13,14},{14,15},{17,18},{18... | collective-permute-start | bytes 2654216 | tf_op jit(solution)/shard_map/ppermute | solution.py:466
  65.1 25.1 %collective-permute-start.12 = (bf16[288,1536]{1,0:T(8,128)(2,1)}, bf16[288,1536]{1,0:T(8,128)(2,1)}, u32[]{:S(2)}, u32[]{:S(2)}) collective-permute-start(bf16[288,1536]{1,0:T(8,128)(2,1)} %collective-permute-done.5), channel_id=1, source_target_pairs={{1,0},{2,1},{5,4},{6,5},{9,8},{10,9},{13,12},{14,13},{17,16},{18,1... | collective-permute-start | bytes 2654216 | tf_op jit(solution)/shard_map/ppermute | solution.py:466
  69.3 10.0 %collective-permute-start.9 = (bf16[192,640]{0,1:T(8,128)(2,1)S(1)}, bf16[192,640]{0,1:T(8,128)(2,1)S(1)}, u32[]{:S(2)}, u32[]{:S(2)}) collective-permute-start(bf16[192,640]{0,1:T(8,128)(2,1)S(1)} %collective-permute-done.2), channel_id=1, source_target_pairs={{0,8},{4,12},{8,0},{12,4},{16,24},{20,28},{24,16},{28,20},{1,9},{5... | collective-permute-start | bytes 737288 | tf_op jit(solution)/shard_map/ppermute | solution.py:431
  69.9 10.0 %collective-permute-start.14 = (bf16[384,192]{0,1:T(8,128)(2,1)}, bf16[384,192]{0,1:T(8,128)(2,1)S(1)}, u32[]{:S(2)}, u32[]{:S(2)}) collective-permute-start(bf16[384,192]{0,1:T(8,128)(2,1)} %copy-done.56), channel_id=1, source_target_pairs={{1,2},{2,3},{5,6},{6,7},{9,10},{10,11},{13,14},{14,15},{17,18},{18... | collective-permute-start | bytes 442376 | tf_op jit(solution)/shard_map/ppermute | solution.py:466
  70.5 22.2 %collective-permute-start.17 = (bf16[384,192]{0,1:T(8,128)(2,1)}, bf16[384,192]{0,1:T(8,128)(2,1)S(1)}, u32[]{:S(2)}, u32[]{:S(2)}) collective-permute-start(bf16[384,192]{0,1:T(8,128)(2,1)} %copy-done.54), channel_id=1, source_target_pairs={{1,0},{2,1},{5,4},{6,5},{9,8},{10,9},{13,12},{14,13},{17,16},{18,1... | collective-permute-start | bytes 442376 | tf_op jit(solution)/shard_map/ppermute | solution.py:466
  79.3 37.0 %collective-permute-start.19 = (bf16[288,1536]{1,0:T(8,128)(2,1)}, bf16[288,1536]{1,0:T(8,128)(2,1)}, u32[]{:S(2)}, u32[]{:S(2)}) collective-permute-start(bf16[288,1536]{1,0:T(8,128)(2,1)} %og_even), channel_id=1, source_target_pairs={{0,8},{4,12},{8,0},{12,4},{16,24},{20,28},{24,16},{28,20},{1,9},{5... | collective-permute-start | bytes 2654216 | tf_op jit(solution)/shard_map/ppermute | solution.py:431
  79.9 37.0 %collective-permute-start.20 = (bf16[288,1536]{1,0:T(8,128)(2,1)}, bf16[288,1536]{1,0:T(8,128)(2,1)}, u32[]{:S(2)}, u32[]{:S(2)}) collective-permute-start(bf16[288,1536]{1,0:T(8,128)(2,1)} %og_even), channel_id=1, source_target_pairs={{0,16},{4,20},{8,24},{12,28},{16,0},{20,4},{24,8},{28,12},{1,17},{... | collective-permute-start | bytes 2654216 | tf_op jit(solution)/shard_map/ppermute | solution.py:431
  81.4 35.5 %collective-permute-start.13 = (bf16[288,1536]{1,0:T(8,128)(2,1)S(1)}, bf16[288,1536]{1,0:T(8,128)(2,1)S(1)}, u32[]{:S(2)}, u32[]{:S(2)}) collective-permute-start(bf16[288,1536]{1,0:T(8,128)(2,1)S(1)} %collective-permute-done.11), channel_id=1, source_target_pairs={{2,3},{6,7},{10,11},{14,15},{18,19},{22,23},{26,27},{30,31}} | collective-permute-start | bytes 2654216 | tf_op jit(solution)/shard_map/ppermute | solution.py:466
  90.3 26.5 %collective-permute-start.16 = (bf16[288,1536]{1,0:T(8,128)(2,1)}, bf16[288,1536]{1,0:T(8,128)(2,1)S(1)}, u32[]{:S(2)}, u32[]{:S(2)}) collective-permute-start(bf16[288,1536]{1,0:T(8,128)(2,1)} %collective-permute-done.12), channel_id=1, source_target_pairs={{1,0},{5,4},{9,8},{13,12},{17,16},{21,20},{25,24},{29,28}} | collective-permute-start | bytes 2654216 | tf_op jit(solution)/shard_map/ppermute | solution.py:466
  96.1 20.1 %collective-permute-start.18 = (bf16[384,192]{0,1:T(8,128)(2,1)S(1)}, bf16[384,192]{0,1:T(8,128)(2,1)S(1)}, u32[]{:S(2)}, u32[]{:S(2)}) collective-permute-start(bf16[384,192]{0,1:T(8,128)(2,1)S(1)} %collective-permute-done.17), channel_id=1, source_target_pairs={{1,0},{5,4},{9,8},{13,12},{17,16},{21,20},{25,24},{29,28}} | collective-permute-start | bytes 442376 | tf_op jit(solution)/shard_map/ppermute | solution.py:466
  116.3 94.6 %collective-permute-start.21 = (bf16[288,1536]{1,0:T(8,128)(2,1)}, bf16[288,1536]{1,0:T(8,128)(2,1)}, u32[]{:S(2)}, u32[]{:S(2)}) collective-permute-start(bf16[288,1536]{1,0:T(8,128)(2,1)} %og_even), channel_id=1, source_target_pairs={{0,4},{4,0},{8,12},{12,8},{16,20},{20,16},{24,28},{28,24},{1,5},{5... | collective-permute-start | bytes 2654216 | tf_op jit(solution)/shard_map/ppermute | solution.py:431
  146.1 64.8 %collective-permute-start.22 = (bf16[288,1536]{1,0:T(8,128)(2,1)}, bf16[288,1536]{1,0:T(8,128)(2,1)}, u32[]{:S(2)}, u32[]{:S(2)}) collective-permute-start(bf16[288,1536]{1,0:T(8,128)(2,1)} %collective-permute-done.19.og_even), channel_id=1, source_target_pairs={{0,4},{4,0},{8,12},{12,8},{16,20},{20,16},{24,28},{28,24},{1,5},{5... | collective-permute-start | bytes 2654216 | tf_op jit(solution)/shard_map/ppermute | solution.py:431
  146.7 64.2 %collective-permute-start.23 = (bf16[288,1536]{1,0:T(8,128)(2,1)}, bf16[288,1536]{1,0:T(8,128)(2,1)}, u32[]{:S(2)}, u32[]{:S(2)}) collective-permute-start(bf16[288,1536]{1,0:T(8,128)(2,1)} %collective-permute-done.20.og_even), channel_id=1, source_target_pairs={{0,4},{4,0},{8,12},{12,8},{16,20},{20,16},{24,28},{28,24},{1,5},{5... | collective-permute-start | bytes 2654216 | tf_op jit(solution)/shard_map/ppermute | solution.py:431
  146.7 64.2 %collective-permute-start.24 = (bf16[288,1536]{1,0:T(8,128)(2,1)}, bf16[288,1536]{1,0:T(8,128)(2,1)}, u32[]{:S(2)}, u32[]{:S(2)}) collective-permute-start(bf16[288,1536]{1,0:T(8,128)(2,1)} %collective-permute-done.20.og_even), channel_id=1, source_target_pairs={{0,8},{4,12},{8,0},{12,4},{16,24},{20,28},{24,16},{28,20},{1,9},{5... | collective-permute-start | bytes 2654216 | tf_op jit(solution)/shard_map/ppermute | solution.py:431
  210.9 27.4 %all-to-all-start = ((bf16[4,288,384]{2,1,0:T(8,128)(2,1)}), bf16[4,288,384]{2,1,0:T(8,128)(2,1)}, u32[]{:S(2)}, u32[]{:S(2)}) async-start(bf16[4,288,384]{2,1,0:T(8,128)(2,1)} %bitcast.229), calls=%async_computation | async-start | bytes 1769472 | tf_op jit(solution)/shard_map/all_to_all | solution.py:799
  215.5 140.0 %all-gather.8.cloned.1.call-start = ((), (), s32[]{:S(2)}) async-start(), calls=%async_computation.11 | async-start | bytes 4915200 | tf_op jit(solution)/shard_map/all_gather | solution.py:809
  249.8 24.3 %collective-permute-start.25 = (bf16[288,1664]{1,0:T(8,128)(2,1)}, bf16[288,1664]{1,0:T(8,128)(2,1)}, u32[]{:S(2)}, u32[]{:S(2)}) collective-permute-start(bf16[288,1664]{1,0:T(8,128)(2,1)} %concatenate.61.x_even), channel_id=1, source_target_pairs={{0,8},{4,12},{8,0},{12,4},{16,24},{20,28},{24,16},{28,20},{1,9},{5... | collective-permute-start | bytes 2875400 | tf_op jit(solution)/shard_map/ppermute | solution.py:431
  250.4 23.7 %collective-permute-start.26 = (bf16[288,1664]{1,0:T(8,128)(2,1)}, bf16[288,1664]{1,0:T(8,128)(2,1)}, u32[]{:S(2)}, u32[]{:S(2)}) collective-permute-start(bf16[288,1664]{1,0:T(8,128)(2,1)} %concatenate.61.x_even), channel_id=1, source_target_pairs={{0,16},{4,20},{8,24},{12,28},{16,0},{20,4},{24,8},{28,12},{1,17},{... | collective-permute-start | bytes 2875400 | tf_op jit(solution)/shard_map/ppermute | solution.py:431
  274.4 378.9 %reduce-scatter.8.cloned.1.call-start = ((), (), s32[]{:S(2)}) async-start(), calls=%async_computation.10 | async-start | bytes 3932160 | tf_op jit(solution)/shard_map/reduce_scatter | solution.py:879
  274.6 24.5 %collective-permute-start.30 = (bf16[288,1664]{1,0:T(8,128)(2,1)}, bf16[288,1664]{1,0:T(8,128)(2,1)}, u32[]{:S(2)}, u32[]{:S(2)}) collective-permute-start(bf16[288,1664]{1,0:T(8,128)(2,1)} %collective-permute-done.26.x_even), channel_id=1, source_target_pairs={{0,8},{4,12},{8,0},{12,4},{16,24},{20,28},{24,16},{28,20},{1,9},{5... | collective-permute-start | bytes 2875400 | tf_op jit(solution)/shard_map/ppermute | solution.py:431
  299.7 32.0 %collective-permute-start.28 = (bf16[288,1664]{1,0:T(8,128)(2,1)}, bf16[288,1664]{1,0:T(8,128)(2,1)}, u32[]{:S(2)}, u32[]{:S(2)}) collective-permute-start(bf16[288,1664]{1,0:T(8,128)(2,1)} %collective-permute-done.26.x_even), channel_id=1, source_target_pairs={{0,4},{4,0},{8,12},{12,8},{16,20},{20,16},{24,28},{28,24},{1,5},{5... | collective-permute-start | bytes 2875400 | tf_op jit(solution)/shard_map/ppermute | solution.py:431
  299.8 25.4 %collective-permute-start.29 = (bf16[288,1664]{1,0:T(8,128)(2,1)}, bf16[288,1664]{1,0:T(8,128)(2,1)}, u32[]{:S(2)}, u32[]{:S(2)}) collective-permute-start(bf16[288,1664]{1,0:T(8,128)(2,1)} %get-tuple-element.171), channel_id=1, source_target_pairs={{0,4},{4,0},{8,12},{12,8},{16,20},{20,16},{24,28},{28,24},{1,5},{5... | collective-permute-start | bytes 2875400 | tf_op jit(solution)/shard_map/ppermute | solution.py:431
  300.2 27.8 %collective-permute-start.32 = (bf16[288,1664]{1,0:T(8,128)(2,1)}, bf16[288,1664]{1,0:T(8,128)(2,1)}, u32[]{:S(2)}, u32[]{:S(2)}) collective-permute-start(bf16[288,1664]{1,0:T(8,128)(2,1)} %get-tuple-element.184), channel_id=1, source_target_pairs={{0,4},{4,0},{8,12},{12,8},{16,20},{20,16},{24,28},{28,24},{1,5},{5... | collective-permute-start | bytes 2875400 | tf_op jit(solution)/shard_map/ppermute | solution.py:431
  331.7 23.8 %collective-permute-start.36 = (bf16[288,1664]{1,0:T(8,128)(2,1)}, bf16[288,1664]{1,0:T(8,128)(2,1)}, u32[]{:S(2)}, u32[]{:S(2)}) collective-permute-start(bf16[288,1664]{1,0:T(8,128)(2,1)} %add_convert_fusion.2), channel_id=1, source_target_pairs={{0,16},{4,20},{8,24},{12,28},{16,0},{20,4},{24,8},{28,12},{1,17},{... | collective-permute-start | bytes 2875400 | tf_op jit(solution)/shard_map/ppermute | solution.py:431
  355.5 41.4 %collective-permute-start.40 = (bf16[4,768,640]{2,1,0:T(8,128)(2,1)}, bf16[4,768,640]{2,1,0:T(8,128)(2,1)}, u32[]{:S(2)}, u32[]{:S(2)}) collective-permute-start(bf16[4,768,640]{2,1,0:T(8,128)(2,1)} %bitcast.211), channel_id=1, source_target_pairs={{0,4},{4,0},{8,12},{12,8},{16,20},{20,16},{24,28},{28,24},{1,5},{5... | collective-permute-start | bytes 11796488 | tf_op jit(solution)/shard_map/ppermute | solution.py:431
  363.4 23.6 %collective-permute-start.38 = (bf16[288,1664]{1,0:T(8,128)(2,1)}, bf16[288,1664]{1,0:T(8,128)(2,1)}, u32[]{:S(2)}, u32[]{:S(2)}) collective-permute-start(bf16[288,1664]{1,0:T(8,128)(2,1)} %add_convert_fusion), channel_id=1, source_target_pairs={{0,8},{4,12},{8,0},{12,4},{16,24},{20,28},{24,16},{28,20},{1,9},{5... | collective-permute-start | bytes 2875400 | tf_op jit(solution)/shard_map/ppermute | solution.py:431
  364.6 23.3 %collective-permute-start.39 = (bf16[288,1664]{1,0:T(8,128)(2,1)}, bf16[288,1664]{1,0:T(8,128)(2,1)}, u32[]{:S(2)}, u32[]{:S(2)}) collective-permute-start(bf16[288,1664]{1,0:T(8,128)(2,1)} %add_convert_fusion.1), channel_id=1, source_target_pairs={{0,16},{4,20},{8,24},{12,28},{16,0},{20,4},{24,8},{28,12},{1,17},{... | collective-permute-start | bytes 2875400 | tf_op jit(solution)/shard_map/ppermute | solution.py:431
  397.9 58.8 %all-to-all-start.1 = ((bf16[288,4,384]{2,0,1:T(8,128)(2,1)}), bf16[288,4,384]{2,0,1:T(8,128)(2,1)}, u32[]{:S(2)}, u32[]{:S(2)}) async-start(bf16[288,4,384]{2,0,1:T(8,128)(2,1)} %bitcast.221), calls=%async_computation.1 | async-start | bytes 1769472 | tf_op jit(solution)/shard_map/all_to_all | solution.py:902
  402.1 254.0 %reduce-scatter.6.cloned.1.call-start = ((), (), s32[]{:S(2)}) async-start(), calls=%async_computation.9 | async-start | bytes 3932160 | tf_op jit(solution)/shard_map/reduce_scatter | solution.py:1016
  402.2 29.8 %collective-permute-start.41 = (bf16[288,1536]{1,0:T(8,128)(2,1)}, bf16[288,1536]{1,0:T(8,128)(2,1)}, u32[]{:S(2)}, u32[]{:S(2)}) collective-permute-start(bf16[288,1536]{1,0:T(8,128)(2,1)} %get-tuple-element.232), channel_id=1, source_target_pairs={{0,4},{4,0},{8,12},{12,8},{16,20},{20,16},{24,28},{28,24},{1,5},{5... | collective-permute-start | bytes 2654216 | tf_op jit(solution)/shard_map/ppermute | solution.py:431
  402.3 30.2 %collective-permute-start.42 = (bf16[288,1536]{1,0:T(8,128)(2,1)}, bf16[288,1536]{1,0:T(8,128)(2,1)}, u32[]{:S(2)}, u32[]{:S(2)}) collective-permute-start(bf16[288,1536]{1,0:T(8,128)(2,1)} %get-tuple-element.233), channel_id=1, source_target_pairs={{0,4},{4,0},{8,12},{12,8},{16,20},{20,16},{24,28},{28,24},{1,5},{5... | collective-permute-start | bytes 2654216 | tf_op jit(solution)/shard_map/ppermute | solution.py:431
  402.8 29.7 %collective-permute-start.43 = (bf16[288,1536]{1,0:T(8,128)(2,1)}, bf16[288,1536]{1,0:T(8,128)(2,1)}, u32[]{:S(2)}, u32[]{:S(2)}) collective-permute-start(bf16[288,1536]{1,0:T(8,128)(2,1)} %get-tuple-element.234), channel_id=1, source_target_pairs={{0,4},{4,0},{8,12},{12,8},{16,20},{20,16},{24,28},{28,24},{1,5},{5... | collective-permute-start | bytes 2654216 | tf_op jit(solution)/shard_map/ppermute | solution.py:431
  402.9 29.6 %collective-permute-start.44 = (bf16[288,1536]{1,0:T(8,128)(2,1)}, bf16[288,1536]{1,0:T(8,128)(2,1)}, u32[]{:S(2)}, u32[]{:S(2)}) collective-permute-start(bf16[288,1536]{1,0:T(8,128)(2,1)} %get-tuple-element.235), channel_id=1, source_target_pairs={{0,4},{4,0},{8,12},{12,8},{16,20},{20,16},{24,28},{28,24},{1,5},{5... | collective-permute-start | bytes 2654216 | tf_op jit(solution)/shard_map/ppermute | solution.py:431
  408.0 48.8 %collective-permute-start.46 = (bf16[192,1536]{1,0:T(8,128)(2,1)}, bf16[192,1536]{1,0:T(8,128)(2,1)}, u32[]{:S(2)}, u32[]{:S(2)}) collective-permute-start(bf16[192,1536]{1,0:T(8,128)(2,1)} %convolution_convert_fusion.10), channel_id=1, source_target_pairs={{0,4},{4,0},{8,12},{12,8},{16,20},{20,16},{24,28},{28,24},{1,5},{5... | collective-permute-start | bytes 1769480 | tf_op jit(solution)/shard_map/ppermute | solution.py:431
  432.0 24.7 %collective-permute-start.47 = (bf16[192,1536]{1,0:T(8,128)(2,1)}, bf16[192,1536]{1,0:T(8,128)(2,1)S(1)}, u32[]{:S(2)}, u32[]{:S(2)}) collective-permute-start(bf16[192,1536]{1,0:T(8,128)(2,1)} %convolution_convert_fusion.8), channel_id=1, source_target_pairs={{0,4},{4,0},{8,12},{12,8},{16,20},{20,16},{24,28},{28,24},{1,5},{5... | collective-permute-start | bytes 1769480 | tf_op jit(solution)/shard_map/ppermute | solution.py:431
  434.8 21.9 %collective-permute-start.45 = (bf16[288,1536]{1,0:T(8,128)(2,1)}, bf16[288,1536]{1,0:T(8,128)(2,1)}, u32[]{:S(2)}, u32[]{:S(2)}) collective-permute-start(bf16[288,1536]{1,0:T(8,128)(2,1)} %add_convert_fusion.10), channel_id=1, source_target_pairs={{0,16},{4,20},{8,24},{12,28},{16,0},{20,4},{24,8},{28,12},{1,17},{... | collective-permute-start | bytes 2654216 | tf_op jit(solution)/shard_map/ppermute | solution.py:431
  456.8 200.6 %reduce-scatter.4.cloned.1.call-start = ((), (), s32[]{:S(2)}) async-start(), calls=%async_computation.8 | async-start | bytes 3932160 | tf_op jit(solution)/shard_map/reduce_scatter | solution.py:1016
  463.4 42.6 %collective-permute-start.49 = (bf16[288,1536]{1,0:T(8,128)(2,1)}, bf16[288,1536]{1,0:T(8,128)(2,1)}, u32[]{:S(2)}, u32[]{:S(2)}) collective-permute-start(bf16[288,1536]{1,0:T(8,128)(2,1)} %add_convert_fusion.6), channel_id=1, source_target_pairs={{0,16},{4,20},{8,24},{12,28},{16,0},{20,4},{24,8},{28,12},{1,17},{... | collective-permute-start | bytes 2654216 | tf_op jit(solution)/shard_map/ppermute | solution.py:431
  469.0 37.0 %collective-permute-start.48 = (bf16[288,1536]{1,0:T(8,128)(2,1)}, bf16[288,1536]{1,0:T(8,128)(2,1)}, u32[]{:S(2)}, u32[]{:S(2)}) collective-permute-start(bf16[288,1536]{1,0:T(8,128)(2,1)} %add_convert_fusion.7), channel_id=1, source_target_pairs={{0,8},{4,12},{8,0},{12,4},{16,24},{20,28},{24,16},{28,20},{1,9},{5... | collective-permute-start | bytes 2654216 | tf_op jit(solution)/shard_map/ppermute | solution.py:431
  470.5 35.5 %collective-permute-start.50 = (bf16[192,1536]{1,0:T(8,128)(2,1)}, bf16[192,1536]{1,0:T(8,128)(2,1)}, u32[]{:S(2)}, u32[]{:S(2)}) collective-permute-start(bf16[192,1536]{1,0:T(8,128)(2,1)} %convolution_convert_fusion.4), channel_id=1, source_target_pairs={{0,4},{4,0},{8,12},{12,8},{16,20},{20,16},{24,28},{28,24},{1,5},{5... | collective-permute-start | bytes 1769480 | tf_op jit(solution)/shard_map/ppermute | solution.py:431
  470.5 35.5 %collective-permute-start.51 = (bf16[192,1536]{1,0:T(8,128)(2,1)}, bf16[192,1536]{1,0:T(8,128)(2,1)}, u32[]{:S(2)}, u32[]{:S(2)}) collective-permute-start(bf16[192,1536]{1,0:T(8,128)(2,1)} %convolution_convert_fusion.6), channel_id=1, source_target_pairs={{0,4},{4,0},{8,12},{12,8},{16,20},{20,16},{24,28},{28,24},{1,5},{5... | collective-permute-start | bytes 1769480 | tf_op jit(solution)/shard_map/ppermute | solution.py:431
  509.0 50.1 %collective-permute-start.54 = (bf16[192,1536]{1,0:T(8,128)(2,1)}, bf16[192,1536]{1,0:T(8,128)(2,1)}, u32[]{:S(2)}, u32[]{:S(2)}) collective-permute-start(bf16[192,1536]{1,0:T(8,128)(2,1)} %add_convert_fusion.12), channel_id=1, source_target_pairs={{0,16},{4,20},{8,24},{12,28},{16,0},{20,4},{24,8},{28,12},{1,17},{... | collective-permute-start | bytes 1769480 | tf_op jit(solution)/shard_map/ppermute | solution.py:431
  512.1 39.3 %collective-permute-start.52 = (bf16[192,1536]{1,0:T(8,128)(2,1)}, bf16[192,1536]{1,0:T(8,128)(2,1)}, u32[]{:S(2)}, u32[]{:S(2)}) collective-permute-start(bf16[192,1536]{1,0:T(8,128)(2,1)} %add_convert_fusion.14), channel_id=1, source_target_pairs={{0,16},{4,20},{8,24},{12,28},{16,0},{20,4},{24,8},{28,12},{1,17},{... | collective-permute-start | bytes 1769480 | tf_op jit(solution)/shard_map/ppermute | solution.py:431
  513.8 15.4 %collective-permute-start.57 = (bf16[128,256]{1,0:T(8,128)(2,1)}, bf16[128,256]{1,0:T(8,128)(2,1)}, u32[]{:S(2)}, u32[]{:S(2)}) collective-permute-start(bf16[128,256]{1,0:T(8,128)(2,1)} %get-tuple-element.392), channel_id=1, source_target_pairs={{0,4},{4,0},{8,12},{12,8},{16,20},{20,16},{24,28},{28,24},{1,5},{5... | collective-permute-start | bytes 196616 | tf_op jit(solution)/shard_map/ppermute | solution.py:431
  513.8 20.7 %collective-permute-start.56 = (bf16[128,256]{1,0:T(8,128)(2,1)}, bf16[128,256]{1,0:T(8,128)(2,1)S(1)}, u32[]{:S(2)}, u32[]{:S(2)}) collective-permute-start(bf16[128,256]{1,0:T(8,128)(2,1)} %get-tuple-element.393), channel_id=1, source_target_pairs={{0,4},{4,0},{8,12},{12,8},{16,20},{20,16},{24,28},{28,24},{1,5},{5... | collective-permute-start | bytes 196616 | tf_op jit(solution)/shard_map/ppermute | solution.py:431
  514.3 20.2 %collective-permute-start.60 = (bf16[128,256]{1,0:T(8,128)(2,1)}, bf16[128,256]{1,0:T(8,128)(2,1)S(1)}, u32[]{:S(2)}, u32[]{:S(2)}) collective-permute-start(bf16[128,256]{1,0:T(8,128)(2,1)} %get-tuple-element.391), channel_id=1, source_target_pairs={{0,4},{4,0},{8,12},{12,8},{16,20},{20,16},{24,28},{28,24},{1,5},{5... | collective-permute-start | bytes 196616 | tf_op jit(solution)/shard_map/ppermute | solution.py:431
  524.2 51.8 %all-to-all-start.2 = ((bf16[4,288,384]{2,1,0:T(8,128)(2,1)}), bf16[4,288,384]{2,1,0:T(8,128)(2,1)S(1)}, u32[]{:S(2)}, u32[]{:S(2)}) async-start(bf16[4,288,384]{2,1,0:T(8,128)(2,1)} %copy.190), calls=%async_computation.2 | async-start | bytes 1769472 | tf_op jit(solution)/shard_map/all_to_all | solution.py:956
  534.4 13.3 %collective-permute-start.55 = (bf16[128,256]{1,0:T(8,128)(2,1)S(1)}, bf16[128,256]{1,0:T(8,128)(2,1)S(1)}, u32[]{:S(2)}, u32[]{:S(2)}) collective-permute-start(bf16[128,256]{1,0:T(8,128)(2,1)S(1)} %copy-done.58), channel_id=1, source_target_pairs={{0,4},{4,0},{8,12},{12,8},{16,20},{20,16},{24,28},{28,24},{1,5},{5... | collective-permute-start | bytes 196616 | tf_op jit(solution)/shard_map/ppermute | solution.py:431
  553.9 14.3 %collective-permute-start.53 = (bf16[192,1536]{1,0:T(8,128)(2,1)}, bf16[192,1536]{1,0:T(8,128)(2,1)}, u32[]{:S(2)}, u32[]{:S(2)}) collective-permute-start(bf16[192,1536]{1,0:T(8,128)(2,1)} %add_convert_fusion.13), channel_id=1, source_target_pairs={{0,8},{4,12},{8,0},{12,4},{16,24},{20,28},{24,16},{28,20},{1,9},{5... | collective-permute-start | bytes 1769480 | tf_op jit(solution)/shard_map/ppermute | solution.py:431
  579.6 46.3 %all-to-all-start.3 = ((bf16[4,288,256]{2,1,0:T(8,128)(2,1)}), bf16[4,288,256]{2,1,0:T(8,128)(2,1)}, u32[]{:S(2)}, u32[]{:S(2)}) async-start(bf16[4,288,256]{2,1,0:T(8,128)(2,1)} %bitcast.29), calls=%async_computation.3 | async-start | bytes 1179648 | tf_op jit(solution)/shard_map/all_to_all | solution.py:958
  590.9 17.3 %collective-permute-start.62 = (bf16[192,657]{0,1:T(8,128)(2,1)S(1)}, bf16[192,657]{0,1:T(8,128)(2,1)S(1)}, u32[]{:S(2)}, u32[]{:S(2)}) collective-permute-start(bf16[192,657]{0,1:T(8,128)(2,1)S(1)} %get-tuple-element.368), channel_id=1, source_target_pairs={{0,4},{4,0},{8,12},{12,8},{16,20},{20,16},{24,28},{28,24},{1,5},{5... | collective-permute-start | bytes 756872 | tf_op jit(solution)/shard_map/ppermute | solution.py:431
  593.0 10.0 %collective-permute-start.65 = (bf16[192,657]{0,1:T(8,128)(2,1)S(1)}, bf16[192,657]{0,1:T(8,128)(2,1)S(1)}, u32[]{:S(2)}, u32[]{:S(2)}) collective-permute-start(bf16[192,657]{0,1:T(8,128)(2,1)S(1)} %add_convert_fusion.19), channel_id=1, source_target_pairs={{0,16},{4,20},{8,24},{12,28},{16,0},{20,4},{24,8},{28,12},{1,17},{... | collective-permute-start | bytes 756872 | tf_op jit(solution)/shard_map/ppermute | solution.py:431
  614.1 10.7 %collective-permute-start.74 = (bf16[48,18]{0,1:T(8,128)(2,1)S(1)}, bf16[48,18]{0,1:T(8,128)(2,1)S(1)}, u32[]{:S(2)}, u32[]{:S(2)}) collective-permute-start(bf16[48,18]{0,1:T(8,128)(2,1)S(1)} %get-tuple-element.398), channel_id=1, source_target_pairs={{0,3},{1,0},{2,1},{3,2},{4,7},{5,4},{6,5},{7,6},{8,11},{9,8},{10,9... | collective-permute-start | bytes 5192 | tf_op jit(solution)/shard_map/ppermute | solution.py:557
  630.7 21.8 %collective-permute-start.71 = (bf16[192,384]{1,0:T(8,128)(2,1)S(1)}, bf16[192,384]{1,0:T(8,128)(2,1)S(1)}, u32[]{:S(2)}, u32[]{:S(2)}) collective-permute-start(bf16[192,384]{1,0:T(8,128)(2,1)S(1)} %bitcast.231), channel_id=1, source_target_pairs={{0,3},{1,0},{2,1},{3,2},{4,7},{5,4},{6,5},{7,6},{8,11},{9,8},{10,9... | collective-permute-start | bytes 442376 | tf_op jit(solution)/shard_map/ppermute | solution.py:557
  633.4 19.1 %collective-permute-start.70 = (bf16[192,384]{1,0:T(8,128)(2,1)S(1)}, bf16[192,384]{1,0:T(8,128)(2,1)S(1)}, u32[]{:S(2)}, u32[]{:S(2)}) collective-permute-start(bf16[192,384]{1,0:T(8,128)(2,1)S(1)} %bitcast.232), channel_id=1, source_target_pairs={{0,2},{1,3},{2,0},{3,1},{4,6},{5,7},{6,4},{7,5},{8,10},{9,11},{10,... | collective-permute-start | bytes 442376 | tf_op jit(solution)/shard_map/ppermute | solution.py:557
  634.6 17.9 %collective-permute-start.69 = (bf16[192,384]{1,0:T(8,128)(2,1)S(1)}, bf16[192,384]{1,0:T(8,128)(2,1)S(1)}, u32[]{:S(2)}, u32[]{:S(2)}) collective-permute-start(bf16[192,384]{1,0:T(8,128)(2,1)S(1)} %bitcast.233), channel_id=1, source_target_pairs={{0,1},{1,2},{2,3},{3,0},{4,5},{5,6},{6,7},{7,4},{8,9},{9,10},{10,1... | collective-permute-start | bytes 442376 | tf_op jit(solution)/shard_map/ppermute | solution.py:557
  (95 other events, 912.5 us)
Sparse Core Ops, SparseCore 0:
  119.1 51.3 all-gather.5
Sparse Core Ops, SparseCore 1:
  274.4 74.4 all-gather.7
  386.8 72.3 reduce-scatter.7
  461.3 63.7 reduce-scatter.5
  527.4 80.1 reduce-scatter.3

commit v6 on v5

--- a/solution.py
+++ b/solution.py
@@ -227,6 +227,8 @@
     grad_ref,
     mixed_ref,
     level_ref,
+    cos_ref,
+    sin_ref,
     kp_ref,
     vp_ref,
     ko_ref,
@@ -331,7 +333,15 @@
         return 0
 
     lax.fori_loop(0, 2 * conts, step, 0)
-    dq_ref[...] = acc[...] * HEAD_DIMENSION ** (-0.5)
+    grads = acc[...] * HEAD_DIMENSION ** (-0.5)
+    half = HEAD_DIMENSION // 2
+    lane = lax.broadcasted_iota(jnp.int32, grads.shape, 1)
+    swapped = jnp.where(
+        lane % HEAD_DIMENSION < half,
+        pltpu.roll(grads, LANES - half, 1),
+        pltpu.roll(grads, half, 1),
+    )
+    dq_ref[...] = (grads * cos_ref[...] + swapped * sin_ref[...]).astype(bf16)
 
     @pl.when(pair == last)
     def _():
@@ -387,21 +397,25 @@
     )(index, queries, kv_prompt, kv_prompt, kv_own, kv_own)
 
 
-def attend_backward(index, queries, grads, mixed, level, kv_prompt, kv_own, group, kv_heads):
+def attend_backward(
+    index, queries, grads, mixed, level, tables, kv_prompt, kv_own, group, kv_heads
+):
     block_len, width = queries.shape
     prompt_len = kv_prompt.shape[0]
     by_pair, levels, sources = pair_specs(block_len, prompt_len)
     return pl.pallas_call(
         partial(attend_backward_body, group, kv_heads),
         out_shape=[
-            jax.ShapeDtypeStruct((block_len, width), jnp.float32),
+            jax.ShapeDtypeStruct((block_len, width), jnp.bfloat16),
             jax.ShapeDtypeStruct((prompt_len, 2 * LANES), jnp.bfloat16),
             jax.ShapeDtypeStruct((block_len, 2 * LANES), jnp.float32),
         ],
         grid_spec=pltpu.PrefetchScalarGridSpec(
             num_scalar_prefetch=1,
             grid=(width // LANES,),
-            in_specs=[by_pair, by_pair, by_pair, levels] + sources,
+            in_specs=[by_pair, by_pair, by_pair, levels]
+            + [pl.BlockSpec((block_len, LANES), lambda b, i: (0, 0))] * 2
+            + sources,
             out_specs=[
                 by_pair,
                 pl.BlockSpec((prompt_len, 2 * LANES), lambda b, i: (0, 0)),
@@ -418,7 +432,7 @@
         ),
         cost_estimate=attention_cost(block_len, prompt_len, width, 5),
         name="attend_backward",
-    )(index, queries, grads, mixed, level, kv_prompt, kv_prompt, kv_own, kv_own)
+    )(index, queries, grads, mixed, level, *tables, kv_prompt, kv_prompt, kv_own, kv_own)
 
 
 def to_lanes(values):
@@ -457,42 +471,6 @@
     return [blocks[j] for j in range(count)]
 
 
-def pass_on(values, axis_name, step, way):
-    count = lax.axis_size(axis_name)
-    if way > 0:
-        pairs = [(i, i + 1) for i in range(step - 1, count - 1)]
-    else:
-        pairs = [(i, i - 1) for i in range(1, count - step + 1)]
-    return lax.ppermute(values, axis_name, pairs)
-
-
-def gather_line(owns, axis_name, after_first, after_last):
-    count = lax.axis_size(axis_name)
-    index = lax.axis_index(axis_name)
-    rising, falling = list(owns), list(owns)
-    arrived = []
-    for step in range(1, count):
-        rising = [pass_on(own, axis_name, step, 1) for own in rising]
-        falling = [pass_on(own, axis_name, step, -1) for own in falling]
-        if step == 1:
-            rising, falling = after_first((rising, falling))
-        if step == count - 1:
-            rising, falling = after_last((rising, falling))
-        arrived.append((rising, falling))
-    results = []
-    for k, own in enumerate(owns):
-        rows = own.shape[0]
-        buffer = jnp.zeros(((count + 1) * rows, own.shape[1]), own.dtype)
-        buffer = lax.dynamic_update_slice_in_dim(buffer, own, index * rows, axis=0)
-        for step, (rising, falling) in enumerate(arrived, 1):
-            slot = jnp.where(index >= step, index - step, count)
-            buffer = lax.dynamic_update_slice_in_dim(buffer, rising[k], slot * rows, axis=0)
-            slot = jnp.where(index + step < count, index + step, count)
-            buffer = lax.dynamic_update_slice_in_dim(buffer, falling[k], slot * rows, axis=0)
-        results.append(buffer[: count * rows])
-    return results
-
-
 def add_rounded(left_side, right_side):
     return (left_side.astype(jnp.float32) + right_side.astype(jnp.float32)).astype(jnp.bfloat16)
 
@@ -524,12 +502,27 @@
     return total
 
 
-def reduce_blocks(blocks, axis_name):
-    singles, several = even_blocks(len(blocks))
-    sums = {
-        j: add_rounded(blocks[j], exchange(blocks[j + 1], axis_name, 1))
-        for j in several[::-1] + singles + [0]
+def halves_by_core(values, axis_name):
+    count = lax.axis_size(axis_name)
+    parity = lax.axis_index(axis_name) % 2
+    paired = values.reshape(count // 2, 2, values.shape[0] // count, values.shape[1])
+    keep = lax.dynamic_index_in_dim(paired, parity, 1, keepdims=False)
+    give = lax.dynamic_index_in_dim(paired, 1 - parity, 1, keepdims=False)
+    return keep, give
+
+
+def chip_sums(keep, arrived, axis_name):
+    index = lax.axis_index(axis_name)
+    total = add_rounded(keep, arrived)
+    return {
+        2 * k: lax.dynamic_index_in_dim(total, (index // 2) ^ k, 0, keepdims=False)
+        for k in range(total.shape[0])
     }
+
+
+def reduce_rows(values, axis_name):
+    keep, give = halves_by_core(values, axis_name)
+    sums = chip_sums(keep, exchange(give, axis_name, 1), axis_name)
     return add_all(reduce_singles(sums, reduce_several(sums, axis_name), axis_name))
 
 
@@ -539,13 +532,6 @@
         [lax.dynamic_index_in_dim(stacked, j ^ index, 0, keepdims=True) for j in range(len(blocks))],
         axis=0,
     )
-
-
-def relative_blocks(values, index, count):
-    rows = values.shape[0] // count
-    return [
-        lax.dynamic_slice_in_dim(values, (index ^ j) * rows, rows, axis=0) for j in range(count)
-    ]
 
 
 def scatter_direct(pieces, axis_name):
@@ -735,39 +721,23 @@
     key_width = key_projection.shape[1]
 
     singles, several = even_blocks(shard_count)
-    own_weight = jnp.concatenate([w_query, key_projection, value_projection], axis=1)
-    held = {}
-
-    def after_first(line):
-        small = jnp.concatenate([w_router, gain_attn[:, None], gain_ffn[:, None]], axis=1)
-        small = lax.all_gather(small, "seq", axis=0, tiled=True)
-        small = lax.all_gather(small, "shard", axis=0, tiled=True)
-
-        def tie(blocks):
-            blocks, held["line"], held["small"] = lax.optimization_barrier((blocks, line, small))
-            return blocks
-
-        blocks = gather_blocks(own_weight, "shard", tie)
-        late = lax.optimization_barrier(([blocks[k] for k in several], out_grad))[1]
-        held["weights"] = blocks
-        held["grads"] = gather_blocks(late, "shard")
-        return held["line"]
-
-    def after_last(line):
-        near = [held["grads"][k] for k in singles]
-        line, near = lax.optimization_barrier((line, near))
-        for k, block in zip(singles, near):
-            held["grads"][k] = block
-        return line
-
-    block_tokens, out_weight = gather_line([tokens, w_out], "seq", after_first, after_last)
-    out_weight = lax.all_gather(out_weight, "shard", axis=1, tiled=True)
-    small = held["small"]
+    small = jnp.concatenate([w_router, gain_attn[:, None], gain_ffn[:, None]], axis=1)
+    small = lax.all_gather(small, "seq", axis=0, tiled=True)
+    small = lax.all_gather(small, "shard", axis=0, tiled=True)
     router_weight = small[:, :experts_all]
     first_gain = small[:, experts_all].astype(jnp.float32)
     second_gain = small[:, experts_all + 1].astype(jnp.float32)
-    qkv_weight = in_order(held["weights"], shard_index).reshape(model_width, -1)
-    grad_blocks = held["grads"]
+    block_tokens = lax.all_gather(tokens, "seq", axis=0, tiled=True)
+    own_weight = jnp.concatenate([w_query, key_projection, value_projection], axis=1)
+    weight_blocks = gather_blocks(own_weight, "shard")
+    out_weight = lax.all_gather(w_out, "seq", axis=0, tiled=True)
+    out_weight = lax.all_gather(out_weight, "shard", axis=1, tiled=True)
+    late = lax.optimization_barrier(([weight_blocks[k] for k in several], out_grad))[1]
+    grad_blocks = gather_blocks(late, "shard")
+    qkv_weight = in_order(weight_blocks, shard_index).reshape(model_width, -1)
+    block_tokens, near = lax.optimization_barrier((block_tokens, [grad_blocks[k] for k in singles]))
+    for k, block in zip(singles, near):
+        grad_blocks[k] = block
 
     block_rows = jnp.arange(block_len, dtype=jnp.int32)
     cos_table, sin_table = rotary_tables(
@@ -877,8 +847,10 @@
     row_sums, all_grads = lax.optimization_barrier((row_sums, all_grads))
     down_sum = transposed_times(all_grads, all_hidden).astype(bf16)
     grad_down = lax.psum_scatter(down_sum, "seq", scatter_dimension=0, tiled=True)
+    all_rows = lax.optimization_barrier((all_rows, down_sum))[0]
+    pre_sums = [transposed_times(all_rows, all_pre[0]).astype(bf16)]
     row_pieces = reduce_singles(row_sums, pending, "shard")
-    row_pieces, down_sum = lax.optimization_barrier((row_pieces, down_sum))
+    row_pieces, pre_sums[0] = lax.optimization_barrier((row_pieces, pre_sums[0]))
     row_total = add_all(row_pieces)
     row_grad = row_total[:, :model_width]
     gate_grad_dense = (
@@ -901,31 +873,25 @@
     )
     mixed_grad = lax.all_to_all(mixed_grad_tokens, "seq", split_axis=1, concat_axis=0, tiled=True)
     odd = [exchange(out_parts[j + 1], "shard", 1) for j in order]
-    pre_sums = [transposed_times(all_rows, all_pre[0]).astype(bf16)]
-    odd, pre_sums[0], all_rows = lax.optimization_barrier((odd, pre_sums[0], all_rows))
-    out_sums = {j: add_rounded(out_parts[j], piece) for j, piece in zip(order, odd)}
-    out_pending = reduce_several(out_sums, "shard")
     pre_sums += [
         transposed_times(all_rows, all_pre[e]).astype(bf16) for e in range(1, local_experts)
     ]
-    arrived, pre_sums = lax.optimization_barrier(([piece for _, piece in out_pending], pre_sums))
+    odd, pre_sums = lax.optimization_barrier((odd, pre_sums))
+    out_sums = {j: add_rounded(out_parts[j], piece) for j, piece in zip(order, odd)}
+    out_pending = reduce_several(out_sums, "shard")
+    whole_out = transposed_times(residual_low, mixed_late).astype(bf16)
+    whole_keep, whole_give = halves_by_core(whole_out, "shard")
+    whole_arrived = exchange(whole_give, "shard", 1)
+    mixed_grad, pre_sums, arrived, whole_arrived = lax.optimization_barrier(
+        (mixed_grad, pre_sums, [piece for _, piece in out_pending], whole_arrived)
+    )
     out_pending = [(j, piece) for (j, _), piece in zip(out_pending, arrived)]
     out_pieces = reduce_singles(out_sums, out_pending, "shard")
-    columns = [
-        lax.dynamic_slice_in_dim(
-            residual_low,
-            (shard_index ^ j) * (model_width // shard_count),
-            model_width // shard_count,
-            axis=1,
-        )
-        for j in range(shard_count)
+    whole_sums = chip_sums(whole_keep, whole_arrived, "shard")
+    whole_pending = reduce_several(whole_sums, "shard")
+    pre_grads = [
+        lax.psum_scatter(part, "seq", scatter_dimension=0, tiled=True) for part in pre_sums
     ]
-    whole_out = [transposed_times(part, mixed_late).astype(bf16) for part in columns]
-    first_odd = [exchange(whole_out[j + 1], "shard", 1) for j in order[:2]]
-    mixed_grad, pre_sums, whole_out, first_odd = lax.optimization_barrier(
-        (mixed_grad, pre_sums, whole_out, first_odd)
-    )
-    whole_odd = first_odd + [exchange(whole_out[j + 1], "shard", 1) for j in order[2:]]
 
     query_grad, prompt_grad, self_grad = attend_backward(
         block_number,
@@ -933,16 +899,24 @@
         to_lanes(mixed_grad),
         mixed_own,
         levels,
+        [
+            jnp.tile(cos_table[:, 0, :], (1, LANES // cos_table.shape[2])),
+            jnp.tile(
+                jnp.concatenate([sin_table, -sin_table], axis=2)[:, 0, :],
+                (1, LANES // HEAD_DIMENSION),
+            ),
+        ],
         kv_prompt,
         kv_own,
         group,
         kv_heads,
     )
-    query_grad, prompt_grad, self_grad, out_pieces, whole_odd = lax.optimization_barrier(
-        (query_grad, prompt_grad, self_grad, out_pieces, whole_odd)
-    )
-    query_grad = query_grad[:, :query_width]
-    own_prompt = reduce_blocks(relative_blocks(prompt_grad, shard_index, shard_count), "shard")
+    query_grad, prompt_grad, self_grad, out_pieces, arrived = lax.optimization_barrier(
+        (query_grad, prompt_grad, self_grad, out_pieces, [piece for _, piece in whole_pending])
+    )
+    whole_pending = [(j, piece) for (j, _), piece in zip(whole_pending, arrived)]
+    lin_query = query_grad[:, :query_width]
+    own_prompt = reduce_rows(prompt_grad, "shard")
     key_grad = jnp.concatenate(
         [own_prompt[:, :key_width], self_grad[PROMPT_BLK:, :key_width]], axis=0
     )
@@ -950,33 +924,31 @@
         [own_prompt[:, LANES : LANES + key_width], self_grad[PROMPT_BLK:, LANES : LANES + key_width]],
         axis=0,
     ).astype(bf16)
-    lin_query = rotate(query_grad, cos_table, -sin_table, HEAD_DIMENSION).astype(bf16)
     lin_key = rotate(key_grad, cos_table, -sin_table, HEAD_DIMENSION).astype(bf16)
-    lin_both = jnp.concatenate([lin_key, value_low], axis=1)
-    query_tokens = lax.all_to_all(lin_query, "seq", split_axis=0, concat_axis=1, tiled=True)
-    lin_both, query_tokens = lax.optimization_barrier((lin_both, query_tokens))
-    both_tokens = lax.all_to_all(lin_both, "seq", split_axis=0, concat_axis=1, tiled=True)
-    whole_sums = {j: add_rounded(whole_out[j], piece) for j, piece in zip(order, whole_odd)}
-    grad_out = add_all(
-        reduce_singles(whole_sums, reduce_several(whole_sums, "shard"), "shard")
-    ).astype(bf16)
-    grad_out, output_sum, both_tokens = lax.optimization_barrier(
-        (grad_out, add_all(out_pieces), both_tokens)
-    )
-    output = (residual + output_sum).astype(bf16)
+    lin_all = jnp.concatenate([lin_query, lin_key, value_low], axis=1)
+    all_columns = lin_all.shape[1]
+    lin_all, out_pieces, whole_sums = lax.optimization_barrier((lin_all, out_pieces, whole_sums))
+    lin_tokens = lax.all_to_all(lin_all, "seq", split_axis=0, concat_axis=1, tiled=True)
+
+    small_grad = jnp.concatenate([grad_router, grad_gain_ffn[:, None]], axis=1)
+    grad_qkv = jnp.concatenate([transposed_times(normed_low, lin_all), small_grad], axis=1)
+    grad_qkv = reduce_rows(grad_qkv.astype(bf16), "shard")
+    output = (residual + add_all(out_pieces)).astype(bf16)
+    grad_out = add_all(reduce_singles(whole_sums, whole_pending, "shard")).astype(bf16)
     grad_out = grad_out.reshape(grad_out.shape[0], seq_count, -1).transpose(1, 0, 2)
     grad_out = scatter_direct(grad_out, "seq").T
+    hidden_units = w_gate.shape[2]
+    grad_down = grad_down.T.reshape(local_experts, hidden_units, -1).astype(jnp.float32)
+    first_grads = pre_grads[0].astype(jnp.float32)
+    lin_tokens, grad_out, output, grad_down, first_grads = lax.optimization_barrier(
+        (lin_tokens, grad_out, output, grad_down, first_grads)
+    )
+    pre_grads = [first_grads] + [part.astype(jnp.float32) for part in pre_grads[1:]]
     parts = [0.0, 0.0]
-    for lin, first, last in (
-        (query_tokens, 0, query_width),
-        (both_tokens, query_width, query_width + 2 * key_width),
-    ):
-        for k, weight in enumerate((wide_half, other_half)):
-            for group_index in range(seq_count):
-                columns = slice(group_index * (last - first), (group_index + 1) * (last - first))
-                parts[k] = parts[k] + times_transposed(
-                    lin[:, columns], weight[group_index, :, first:last]
-                )
+    for k, weight in enumerate((wide_half, other_half)):
+        for group_index in range(seq_count):
+            columns = slice(group_index * all_columns, (group_index + 1) * all_columns)
+            parts[k] = parts[k] + times_transposed(lin_tokens[:, columns], weight[group_index])
     normed_grad = jnp.concatenate(
         [
             jnp.where(core_bit == 0, parts[0], parts[1]),
@@ -984,21 +956,8 @@
         ],
         axis=1,
     )
-    small_grad = jnp.concatenate([grad_router, grad_gain_ffn[:, None]], axis=1)
-    grad_qkv = jnp.concatenate(
-        [
-            transposed_times(normed_low, lin_query),
-            transposed_times(normed_low, lin_both),
-            small_grad,
-        ],
-        axis=1,
-    )
-    grad_qkv = reduce_blocks(
-        relative_blocks(grad_qkv.astype(bf16), shard_index, shard_count), "shard"
-    )
     own_features = own_weight.shape[0]
     gain_own = lax.dynamic_slice_in_dim(first_gain, shard_index * own_features, own_features)
-    all_columns = own_weight.shape[1]
     gain_part = (
         jnp.sum(own_weight.astype(jnp.float32) * grad_qkv[:, :all_columns], axis=1) / gain_own
     )
@@ -1012,11 +971,6 @@
     own_factor = rms_parts(own_inputs)
     input_part, _ = rms_backward(own_inputs, own_factor, first_gain, normed_grad)
     tokens_grad = residual_grad + input_part
-    pre_grads = [
-        lax.psum_scatter(part, "seq", scatter_dimension=0, tiled=True) for part in pre_sums
-    ]
-    hidden_units = w_gate.shape[2]
-    grad_down = grad_down.T.reshape(local_experts, hidden_units, -1)
     grad_gate = jnp.stack([part[:, :hidden_units] for part in pre_grads])
     grad_up = jnp.stack([part[:, hidden_units:] for part in pre_grads])
     return (
@@ -1029,9 +983,9 @@
         small_grad[:, experts_all + 1],
         small_grad[:, experts_all],
         small_grad[:, :experts_all],
-        grad_gate.astype(jnp.float32),
-        grad_up.astype(jnp.float32),
-        grad_down.astype(jnp.float32),
+        grad_gate,
+        grad_up,
+        grad_down,
     )
 
 

time: 680 us -> 625 us (0.919)
  local copies, waits for them, and re-layouts: 96.7 us -> 48.9 us
  matrix products: 112 us -> 72.4 us
  waiting for transfers between devices: 107 us -> 142 us
  blocking collectives: 42.3 us -> 75.8 us
  starting transfers between devices: 78.7 us -> 52.7 us
    ppermute x6, waiting for transfers between devices: 0.02 us -> 51.3 us  [scatter_direct(): lax.ppermute(piece, axis_name, [(i, (i + step) % count) for i in range(co...]
    ppermute x12 -> x0, waiting for transfers between devices: 32.8 us -> none  [pass_on(): return lax.ppermute(values, axis_name, pairs)]
    all_gather x2 -> x3, blocking collectives: 23.4 us -> 47.1 us  [the longest x1 24.9 us: on_device(): out_weight = lax.all_gather(w_out, 'seq', axis=0, tiled=True)]
    dot_general x14 -> x6, matrix products: 73.8 us -> 50.7 us  [transposed_times(): lax.dot_general(left_side, right_side, (((0,), (0,)), ((), ())), precisio...]
    unnamed x173 -> x116, local copies, waits for them, and re-layouts: 39 us -> 16.3 us
    all_to_all x1, waiting for transfers between devices: 0.01 us -> 21.5 us  [on_device(): lax.all_to_all(mixed_grad_tokens, 'seq', split_axis=1, concat_axis=0, til...]
    ppermute x12 -> x0, starting transfers between devices: 20.2 us -> none  [pass_on(): return lax.ppermute(values, axis_name, pairs)]
    dot_general x18 -> x10, matrix products: 28.2 us -> 12.3 us  [times_transposed(): lax.dot_general(left_side, right_side, (((1,), (1,)), ((), ())), precisio...]
  transfers between devices with their start and end apart: 84 -> 63, of which waited for: 20 -> 19; matrix products, arithmetic and copies ran while one was open for 38% -> 25% of each run, Pallas kernels for 22% -> 24%
where the time goes in v6:
time: 625 us; the launch traced here: 617 us
  Pallas kernels  148 us (24%)
  waiting for transfers between devices  142 us (23%)
  blocking collectives  75.8 us (12%)
  matrix products  72.4 us (12%)
  other arithmetic  61.5 us (10%)
  starting transfers between devices  52.7 us (8%)
  local copies, waits for them, and re-layouts  48.9 us (8%)
  between operations  15.7 us (3%)
    pallas_call x4, Pallas kernels, expert_pair(): pl.pallas_call(partial(expert_body, experts_all), out_shape=out_shape, gr...  87 us
    ppermute x6, waiting for transfers between devices, scatter_direct(): lax.ppermute(piece, axis_name, [(i, (i + step) % count) for i in range(co...  51.3 us
    dot_general x6, matrix products, transposed_times(): lax.dot_general(left_side, right_side, (((0,), (0,)), ((), ())), precisio...  50.7 us
    ppermute x48, waiting for transfers between devices, exchange(): return lax.ppermute(values, axis_name, [(i, i ^ bit) for i in range(count)])  47.6 us
    pallas_call x1, Pallas kernels, attend_backward(): pl.pallas_call(partial(attend_backward_body, group, kv_heads), out_shape=...  36.3 us
    ppermute x48, starting transfers between devices, exchange(): return lax.ppermute(values, axis_name, [(i, i ^ bit) for i in range(count)])  30.9 us
    all_gather x1, blocking collectives, on_device(): kv_prompt = lax.all_gather(kv_own[:PROMPT_BLK], 'shard', axis=0, tiled=True)  28.7 us
    convert_element_type x15, other arithmetic, add_rounded(): (left_side.astype(jnp.float32) + right_side.astype(jnp.float32)).astype(j...  26.2 us
  transfers between devices with their start and end apart: 63, of which 19 were waited for; matrix products, arithmetic and copies ran while one was open for 25% of the time, Pallas kernels for 24%

profile of v6, /device:TPU:0, one launch (start us, length us, event | category | flops | bytes accessed | tf_op | source)
XLA Modules:
  0.0 616.8 jit_solution(10401371386087129469)
XLA Ops:
  11.1 2.6 collective-permute-start.5
  15.2 24.9 %all_gather.28 = bf16[1536,192]{0,1:T(8,128)(2,1)} all-gather(bf16[384,192]{0,1:T(8,128)(2,1)} %param.18), channel_id=1, replica_groups=mesh['shard'=8,'seq'=4] {'seq'}, dimensions={0}, use_global_device_ids=true | all-gather | bytes 737280 | tf_op jit(solution)/shard_map/all_gather | solution.py:733
  40.2 14.4 %all-gather.1 = bf16[4,48,18]{1,2,0:T(8,128)(2,1)S(1)} all-gather(bf16[1,48,18]{1,2,0:T(8,128)(2,1)S(1)} %maximum_bitcast_fusion.1), channel_id=1, replica_groups=mesh['shard'=8,'seq'=4] {'seq'}, dimensions={0}, use_global_device_ids=true | all-gather | bytes 8640 | tf_op jit(solution)/shard_map/all_gather | solution.py:725
  54.7 7.8 %all-gather.2 = bf16[8,192,18]{1,2,0:T(8,128)(2,1)S(1)} all-gather(bf16[1,192,18]{1,2,0:T(8,128)(2,1)S(1)} %reshape.382), channel_id=1, replica_groups=mesh['shard'=8,'seq'=4] {'shard'}, dimensions={0}, use_global_device_ids=true | all-gather | bytes 62208 | tf_op jit(solution)/shard_map/all_gather | solution.py:726
  64.5 1.9 collective-permute-start.1
  66.6 6.2 %collective-permute-done.1 = bf16[192,640]{1,0:T(8,128)(2,1)S(1)} collective-permute-done((bf16[192,640]{1,0:T(8,128)(2,1)S(1)}, bf16[192,640]{1,0:T(8,128)(2,1)S(1)}, u32[]{:S(2)}, u32[]{:S(2)}) %collective-permute-start.1) | collective-permute-done | bytes 245792 | tf_op jit(solution)/shard_map/ppermute | solution.py:445
  72.7 1.7 collective-permute-start.2
  75.5 2.3 collective-permute-done.8
  79.4 16.0 %collective-permute-done.3.og_even = bf16[288,1536]{1,0:T(8,128)(2,1)} collective-permute-done((bf16[288,1536]{1,0:T(8,128)(2,1)}, bf16[288,1536]{1,0:T(8,128)(2,1)}, u32[]{:S(2)}, u32[]{:S(2)}) %collective-permute-start.3) | collective-permute-done | bytes 884768 | tf_op jit(solution)/shard_map/ppermute | solution.py:445
  96.2 3.1 fusion
  99.4 4.7 fusion.24
  107.7 28.7 %all_gather.27.kp_ref.vp_ref = bf16[1024,256]{1,0:T(8,128)(2,1)} all-gather(bf16[128,256]{1,0:T(8,128)(2,1)S(1)} %fusion.63), channel_id=1, replica_groups=mesh['shard'=8,'seq'=4] {'shard'}, dimensions={0}, use_global_device_ids=true | all-gather | bytes 589824 | tf_op jit(solution)/shard_map/all_gather | solution.py:759
  137.7 25.0 %attend_forward.1 = (bf16[1152,384]{1,0:T(8,128)(2,1)}, f32[6,1,1152]{2,1,0:T(1,128)}) custom-call(s32[1]{0:T(128)} %bitcast.index_ref, bf16[1152,384]{1,0:T(8,128)(2,1)} %copy.142.q_ref, bf16[1024,256]{1,0:T(8,128)(2,1)} %all_gather.27.kp_ref.vp_ref, bf16[1024,256]{1,0:T(8,128)(2,1)} %all_gather.27.kp_ref.vp_ref, ...), custom_call_target="tpu_custom_call" | custom-call | flops 9059696640 | bytes 3538944 | tf_op jit(solution)/shard_map/attend_forward/pallas_call | solution.py:376
  162.7 4.8 all-to-all-start
  167.6 2.3 constant_dynamic-slice_fusion.8
  170.0 20.3 %all-to-all-done = bf16[4,288,384]{2,1,0:T(8,128)(2,1)S(1)} async-done(((bf16[4,288,384]{2,1,0:T(8,128)(2,1)}), bf16[4,288,384]{2,1,0:T(8,128)(2,1)S(1)}, u32[]{:S(2)}, u32[]{:S(2)}) %all-to-all-start) | async-done | bytes 884768 | tf_op jit(solution)/shard_map/all_to_all | solution.py:769
  191.2 4.3 multiply_reduce_fusion.2
  200.7 21.4 %experts.4 = (bf16[2304,1536]{1,0:T(8,128)(2,1)}, bf16[2304,1536]{1,0:T(8,128)(2,1)}, bf16[2,2304,1024]{2,1,0:T(8,128)(2,1)}, bf16[2304,1024]{1,0:T(8,128)(2,1)}...) custom-call(s32[1]{0:T(128)} %bitcast.19.index_ref, ...), custom_call_target="tpu_custom_call" | custom-call | flops 10871635968 | bytes 27131904 | tf_op jit(solution)/shard_map/experts/pallas_call | solution.py:665
  225.8 22.1 %experts.5 = (bf16[2304,1536]{1,0:T(8,128)(2,1)}, bf16[2304,1536]{1,0:T(8,128)(2,1)}, bf16[2,2304,1024]{2,1,0:T(8,128)(2,1)}, bf16[2304,1024]{1,0:T(8,128)(2,1)}...) custom-call(s32[1]{0:T(128)} %bitcast.19.index_ref, ...), custom_call_target="tpu_custom_call", output_to_operand_aliasing={{0}: (8, {}), {1}: (9, {}), {2}: (10, {}), {3}: (11, {})} | custom-call | flops 10871635968 | bytes 27131904 | tf_op jit(solution)/shard_map/experts/pallas_call | solution.py:665
  249.1 3.0 collective-permute-done.22.og_odd
  252.1 21.9 %experts.6 = (bf16[2304,1536]{1,0:T(8,128)(2,1)}, bf16[2304,1536]{1,0:T(8,128)(2,1)}, bf16[2,2304,1024]{2,1,0:T(8,128)(2,1)}, bf16[2304,1024]{1,0:T(8,128)(2,1)}...) custom-call(s32[1]{0:T(128)} %bitcast.19.index_ref, ...), custom_call_target="tpu_custom_call", output_to_operand_aliasing={{0}: (8, {}), {1}: (9, {}), {2}: (10, {}), {3}: (11, {})} | custom-call | flops 10871635968 | bytes 27131904 | tf_op jit(solution)/shard_map/experts/pallas_call | solution.py:665
  274.3 2.7 add_convert_fusion.4
  277.0 2.5 add_convert_fusion.3
  281.1 21.6 %experts.7 = (bf16[2304,1536]{1,0:T(8,128)(2,1)}, bf16[2304,1536]{1,0:T(8,128)(2,1)}, bf16[2,2304,1024]{2,1,0:T(8,128)(2,1)}, bf16[2304,1024]{1,0:T(8,128)(2,1)}...) custom-call(s32[1]{0:T(128)} %bitcast.19.index_ref, ...), custom_call_target="tpu_custom_call", output_to_operand_aliasing={{0}: (8, {}), {1}: (9, {}), {2}: (10, {}), {3}: (11, {})} | custom-call | flops 10871635968 | bytes 27131904 | tf_op jit(solution)/shard_map/experts/pallas_call | solution.py:665
  302.7 1.7 collective-permute-done.24
  305.0 2.4 collective-permute-done.25
  307.3 2.8 add_convert_fusion.1
  310.1 2.4 add_convert_fusion
  314.2 11.1 %convolution_convert_fusion.1 = bf16[1536,1024]{1,0:T(8,128)(2,1)} fusion(bf16[2304,1536]{1,0:T(8,128)(2,1)} %get-tuple-element.193, bf16[2304,1024]{1,0:T(8,128)(2,1)S(1)} %copy-done), kind=kOutput, calls=%fused_computation.16 | convolution fusion | flops 7249330176 | bytes 14942208 | tf_op jit(solution)/shard_map/dot_general | solution.py:71
  325.4 13.0 %fusion.10 = bf16[1536,1024]{1,0:T(8,128)(2,1)} fusion(bf16[2304,1536]{1,0:T(8,128)(2,1)} %get-tuple-element.215, bf16[2,2304,1024]{2,1,0:T(8,128)(2,1)} %get-tuple-element.196), kind=kOutput, calls=%fused_computation.14 | convolution fusion | flops 7249330176 | bytes 14942208 | tf_op jit(solution)/shard_map/dot_general | solution.py:71
  338.3 2.2 convert_add_fusion.3
  342.3 1.7 subtract_add_fusion
  346.6 4.2 all-to-all-start.1
  352.0 4.4 convolution_convert_fusion
  359.3 13.0 %fusion.13 = bf16[1536,1024]{1,0:T(8,128)(2,1)} fusion(bf16[2304,1536]{1,0:T(8,128)(2,1)} %get-tuple-element.215, bf16[2,2304,1024]{2,1,0:T(8,128)(2,1)} %get-tuple-element.196), kind=kOutput, calls=%fused_computation.15 | convolution fusion | flops 7249330176 | bytes 14942208 | tf_op jit(solution)/shard_map/dot_general | solution.py:71
  372.3 2.6 add_convert_fusion.10
  376.2 21.5 %all-to-all-done.1 = bf16[288,4,384]{2,0,1:T(8,128)(2,1)} async-done(((bf16[288,4,384]{2,0,1:T(8,128)(2,1)}), bf16[288,4,384]{2,0,1:T(8,128)(2,1)}, u32[]{:S(2)}, u32[]{:S(2)}) %all-to-all-start.1) | async-done | bytes 884768 | tf_op jit(solution)/shard_map/all_to_all | solution.py:874
  401.7 1.7 add_convert_fusion.6
  404.6 2.3 add_convert_fusion.9
  406.9 1.8 add_convert_fusion.7
  410.3 3.0 fusion.3
  415.4 36.3 %attend_backward.1 = (bf16[1152,384]{1,0:T(8,128)(2,1)}, bf16[1024,256]{1,0:T(8,128)(2,1)}, f32[1152,256]{1,0:T(8,128)}) custom-call(s32[1]{0:T(128)} %bitcast.index_ref, bf16[1152,384]{1,0:T(8,128)(2,1)} %copy.142.q_ref, bf16[1152,384]{1,0:T(8,128)(2,1)} %bitcast.23.grad_ref, bf16[1152,384]{1,0:T(8,128)(2,1)} %get-tuple-element.139.mixed_ref, ...), custom_call_target="tpu_custom_call" | custom-call | flops 22649241600 | bytes 3538944 | tf_op jit(solution)/shard_map/attend_backward/pallas_call | solution.py:406
  468.3 2.4 maximum_maximum_fusion
  470.7 7.7 %convolution_convert_fusion.2 = bf16[1536,640]{1,0:T(8,128)(2,1)} fusion(bf16[1152,640]{1,0:T(8,128)(2,1)} %maximum_maximum_fusion, bf16[1152,1536]{1,0:T(8,128)(2,1)} %all-gather.7.cloned.1.call-done, f32[1536]{0:T(1024)S(1)} %get-tuple-element.333, f32[1152]{0:T(1024)S(1)} %copy-done.38), kind=kOutput, calls=%fused_computation.17 | convolution fusion | flops 2272985088 | bytes 6990336 | tf_op jit(solution)/shard_map/dot_general | solution.py:71
  478.4 4.9 all-to-all-start.2
  483.4 2.2 pad_maximum_fusion
  492.1 7.5 %collective-permute-done.43 = bf16[192,1536]{1,0:T(8,128)(2,1)S(1)} collective-permute-done((bf16[192,1536]{1,0:T(8,128)(2,1)}, bf16[192,1536]{1,0:T(8,128)(2,1)S(1)}, u32[]{:S(2)}, u32[]{:S(2)}) %collective-permute-start.43) | collective-permute-done | bytes 589856 | tf_op jit(solution)/shard_map/ppermute | solution.py:445
  499.6 2.1 collective-permute-done.42
  506.2 3.8 collective-permute-start.46
  512.5 2.0 collective-permute-start.50
  514.5 1.8 fusion.40
  517.9 2.5 reshape.366
  520.4 18.0 %collective-permute-done.46 = bf16[192,384]{1,0:T(8,128)(2,1)} collective-permute-done((bf16[192,384]{1,0:T(8,128)(2,1)}, bf16[192,384]{1,0:T(8,128)(2,1)}, u32[]{:S(2)}, u32[]{:S(2)}) %collective-permute-start.46) | collective-permute-done | bytes 147488 | tf_op jit(solution)/shard_map/ppermute | solution.py:543
  538.4 31.3 %collective-permute-done.45 = bf16[192,384]{1,0:T(8,128)(2,1)} collective-permute-done((bf16[192,384]{1,0:T(8,128)(2,1)}, bf16[192,384]{1,0:T(8,128)(2,1)}, u32[]{:S(2)}, u32[]{:S(2)}) %collective-permute-start.45) | collective-permute-done | bytes 147488 | tf_op jit(solution)/shard_map/ppermute | solution.py:543
  569.6 1.8 fusion.56
  573.8 1.9 collective-permute-start.51
  583.1 2.6 convert_element_type.441
  585.7 1.7 fusion.34
  588.0 1.7 convolution_add_fusion.3
  589.7 1.8 convolution_add_fusion.2
  591.5 1.8 convolution_add_fusion.1
  600.7 3.7 copy.153
  604.5 3.3 fusion.20
  607.8 2.0 pad_maximum_fusion.1
  (328 shorter events, 98.5 us)
Async XLA Ops:
  7.2 89.0 %all-gather.7.cloned.1.call-start = ((), (), s32[]{:S(2)}) async-start(), calls=%async_computation.6 | async-start | bytes 4423680 | tf_op jit(solution)/shard_map/all_gather | solution.py:730
  7.9 183.3 %all-gather.9.cloned.1.call-start = ((), (), s32[]{:S(2)}) async-start(), calls=%async_computation.7 | async-start | bytes 5308416 | tf_op jit(solution)/shard_map/all_gather | solution.py:734
  10.6 55.9 %collective-permute-start.4 = (bf16[192,640]{1,0:T(8,128)(2,1)S(1)}, bf16[192,640]{1,0:T(8,128)(2,1)S(1)}, u32[]{:S(2)}, u32[]{:S(2)}) collective-permute-start(bf16[192,640]{1,0:T(8,128)(2,1)S(1)} %constant_dynamic-update-slice_fusion), channel_id=1, source_target_pairs={{0,4},{4,0},{8,12},{12,8},{16,20},{20,16},{24,28},{28,24},{1,5},{5... | collective-permute-start | bytes 737288 | tf_op jit(solution)/shard_map/ppermute | solution.py:445
  11.1 55.3 %collective-permute-start.5 = (bf16[192,640]{1,0:T(8,128)(2,1)S(1)}, bf16[192,640]{1,0:T(8,128)(2,1)S(1)}, u32[]{:S(2)}, u32[]{:S(2)}) collective-permute-start(bf16[192,640]{1,0:T(8,128)(2,1)S(1)} %constant_dynamic-update-slice_fusion), channel_id=1, source_target_pairs={{0,8},{4,12},{8,0},{12,4},{16,24},{20,28},{24,16},{28,20},{1,9},{5... | collective-permute-start | bytes 737288 | tf_op jit(solution)/shard_map/ppermute | solution.py:445
  13.7 50.4 %collective-permute-start = (bf16[192,640]{1,0:T(8,128)(2,1)S(1)}, bf16[192,640]{1,0:T(8,128)(2,1)S(1)}, u32[]{:S(2)}, u32[]{:S(2)}) collective-permute-start(bf16[192,640]{1,0:T(8,128)(2,1)S(1)} %constant_dynamic-update-slice_fusion), channel_id=1, source_target_pairs={{0,16},{4,20},{8,24},{12,28},{16,0},{20,4},{24,8},{28,12},{1,17},{... | collective-permute-start | bytes 737288 | tf_op jit(solution)/shard_map/ppermute | solution.py:445
  62.7 278.1 %copy-start.35 = (bf16[1536,18]{0,1:T(8,128)(2,1)}, bf16[1536,18]{0,1:T(8,128)(2,1)S(1)}, u32[]{:S(2)}) copy-start(bf16[1536,18]{0,1:T(8,128)(2,1)S(1)} %reshape.383) | copy-start | bytes 165892
  64.1 11.3 %collective-permute-start.7 = (bf16[192,640]{1,0:T(8,128)(2,1)S(1)}, bf16[192,640]{1,0:T(8,128)(2,1)S(1)}, u32[]{:S(2)}, u32[]{:S(2)}) collective-permute-start(bf16[192,640]{1,0:T(8,128)(2,1)S(1)} %collective-permute-done), channel_id=1, source_target_pairs={{0,4},{4,0},{8,12},{12,8},{16,20},{20,16},{24,28},{28,24},{1,5},{5... | collective-permute-start | bytes 737288 | tf_op jit(solution)/shard_map/ppermute | solution.py:445
  64.5 8.2 %collective-permute-start.1 = (bf16[192,640]{1,0:T(8,128)(2,1)S(1)}, bf16[192,640]{1,0:T(8,128)(2,1)S(1)}, u32[]{:S(2)}, u32[]{:S(2)}) collective-permute-start(bf16[192,640]{1,0:T(8,128)(2,1)S(1)} %collective-permute-done), channel_id=1, source_target_pairs={{0,8},{4,12},{8,0},{12,4},{16,24},{20,28},{24,16},{28,20},{1,9},{5... | collective-permute-start | bytes 737288 | tf_op jit(solution)/shard_map/ppermute | solution.py:445
  66.5 8.3 %collective-permute-start.6 = (bf16[192,640]{1,0:T(8,128)(2,1)S(1)}, bf16[192,640]{1,0:T(8,128)(2,1)S(1)}, u32[]{:S(2)}, u32[]{:S(2)}) collective-permute-start(bf16[192,640]{1,0:T(8,128)(2,1)S(1)} %collective-permute-done.5), channel_id=1, source_target_pairs={{0,4},{4,0},{8,12},{12,8},{16,20},{20,16},{24,28},{28,24},{1,5},{5... | collective-permute-start | bytes 737288 | tf_op jit(solution)/shard_map/ppermute | solution.py:445
  72.7 23.2 %collective-permute-start.2 = (bf16[288,1536]{1,0:T(8,128)(2,1)}, bf16[288,1536]{1,0:T(8,128)(2,1)}, u32[]{:S(2)}, u32[]{:S(2)}) collective-permute-start(bf16[288,1536]{1,0:T(8,128)(2,1)} %og_even), channel_id=1, source_target_pairs={{0,8},{4,12},{8,0},{12,4},{16,24},{20,28},{24,16},{28,20},{1,9},{5... | collective-permute-start | bytes 2654216 | tf_op jit(solution)/shard_map/ppermute | solution.py:445
  74.5 21.0 %collective-permute-start.3 = (bf16[288,1536]{1,0:T(8,128)(2,1)}, bf16[288,1536]{1,0:T(8,128)(2,1)}, u32[]{:S(2)}, u32[]{:S(2)}) collective-permute-start(bf16[288,1536]{1,0:T(8,128)(2,1)} %og_even), channel_id=1, source_target_pairs={{0,16},{4,20},{8,24},{12,28},{16,0},{20,4},{24,8},{28,12},{1,17},{... | collective-permute-start | bytes 2654216 | tf_op jit(solution)/shard_map/ppermute | solution.py:445
  74.8 87.9 %collective-permute-start.9 = (bf16[288,1536]{1,0:T(8,128)(2,1)}, bf16[288,1536]{1,0:T(8,128)(2,1)}, u32[]{:S(2)}, u32[]{:S(2)}) collective-permute-start(bf16[288,1536]{1,0:T(8,128)(2,1)} %og_even), channel_id=1, source_target_pairs={{0,4},{4,0},{8,12},{12,8},{16,20},{20,16},{24,28},{28,24},{1,5},{5... | collective-permute-start | bytes 2654216 | tf_op jit(solution)/shard_map/ppermute | solution.py:445
  74.8 3.0 collective-permute-start.8
  95.5 67.2 %collective-permute-start.11 = (bf16[288,1536]{1,0:T(8,128)(2,1)}, bf16[288,1536]{1,0:T(8,128)(2,1)}, u32[]{:S(2)}, u32[]{:S(2)}) collective-permute-start(bf16[288,1536]{1,0:T(8,128)(2,1)} %collective-permute-done.3.og_even), channel_id=1, source_target_pairs={{0,4},{4,0},{8,12},{12,8},{16,20},{20,16},{24,28},{28,24},{1,5},{5... | collective-permute-start | bytes 2654216 | tf_op jit(solution)/shard_map/ppermute | solution.py:445
  95.5 67.2 %collective-permute-start.12 = (bf16[288,1536]{1,0:T(8,128)(2,1)}, bf16[288,1536]{1,0:T(8,128)(2,1)}, u32[]{:S(2)}, u32[]{:S(2)}) collective-permute-start(bf16[288,1536]{1,0:T(8,128)(2,1)} %collective-permute-done.3.og_even), channel_id=1, source_target_pairs={{0,8},{4,12},{8,0},{12,4},{16,24},{20,28},{24,16},{28,20},{1,9},{5... | collective-permute-start | bytes 2654216 | tf_op jit(solution)/shard_map/ppermute | solution.py:445
  96.0 66.7 %collective-permute-start.10 = (bf16[288,1536]{1,0:T(8,128)(2,1)}, bf16[288,1536]{1,0:T(8,128)(2,1)}, u32[]{:S(2)}, u32[]{:S(2)}) collective-permute-start(bf16[288,1536]{1,0:T(8,128)(2,1)} %collective-permute-done.2.og_even), channel_id=1, source_target_pairs={{0,4},{4,0},{8,12},{12,8},{16,20},{20,16},{24,28},{28,24},{1,5},{5... | collective-permute-start | bytes 2654216 | tf_op jit(solution)/shard_map/ppermute | solution.py:445
  162.7 27.5 %all-to-all-start = ((bf16[4,288,384]{2,1,0:T(8,128)(2,1)}), bf16[4,288,384]{2,1,0:T(8,128)(2,1)S(1)}, u32[]{:S(2)}, u32[]{:S(2)}) async-start(bf16[4,288,384]{2,1,0:T(8,128)(2,1)} %bitcast.212), calls=%async_computation | async-start | bytes 1769472 | tf_op jit(solution)/shard_map/all_to_all | solution.py:769
  167.5 137.0 %all-gather.11.cloned.1.call-start = ((), (), s32[]{:S(2)}) async-start(), calls=%async_computation.11 | async-start | bytes 4915200 | tf_op jit(solution)/shard_map/all_gather | solution.py:779
  197.8 2.9 collective-permute-start.15
  197.8 24.3 %collective-permute-start.13 = (bf16[288,1664]{1,0:T(8,128)(2,1)}, bf16[288,1664]{1,0:T(8,128)(2,1)}, u32[]{:S(2)}, u32[]{:S(2)}) collective-permute-start(bf16[288,1664]{1,0:T(8,128)(2,1)} %concatenate.68.x_even), channel_id=1, source_target_pairs={{0,8},{4,12},{8,0},{12,4},{16,24},{20,28},{24,16},{28,20},{1,9},{5... | collective-permute-start | bytes 2875400 | tf_op jit(solution)/shard_map/ppermute | solution.py:445
  199.3 23.7 %collective-permute-start.14 = (bf16[288,1664]{1,0:T(8,128)(2,1)}, bf16[288,1664]{1,0:T(8,128)(2,1)}, u32[]{:S(2)}, u32[]{:S(2)}) collective-permute-start(bf16[288,1664]{1,0:T(8,128)(2,1)} %concatenate.68.x_even), channel_id=1, source_target_pairs={{0,16},{4,20},{8,24},{12,28},{16,0},{20,4},{24,8},{28,12},{1,17},{... | collective-permute-start | bytes 2875400 | tf_op jit(solution)/shard_map/ppermute | solution.py:445
  222.9 2.9 collective-permute-start.19
  223.0 293.6 %reduce-scatter.4.cloned.1.call-start = ((), (), s32[]{:S(2)}) async-start(), calls=%async_computation.8 | async-start | bytes 3932160 | tf_op jit(solution)/shard_map/reduce_scatter | solution.py:849
  223.3 24.6 %collective-permute-start.18 = (bf16[288,1664]{1,0:T(8,128)(2,1)}, bf16[288,1664]{1,0:T(8,128)(2,1)}, u32[]{:S(2)}, u32[]{:S(2)}) collective-permute-start(bf16[288,1664]{1,0:T(8,128)(2,1)} %collective-permute-done.14.x_even), channel_id=1, source_target_pairs={{0,8},{4,12},{8,0},{12,4},{16,24},{20,28},{24,16},{28,20},{1,9},{5... | collective-permute-start | bytes 2875400 | tf_op jit(solution)/shard_map/ppermute | solution.py:445
  247.9 4.2 collective-permute-start.21
  248.0 4.0 collective-permute-start.22
  248.5 32.2 %collective-permute-start.16 = (bf16[288,1664]{1,0:T(8,128)(2,1)}, bf16[288,1664]{1,0:T(8,128)(2,1)}, u32[]{:S(2)}, u32[]{:S(2)}) collective-permute-start(bf16[288,1664]{1,0:T(8,128)(2,1)} %collective-permute-done.14.x_even), channel_id=1, source_target_pairs={{0,4},{4,0},{8,12},{12,8},{16,20},{20,16},{24,28},{28,24},{1,5},{5... | collective-permute-start | bytes 2875400 | tf_op jit(solution)/shard_map/ppermute | solution.py:445
  248.6 25.7 %collective-permute-start.17 = (bf16[288,1664]{1,0:T(8,128)(2,1)}, bf16[288,1664]{1,0:T(8,128)(2,1)}, u32[]{:S(2)}, u32[]{:S(2)}) collective-permute-start(bf16[288,1664]{1,0:T(8,128)(2,1)} %get-tuple-element.148), channel_id=1, source_target_pairs={{0,4},{4,0},{8,12},{12,8},{16,20},{20,16},{24,28},{28,24},{1,5},{5... | collective-permute-start | bytes 2875400 | tf_op jit(solution)/shard_map/ppermute | solution.py:445
  249.0 28.0 %collective-permute-start.20 = (bf16[288,1664]{1,0:T(8,128)(2,1)}, bf16[288,1664]{1,0:T(8,128)(2,1)}, u32[]{:S(2)}, u32[]{:S(2)}) collective-permute-start(bf16[288,1664]{1,0:T(8,128)(2,1)} %get-tuple-element.161), channel_id=1, source_target_pairs={{0,4},{4,0},{8,12},{12,8},{16,20},{20,16},{24,28},{28,24},{1,5},{5... | collective-permute-start | bytes 2875400 | tf_op jit(solution)/shard_map/ppermute | solution.py:445
  274.0 5.4 collective-permute-start.23
  280.7 23.8 %collective-permute-start.24 = (bf16[288,1664]{1,0:T(8,128)(2,1)}, bf16[288,1664]{1,0:T(8,128)(2,1)}, u32[]{:S(2)}, u32[]{:S(2)}) collective-permute-start(bf16[288,1664]{1,0:T(8,128)(2,1)} %add_convert_fusion.2), channel_id=1, source_target_pairs={{0,16},{4,20},{8,24},{12,28},{16,0},{20,4},{24,8},{28,12},{1,17},{... | collective-permute-start | bytes 2875400 | tf_op jit(solution)/shard_map/ppermute | solution.py:445
  304.4 2.9 collective-permute-start.25
  304.4 41.2 %collective-permute-start.28 = (bf16[4,768,640]{2,1,0:T(8,128)(2,1)}, bf16[4,768,640]{2,1,0:T(8,128)(2,1)}, u32[]{:S(2)}, u32[]{:S(2)}) collective-permute-start(bf16[4,768,640]{2,1,0:T(8,128)(2,1)} %bitcast.201), channel_id=1, source_target_pairs={{0,4},{4,0},{8,12},{12,8},{16,20},{20,16},{24,28},{28,24},{1,5},{5... | collective-permute-start | bytes 11796488 | tf_op jit(solution)/shard_map/ppermute | solution.py:445
  312.5 25.8 %collective-permute-start.26 = (bf16[288,1664]{1,0:T(8,128)(2,1)}, bf16[288,1664]{1,0:T(8,128)(2,1)}, u32[]{:S(2)}, u32[]{:S(2)}) collective-permute-start(bf16[288,1664]{1,0:T(8,128)(2,1)} %add_convert_fusion), channel_id=1, source_target_pairs={{0,8},{4,12},{8,0},{12,4},{16,24},{20,28},{24,16},{28,20},{1,9},{5... | collective-permute-start | bytes 2875400 | tf_op jit(solution)/shard_map/ppermute | solution.py:445
  312.9 25.4 %collective-permute-start.27 = (bf16[288,1664]{1,0:T(8,128)(2,1)}, bf16[288,1664]{1,0:T(8,128)(2,1)}, u32[]{:S(2)}, u32[]{:S(2)}) collective-permute-start(bf16[288,1664]{1,0:T(8,128)(2,1)} %add_convert_fusion.1), channel_id=1, source_target_pairs={{0,16},{4,20},{8,24},{12,28},{16,0},{20,4},{24,8},{28,12},{1,17},{... | collective-permute-start | bytes 2875400 | tf_op jit(solution)/shard_map/ppermute | solution.py:445
  346.6 51.1 %all-to-all-start.1 = ((bf16[288,4,384]{2,0,1:T(8,128)(2,1)}), bf16[288,4,384]{2,0,1:T(8,128)(2,1)}, u32[]{:S(2)}, u32[]{:S(2)}) async-start(bf16[288,4,384]{2,0,1:T(8,128)(2,1)} %bitcast.202), calls=%async_computation.1 | async-start | bytes 1769472 | tf_op jit(solution)/shard_map/all_to_all | solution.py:874
  350.8 232.2 %reduce-scatter.6.cloned.1.call-start = ((), (), s32[]{:S(2)}) async-start(), calls=%async_computation.9 | async-start | bytes 3932160 | tf_op jit(solution)/shard_map/reduce_scatter | solution.py:893
  350.9 21.4 %collective-permute-start.29 = (bf16[288,1536]{1,0:T(8,128)(2,1)}, bf16[288,1536]{1,0:T(8,128)(2,1)}, u32[]{:S(2)}, u32[]{:S(2)}) collective-permute-start(bf16[288,1536]{1,0:T(8,128)(2,1)} %get-tuple-element.210), channel_id=1, source_target_pairs={{0,4},{4,0},{8,12},{12,8},{16,20},{20,16},{24,28},{28,24},{1,5},{5... | collective-permute-start | bytes 2654216 | tf_op jit(solution)/shard_map/ppermute | solution.py:445
  351.0 21.3 %collective-permute-start.30 = (bf16[288,1536]{1,0:T(8,128)(2,1)}, bf16[288,1536]{1,0:T(8,128)(2,1)}, u32[]{:S(2)}, u32[]{:S(2)}) collective-permute-start(bf16[288,1536]{1,0:T(8,128)(2,1)} %get-tuple-element.211), channel_id=1, source_target_pairs={{0,4},{4,0},{8,12},{12,8},{16,20},{20,16},{24,28},{28,24},{1,5},{5... | collective-permute-start | bytes 2654216 | tf_op jit(solution)/shard_map/ppermute | solution.py:445
  351.5 20.8 %collective-permute-start.31 = (bf16[288,1536]{1,0:T(8,128)(2,1)}, bf16[288,1536]{1,0:T(8,128)(2,1)}, u32[]{:S(2)}, u32[]{:S(2)}) collective-permute-start(bf16[288,1536]{1,0:T(8,128)(2,1)} %get-tuple-element.212), channel_id=1, source_target_pairs={{0,4},{4,0},{8,12},{12,8},{16,20},{20,16},{24,28},{28,24},{1,5},{5... | collective-permute-start | bytes 2654216 | tf_op jit(solution)/shard_map/ppermute | solution.py:445
  351.6 20.7 %collective-permute-start.32 = (bf16[288,1536]{1,0:T(8,128)(2,1)}, bf16[288,1536]{1,0:T(8,128)(2,1)}, u32[]{:S(2)}, u32[]{:S(2)}) collective-permute-start(bf16[288,1536]{1,0:T(8,128)(2,1)} %get-tuple-element.213), channel_id=1, source_target_pairs={{0,4},{4,0},{8,12},{12,8},{16,20},{20,16},{24,28},{28,24},{1,5},{5... | collective-permute-start | bytes 2654216 | tf_op jit(solution)/shard_map/ppermute | solution.py:445
  359.2 38.5 %collective-permute-start.34 = (bf16[4,192,1536]{2,1,0:T(8,128)(2,1)}, bf16[4,192,1536]{2,1,0:T(8,128)(2,1)}, u32[]{:S(2)}, u32[]{:S(2)}) collective-permute-start(bf16[4,192,1536]{2,1,0:T(8,128)(2,1)} %dynamic-slice_bitcast_fusion), channel_id=1, source_target_pairs={{0,4},{4,0},{8,12},{12,8},{16,20},{20,16},{24,28},{28,24},{1,5},{5... | collective-permute-start | bytes 7077896 | tf_op jit(solution)/shard_map/ppermute | solution.py:445
  374.9 22.8 %collective-permute-start.33 = (bf16[288,1536]{1,0:T(8,128)(2,1)}, bf16[288,1536]{1,0:T(8,128)(2,1)}, u32[]{:S(2)}, u32[]{:S(2)}) collective-permute-start(bf16[288,1536]{1,0:T(8,128)(2,1)} %add_convert_fusion.10), channel_id=1, source_target_pairs={{0,16},{4,20},{8,24},{12,28},{16,0},{20,4},{24,8},{28,12},{1,17},{... | collective-permute-start | bytes 2654216 | tf_op jit(solution)/shard_map/ppermute | solution.py:445
  397.7 198.7 %reduce-scatter.8.cloned.1.call-start = ((), (), s32[]{:S(2)}) async-start(), calls=%async_computation.10 | async-start | bytes 3932160 | tf_op jit(solution)/shard_map/reduce_scatter | solution.py:893
  403.4 48.2 %collective-permute-start.36 = (bf16[288,1536]{1,0:T(8,128)(2,1)S(1)}, bf16[288,1536]{1,0:T(8,128)(2,1)S(1)}, u32[]{:S(2)}, u32[]{:S(2)}) collective-permute-start(bf16[288,1536]{1,0:T(8,128)(2,1)S(1)} %add_convert_fusion.6), channel_id=1, source_target_pairs={{0,16},{4,20},{8,24},{12,28},{16,0},{20,4},{24,8},{28,12},{1,17},{... | collective-permute-start | bytes 2654216 | tf_op jit(solution)/shard_map/ppermute | solution.py:445
  408.6 43.1 %collective-permute-start.35 = (bf16[288,1536]{1,0:T(8,128)(2,1)S(1)}, bf16[288,1536]{1,0:T(8,128)(2,1)S(1)}, u32[]{:S(2)}, u32[]{:S(2)}) collective-permute-start(bf16[288,1536]{1,0:T(8,128)(2,1)S(1)} %add_convert_fusion.7), channel_id=1, source_target_pairs={{0,8},{4,12},{8,0},{12,4},{16,24},{20,28},{24,16},{28,20},{1,9},{5... | collective-permute-start | bytes 2654216 | tf_op jit(solution)/shard_map/ppermute | solution.py:445
  414.6 37.1 %collective-permute-start.37 = (bf16[192,1536]{1,0:T(8,128)(2,1)S(1)}, bf16[192,1536]{1,0:T(8,128)(2,1)S(1)}, u32[]{:S(2)}, u32[]{:S(2)}) collective-permute-start(bf16[192,1536]{1,0:T(8,128)(2,1)S(1)} %get-tuple-element.339), channel_id=1, source_target_pairs={{0,16},{4,20},{8,24},{12,28},{16,0},{20,4},{24,8},{28,12},{1,17},{... | collective-permute-start | bytes 1769480 | tf_op jit(solution)/shard_map/ppermute | solution.py:445
  452.9 1.6 collective-permute-start.38
  455.6 4.3 collective-permute-start.39
  457.5 10.1 %collective-permute-start.41 = (bf16[128,256]{1,0:T(8,128)(2,1)S(1)}, bf16[128,256]{1,0:T(8,128)(2,1)S(1)}, u32[]{:S(2)}, u32[]{:S(2)}) collective-permute-start(bf16[128,256]{1,0:T(8,128)(2,1)S(1)} %get-tuple-element.361), channel_id=1, source_target_pairs={{0,16},{4,20},{8,24},{12,28},{16,0},{20,4},{24,8},{28,12},{1,17},{... | collective-permute-start | bytes 196616 | tf_op jit(solution)/shard_map/ppermute | solution.py:445
  459.9 7.7 %collective-permute-start.40 = (bf16[128,256]{1,0:T(8,128)(2,1)S(1)}, bf16[128,256]{1,0:T(8,128)(2,1)S(1)}, u32[]{:S(2)}, u32[]{:S(2)}) collective-permute-start(bf16[128,256]{1,0:T(8,128)(2,1)S(1)} %fusion.60), channel_id=1, source_target_pairs={{0,8},{4,12},{8,0},{12,4},{16,24},{20,28},{24,16},{28,20},{1,9},{5... | collective-permute-start | bytes 196616 | tf_op jit(solution)/shard_map/ppermute | solution.py:445
  478.4 102.0 %all-to-all-start.2 = ((bf16[4,288,640]{2,1,0:T(8,128)(2,1)}), bf16[4,288,640]{2,1,0:T(8,128)(2,1)S(1)}, u32[]{:S(2)}, u32[]{:S(2)}) async-start(bf16[4,288,640]{2,1,0:T(8,128)(2,1)} %bitcast.44), calls=%async_computation.2 | async-start | bytes 2949120 | tf_op jit(solution)/shard_map/all_to_all | solution.py:931
  483.3 16.3 %collective-permute-start.43 = (bf16[192,1536]{1,0:T(8,128)(2,1)}, bf16[192,1536]{1,0:T(8,128)(2,1)S(1)}, u32[]{:S(2)}, u32[]{:S(2)}) collective-permute-start(bf16[192,1536]{1,0:T(8,128)(2,1)} %get-tuple-element.244), channel_id=1, source_target_pairs={{0,16},{4,20},{8,24},{12,28},{16,0},{20,4},{24,8},{28,12},{1,17},{... | collective-permute-start | bytes 1769480 | tf_op jit(solution)/shard_map/ppermute | solution.py:445
  485.7 3.5 collective-permute-start.47
  486.8 15.0 %collective-permute-start.42 = (bf16[192,1536]{1,0:T(8,128)(2,1)S(1)}, bf16[192,1536]{1,0:T(8,128)(2,1)S(1)}, u32[]{:S(2)}, u32[]{:S(2)}) collective-permute-start(bf16[192,1536]{1,0:T(8,128)(2,1)S(1)} %add_convert_fusion.12), channel_id=1, source_target_pairs={{0,8},{4,12},{8,0},{12,4},{16,24},{20,28},{24,16},{28,20},{1,9},{5... | collective-permute-start | bytes 1769480 | tf_op jit(solution)/shard_map/ppermute | solution.py:445
  490.5 24.0 %collective-permute-start.48 = (bf16[192,657]{1,0:T(8,128)(2,1)}, bf16[192,657]{1,0:T(8,128)(2,1)}, u32[]{:S(2)}, u32[]{:S(2)}) collective-permute-start(bf16[192,657]{1,0:T(8,128)(2,1)} %get-tuple-element.348), channel_id=1, source_target_pairs={{0,16},{4,20},{8,24},{12,28},{16,0},{20,4},{24,8},{28,12},{1,17},{... | collective-permute-start | bytes 756872 | tf_op jit(solution)/shard_map/ppermute | solution.py:445
  506.2 32.1 %collective-permute-start.46 = (bf16[192,384]{1,0:T(8,128)(2,1)}, bf16[192,384]{1,0:T(8,128)(2,1)}, u32[]{:S(2)}, u32[]{:S(2)}) collective-permute-start(bf16[192,384]{1,0:T(8,128)(2,1)} %bitcast.183), channel_id=1, source_target_pairs={{0,3},{1,0},{2,1},{3,2},{4,7},{5,4},{6,5},{7,6},{8,11},{9,8},{10,9... | collective-permute-start | bytes 442376 | tf_op jit(solution)/shard_map/ppermute | solution.py:543
  510.7 58.9 %collective-permute-start.45 = (bf16[192,384]{1,0:T(8,128)(2,1)}, bf16[192,384]{1,0:T(8,128)(2,1)}, u32[]{:S(2)}, u32[]{:S(2)}) collective-permute-start(bf16[192,384]{1,0:T(8,128)(2,1)} %bitcast.184), channel_id=1, source_target_pairs={{0,2},{1,3},{2,0},{3,1},{4,6},{5,7},{6,4},{7,5},{8,10},{9,11},{10,... | collective-permute-start | bytes 442376 | tf_op jit(solution)/shard_map/ppermute | solution.py:543
  511.4 58.2 %collective-permute-start.44 = (bf16[192,384]{1,0:T(8,128)(2,1)}, bf16[192,384]{1,0:T(8,128)(2,1)}, u32[]{:S(2)}, u32[]{:S(2)}) collective-permute-start(bf16[192,384]{1,0:T(8,128)(2,1)} %bitcast.185), channel_id=1, source_target_pairs={{0,1},{1,2},{2,3},{3,0},{4,5},{5,6},{6,7},{7,4},{8,9},{9,10},{10,1... | collective-permute-start | bytes 442376 | tf_op jit(solution)/shard_map/ppermute | solution.py:543
  512.5 58.9 %collective-permute-start.50 = (bf16[192,657]{1,0:T(8,128)(2,1)}, bf16[192,657]{1,0:T(8,128)(2,1)}, u32[]{:S(2)}, u32[]{:S(2)}) collective-permute-start(bf16[192,657]{1,0:T(8,128)(2,1)} %get-tuple-element.349), channel_id=1, source_target_pairs={{0,16},{4,20},{8,24},{12,28},{16,0},{20,4},{24,8},{28,12},{1,17},{... | collective-permute-start | bytes 756872 | tf_op jit(solution)/shard_map/ppermute | solution.py:445
  516.3 55.2 %collective-permute-start.49 = (bf16[192,657]{1,0:T(8,128)(2,1)}, bf16[192,657]{1,0:T(8,128)(2,1)}, u32[]{:S(2)}, u32[]{:S(2)}) collective-permute-start(bf16[192,657]{1,0:T(8,128)(2,1)} %fusion.40), channel_id=1, source_target_pairs={{0,8},{4,12},{8,0},{12,4},{16,24},{20,28},{24,16},{28,20},{1,9},{5... | collective-permute-start | bytes 756872 | tf_op jit(solution)/shard_map/ppermute | solution.py:445
  573.2 4.0 collective-permute-start.53
  573.2 4.6 collective-permute-start.52
  573.8 5.4 collective-permute-start.51
  (45 other events, 483.3 us)
Sparse Core Ops, SparseCore 0:
  9.6 79.3 all-gather.6
  90.8 49.2 all-gather.8
  223.1 74.7 all-gather.10
  325.5 72.3 reduce-scatter.3
  400.0 63.7 reduce-scatter.5
  465.9 93.1 reduce-scatter.7

commit v7 on v6

--- a/solution.py
+++ b/solution.py
@@ -532,17 +532,6 @@
         [lax.dynamic_index_in_dim(stacked, j ^ index, 0, keepdims=True) for j in range(len(blocks))],
         axis=0,
     )
-
-
-def scatter_direct(pieces, axis_name):
-    count = lax.axis_size(axis_name)
-    index = lax.axis_index(axis_name)
-    total = lax.dynamic_index_in_dim(pieces, index, 0, keepdims=False).astype(jnp.float32)
-    for step in range(1, count):
-        piece = lax.dynamic_index_in_dim(pieces, (index + step) % count, 0, keepdims=False)
-        arrived = lax.ppermute(piece, axis_name, [(i, (i + step) % count) for i in range(count)])
-        total = total + arrived.astype(jnp.float32)
-    return total
 
 
 def expert_body(
@@ -729,15 +718,19 @@
     second_gain = small[:, experts_all + 1].astype(jnp.float32)
     block_tokens = lax.all_gather(tokens, "seq", axis=0, tiled=True)
     own_weight = jnp.concatenate([w_query, key_projection, value_projection], axis=1)
-    weight_blocks = gather_blocks(own_weight, "shard")
+    grad_blocks = {0: out_grad}
+    near = [exchange(out_grad, "shard", bit) for bit in singles]
+
+    def with_near(blocks):
+        blocks, near[:] = lax.optimization_barrier((blocks, near))
+        return blocks
+
+    weight_blocks = gather_blocks(own_weight, "shard", with_near)
+    grad_blocks.update(zip(singles, near))
+    for j in [0] + singles:
+        grad_blocks[j + 1] = exchange(grad_blocks[j], "shard", 1)
     out_weight = lax.all_gather(w_out, "seq", axis=0, tiled=True)
-    out_weight = lax.all_gather(out_weight, "shard", axis=1, tiled=True)
-    late = lax.optimization_barrier(([weight_blocks[k] for k in several], out_grad))[1]
-    grad_blocks = gather_blocks(late, "shard")
     qkv_weight = in_order(weight_blocks, shard_index).reshape(model_width, -1)
-    block_tokens, near = lax.optimization_barrier((block_tokens, [grad_blocks[k] for k in singles]))
-    for k, block in zip(singles, near):
-        grad_blocks[k] = block
 
     block_rows = jnp.arange(block_len, dtype=jnp.int32)
     cos_table, sin_table = rotary_tables(
@@ -757,6 +750,14 @@
     value_heads = lin[:, query_width + key_width :].astype(bf16)
     kv_own = jnp.concatenate([to_lanes(key_heads), to_lanes(value_heads)], axis=1)
     kv_prompt = lax.all_gather(kv_own[:PROMPT_BLK], "shard", axis=0, tiled=True)
+    kv_prompt, out_weight, near = lax.optimization_barrier(
+        (kv_prompt, out_weight, [grad_blocks[bit] for bit in singles])
+    )
+    grad_blocks.update(zip(singles, near))
+    out_weight = lax.all_gather(out_weight, "shard", axis=1, tiled=True)
+    for j in several:
+        low_bit = bits_of(j)[0]
+        grad_blocks[j] = exchange(grad_blocks[j ^ low_bit], "shard", low_bit)
     block_number = shard_index.astype(jnp.int32).reshape(1)
     mixed_own, levels = attend_forward(block_number, queries, kv_prompt, kv_own, group, kv_heads)
     sooner = [j for j in range(1, shard_count) if j - 1 not in several]
@@ -819,7 +820,7 @@
             first_expert,
             experts_all,
             row_pair,
-            grad_blocks[j : j + 2],
+            [grad_blocks[j], grad_blocks[j + 1]],
             (w_gate, w_up, w_down),
             carried,
         )
@@ -841,13 +842,15 @@
         elif j == order[-1]:
             arrived, pieces = lax.optimization_barrier(([piece for _, piece in pending], pieces))
             pending = [(k, piece) for (k, _), piece in zip(pending, arrived)]
-        row_sums[j] = add_rounded(pieces[0], exchange(pieces[1], "shard", 1))
+        arrived = exchange(pieces[1], "shard", 1)
+        if j != order[-1]:
+            row_sums[j] = add_rounded(pieces[0], arrived)
         out_parts[j], out_parts[j + 1] = pieces[2], pieces[3]
     all_rows, all_grads, all_pre, all_hidden = carried
-    row_sums, all_grads = lax.optimization_barrier((row_sums, all_grads))
     down_sum = transposed_times(all_grads, all_hidden).astype(bf16)
     grad_down = lax.psum_scatter(down_sum, "seq", scatter_dimension=0, tiled=True)
-    all_rows = lax.optimization_barrier((all_rows, down_sum))[0]
+    all_rows, arrived, down_sum = lax.optimization_barrier((all_rows, arrived, down_sum))
+    row_sums[order[-1]] = add_rounded(pieces[0], arrived)
     pre_sums = [transposed_times(all_rows, all_pre[0]).astype(bf16)]
     row_pieces = reduce_singles(row_sums, pending, "shard")
     row_pieces, pre_sums[0] = lax.optimization_barrier((row_pieces, pre_sums[0]))
@@ -873,9 +876,11 @@
     )
     mixed_grad = lax.all_to_all(mixed_grad_tokens, "seq", split_axis=1, concat_axis=0, tiled=True)
     odd = [exchange(out_parts[j + 1], "shard", 1) for j in order]
-    pre_sums += [
-        transposed_times(all_rows, all_pre[e]).astype(bf16) for e in range(1, local_experts)
-    ]
+    hidden_units = w_gate.shape[2]
+    for e in range(1, local_experts):
+        for first in (0, hidden_units):
+            columns = all_pre[e, :, first : first + hidden_units]
+            pre_sums.append(transposed_times(all_rows, columns).astype(bf16))
     odd, pre_sums = lax.optimization_barrier((odd, pre_sums))
     out_sums = {j: add_rounded(out_parts[j], piece) for j, piece in zip(order, odd)}
     out_pending = reduce_several(out_sums, "shard")
@@ -890,7 +895,7 @@
     whole_sums = chip_sums(whole_keep, whole_arrived, "shard")
     whole_pending = reduce_several(whole_sums, "shard")
     pre_grads = [
-        lax.psum_scatter(part, "seq", scatter_dimension=0, tiled=True) for part in pre_sums
+        lax.psum_scatter(part, "seq", scatter_dimension=0, tiled=True) for part in pre_sums[:-1]
     ]
 
     query_grad, prompt_grad, self_grad = attend_backward(
@@ -934,16 +939,12 @@
     grad_qkv = jnp.concatenate([transposed_times(normed_low, lin_all), small_grad], axis=1)
     grad_qkv = reduce_rows(grad_qkv.astype(bf16), "shard")
     output = (residual + add_all(out_pieces)).astype(bf16)
-    grad_out = add_all(reduce_singles(whole_sums, whole_pending, "shard")).astype(bf16)
-    grad_out = grad_out.reshape(grad_out.shape[0], seq_count, -1).transpose(1, 0, 2)
-    grad_out = scatter_direct(grad_out, "seq").T
-    hidden_units = w_gate.shape[2]
+    grad_out = add_all(reduce_singles(whole_sums, whole_pending, "shard")).astype(bf16).T
     grad_down = grad_down.T.reshape(local_experts, hidden_units, -1).astype(jnp.float32)
     first_grads = pre_grads[0].astype(jnp.float32)
     lin_tokens, grad_out, output, grad_down, first_grads = lax.optimization_barrier(
         (lin_tokens, grad_out, output, grad_down, first_grads)
     )
-    pre_grads = [first_grads] + [part.astype(jnp.float32) for part in pre_grads[1:]]
     parts = [0.0, 0.0]
     for k, weight in enumerate((wide_half, other_half)):
         for group_index in range(seq_count):
@@ -964,15 +965,24 @@
     grad_query = grad_qkv[:, :query_width]
     grad_key = grad_qkv[:, query_width : query_width + key_width]
     grad_value = grad_qkv[:, query_width + key_width : query_width + 2 * key_width]
-    small_grad = jnp.concatenate([grad_qkv[:, all_columns:], gain_part[:, None]], axis=1).astype(bf16)
-    small_grad = scatter_direct(
-        small_grad.reshape(seq_count, -1, small_grad.shape[1]), "seq"
-    )
+    small_grad = jnp.concatenate([grad_qkv[:, all_columns:], gain_part[:, None]], axis=1)
+    own_small = own_features // seq_count
+    small_grad = small_grad.astype(bf16).reshape(seq_count, own_small, -1)
+    small_grad = jnp.pad(small_grad, ((0, 0), (0, model_width // seq_count - own_small), (0, 0)))
+    last_sum = jnp.concatenate(
+        [pre_sums[-1], grad_out, small_grad.reshape(model_width, -1)], axis=1
+    )
+    last_sum = lax.psum_scatter(last_sum, "seq", scatter_dimension=0, tiled=True)
+    last_sum = last_sum.astype(jnp.float32)
+    grad_out = last_sum[:, hidden_units : hidden_units + w_out.shape[1]]
+    small_grad = last_sum[:own_small, hidden_units + w_out.shape[1] :]
     own_factor = rms_parts(own_inputs)
     input_part, _ = rms_backward(own_inputs, own_factor, first_gain, normed_grad)
     tokens_grad = residual_grad + input_part
-    grad_gate = jnp.stack([part[:, :hidden_units] for part in pre_grads])
-    grad_up = jnp.stack([part[:, hidden_units:] for part in pre_grads])
+    halves = [first_grads[:, :hidden_units], first_grads[:, hidden_units:]]
+    halves += [part.astype(jnp.float32) for part in pre_grads[1:]] + [last_sum[:, :hidden_units]]
+    grad_gate = jnp.stack(halves[0::2])
+    grad_up = jnp.stack(halves[1::2])
     return (
         output,
         tokens_grad,

time: 625 us -> 625 us (level)
  blocking collectives: 75.8 us -> 64.9 us
  other arithmetic: 61.5 us -> 70.6 us
  starting transfers between devices: 52.7 us -> 44.9 us
    ppermute x6 -> x0, waiting for transfers between devices: 51.3 us -> none  [scatter_direct(): lax.ppermute(piece, axis_name, [(i, (i + step) % count) for i in range(co...]
    reduce_scatter x0 -> x1, waiting for transfers between devices: none -> 23.6 us  [on_device(): lax.psum_scatter(last_sum, 'seq', scatter_dimension=0, tiled=True)]
    all_to_all x1, waiting for transfers between devices: 0.01 us -> 22.2 us  [on_device(): lax.all_to_all(lin_all, 'seq', split_axis=0, concat_axis=1, tiled=True)]
    all_to_all x1, waiting for transfers between devices: 21.5 us -> 0.01 us  [on_device(): lax.all_to_all(mixed_grad_tokens, 'seq', split_axis=1, concat_axis=0, til...]
    all_gather x1, blocking collectives: 28.7 us -> 11.1 us  [on_device(): kv_prompt = lax.all_gather(kv_own[:PROMPT_BLK], 'shard', axis=0, tiled=True)]
    all_gather x1, waiting for transfers between devices: 0.01 us -> 13.2 us  [on_device(): wide_half = lax.all_gather(half_weight, 'seq', axis=0, tiled=False)]
    all_gather x1, waiting for transfers between devices: 0.01 us -> 9.48 us  [on_device(): block_tokens = lax.all_gather(tokens, 'seq', axis=0, tiled=True)]
    ppermute x48, waiting for transfers between devices: 47.6 us -> 56.2 us  [exchange(): return lax.ppermute(values, axis_name, [(i, i ^ bit) for i in range(count)])]
  transfers between devices with their start and end apart: 63 -> 58, of which waited for: 19 -> 22; matrix products, arithmetic and copies ran while one was open for 25% -> 30% of each run, Pallas kernels for 24% -> 24%
where the time goes in v7:
time: 625 us; the launch traced here: 617 us
  Pallas kernels  147 us (24%)
  waiting for transfers between devices  143 us (23%)
  matrix products  76.3 us (12%)
  other arithmetic  70.6 us (11%)
  blocking collectives  64.9 us (10%)
  local copies, waits for them, and re-layouts  53.7 us (9%)
  starting transfers between devices  44.9 us (7%)
  between operations  15.9 us (3%)
    pallas_call x4, Pallas kernels, expert_pair(): pl.pallas_call(partial(expert_body, experts_all), out_shape=out_shape, gr...  86.3 us
    ppermute x48, waiting for transfers between devices, exchange(): return lax.ppermute(values, axis_name, [(i, i ^ bit) for i in range(count)])  56.2 us
    dot_general x7, matrix products, transposed_times(): lax.dot_general(left_side, right_side, (((0,), (0,)), ((), ())), precisio...  55.7 us
    pallas_call x1, Pallas kernels, attend_backward(): pl.pallas_call(partial(attend_backward_body, group, kv_heads), out_shape=...  35.8 us
    convert_element_type x15, other arithmetic, add_rounded(): (left_side.astype(jnp.float32) + right_side.astype(jnp.float32)).astype(j...  31.6 us
    ppermute x48, starting transfers between devices, exchange(): return lax.ppermute(values, axis_name, [(i, i ^ bit) for i in range(count)])  30.7 us
    all_gather x1, blocking collectives, on_device(): out_weight = lax.all_gather(w_out, 'seq', axis=0, tiled=True)  25.3 us
    pallas_call x1, Pallas kernels, attend_forward(): pl.pallas_call(partial(attend_forward_body, group, kv_heads), out_shape=[...  25 us
  transfers between devices with their start and end apart: 58, of which 22 were waited for; matrix products, arithmetic and copies ran while one was open for 30% of the time, Pallas kernels for 24%

profile of v7, /device:TPU:0, one launch (start us, length us, event | category | flops | bytes accessed | tf_op | source)
XLA Modules:
  0.0 616.7 jit_solution(1279649305522046889)
XLA Ops:
  11.1 2.6 collective-permute-start.1
  16.5 14.2 %all-gather.1 = bf16[4,48,18]{1,2,0:T(8,128)(2,1)S(1)} all-gather(bf16[1,48,18]{1,2,0:T(8,128)(2,1)S(1)} %maximum_bitcast_fusion.1), channel_id=1, replica_groups=mesh['shard'=8,'seq'=4] {'seq'}, dimensions={0}, use_global_device_ids=true | all-gather | bytes 8640 | tf_op jit(solution)/shard_map/all_gather | solution.py:714
  30.8 14.3 %all-gather.2 = bf16[8,192,18]{1,2,0:T(8,128)(2,1)S(1)} all-gather(bf16[1,192,18]{1,2,0:T(8,128)(2,1)S(1)} %reshape.369), channel_id=1, replica_groups=mesh['shard'=8,'seq'=4] {'shard'}, dimensions={0}, use_global_device_ids=true | all-gather | bytes 62208 | tf_op jit(solution)/shard_map/all_gather | solution.py:715
  45.3 25.3 %all_gather.28 = bf16[1536,192]{0,1:T(8,128)(2,1)} all-gather(bf16[384,192]{0,1:T(8,128)(2,1)S(1)} %copy-done.35), channel_id=1, replica_groups=mesh['shard'=8,'seq'=4] {'seq'}, dimensions={0}, use_global_device_ids=true | all-gather | bytes 737280 | tf_op jit(solution)/shard_map/all_gather | solution.py:732
  73.5 6.9 %collective-permute-done.7 = bf16[192,640]{1,0:T(8,128)(2,1)S(1)} collective-permute-done((bf16[192,640]{1,0:T(8,128)(2,1)S(1)}, bf16[192,640]{1,0:T(8,128)(2,1)S(1)}, u32[]{:S(2)}, u32[]{:S(2)}) %collective-permute-start.7) | collective-permute-done | bytes 245792 | tf_op jit(solution)/shard_map/ppermute | solution.py:445
  82.3 9.5 %all-gather.7.cloned.1.call-done = bf16[1152,1536]{1,0:T(8,128)(2,1)} async-done(((bf16[288,1536]{1,0:T(8,128)(2,1)}), bf16[1152,1536]{1,0:T(8,128)(2,1)}) %all-gather.7.cloned.1.call-update) | async-done | bytes 3538960 | tf_op jit(solution)/shard_map/all_gather | solution.py:719
  91.8 2.9 fusion
  94.9 3.1 fusion.22
  100.1 11.1 %all_gather.27.kp_ref.vp_ref = bf16[1024,256]{1,0:T(8,128)(2,1)} all-gather(bf16[128,256]{1,0:T(8,128)(2,1)S(1)} %fusion.59), channel_id=1, replica_groups=mesh['shard'=8,'seq'=4] {'shard'}, dimensions={0}, use_global_device_ids=true | all-gather | bytes 589824 | tf_op jit(solution)/shard_map/all_gather | solution.py:752
  117.8 25.0 %attend_forward.1 = (bf16[1152,384]{1,0:T(8,128)(2,1)}, f32[6,1,1152]{2,1,0:T(1,128)}) custom-call(s32[1]{0:T(128)} %bitcast.index_ref, bf16[1152,384]{1,0:T(8,128)(2,1)} %copy.168.q_ref, bf16[1024,256]{1,0:T(8,128)(2,1)} %all_gather.27.kp_ref.vp_ref, bf16[1024,256]{1,0:T(8,128)(2,1)} %all_gather.27.kp_ref.vp_ref, ...), custom_call_target="tpu_custom_call" | custom-call | flops 9059696640 | bytes 3538944 | tf_op jit(solution)/shard_map/attend_forward/pallas_call | solution.py:376
  142.9 2.5 collective-permute-done.12.og_even
  145.3 3.5 all-to-all-start
  149.1 2.3 constant_dynamic-slice_fusion.2
  151.4 17.7 %all-to-all-done = bf16[4,288,384]{2,1,0:T(8,128)(2,1)S(1)} async-done(((bf16[4,288,384]{2,1,0:T(8,128)(2,1)}), bf16[4,288,384]{2,1,0:T(8,128)(2,1)S(1)}, u32[]{:S(2)}, u32[]{:S(2)}) %all-to-all-start) | async-done | bytes 884768 | tf_op jit(solution)/shard_map/all_to_all | solution.py:770
  170.8 4.3 multiply_reduce_fusion.2
  178.0 2.5 collective-permute-start.13
  180.9 21.4 %experts.4 = (bf16[2304,1536]{1,0:T(8,128)(2,1)}, bf16[2304,1536]{1,0:T(8,128)(2,1)}, bf16[2,2304,1024]{2,1,0:T(8,128)(2,1)}, bf16[2304,1024]{1,0:T(8,128)(2,1)}...) custom-call(s32[1]{0:T(128)} %bitcast.19.index_ref, ...), custom_call_target="tpu_custom_call" | custom-call | flops 10871635968 | bytes 27131904 | tf_op jit(solution)/shard_map/experts/pallas_call | solution.py:654
  205.0 2.0 collective-permute-done.19.x_odd
  207.1 21.6 %experts.5 = (bf16[2304,1536]{1,0:T(8,128)(2,1)}, bf16[2304,1536]{1,0:T(8,128)(2,1)}, bf16[2,2304,1024]{2,1,0:T(8,128)(2,1)}, bf16[2304,1024]{1,0:T(8,128)(2,1)}...) custom-call(s32[1]{0:T(128)} %bitcast.19.index_ref, ...), custom_call_target="tpu_custom_call", output_to_operand_aliasing={{0}: (8, {}), {1}: (9, {}), {2}: (10, {}), {3}: (11, {})} | custom-call | flops 10871635968 | bytes 27131904 | tf_op jit(solution)/shard_map/experts/pallas_call | solution.py:654
  232.7 13.2 %all-gather.11.cloned.1.call-done = bf16[3072,640]{1,0:T(8,128)(2,1)} async-done(((bf16[768,640]{1,0:T(8,128)(2,1)}), bf16[3072,640]{1,0:T(8,128)(2,1)}) %all-gather.11.cloned.1.call-update) | async-done | bytes 3932176 | tf_op jit(solution)/shard_map/all_gather | solution.py:780
  246.9 21.6 %experts.6 = (bf16[2304,1536]{1,0:T(8,128)(2,1)}, bf16[2304,1536]{1,0:T(8,128)(2,1)}, bf16[2,2304,1024]{2,1,0:T(8,128)(2,1)}, bf16[2304,1024]{1,0:T(8,128)(2,1)}...) custom-call(s32[1]{0:T(128)} %bitcast.19.index_ref, ...), custom_call_target="tpu_custom_call", output_to_operand_aliasing={{0}: (8, {}), {1}: (9, {}), {2}: (10, {}), {3}: (11, {})} | custom-call | flops 10871635968 | bytes 27131904 | tf_op jit(solution)/shard_map/experts/pallas_call | solution.py:654
  268.6 2.8 add_convert_fusion.4
  271.4 2.5 add_convert_fusion.3
  276.6 21.7 %experts.7 = (bf16[2304,1536]{1,0:T(8,128)(2,1)}, bf16[2304,1536]{1,0:T(8,128)(2,1)}, bf16[2,2304,1024]{2,1,0:T(8,128)(2,1)}, bf16[2304,1024]{1,0:T(8,128)(2,1)}...) custom-call(s32[1]{0:T(128)} %bitcast.19.index_ref, ...), custom_call_target="tpu_custom_call", output_to_operand_aliasing={{0}: (8, {}), {1}: (9, {}), {2}: (10, {}), {3}: (11, {})} | custom-call | flops 10871635968 | bytes 27131904 | tf_op jit(solution)/shard_map/experts/pallas_call | solution.py:654
  299.0 12.3 %convolution_convert_fusion.1 = bf16[1536,1024]{1,0:T(8,128)(2,1)} fusion(bf16[2304,1536]{1,0:T(8,128)(2,1)} %get-tuple-element.196, bf16[2304,1024]{1,0:T(8,128)(2,1)} %get-tuple-element.197), kind=kOutput, calls=%fused_computation.12 | convolution fusion | flops 7249330176 | bytes 14942208 | tf_op jit(solution)/shard_map/dot_general | solution.py:71
  311.3 2.7 add_convert_fusion.1
  315.5 2.6 add_convert_fusion
  319.6 13.1 %fusion.7 = bf16[1536,1024]{1,0:T(8,128)(2,1)} fusion(bf16[2304,1536]{1,0:T(8,128)(2,1)} %get-tuple-element.219, bf16[2,2304,1024]{2,1,0:T(8,128)(2,1)} %get-tuple-element.200), kind=kOutput, calls=%fused_computation.11 | convolution fusion | flops 7249330176 | bytes 14942208 | tf_op jit(solution)/shard_map/dot_general | solution.py:71
  332.7 5.3 collective-permute-done.25
  338.0 3.8 collective-permute-done.27
  341.8 2.3 convert_add_fusion.3
  350.2 4.2 all-to-all-start.1
  355.8 4.4 convolution_convert_fusion
  363.2 8.8 %convolution_convert_fusion.4 = bf16[1536,512]{1,0:T(8,128)(2,1)} fusion(bf16[2304,1536]{1,0:T(8,128)(2,1)} %get-tuple-element.219, bf16[2,2304,1024]{2,1,0:T(8,128)(2,1)} %get-tuple-element.200), kind=kOutput, calls=%fused_computation.19 | convolution fusion | flops 3624665088 | bytes 11010048 | tf_op jit(solution)/shard_map/dot_general | solution.py:71
  372.0 8.8 %convolution_convert_fusion.3 = bf16[1536,512]{1,0:T(8,128)(2,1)} fusion(bf16[2304,1536]{1,0:T(8,128)(2,1)} %get-tuple-element.219, bf16[2,2304,1024]{2,1,0:T(8,128)(2,1)} %get-tuple-element.200), kind=kOutput, calls=%fused_computation.18 | convolution fusion | flops 3624665088 | bytes 11010048 | tf_op jit(solution)/shard_map/dot_general | solution.py:71
  380.9 2.4 add_convert_fusion.10
  384.7 2.3 add_convert_fusion.6
  387.6 2.3 add_convert_fusion.9
  389.9 16.2 %collective-permute-done.33 = bf16[288,1536]{1,0:T(8,128)(2,1)} collective-permute-done((bf16[288,1536]{1,0:T(8,128)(2,1)}, bf16[288,1536]{1,0:T(8,128)(2,1)}, u32[]{:S(2)}, u32[]{:S(2)}) %collective-permute-start.33) | collective-permute-done | bytes 884768 | tf_op jit(solution)/shard_map/ppermute | solution.py:445
  406.1 2.9 add_convert_fusion.7
  409.1 3.0 fusion.3
  415.1 35.8 %attend_backward.1 = (bf16[1152,384]{1,0:T(8,128)(2,1)}, bf16[1024,256]{1,0:T(8,128)(2,1)}, f32[1152,256]{1,0:T(8,128)}) custom-call(s32[1]{0:T(128)} %bitcast.index_ref, bf16[1152,384]{1,0:T(8,128)(2,1)} %copy.168.q_ref, bf16[1152,384]{1,0:T(8,128)(2,1)} %bitcast.23.grad_ref, bf16[1152,384]{1,0:T(8,128)(2,1)} %get-tuple-element.145.mixed_ref, ...), custom_call_target="tpu_custom_call" | custom-call | flops 22649241600 | bytes 3538944 | tf_op jit(solution)/shard_map/attend_backward/pallas_call | solution.py:406
  457.4 2.8 collective-permute-done.39
  462.7 2.3 convolution_convert_fusion.6
  475.3 6.0 convolution_convert_fusion.2
  485.1 2.5 convert_bitcast_fusion
  487.5 2.6 reshape.353
  490.1 5.0 all-to-all-start.2
  495.5 2.2 add_convert_fusion.12
  497.9 2.0 fusion.10
  503.7 2.8 add_convert_fusion.5
  506.5 5.5 collective-permute-done.43
  512.0 2.2 copy.178
  514.2 2.3 copy.177
  518.9 2.8 fusion.38
  521.7 2.4 collective-permute-done.47
  524.1 2.9 collective-permute-done.46
  528.5 22.2 %all-to-all-done.2 = bf16[4,288,640]{2,1,0:T(8,128)(2,1)} async-done(((bf16[4,288,640]{2,1,0:T(8,128)(2,1)}), bf16[4,288,640]{2,1,0:T(8,128)(2,1)}, u32[]{:S(2)}, u32[]{:S(2)}) %all-to-all-start.2) | async-done | bytes 1474592 | tf_op jit(solution)/shard_map/all_to_all | solution.py:936
  552.3 2.6 convert_element_type.413
  554.9 2.7 pad_maximum_fusion.1
  560.9 2.0 bitcast_convert_fusion
  562.9 2.1 copy.186
  567.8 2.2 fusion.32
  580.9 23.6 %reduce-scatter.9.cloned.1.call-done = bf16[384,722]{1,0:T(8,128)(2,1)} async-done(((bf16[1536,722]{1,0:T(8,128)(2,1)}), bf16[384,722]{1,0:T(8,128)(2,1)}) %reduce-scatter.9.cloned.1.call-update) | async-done | bytes 554512 | tf_op jit(solution)/shard_map/reduce_scatter | solution.py:975
  (324 shorter events, 109.4 us)
Async XLA Ops:
  7.2 38.1 %copy-start.35 = (bf16[384,192]{0,1:T(8,128)(2,1)S(1)}, bf16[384,192]{0,1:T(8,128)(2,1)}, u32[]{:S(2)}) copy-start(bf16[384,192]{0,1:T(8,128)(2,1)} %param.18) | copy-start | bytes 442372
  7.2 84.6 %all-gather.7.cloned.1.call-start = ((), (), s32[]{:S(2)}) async-start(), calls=%async_computation.7 | async-start | bytes 4423680 | tf_op jit(solution)/shard_map/all_gather | solution.py:719
  7.9 162.8 %all-gather.9.cloned.1.call-start = ((), (), s32[]{:S(2)}) async-start(), calls=%async_computation.8 | async-start | bytes 5308416 | tf_op jit(solution)/shard_map/all_gather | solution.py:757
  10.5 70.0 %copy-start.18 = (bf16[192,640]{1,0:T(8,128)(2,1)}, bf16[192,640]{1,0:T(8,128)(2,1)S(1)}, u32[]{:S(2)}) copy-start(bf16[192,640]{1,0:T(8,128)(2,1)S(1)} %constant_dynamic-update-slice_fusion) | copy-start | bytes 737284
  10.5 62.7 %collective-permute-start = (bf16[192,640]{1,0:T(8,128)(2,1)S(1)}, bf16[192,640]{1,0:T(8,128)(2,1)S(1)}, u32[]{:S(2)}, u32[]{:S(2)}) collective-permute-start(bf16[192,640]{1,0:T(8,128)(2,1)S(1)} %constant_dynamic-update-slice_fusion), channel_id=1, source_target_pairs={{0,4},{4,0},{8,12},{12,8},{16,20},{20,16},{24,28},{28,24},{1,5},{5... | collective-permute-start | bytes 737288 | tf_op jit(solution)/shard_map/ppermute | solution.py:445
  11.1 60.8 %collective-permute-start.1 = (bf16[192,640]{1,0:T(8,128)(2,1)S(1)}, bf16[192,640]{1,0:T(8,128)(2,1)S(1)}, u32[]{:S(2)}, u32[]{:S(2)}) collective-permute-start(bf16[192,640]{1,0:T(8,128)(2,1)S(1)} %constant_dynamic-update-slice_fusion), channel_id=1, source_target_pairs={{0,8},{4,12},{8,0},{12,4},{16,24},{20,28},{24,16},{28,20},{1,9},{5... | collective-permute-start | bytes 737288 | tf_op jit(solution)/shard_map/ppermute | solution.py:445
  13.7 58.3 %collective-permute-start.2 = (bf16[192,640]{1,0:T(8,128)(2,1)S(1)}, bf16[192,640]{1,0:T(8,128)(2,1)S(1)}, u32[]{:S(2)}, u32[]{:S(2)}) collective-permute-start(bf16[192,640]{1,0:T(8,128)(2,1)S(1)} %constant_dynamic-update-slice_fusion), channel_id=1, source_target_pairs={{0,16},{4,20},{8,24},{12,28},{16,0},{20,4},{24,8},{28,12},{1,17},{... | collective-permute-start | bytes 737288 | tf_op jit(solution)/shard_map/ppermute | solution.py:445
  15.2 56.8 %collective-permute-start.3 = (bf16[288,1536]{1,0:T(8,128)(2,1)}, bf16[288,1536]{1,0:T(8,128)(2,1)}, u32[]{:S(2)}, u32[]{:S(2)}) collective-permute-start(bf16[288,1536]{1,0:T(8,128)(2,1)} %og_even.1), channel_id=1, source_target_pairs={{0,8},{4,12},{8,0},{12,4},{16,24},{20,28},{24,16},{28,20},{1,9},{5... | collective-permute-start | bytes 2654216 | tf_op jit(solution)/shard_map/ppermute | solution.py:445
  15.7 56.3 %collective-permute-start.4 = (bf16[288,1536]{1,0:T(8,128)(2,1)}, bf16[288,1536]{1,0:T(8,128)(2,1)}, u32[]{:S(2)}, u32[]{:S(2)}) collective-permute-start(bf16[288,1536]{1,0:T(8,128)(2,1)} %og_even.1), channel_id=1, source_target_pairs={{0,16},{4,20},{8,24},{12,28},{16,0},{20,4},{24,8},{28,12},{1,17},{... | collective-permute-start | bytes 2654216 | tf_op jit(solution)/shard_map/ppermute | solution.py:445
  45.2 35.3 %copy-start.32 = (bf16[1536,18]{0,1:T(8,128)(2,1)}, bf16[1536,18]{0,1:T(8,128)(2,1)S(1)}, u32[]{:S(2)}) copy-start(bf16[1536,18]{0,1:T(8,128)(2,1)S(1)} %reshape.370) | copy-start | bytes 165892
  71.9 22.9 %copy-start.36 = (f32[1536]{0:T(1024)}, f32[1536]{0:T(1024)S(1)}, u32[]{:S(2)}) copy-start(f32[1536]{0:T(1024)S(1)} %get-tuple-element.341) | copy-start | bytes 18436
  72.0 8.4 %collective-permute-start.5 = (bf16[192,640]{1,0:T(8,128)(2,1)S(1)}, bf16[192,640]{1,0:T(8,128)(2,1)S(1)}, u32[]{:S(2)}, u32[]{:S(2)}) collective-permute-start(bf16[192,640]{1,0:T(8,128)(2,1)S(1)} %collective-permute-done.1), channel_id=1, source_target_pairs={{0,4},{4,0},{8,12},{12,8},{16,20},{20,16},{24,28},{28,24},{1,5},{5... | collective-permute-start | bytes 737288 | tf_op jit(solution)/shard_map/ppermute | solution.py:445
  72.1 8.4 %collective-permute-start.7 = (bf16[192,640]{1,0:T(8,128)(2,1)S(1)}, bf16[192,640]{1,0:T(8,128)(2,1)S(1)}, u32[]{:S(2)}, u32[]{:S(2)}) collective-permute-start(bf16[192,640]{1,0:T(8,128)(2,1)S(1)} %collective-permute-done.2), channel_id=1, source_target_pairs={{0,8},{4,12},{8,0},{12,4},{16,24},{20,28},{24,16},{28,20},{1,9},{5... | collective-permute-start | bytes 737288 | tf_op jit(solution)/shard_map/ppermute | solution.py:445
  73.3 7.2 %collective-permute-start.6 = (bf16[192,640]{1,0:T(8,128)(2,1)S(1)}, bf16[192,640]{1,0:T(8,128)(2,1)S(1)}, u32[]{:S(2)}, u32[]{:S(2)}) collective-permute-start(bf16[192,640]{1,0:T(8,128)(2,1)S(1)} %collective-permute-done.2), channel_id=1, source_target_pairs={{0,4},{4,0},{8,12},{12,8},{16,20},{20,16},{24,28},{28,24},{1,5},{5... | collective-permute-start | bytes 737288 | tf_op jit(solution)/shard_map/ppermute | solution.py:445
  80.4 1.5 collective-permute-start.8
  111.2 31.6 %collective-permute-start.9 = (bf16[288,1536]{1,0:T(8,128)(2,1)}, bf16[288,1536]{1,0:T(8,128)(2,1)}, u32[]{:S(2)}, u32[]{:S(2)}) collective-permute-start(bf16[288,1536]{1,0:T(8,128)(2,1)} %og_even.1), channel_id=1, source_target_pairs={{0,4},{4,0},{8,12},{12,8},{16,20},{20,16},{24,28},{28,24},{1,5},{5... | collective-permute-start | bytes 2654216 | tf_op jit(solution)/shard_map/ppermute | solution.py:445
  111.7 31.2 %collective-permute-start.10 = (bf16[288,1536]{1,0:T(8,128)(2,1)}, bf16[288,1536]{1,0:T(8,128)(2,1)}, u32[]{:S(2)}, u32[]{:S(2)}) collective-permute-start(bf16[288,1536]{1,0:T(8,128)(2,1)} %collective-permute-done.3.og_even), channel_id=1, source_target_pairs={{0,4},{4,0},{8,12},{12,8},{16,20},{20,16},{24,28},{28,24},{1,5},{5... | collective-permute-start | bytes 2654216 | tf_op jit(solution)/shard_map/ppermute | solution.py:445
  111.8 31.0 %collective-permute-start.11 = (bf16[288,1536]{1,0:T(8,128)(2,1)}, bf16[288,1536]{1,0:T(8,128)(2,1)}, u32[]{:S(2)}, u32[]{:S(2)}) collective-permute-start(bf16[288,1536]{1,0:T(8,128)(2,1)} %collective-permute-done.4.og_even), channel_id=1, source_target_pairs={{0,4},{4,0},{8,12},{12,8},{16,20},{20,16},{24,28},{28,24},{1,5},{5... | collective-permute-start | bytes 2654216 | tf_op jit(solution)/shard_map/ppermute | solution.py:445
  113.8 31.6 %collective-permute-start.12 = (bf16[288,1536]{1,0:T(8,128)(2,1)}, bf16[288,1536]{1,0:T(8,128)(2,1)}, u32[]{:S(2)}, u32[]{:S(2)}) collective-permute-start(bf16[288,1536]{1,0:T(8,128)(2,1)} %collective-permute-done.4.og_even), channel_id=1, source_target_pairs={{0,8},{4,12},{8,0},{12,4},{16,24},{20,28},{24,16},{28,20},{1,9},{5... | collective-permute-start | bytes 2654216 | tf_op jit(solution)/shard_map/ppermute | solution.py:445
  117.8 31.1 %copy-start.40 = (s32[288,8]{0,1:T(8,128)S(1)}, s32[288,8]{0,1:T(8,128)}, u32[]{:S(2)}) copy-start(s32[288,8]{0,1:T(8,128)} %param.14) | copy-start | bytes 27652
  145.3 23.8 %all-to-all-start = ((bf16[4,288,384]{2,1,0:T(8,128)(2,1)}), bf16[4,288,384]{2,1,0:T(8,128)(2,1)S(1)}, u32[]{:S(2)}, u32[]{:S(2)}) async-start(bf16[4,288,384]{2,1,0:T(8,128)(2,1)} %bitcast.185), calls=%async_computation | async-start | bytes 1769472 | tf_op jit(solution)/shard_map/all_to_all | solution.py:770
  148.9 97.0 %all-gather.11.cloned.1.call-start = ((), (), s32[]{:S(2)}) async-start(), calls=%async_computation.13 | async-start | bytes 4915200 | tf_op jit(solution)/shard_map/all_gather | solution.py:780
  170.2 314.9 %reduce-scatter.5.cloned.1.call-start = ((), (), s32[]{:S(2)}) async-start(), calls=%async_computation.9 | async-start | bytes 3932160 | tf_op jit(solution)/shard_map/reduce_scatter | solution.py:851
  178.0 2.9 collective-permute-start.15
  178.0 24.7 %collective-permute-start.13 = (bf16[288,1664]{1,0:T(8,128)(2,1)}, bf16[288,1664]{1,0:T(8,128)(2,1)}, u32[]{:S(2)}, u32[]{:S(2)}) collective-permute-start(bf16[288,1664]{1,0:T(8,128)(2,1)} %concatenate.71.x_even), channel_id=1, source_target_pairs={{0,8},{4,12},{8,0},{12,4},{16,24},{20,28},{24,16},{28,20},{1,9},{5... | collective-permute-start | bytes 2875400 | tf_op jit(solution)/shard_map/ppermute | solution.py:445
  180.5 23.7 %collective-permute-start.14 = (bf16[288,1664]{1,0:T(8,128)(2,1)}, bf16[288,1664]{1,0:T(8,128)(2,1)}, u32[]{:S(2)}, u32[]{:S(2)}) collective-permute-start(bf16[288,1664]{1,0:T(8,128)(2,1)} %concatenate.71.x_even), channel_id=1, source_target_pairs={{0,16},{4,20},{8,24},{12,28},{16,0},{20,4},{24,8},{28,12},{1,17},{... | collective-permute-start | bytes 2875400 | tf_op jit(solution)/shard_map/ppermute | solution.py:445
  204.2 2.9 collective-permute-start.19
  204.2 24.5 %collective-permute-start.18 = (bf16[288,1664]{1,0:T(8,128)(2,1)}, bf16[288,1664]{1,0:T(8,128)(2,1)}, u32[]{:S(2)}, u32[]{:S(2)}) collective-permute-start(bf16[288,1664]{1,0:T(8,128)(2,1)} %collective-permute-done.14.x_even), channel_id=1, source_target_pairs={{0,8},{4,12},{8,0},{12,4},{16,24},{20,28},{24,16},{28,20},{1,9},{5... | collective-permute-start | bytes 2875400 | tf_op jit(solution)/shard_map/ppermute | solution.py:445
  228.7 18.2 %collective-permute-start.21 = (bf16[288,1664]{1,0:T(8,128)(2,1)}, bf16[288,1664]{1,0:T(8,128)(2,1)}, u32[]{:S(2)}, u32[]{:S(2)}) collective-permute-start(bf16[288,1664]{1,0:T(8,128)(2,1)} %collective-permute-done.18.x_even), channel_id=1, source_target_pairs={{0,4},{4,0},{8,12},{12,8},{16,20},{20,16},{24,28},{28,24},{1,5},{5... | collective-permute-start | bytes 2875400 | tf_op jit(solution)/shard_map/ppermute | solution.py:445
  228.9 17.5 %collective-permute-start.22 = (bf16[288,1536]{1,0:T(8,128)(2,1)}, bf16[288,1536]{1,0:T(8,128)(2,1)}, u32[]{:S(2)}, u32[]{:S(2)}) collective-permute-start(bf16[288,1536]{1,0:T(8,128)(2,1)} %collective-permute-done.12.og_even), channel_id=1, source_target_pairs={{0,4},{4,0},{8,12},{12,8},{16,20},{20,16},{24,28},{28,24},{1,5},{5... | collective-permute-start | bytes 2654216 | tf_op jit(solution)/shard_map/ppermute | solution.py:445
  245.9 103.3 %collective-permute-start.28 = (bf16[4,768,640]{2,1,0:T(8,128)(2,1)}, bf16[4,768,640]{2,1,0:T(8,128)(2,1)}, u32[]{:S(2)}, u32[]{:S(2)}) collective-permute-start(bf16[4,768,640]{2,1,0:T(8,128)(2,1)} %bitcast.172), channel_id=1, source_target_pairs={{0,4},{4,0},{8,12},{12,8},{16,20},{20,16},{24,28},{28,24},{1,5},{5... | collective-permute-start | bytes 11796488 | tf_op jit(solution)/shard_map/ppermute | solution.py:445
  245.9 29.2 %collective-permute-start.16 = (bf16[288,1664]{1,0:T(8,128)(2,1)}, bf16[288,1664]{1,0:T(8,128)(2,1)}, u32[]{:S(2)}, u32[]{:S(2)}) collective-permute-start(bf16[288,1664]{1,0:T(8,128)(2,1)} %collective-permute-done.14.x_even), channel_id=1, source_target_pairs={{0,4},{4,0},{8,12},{12,8},{16,20},{20,16},{24,28},{28,24},{1,5},{5... | collective-permute-start | bytes 2875400 | tf_op jit(solution)/shard_map/ppermute | solution.py:445
  246.4 22.2 %collective-permute-start.17 = (bf16[288,1664]{1,0:T(8,128)(2,1)}, bf16[288,1664]{1,0:T(8,128)(2,1)}, u32[]{:S(2)}, u32[]{:S(2)}) collective-permute-start(bf16[288,1664]{1,0:T(8,128)(2,1)} %get-tuple-element.155), channel_id=1, source_target_pairs={{0,4},{4,0},{8,12},{12,8},{16,20},{20,16},{24,28},{28,24},{1,5},{5... | collective-permute-start | bytes 2875400 | tf_op jit(solution)/shard_map/ppermute | solution.py:445
  246.4 25.0 %collective-permute-start.20 = (bf16[288,1664]{1,0:T(8,128)(2,1)}, bf16[288,1664]{1,0:T(8,128)(2,1)}, u32[]{:S(2)}, u32[]{:S(2)}) collective-permute-start(bf16[288,1664]{1,0:T(8,128)(2,1)} %get-tuple-element.168), channel_id=1, source_target_pairs={{0,4},{4,0},{8,12},{12,8},{16,20},{20,16},{24,28},{28,24},{1,5},{5... | collective-permute-start | bytes 2875400 | tf_op jit(solution)/shard_map/ppermute | solution.py:445
  268.5 5.3 collective-permute-start.23
  275.1 23.9 %collective-permute-start.24 = (bf16[288,1664]{1,0:T(8,128)(2,1)}, bf16[288,1664]{1,0:T(8,128)(2,1)}, u32[]{:S(2)}, u32[]{:S(2)}) collective-permute-start(bf16[288,1664]{1,0:T(8,128)(2,1)} %add_convert_fusion.2), channel_id=1, source_target_pairs={{0,16},{4,20},{8,24},{12,28},{16,0},{20,4},{24,8},{28,12},{1,17},{... | collective-permute-start | bytes 2875400 | tf_op jit(solution)/shard_map/ppermute | solution.py:445
  299.0 16.5 %collective-permute-start.26 = (bf16[288,1664]{1,0:T(8,128)(2,1)}, bf16[288,1664]{1,0:T(8,128)(2,1)}, u32[]{:S(2)}, u32[]{:S(2)}) collective-permute-start(bf16[288,1664]{1,0:T(8,128)(2,1)} %get-tuple-element.195), channel_id=1, source_target_pairs={{0,4},{4,0},{8,12},{12,8},{16,20},{20,16},{24,28},{28,24},{1,5},{5... | collective-permute-start | bytes 2875400 | tf_op jit(solution)/shard_map/ppermute | solution.py:445
  314.0 24.0 %collective-permute-start.25 = (bf16[288,1664]{1,0:T(8,128)(2,1)}, bf16[288,1664]{1,0:T(8,128)(2,1)}, u32[]{:S(2)}, u32[]{:S(2)}) collective-permute-start(bf16[288,1664]{1,0:T(8,128)(2,1)} %add_convert_fusion.1), channel_id=1, source_target_pairs={{0,8},{4,12},{8,0},{12,4},{16,24},{20,28},{24,16},{28,20},{1,9},{5... | collective-permute-start | bytes 2875400 | tf_op jit(solution)/shard_map/ppermute | solution.py:445
  318.2 23.7 %collective-permute-start.27 = (bf16[288,1664]{1,0:T(8,128)(2,1)}, bf16[288,1664]{1,0:T(8,128)(2,1)}, u32[]{:S(2)}, u32[]{:S(2)}) collective-permute-start(bf16[288,1664]{1,0:T(8,128)(2,1)} %add_convert_fusion), channel_id=1, source_target_pairs={{0,16},{4,20},{8,24},{12,28},{16,0},{20,4},{24,8},{28,12},{1,17},{... | collective-permute-start | bytes 2875400 | tf_op jit(solution)/shard_map/ppermute | solution.py:445
  350.2 39.7 %all-to-all-start.1 = ((bf16[288,4,384]{2,0,1:T(8,128)(2,1)}), bf16[288,4,384]{2,0,1:T(8,128)(2,1)}, u32[]{:S(2)}, u32[]{:S(2)}) async-start(bf16[288,4,384]{2,0,1:T(8,128)(2,1)} %bitcast.173), calls=%async_computation.1 | async-start | bytes 1769472 | tf_op jit(solution)/shard_map/all_to_all | solution.py:877
  354.4 197.8 %reduce-scatter.7.cloned.1.call-start = ((), (), s32[]{:S(2)}) async-start(), calls=%async_computation.10 | async-start | bytes 3932160 | tf_op jit(solution)/shard_map/reduce_scatter | solution.py:898
  354.7 26.2 %collective-permute-start.29 = (bf16[288,1536]{1,0:T(8,128)(2,1)}, bf16[288,1536]{1,0:T(8,128)(2,1)}, u32[]{:S(2)}, u32[]{:S(2)}) collective-permute-start(bf16[288,1536]{1,0:T(8,128)(2,1)} %get-tuple-element.214), channel_id=1, source_target_pairs={{0,4},{4,0},{8,12},{12,8},{16,20},{20,16},{24,28},{28,24},{1,5},{5... | collective-permute-start | bytes 2654216 | tf_op jit(solution)/shard_map/ppermute | solution.py:445
  354.7 26.1 %collective-permute-start.30 = (bf16[288,1536]{1,0:T(8,128)(2,1)}, bf16[288,1536]{1,0:T(8,128)(2,1)}, u32[]{:S(2)}, u32[]{:S(2)}) collective-permute-start(bf16[288,1536]{1,0:T(8,128)(2,1)} %get-tuple-element.215), channel_id=1, source_target_pairs={{0,4},{4,0},{8,12},{12,8},{16,20},{20,16},{24,28},{28,24},{1,5},{5... | collective-permute-start | bytes 2654216 | tf_op jit(solution)/shard_map/ppermute | solution.py:445
  355.2 25.6 %collective-permute-start.31 = (bf16[288,1536]{1,0:T(8,128)(2,1)}, bf16[288,1536]{1,0:T(8,128)(2,1)}, u32[]{:S(2)}, u32[]{:S(2)}) collective-permute-start(bf16[288,1536]{1,0:T(8,128)(2,1)} %get-tuple-element.216), channel_id=1, source_target_pairs={{0,4},{4,0},{8,12},{12,8},{16,20},{20,16},{24,28},{28,24},{1,5},{5... | collective-permute-start | bytes 2654216 | tf_op jit(solution)/shard_map/ppermute | solution.py:445
  355.3 25.6 %collective-permute-start.32 = (bf16[288,1536]{1,0:T(8,128)(2,1)}, bf16[288,1536]{1,0:T(8,128)(2,1)}, u32[]{:S(2)}, u32[]{:S(2)}) collective-permute-start(bf16[288,1536]{1,0:T(8,128)(2,1)} %get-tuple-element.217), channel_id=1, source_target_pairs={{0,4},{4,0},{8,12},{12,8},{16,20},{20,16},{24,28},{28,24},{1,5},{5... | collective-permute-start | bytes 2654216 | tf_op jit(solution)/shard_map/ppermute | solution.py:445
  363.1 43.0 %collective-permute-start.34 = (bf16[4,192,1536]{2,1,0:T(8,128)(2,1)}, bf16[4,192,1536]{2,1,0:T(8,128)(2,1)}, u32[]{:S(2)}, u32[]{:S(2)}) collective-permute-start(bf16[4,192,1536]{2,1,0:T(8,128)(2,1)} %dynamic-slice_bitcast_fusion), channel_id=1, source_target_pairs={{0,4},{4,0},{8,12},{12,8},{16,20},{20,16},{24,28},{28,24},{1,5},{5... | collective-permute-start | bytes 7077896 | tf_op jit(solution)/shard_map/ppermute | solution.py:445
  383.3 22.8 %collective-permute-start.33 = (bf16[288,1536]{1,0:T(8,128)(2,1)}, bf16[288,1536]{1,0:T(8,128)(2,1)}, u32[]{:S(2)}, u32[]{:S(2)}) collective-permute-start(bf16[288,1536]{1,0:T(8,128)(2,1)} %add_convert_fusion.10), channel_id=1, source_target_pairs={{0,16},{4,20},{8,24},{12,28},{16,0},{20,4},{24,8},{28,12},{1,17},{... | collective-permute-start | bytes 2654216 | tf_op jit(solution)/shard_map/ppermute | solution.py:445
  387.1 63.9 %collective-permute-start.36 = (bf16[288,1536]{1,0:T(8,128)(2,1)}, bf16[288,1536]{1,0:T(8,128)(2,1)}, u32[]{:S(2)}, u32[]{:S(2)}) collective-permute-start(bf16[288,1536]{1,0:T(8,128)(2,1)} %add_convert_fusion.6), channel_id=1, source_target_pairs={{0,16},{4,20},{8,24},{12,28},{16,0},{20,4},{24,8},{28,12},{1,17},{... | collective-permute-start | bytes 2654216 | tf_op jit(solution)/shard_map/ppermute | solution.py:445
  409.1 41.9 %collective-permute-start.35 = (bf16[288,1536]{1,0:T(8,128)(2,1)}, bf16[288,1536]{1,0:T(8,128)(2,1)}, u32[]{:S(2)}, u32[]{:S(2)}) collective-permute-start(bf16[288,1536]{1,0:T(8,128)(2,1)} %add_convert_fusion.7), channel_id=1, source_target_pairs={{0,8},{4,12},{8,0},{12,4},{16,24},{20,28},{24,16},{28,20},{1,9},{5... | collective-permute-start | bytes 2654216 | tf_op jit(solution)/shard_map/ppermute | solution.py:445
  413.4 37.6 %collective-permute-start.37 = (bf16[192,1536]{1,0:T(8,128)(2,1)}, bf16[192,1536]{1,0:T(8,128)(2,1)}, u32[]{:S(2)}, u32[]{:S(2)}) collective-permute-start(bf16[192,1536]{1,0:T(8,128)(2,1)} %get-tuple-element.347), channel_id=1, source_target_pairs={{0,16},{4,20},{8,24},{12,28},{16,0},{20,4},{24,8},{28,12},{1,17},{... | collective-permute-start | bytes 1769480 | tf_op jit(solution)/shard_map/ppermute | solution.py:445
  414.9 146.0 %reduce-scatter.11.cloned.1.call-start = ((), (), s32[]{:S(2)}) async-start(), calls=%async_computation.12 | async-start | bytes 1966080 | tf_op jit(solution)/shard_map/reduce_scatter | solution.py:898
  452.0 1.6 collective-permute-start.38
  455.3 4.8 collective-permute-start.39
  455.9 15.5 %collective-permute-start.41 = (bf16[128,256]{1,0:T(8,128)(2,1)}, bf16[128,256]{1,0:T(8,128)(2,1)}, u32[]{:S(2)}, u32[]{:S(2)}) collective-permute-start(bf16[128,256]{1,0:T(8,128)(2,1)} %get-tuple-element.363), channel_id=1, source_target_pairs={{0,16},{4,20},{8,24},{12,28},{16,0},{20,4},{24,8},{28,12},{1,17},{... | collective-permute-start | bytes 196616 | tf_op jit(solution)/shard_map/ppermute | solution.py:445
  460.8 10.6 %collective-permute-start.40 = (bf16[128,256]{1,0:T(8,128)(2,1)}, bf16[128,256]{1,0:T(8,128)(2,1)}, u32[]{:S(2)}, u32[]{:S(2)}) collective-permute-start(bf16[128,256]{1,0:T(8,128)(2,1)} %fusion.56), channel_id=1, source_target_pairs={{0,8},{4,12},{8,0},{12,4},{16,24},{20,28},{24,16},{28,20},{1,9},{5... | collective-permute-start | bytes 196616 | tf_op jit(solution)/shard_map/ppermute | solution.py:445
  484.2 13.7 %collective-permute-start.44 = (bf16[4,192,657]{2,1,0:T(8,128)(2,1)}, bf16[4,192,657]{2,1,0:T(8,128)(2,1)}, u32[]{:S(2)}, u32[]{:S(2)}) collective-permute-start(bf16[4,192,657]{2,1,0:T(8,128)(2,1)} %dynamic-slice_bitcast_fusion.1), channel_id=1, source_target_pairs={{0,4},{4,0},{8,12},{12,8},{16,20},{20,16},{24,28},{28,24},{1,5},{5... | collective-permute-start | bytes 3027464 | tf_op jit(solution)/shard_map/ppermute | solution.py:445
  490.1 60.6 %all-to-all-start.2 = ((bf16[4,288,640]{2,1,0:T(8,128)(2,1)}), bf16[4,288,640]{2,1,0:T(8,128)(2,1)}, u32[]{:S(2)}, u32[]{:S(2)}) async-start(bf16[4,288,640]{2,1,0:T(8,128)(2,1)} %bitcast.169), calls=%async_computation.2 | async-start | bytes 2949120 | tf_op jit(solution)/shard_map/all_to_all | solution.py:936
  495.2 109.3 %reduce-scatter.9.cloned.1.call-start = ((), (), s32[]{:S(2)}) async-start(), calls=%async_computation.11 | async-start | bytes 2949120 | tf_op jit(solution)/shard_map/reduce_scatter | solution.py:975
  495.4 16.6 %collective-permute-start.43 = (bf16[192,1536]{1,0:T(8,128)(2,1)}, bf16[192,1536]{1,0:T(8,128)(2,1)}, u32[]{:S(2)}, u32[]{:S(2)}) collective-permute-start(bf16[192,1536]{1,0:T(8,128)(2,1)} %get-tuple-element.249), channel_id=1, source_target_pairs={{0,16},{4,20},{8,24},{12,28},{16,0},{20,4},{24,8},{28,12},{1,17},{... | collective-permute-start | bytes 1769480 | tf_op jit(solution)/shard_map/ppermute | solution.py:445
  497.7 16.5 %collective-permute-start.42 = (bf16[192,1536]{1,0:T(8,128)(2,1)}, bf16[192,1536]{1,0:T(8,128)(2,1)}, u32[]{:S(2)}, u32[]{:S(2)}) collective-permute-start(bf16[192,1536]{1,0:T(8,128)(2,1)} %add_convert_fusion.12), channel_id=1, source_target_pairs={{0,8},{4,12},{8,0},{12,4},{16,24},{20,28},{24,16},{28,20},{1,9},{5... | collective-permute-start | bytes 1769480 | tf_op jit(solution)/shard_map/ppermute | solution.py:445
  501.7 15.8 %collective-permute-start.45 = (bf16[192,657]{1,0:T(8,128)(2,1)}, bf16[192,657]{1,0:T(8,128)(2,1)}, u32[]{:S(2)}, u32[]{:S(2)}) collective-permute-start(bf16[192,657]{1,0:T(8,128)(2,1)} %get-tuple-element.354), channel_id=1, source_target_pairs={{0,16},{4,20},{8,24},{12,28},{16,0},{20,4},{24,8},{28,12},{1,17},{... | collective-permute-start | bytes 756872 | tf_op jit(solution)/shard_map/ppermute | solution.py:445
  516.5 7.6 %collective-permute-start.47 = (bf16[192,657]{1,0:T(8,128)(2,1)S(1)}, bf16[192,657]{1,0:T(8,128)(2,1)S(1)}, u32[]{:S(2)}, u32[]{:S(2)}) collective-permute-start(bf16[192,657]{1,0:T(8,128)(2,1)S(1)} %copy-done.31), channel_id=1, source_target_pairs={{0,16},{4,20},{8,24},{12,28},{16,0},{20,4},{24,8},{28,12},{1,17},{... | collective-permute-start | bytes 756872 | tf_op jit(solution)/shard_map/ppermute | solution.py:445
  518.6 8.4 %collective-permute-start.46 = (bf16[192,657]{1,0:T(8,128)(2,1)S(1)}, bf16[192,657]{1,0:T(8,128)(2,1)S(1)}, u32[]{:S(2)}, u32[]{:S(2)}) collective-permute-start(bf16[192,657]{1,0:T(8,128)(2,1)S(1)} %fusion.39), channel_id=1, source_target_pairs={{0,8},{4,12},{8,0},{12,4},{16,24},{20,28},{24,16},{28,20},{1,9},{5... | collective-permute-start | bytes 756872 | tf_op jit(solution)/shard_map/ppermute | solution.py:445
  527.1 23.6 %copy-start.9 = (f32[192,657]{1,0:T(8,128)}, f32[192,657]{1,0:T(8,128)S(1)}, u32[]{:S(2)}) copy-start(f32[192,657]{1,0:T(8,128)S(1)} %fusion.40) | copy-start | bytes 1513732
  (41 other events, 199.7 us)
Sparse Core Ops, SparseCore 0:
  9.6 82.2 all-gather.6
  111.4 44.8 all-gather.8
  170.3 75.5 all-gather.10
  311.4 69.0 reduce-scatter.4
  415.0 61.2 reduce-scatter.6
  485.1 53.9 reduce-scatter.10
  557.7 46.7 reduce-scatter.8

commit v8 on v7

--- a/solution.py
+++ b/solution.py
@@ -840,18 +840,22 @@
             for k in several:
                 row_blocks[k + 1] = exchange(row_blocks[k], "shard", 1)
         elif j == order[-1]:
-            arrived, pieces = lax.optimization_barrier(([piece for _, piece in pending], pieces))
+            arrived, pieces, carried = lax.optimization_barrier(
+                ([piece for _, piece in pending], pieces, carried)
+            )
             pending = [(k, piece) for (k, _), piece in zip(pending, arrived)]
         arrived = exchange(pieces[1], "shard", 1)
         if j != order[-1]:
             row_sums[j] = add_rounded(pieces[0], arrived)
         out_parts[j], out_parts[j + 1] = pieces[2], pieces[3]
+    carried, wide_half = lax.optimization_barrier((carried, wide_half))
     all_rows, all_grads, all_pre, all_hidden = carried
     down_sum = transposed_times(all_grads, all_hidden).astype(bf16)
     grad_down = lax.psum_scatter(down_sum, "seq", scatter_dimension=0, tiled=True)
     all_rows, arrived, down_sum = lax.optimization_barrier((all_rows, arrived, down_sum))
     row_sums[order[-1]] = add_rounded(pieces[0], arrived)
     pre_sums = [transposed_times(all_rows, all_pre[0]).astype(bf16)]
+    pre_grads = [lax.psum_scatter(pre_sums[0], "seq", scatter_dimension=0, tiled=True)]
     row_pieces = reduce_singles(row_sums, pending, "shard")
     row_pieces, pre_sums[0] = lax.optimization_barrier((row_pieces, pre_sums[0]))
     row_total = add_all(row_pieces)
@@ -862,7 +866,6 @@
     )
     weighted = gate_dense * gate_grad_dense
     logit_grad = weighted - gate_dense * jnp.sum(weighted, axis=-1, keepdims=True)
-    grad_router = transposed_times(second_low.astype(jnp.float32), logit_grad, highest)
     second_grad = row_grad + times_transposed(
         logit_grad, router_weight.astype(jnp.float32), highest
     )
@@ -876,27 +879,24 @@
     )
     mixed_grad = lax.all_to_all(mixed_grad_tokens, "seq", split_axis=1, concat_axis=0, tiled=True)
     odd = [exchange(out_parts[j + 1], "shard", 1) for j in order]
-    hidden_units = w_gate.shape[2]
-    for e in range(1, local_experts):
-        for first in (0, hidden_units):
-            columns = all_pre[e, :, first : first + hidden_units]
-            pre_sums.append(transposed_times(all_rows, columns).astype(bf16))
+    pre_sums += [
+        transposed_times(all_rows, all_pre[e]).astype(bf16) for e in range(1, local_experts)
+    ]
+    pre_grads += [
+        lax.psum_scatter(part, "seq", scatter_dimension=0, tiled=True) for part in pre_sums[1:]
+    ]
     odd, pre_sums = lax.optimization_barrier((odd, pre_sums))
-    out_sums = {j: add_rounded(out_parts[j], piece) for j, piece in zip(order, odd)}
-    out_pending = reduce_several(out_sums, "shard")
+    odd = dict(zip(order, odd))
+    out_sums = {j: add_rounded(out_parts[j], odd[j]) for j in several}
     whole_out = transposed_times(residual_low, mixed_late).astype(bf16)
     whole_keep, whole_give = halves_by_core(whole_out, "shard")
     whole_arrived = exchange(whole_give, "shard", 1)
-    mixed_grad, pre_sums, arrived, whole_arrived = lax.optimization_barrier(
-        (mixed_grad, pre_sums, [piece for _, piece in out_pending], whole_arrived)
-    )
-    out_pending = [(j, piece) for (j, _), piece in zip(out_pending, arrived)]
-    out_pieces = reduce_singles(out_sums, out_pending, "shard")
+    mixed_grad, pre_sums, out_sums, whole_arrived, odd = lax.optimization_barrier(
+        (mixed_grad, pre_sums, out_sums, whole_arrived, odd)
+    )
+    out_pending = reduce_several(out_sums, "shard")
     whole_sums = chip_sums(whole_keep, whole_arrived, "shard")
     whole_pending = reduce_several(whole_sums, "shard")
-    pre_grads = [
-        lax.psum_scatter(part, "seq", scatter_dimension=0, tiled=True) for part in pre_sums[:-1]
-    ]
 
     query_grad, prompt_grad, self_grad = attend_backward(
         block_number,
@@ -916,10 +916,17 @@
         group,
         kv_heads,
     )
-    query_grad, prompt_grad, self_grad, out_pieces, arrived = lax.optimization_barrier(
-        (query_grad, prompt_grad, self_grad, out_pieces, [piece for _, piece in whole_pending])
+    query_grad, prompt_grad, self_grad, arrived, out_arrived = lax.optimization_barrier(
+        (
+            query_grad,
+            prompt_grad,
+            self_grad,
+            [piece for _, piece in whole_pending],
+            [piece for _, piece in out_pending],
+        )
     )
     whole_pending = [(j, piece) for (j, _), piece in zip(whole_pending, arrived)]
+    out_pending = [(j, piece) for (j, _), piece in zip(out_pending, out_arrived)]
     lin_query = query_grad[:, :query_width]
     own_prompt = reduce_rows(prompt_grad, "shard")
     key_grad = jnp.concatenate(
@@ -932,19 +939,28 @@
     lin_key = rotate(key_grad, cos_table, -sin_table, HEAD_DIMENSION).astype(bf16)
     lin_all = jnp.concatenate([lin_query, lin_key, value_low], axis=1)
     all_columns = lin_all.shape[1]
-    lin_all, out_pieces, whole_sums = lax.optimization_barrier((lin_all, out_pieces, whole_sums))
+    lin_all, whole_sums = lax.optimization_barrier((lin_all, whole_sums))
     lin_tokens = lax.all_to_all(lin_all, "seq", split_axis=0, concat_axis=1, tiled=True)
 
+    keep, give = halves_by_core(transposed_times(normed_low, lin_all).astype(bf16), "shard")
+    arrived, odd, logit_grad = lax.optimization_barrier(
+        (exchange(give, "shard", 1), odd, logit_grad)
+    )
+    qkv_sums = chip_sums(keep, arrived, "shard")
+    grad_qkv = add_all(reduce_singles(qkv_sums, reduce_several(qkv_sums, "shard"), "shard"))
+    grad_router = transposed_times(second_low.astype(jnp.float32), logit_grad, highest)
     small_grad = jnp.concatenate([grad_router, grad_gain_ffn[:, None]], axis=1)
-    grad_qkv = jnp.concatenate([transposed_times(normed_low, lin_all), small_grad], axis=1)
-    grad_qkv = reduce_rows(grad_qkv.astype(bf16), "shard")
-    output = (residual + add_all(out_pieces)).astype(bf16)
+    small_grad = reduce_rows(small_grad.astype(bf16), "shard")
+    for j in [0] + singles:
+        out_sums[j] = add_rounded(out_parts[j], odd[j])
+    out_sums = {j: out_sums[j] for j in [0] + singles}
+    output = (residual + add_all(reduce_singles(out_sums, out_pending, "shard"))).astype(bf16)
     grad_out = add_all(reduce_singles(whole_sums, whole_pending, "shard")).astype(bf16).T
+    hidden_units = w_gate.shape[2]
+    lin_tokens, grad_down, pre_grads[0] = lax.optimization_barrier(
+        (lin_tokens, grad_down, pre_grads[0])
+    )
     grad_down = grad_down.T.reshape(local_experts, hidden_units, -1).astype(jnp.float32)
-    first_grads = pre_grads[0].astype(jnp.float32)
-    lin_tokens, grad_out, output, grad_down, first_grads = lax.optimization_barrier(
-        (lin_tokens, grad_out, output, grad_down, first_grads)
-    )
     parts = [0.0, 0.0]
     for k, weight in enumerate((wide_half, other_half)):
         for group_index in range(seq_count):
@@ -965,24 +981,21 @@
     grad_query = grad_qkv[:, :query_width]
     grad_key = grad_qkv[:, query_width : query_width + key_width]
     grad_value = grad_qkv[:, query_width + key_width : query_width + 2 * key_width]
-    small_grad = jnp.concatenate([grad_qkv[:, all_columns:], gain_part[:, None]], axis=1)
+    small_grad = jnp.concatenate([small_grad, gain_part[:, None]], axis=1)
     own_small = own_features // seq_count
     small_grad = small_grad.astype(bf16).reshape(seq_count, own_small, -1)
     small_grad = jnp.pad(small_grad, ((0, 0), (0, model_width // seq_count - own_small), (0, 0)))
-    last_sum = jnp.concatenate(
-        [pre_sums[-1], grad_out, small_grad.reshape(model_width, -1)], axis=1
-    )
+    last_sum = jnp.concatenate([grad_out, small_grad.reshape(model_width, -1)], axis=1)
     last_sum = lax.psum_scatter(last_sum, "seq", scatter_dimension=0, tiled=True)
     last_sum = last_sum.astype(jnp.float32)
-    grad_out = last_sum[:, hidden_units : hidden_units + w_out.shape[1]]
-    small_grad = last_sum[:own_small, hidden_units + w_out.shape[1] :]
+    grad_out = last_sum[:, : w_out.shape[1]]
+    small_grad = last_sum[:own_small, w_out.shape[1] :]
     own_factor = rms_parts(own_inputs)
     input_part, _ = rms_backward(own_inputs, own_factor, first_gain, normed_grad)
     tokens_grad = residual_grad + input_part
-    halves = [first_grads[:, :hidden_units], first_grads[:, hidden_units:]]
-    halves += [part.astype(jnp.float32) for part in pre_grads[1:]] + [last_sum[:, :hidden_units]]
-    grad_gate = jnp.stack(halves[0::2])
-    grad_up = jnp.stack(halves[1::2])
+    pre_grads = [part.astype(jnp.float32) for part in pre_grads]
+    grad_gate = jnp.stack([part[:, :hidden_units] for part in pre_grads])
+    grad_up = jnp.stack([part[:, hidden_units:] for part in pre_grads])
     return (
         output,
         tokens_grad,

time: 625 us -> 583 us (0.933)
  waiting for transfers between devices: 143 us -> 99.8 us
  local copies, waits for them, and re-layouts: 53.7 us -> 61.9 us
    reduce_scatter x1, waiting for transfers between devices: 23.6 us -> 0.02 us  [on_device(): lax.psum_scatter(pre_sums[0], 'seq', scatter_dimension=0, tiled=True)]
    all_to_all x1, waiting for transfers between devices: 22.2 us -> 0.01 us  [on_device(): lax.all_to_all(lin_all, 'seq', split_axis=0, concat_axis=1, tiled=True)]
    all_gather x1, waiting for transfers between devices: 13.2 us -> 0.01 us  [on_device(): wide_half = lax.all_gather(half_weight, 'seq', axis=0, tiled=False)]
    ppermute x48 -> x52, waiting for transfers between devices: 56.2 us -> 68 us  [exchange(): return lax.ppermute(values, axis_name, [(i, i ^ bit) for i in range(count)])]
    all_to_all x1, waiting for transfers between devices: 0.01 us -> 9.45 us  [on_device(): lax.all_to_all(mixed_grad_tokens, 'seq', split_axis=1, concat_axis=0, til...]
    dot_general x7 -> x6, matrix products: 55.7 us -> 47.4 us  [transposed_times(): lax.dot_general(left_side, right_side, (((0,), (0,)), ((), ())), precisio...]
    unnamed x117 -> x135, local copies, waits for them, and re-layouts: 12.8 us -> 20.6 us
    convert_element_type x15 -> x16, other arithmetic: 31.6 us -> 28.2 us  [add_rounded(): (left_side.astype(jnp.float32) + right_side.astype(jnp.float32)).astype(j...]
  transfers between devices with their start and end apart: 58 -> 62, of which waited for: 22 -> 20; matrix products, arithmetic and copies ran while one was open for 30% -> 28% of each run, Pallas kernels for 24% -> 26%
where the time goes in v8:
time: 583 us; the launch traced here: 575 us
  Pallas kernels  148 us (25%)
  waiting for transfers between devices  99.8 us (17%)
  matrix products  72.1 us (12%)
  other arithmetic  66 us (11%)
  blocking collectives  64.8 us (11%)
  local copies, waits for them, and re-layouts  61.9 us (11%)
  starting transfers between devices  47.2 us (8%)
  between operations  15.6 us (3%)
    pallas_call x4, Pallas kernels, expert_pair(): pl.pallas_call(partial(expert_body, experts_all), out_shape=out_shape, gr...  87 us
    ppermute x52, waiting for transfers between devices, exchange(): return lax.ppermute(values, axis_name, [(i, i ^ bit) for i in range(count)])  68 us
    dot_general x6, matrix products, transposed_times(): lax.dot_general(left_side, right_side, (((0,), (0,)), ((), ())), precisio...  47.4 us
    pallas_call x1, Pallas kernels, attend_backward(): pl.pallas_call(partial(attend_backward_body, group, kv_heads), out_shape=...  35.8 us
    ppermute x52, starting transfers between devices, exchange(): return lax.ppermute(values, axis_name, [(i, i ^ bit) for i in range(count)])  33 us
    convert_element_type x16, other arithmetic, add_rounded(): (left_side.astype(jnp.float32) + right_side.astype(jnp.float32)).astype(j...  28.2 us
    all_gather x1, blocking collectives, on_device(): out_weight = lax.all_gather(w_out, 'seq', axis=0, tiled=True)  25.3 us
    pallas_call x1, Pallas kernels, attend_forward(): pl.pallas_call(partial(attend_forward_body, group, kv_heads), out_shape=[...  24.9 us
  transfers between devices with their start and end apart: 62, of which 20 were waited for; matrix products, arithmetic and copies ran while one was open for 28% of the time, Pallas kernels for 26%

profile of v8, /device:TPU:0, one launch (start us, length us, event | category | flops | bytes accessed | tf_op | source)
XLA Modules:
  0.0 575.1 jit_solution(16142947853414850530)
XLA Ops:
  11.1 2.6 collective-permute-start.1
  16.5 14.2 %all-gather.1 = bf16[4,48,18]{1,2,0:T(8,128)(2,1)S(1)} all-gather(bf16[1,48,18]{1,2,0:T(8,128)(2,1)S(1)} %maximum_bitcast_fusion.1), channel_id=1, replica_groups=mesh['shard'=8,'seq'=4] {'seq'}, dimensions={0}, use_global_device_ids=true | all-gather | bytes 8640 | tf_op jit(solution)/shard_map/all_gather | solution.py:714
  30.8 14.2 %all-gather.2 = bf16[8,192,18]{1,2,0:T(8,128)(2,1)S(1)} all-gather(bf16[1,192,18]{1,2,0:T(8,128)(2,1)S(1)} %reshape.371), channel_id=1, replica_groups=mesh['shard'=8,'seq'=4] {'shard'}, dimensions={0}, use_global_device_ids=true | all-gather | bytes 62208 | tf_op jit(solution)/shard_map/all_gather | solution.py:715
  45.3 25.3 %all_gather.28 = bf16[1536,192]{0,1:T(8,128)(2,1)} all-gather(bf16[384,192]{0,1:T(8,128)(2,1)S(1)} %copy-done.41), channel_id=1, replica_groups=mesh['shard'=8,'seq'=4] {'seq'}, dimensions={0}, use_global_device_ids=true | all-gather | bytes 737280 | tf_op jit(solution)/shard_map/all_gather | solution.py:732
  73.5 6.9 %collective-permute-done.7 = bf16[192,640]{1,0:T(8,128)(2,1)S(1)} collective-permute-done((bf16[192,640]{1,0:T(8,128)(2,1)S(1)}, bf16[192,640]{1,0:T(8,128)(2,1)S(1)}, u32[]{:S(2)}, u32[]{:S(2)}) %collective-permute-start.7) | collective-permute-done | bytes 245792 | tf_op jit(solution)/shard_map/ppermute | solution.py:445
  87.7 4.1 all-gather.7.cloned.1.call-done
  91.8 2.9 fusion
  94.9 4.7 fusion.24
  101.6 11.0 %all_gather.27.kp_ref.vp_ref = bf16[1024,256]{1,0:T(8,128)(2,1)} all-gather(bf16[128,256]{1,0:T(8,128)(2,1)S(1)} %fusion.67), channel_id=1, replica_groups=mesh['shard'=8,'seq'=4] {'shard'}, dimensions={0}, use_global_device_ids=true | all-gather | bytes 589824 | tf_op jit(solution)/shard_map/all_gather | solution.py:752
  119.2 24.9 %attend_forward.1 = (bf16[1152,384]{1,0:T(8,128)(2,1)}, f32[6,1,1152]{2,1,0:T(1,128)}) custom-call(s32[1]{0:T(128)} %bitcast.9.index_ref, bf16[1152,384]{1,0:T(8,128)(2,1)} %copy.135.q_ref, bf16[1024,256]{1,0:T(8,128)(2,1)} %all_gather.27.kp_ref.vp_ref, bf16[1024,256]{1,0:T(8,128)(2,1)} %all_gather.27.kp_ref.vp_ref, ...), custom_call_target="tpu_custom_call" | custom-call | flops 9059696640 | bytes 3538944 | tf_op jit(solution)/shard_map/attend_forward/pallas_call | solution.py:376
  144.2 2.1 collective-permute-done.12.og_even
  146.3 3.5 all-to-all-start
  150.7 2.2 constant_dynamic-slice_fusion.4
  152.9 17.4 %all-to-all-done = bf16[4,288,384]{2,1,0:T(8,128)(2,1)S(1)} async-done(((bf16[4,288,384]{2,1,0:T(8,128)(2,1)}), bf16[4,288,384]{2,1,0:T(8,128)(2,1)S(1)}, u32[]{:S(2)}, u32[]{:S(2)}) %all-to-all-start) | async-done | bytes 884768 | tf_op jit(solution)/shard_map/all_to_all | solution.py:770
  170.4 4.3 multiply_reduce_fusion.2
  179.0 1.9 concatenate.69.x_even
  180.9 2.4 collective-permute-start.13
  183.8 21.4 %experts.4 = (bf16[2304,1536]{1,0:T(8,128)(2,1)}, bf16[2304,1536]{1,0:T(8,128)(2,1)}, bf16[2,2304,1024]{2,1,0:T(8,128)(2,1)}, bf16[2304,1024]{1,0:T(8,128)(2,1)}...) custom-call(s32[1]{0:T(128)} %bitcast.19.index_ref, ...), custom_call_target="tpu_custom_call" | custom-call | flops 10871635968 | bytes 27131904 | tf_op jit(solution)/shard_map/experts/pallas_call | solution.py:654
  209.8 22.2 %experts.5 = (bf16[2304,1536]{1,0:T(8,128)(2,1)}, bf16[2304,1536]{1,0:T(8,128)(2,1)}, bf16[2,2304,1024]{2,1,0:T(8,128)(2,1)}, bf16[2304,1024]{1,0:T(8,128)(2,1)}...) custom-call(s32[1]{0:T(128)} %bitcast.19.index_ref, ...), custom_call_target="tpu_custom_call", output_to_operand_aliasing={{0}: (8, {}), {1}: (9, {}), {2}: (10, {}), {3}: (11, {})} | custom-call | flops 10871635968 | bytes 27131904 | tf_op jit(solution)/shard_map/experts/pallas_call | solution.py:654
  233.1 3.0 collective-permute-done.22.og_odd
  236.2 21.8 %experts.6 = (bf16[2304,1536]{1,0:T(8,128)(2,1)}, bf16[2304,1536]{1,0:T(8,128)(2,1)}, bf16[2,2304,1024]{2,1,0:T(8,128)(2,1)}, bf16[2304,1024]{1,0:T(8,128)(2,1)}...) custom-call(s32[1]{0:T(128)} %bitcast.19.index_ref, ...), custom_call_target="tpu_custom_call", output_to_operand_aliasing={{0}: (8, {}), {1}: (9, {}), {2}: (10, {}), {3}: (11, {})} | custom-call | flops 10871635968 | bytes 27131904 | tf_op jit(solution)/shard_map/experts/pallas_call | solution.py:654
  258.3 2.7 add_convert_fusion.4
  261.0 2.5 add_convert_fusion.3
  264.7 21.6 %experts.7 = (bf16[2304,1536]{1,0:T(8,128)(2,1)}, bf16[2304,1536]{1,0:T(8,128)(2,1)}, bf16[2,2304,1024]{2,1,0:T(8,128)(2,1)}, bf16[2304,1024]{1,0:T(8,128)(2,1)}...) custom-call(s32[1]{0:T(128)} %bitcast.19.index_ref, ...), custom_call_target="tpu_custom_call", output_to_operand_aliasing={{0}: (8, {}), {1}: (9, {}), {2}: (10, {}), {3}: (11, {})} | custom-call | flops 10871635968 | bytes 27131904 | tf_op jit(solution)/shard_map/experts/pallas_call | solution.py:654
  286.2 2.2 collective-permute-done.24
  288.4 12.3 %convolution_convert_fusion.1 = bf16[1536,1024]{1,0:T(8,128)(2,1)} fusion(bf16[2304,1536]{1,0:T(8,128)(2,1)} %get-tuple-element.208, bf16[2304,1024]{1,0:T(8,128)(2,1)} %get-tuple-element.209), kind=kOutput, calls=%fused_computation.16 | convolution fusion | flops 7249330176 | bytes 14942208 | tf_op jit(solution)/shard_map/dot_general | solution.py:71
  300.9 2.0 multiply_sine_fusion.1
  302.8 1.8 tile.18
  304.7 2.1 copy.142.cos_ref
  308.7 2.1 copy.143.sin_ref
  310.8 2.8 add_convert_fusion.1
  314.3 2.4 add_convert_fusion
  316.9 13.0 %fusion.10 = bf16[1536,1024]{1,0:T(8,128)(2,1)} fusion(bf16[2304,1536]{1,0:T(8,128)(2,1)} %get-tuple-element.232, bf16[2,2304,1024]{2,1,0:T(8,128)(2,1)} %get-tuple-element.212), kind=kOutput, calls=%fused_computation.14 | convolution fusion | flops 7249330176 | bytes 14942208 | tf_op jit(solution)/shard_map/dot_general | solution.py:71
  329.9 7.5 %collective-permute-done.25 = bf16[288,1664]{1,0:T(8,128)(2,1)} collective-permute-done((bf16[288,1664]{1,0:T(8,128)(2,1)}, bf16[288,1664]{1,0:T(8,128)(2,1)}, u32[]{:S(2)}, u32[]{:S(2)}) %collective-permute-start.25) | collective-permute-done | bytes 958496 | tf_op jit(solution)/shard_map/ppermute | solution.py:445
  337.4 3.1 collective-permute-done.27
  340.5 2.2 convert_add_fusion.3
  343.2 1.9 multiply_reduce_fusion
  348.2 4.2 all-to-all-start.1
  353.6 4.4 convolution_convert_fusion
  360.9 13.1 %fusion.13 = bf16[1536,1024]{1,0:T(8,128)(2,1)} fusion(bf16[2304,1536]{1,0:T(8,128)(2,1)} %get-tuple-element.232, bf16[2,2304,1024]{2,1,0:T(8,128)(2,1)} %get-tuple-element.212), kind=kOutput, calls=%fused_computation.15 | convolution fusion | flops 7249330176 | bytes 14942208 | tf_op jit(solution)/shard_map/dot_general | solution.py:71
  374.0 2.6 add_convert_fusion.10
  376.6 9.4 %all-to-all-done.1 = bf16[288,4,384]{2,0,1:T(8,128)(2,1)} async-done(((bf16[288,4,384]{2,0,1:T(8,128)(2,1)}), bf16[288,4,384]{2,0,1:T(8,128)(2,1)}, u32[]{:S(2)}, u32[]{:S(2)}) %all-to-all-start.1) | async-done | bytes 884768 | tf_op jit(solution)/shard_map/all_to_all | solution.py:880
  386.0 3.0 fusion.3
  392.4 35.8 %attend_backward.1 = (bf16[1152,384]{1,0:T(8,128)(2,1)}, bf16[1024,256]{1,0:T(8,128)(2,1)}, f32[1152,256]{1,0:T(8,128)}) custom-call(s32[1]{0:T(128)} %bitcast.9.index_ref, bf16[1152,384]{1,0:T(8,128)(2,1)} %copy.135.q_ref, bf16[1152,384]{1,0:T(8,128)(2,1)} %bitcast.23.grad_ref, bf16[1152,384]{1,0:T(8,128)(2,1)} %get-tuple-element.148.mixed_ref, ...), custom_call_target="tpu_custom_call" | custom-call | flops 22649241600 | bytes 3538944 | tf_op jit(solution)/shard_map/attend_backward/pallas_call | solution.py:406
  434.7 2.6 collective-permute-done.37
  439.4 1.8 slice.331
  445.0 2.1 copy.145
  449.1 1.8 copy.146
  454.3 2.2 add_convert_fusion.12
  458.0 3.5 convolution_convert_fusion.2
  465.3 5.8 %all-to-all-start.2 = ((bf16[4,288,640]{2,1,0:T(8,128)(2,1)}), bf16[4,288,640]{2,1,0:T(8,128)(2,1)}, u32[]{:S(2)}, u32[]{:S(2)}) async-start(bf16[4,288,640]{2,1,0:T(8,128)(2,1)} %bitcast.212), calls=%async_computation.2 | async-start | bytes 2949120 | tf_op jit(solution)/shard_map/all_to_all | solution.py:943
  471.3 2.5 fusion.44
  481.1 2.3 add_convert_fusion.6
  490.8 2.4 add_convert_fusion.7
  493.2 18.6 %collective-permute-done.51 = bf16[192,17]{0,1:T(8,128)(2,1)S(1)} collective-permute-done((bf16[192,17]{0,1:T(8,128)(2,1)S(1)}, bf16[192,17]{0,1:T(8,128)(2,1)S(1)}, u32[]{:S(2)}, u32[]{:S(2)}) %collective-permute-start.51) | collective-permute-done | bytes 6560 | tf_op jit(solution)/shard_map/ppermute | solution.py:445
  519.2 14.0 %collective-permute-done.41 = bf16[288,1536]{1,0:T(8,128)(2,1)} collective-permute-done((bf16[288,1536]{1,0:T(8,128)(2,1)}, bf16[288,1536]{1,0:T(8,128)(2,1)}, u32[]{:S(2)}, u32[]{:S(2)}) %collective-permute-start.41) | collective-permute-done | bytes 884768 | tf_op jit(solution)/shard_map/ppermute | solution.py:445
  533.2 3.4 add_convert_fusion.5
  538.3 1.9 fusion.34
  544.8 1.8 convolution_add_fusion.3
  546.6 1.8 convolution_add_fusion.2
  548.4 1.8 broadcast_select_fusion.1
  554.4 3.1 copy.154
  557.5 3.2 fusion.20
  563.1 2.0 pad_maximum_fusion
  (344 shorter events, 113.3 us)
Async XLA Ops:
  7.2 84.6 %all-gather.7.cloned.1.call-start = ((), (), s32[]{:S(2)}) async-start(), calls=%async_computation.7 | async-start | bytes 4423680 | tf_op jit(solution)/shard_map/all_gather | solution.py:719
  7.9 162.5 %all-gather.9.cloned.1.call-start = ((), (), s32[]{:S(2)}) async-start(), calls=%async_computation.8 | async-start | bytes 5308416 | tf_op jit(solution)/shard_map/all_gather | solution.py:757
  10.5 70.0 %copy-start.17 = (bf16[192,640]{1,0:T(8,128)(2,1)}, bf16[192,640]{1,0:T(8,128)(2,1)S(1)}, u32[]{:S(2)}) copy-start(bf16[192,640]{1,0:T(8,128)(2,1)S(1)} %constant_dynamic-update-slice_fusion) | copy-start | bytes 737284
  10.5 62.7 %collective-permute-start = (bf16[192,640]{1,0:T(8,128)(2,1)S(1)}, bf16[192,640]{1,0:T(8,128)(2,1)S(1)}, u32[]{:S(2)}, u32[]{:S(2)}) collective-permute-start(bf16[192,640]{1,0:T(8,128)(2,1)S(1)} %constant_dynamic-update-slice_fusion), channel_id=1, source_target_pairs={{0,4},{4,0},{8,12},{12,8},{16,20},{20,16},{24,28},{28,24},{1,5},{5... | collective-permute-start | bytes 737288 | tf_op jit(solution)/shard_map/ppermute | solution.py:445
  11.1 60.8 %collective-permute-start.1 = (bf16[192,640]{1,0:T(8,128)(2,1)S(1)}, bf16[192,640]{1,0:T(8,128)(2,1)S(1)}, u32[]{:S(2)}, u32[]{:S(2)}) collective-permute-start(bf16[192,640]{1,0:T(8,128)(2,1)S(1)} %constant_dynamic-update-slice_fusion), channel_id=1, source_target_pairs={{0,8},{4,12},{8,0},{12,4},{16,24},{20,28},{24,16},{28,20},{1,9},{5... | collective-permute-start | bytes 737288 | tf_op jit(solution)/shard_map/ppermute | solution.py:445
  13.7 58.3 %collective-permute-start.2 = (bf16[192,640]{1,0:T(8,128)(2,1)S(1)}, bf16[192,640]{1,0:T(8,128)(2,1)S(1)}, u32[]{:S(2)}, u32[]{:S(2)}) collective-permute-start(bf16[192,640]{1,0:T(8,128)(2,1)S(1)} %constant_dynamic-update-slice_fusion), channel_id=1, source_target_pairs={{0,16},{4,20},{8,24},{12,28},{16,0},{20,4},{24,8},{28,12},{1,17},{... | collective-permute-start | bytes 737288 | tf_op jit(solution)/shard_map/ppermute | solution.py:445
  15.2 56.8 %collective-permute-start.3 = (bf16[288,1536]{1,0:T(8,128)(2,1)}, bf16[288,1536]{1,0:T(8,128)(2,1)S(1)}, u32[]{:S(2)}, u32[]{:S(2)}) collective-permute-start(bf16[288,1536]{1,0:T(8,128)(2,1)} %og_even.1), channel_id=1, source_target_pairs={{0,8},{4,12},{8,0},{12,4},{16,24},{20,28},{24,16},{28,20},{1,9},{5... | collective-permute-start | bytes 2654216 | tf_op jit(solution)/shard_map/ppermute | solution.py:445
  15.7 56.3 %collective-permute-start.4 = (bf16[288,1536]{1,0:T(8,128)(2,1)}, bf16[288,1536]{1,0:T(8,128)(2,1)S(1)}, u32[]{:S(2)}, u32[]{:S(2)}) collective-permute-start(bf16[288,1536]{1,0:T(8,128)(2,1)} %og_even.1), channel_id=1, source_target_pairs={{0,16},{4,20},{8,24},{12,28},{16,0},{20,4},{24,8},{28,12},{1,17},{... | collective-permute-start | bytes 2654216 | tf_op jit(solution)/shard_map/ppermute | solution.py:445
  71.8 44.8 %copy-start.8 = (f32[1152,32]{0,1:T(8,128)}, f32[1152,32]{0,1:T(8,128)S(1)}, u32[]{:S(2)}) copy-start(f32[1152,32]{0,1:T(8,128)S(1)} %get-tuple-element.380) | copy-start | bytes 442372
  72.0 8.4 %collective-permute-start.5 = (bf16[192,640]{1,0:T(8,128)(2,1)S(1)}, bf16[192,640]{1,0:T(8,128)(2,1)S(1)}, u32[]{:S(2)}, u32[]{:S(2)}) collective-permute-start(bf16[192,640]{1,0:T(8,128)(2,1)S(1)} %collective-permute-done.1), channel_id=1, source_target_pairs={{0,4},{4,0},{8,12},{12,8},{16,20},{20,16},{24,28},{28,24},{1,5},{5... | collective-permute-start | bytes 737288 | tf_op jit(solution)/shard_map/ppermute | solution.py:445
  72.1 8.4 %collective-permute-start.7 = (bf16[192,640]{1,0:T(8,128)(2,1)S(1)}, bf16[192,640]{1,0:T(8,128)(2,1)S(1)}, u32[]{:S(2)}, u32[]{:S(2)}) collective-permute-start(bf16[192,640]{1,0:T(8,128)(2,1)S(1)} %collective-permute-done.2), channel_id=1, source_target_pairs={{0,8},{4,12},{8,0},{12,4},{16,24},{20,28},{24,16},{28,20},{1,9},{5... | collective-permute-start | bytes 737288 | tf_op jit(solution)/shard_map/ppermute | solution.py:445
  73.3 7.2 %collective-permute-start.6 = (bf16[192,640]{1,0:T(8,128)(2,1)S(1)}, bf16[192,640]{1,0:T(8,128)(2,1)S(1)}, u32[]{:S(2)}, u32[]{:S(2)}) collective-permute-start(bf16[192,640]{1,0:T(8,128)(2,1)S(1)} %collective-permute-done.2), channel_id=1, source_target_pairs={{0,4},{4,0},{8,12},{12,8},{16,20},{20,16},{24,28},{28,24},{1,5},{5... | collective-permute-start | bytes 737288 | tf_op jit(solution)/shard_map/ppermute | solution.py:445
  80.4 1.5 collective-permute-start.8
  112.6 31.5 %collective-permute-start.9 = (bf16[288,1536]{1,0:T(8,128)(2,1)}, bf16[288,1536]{1,0:T(8,128)(2,1)}, u32[]{:S(2)}, u32[]{:S(2)}) collective-permute-start(bf16[288,1536]{1,0:T(8,128)(2,1)} %og_even.1), channel_id=1, source_target_pairs={{0,4},{4,0},{8,12},{12,8},{16,20},{20,16},{24,28},{28,24},{1,5},{5... | collective-permute-start | bytes 2654216 | tf_op jit(solution)/shard_map/ppermute | solution.py:445
  113.1 31.1 %collective-permute-start.10 = (bf16[288,1536]{1,0:T(8,128)(2,1)S(1)}, bf16[288,1536]{1,0:T(8,128)(2,1)}, u32[]{:S(2)}, u32[]{:S(2)}) collective-permute-start(bf16[288,1536]{1,0:T(8,128)(2,1)S(1)} %collective-permute-done.3.og_even), channel_id=1, source_target_pairs={{0,4},{4,0},{8,12},{12,8},{16,20},{20,16},{24,28},{28,24},{1,5},{5... | collective-permute-start | bytes 2654216 | tf_op jit(solution)/shard_map/ppermute | solution.py:445
  113.2 31.0 %collective-permute-start.11 = (bf16[288,1536]{1,0:T(8,128)(2,1)S(1)}, bf16[288,1536]{1,0:T(8,128)(2,1)}, u32[]{:S(2)}, u32[]{:S(2)}) collective-permute-start(bf16[288,1536]{1,0:T(8,128)(2,1)S(1)} %collective-permute-done.4.og_even), channel_id=1, source_target_pairs={{0,4},{4,0},{8,12},{12,8},{16,20},{20,16},{24,28},{28,24},{1,5},{5... | collective-permute-start | bytes 2654216 | tf_op jit(solution)/shard_map/ppermute | solution.py:445
  115.2 31.1 %collective-permute-start.12 = (bf16[288,1536]{1,0:T(8,128)(2,1)S(1)}, bf16[288,1536]{1,0:T(8,128)(2,1)}, u32[]{:S(2)}, u32[]{:S(2)}) collective-permute-start(bf16[288,1536]{1,0:T(8,128)(2,1)S(1)} %collective-permute-done.4.og_even), channel_id=1, source_target_pairs={{0,8},{4,12},{8,0},{12,4},{16,24},{20,28},{24,16},{28,20},{1,9},{5... | collective-permute-start | bytes 2654216 | tf_op jit(solution)/shard_map/ppermute | solution.py:445
  146.3 24.0 %all-to-all-start = ((bf16[4,288,384]{2,1,0:T(8,128)(2,1)}), bf16[4,288,384]{2,1,0:T(8,128)(2,1)S(1)}, u32[]{:S(2)}, u32[]{:S(2)}) async-start(bf16[4,288,384]{2,1,0:T(8,128)(2,1)} %bitcast.232), calls=%async_computation | async-start | bytes 1769472 | tf_op jit(solution)/shard_map/all_to_all | solution.py:770
  149.8 138.6 %all-gather.11.cloned.1.call-start = ((), (), s32[]{:S(2)}) async-start(), calls=%async_computation.12 | async-start | bytes 4915200 | tf_op jit(solution)/shard_map/all_gather | solution.py:780
  180.9 2.9 collective-permute-start.15
  180.9 24.6 %collective-permute-start.13 = (bf16[288,1664]{1,0:T(8,128)(2,1)}, bf16[288,1664]{1,0:T(8,128)(2,1)}, u32[]{:S(2)}, u32[]{:S(2)}) collective-permute-start(bf16[288,1664]{1,0:T(8,128)(2,1)} %concatenate.69.x_even), channel_id=1, source_target_pairs={{0,8},{4,12},{8,0},{12,4},{16,24},{20,28},{24,16},{28,20},{1,9},{5... | collective-permute-start | bytes 2875400 | tf_op jit(solution)/shard_map/ppermute | solution.py:445
  183.3 23.7 %collective-permute-start.14 = (bf16[288,1664]{1,0:T(8,128)(2,1)}, bf16[288,1664]{1,0:T(8,128)(2,1)}, u32[]{:S(2)}, u32[]{:S(2)}) collective-permute-start(bf16[288,1664]{1,0:T(8,128)(2,1)} %concatenate.69.x_even), channel_id=1, source_target_pairs={{0,16},{4,20},{8,24},{12,28},{16,0},{20,4},{24,8},{28,12},{1,17},{... | collective-permute-start | bytes 2875400 | tf_op jit(solution)/shard_map/ppermute | solution.py:445
  206.9 2.9 collective-permute-start.19
  207.0 331.3 %reduce-scatter.7.cloned.1.call-start = ((), (), s32[]{:S(2)}) async-start(), calls=%async_computation.9 | async-start | bytes 3932160 | tf_op jit(solution)/shard_map/reduce_scatter | solution.py:854
  207.2 24.8 %collective-permute-start.18 = (bf16[288,1664]{1,0:T(8,128)(2,1)}, bf16[288,1664]{1,0:T(8,128)(2,1)}, u32[]{:S(2)}, u32[]{:S(2)}) collective-permute-start(bf16[288,1664]{1,0:T(8,128)(2,1)} %collective-permute-done.14.x_even), channel_id=1, source_target_pairs={{0,8},{4,12},{8,0},{12,4},{16,24},{20,28},{24,16},{28,20},{1,9},{5... | collective-permute-start | bytes 2875400 | tf_op jit(solution)/shard_map/ppermute | solution.py:445
  232.0 4.2 collective-permute-start.21
  232.1 4.1 collective-permute-start.22
  232.6 32.1 %collective-permute-start.16 = (bf16[288,1664]{1,0:T(8,128)(2,1)}, bf16[288,1664]{1,0:T(8,128)(2,1)}, u32[]{:S(2)}, u32[]{:S(2)}) collective-permute-start(bf16[288,1664]{1,0:T(8,128)(2,1)} %collective-permute-done.14.x_even), channel_id=1, source_target_pairs={{0,4},{4,0},{8,12},{12,8},{16,20},{20,16},{24,28},{28,24},{1,5},{5... | collective-permute-start | bytes 2875400 | tf_op jit(solution)/shard_map/ppermute | solution.py:445
  232.6 25.6 %collective-permute-start.17 = (bf16[288,1664]{1,0:T(8,128)(2,1)}, bf16[288,1664]{1,0:T(8,128)(2,1)}, u32[]{:S(2)}, u32[]{:S(2)}) collective-permute-start(bf16[288,1664]{1,0:T(8,128)(2,1)} %get-tuple-element.158), channel_id=1, source_target_pairs={{0,4},{4,0},{8,12},{12,8},{16,20},{20,16},{24,28},{28,24},{1,5},{5... | collective-permute-start | bytes 2875400 | tf_op jit(solution)/shard_map/ppermute | solution.py:445
  233.1 27.9 %collective-permute-start.20 = (bf16[288,1664]{1,0:T(8,128)(2,1)}, bf16[288,1664]{1,0:T(8,128)(2,1)}, u32[]{:S(2)}, u32[]{:S(2)}) collective-permute-start(bf16[288,1664]{1,0:T(8,128)(2,1)} %get-tuple-element.171), channel_id=1, source_target_pairs={{0,4},{4,0},{8,12},{12,8},{16,20},{20,16},{24,28},{28,24},{1,5},{5... | collective-permute-start | bytes 2875400 | tf_op jit(solution)/shard_map/ppermute | solution.py:445
  258.0 5.4 collective-permute-start.23
  264.7 23.7 %collective-permute-start.24 = (bf16[288,1664]{1,0:T(8,128)(2,1)}, bf16[288,1664]{1,0:T(8,128)(2,1)}, u32[]{:S(2)}, u32[]{:S(2)}) collective-permute-start(bf16[288,1664]{1,0:T(8,128)(2,1)} %add_convert_fusion.2), channel_id=1, source_target_pairs={{0,16},{4,20},{8,24},{12,28},{16,0},{20,4},{24,8},{28,12},{1,17},{... | collective-permute-start | bytes 2875400 | tf_op jit(solution)/shard_map/ppermute | solution.py:445
  300.7 237.5 %reduce-scatter.9.cloned.1.call-start = ((), (), s32[]{:S(2)}) async-start(), calls=%async_computation.10 | async-start | bytes 3932160 | tf_op jit(solution)/shard_map/reduce_scatter | solution.py:858
  300.8 13.5 %collective-permute-start.26 = (bf16[288,1664]{1,0:T(8,128)(2,1)}, bf16[288,1664]{1,0:T(8,128)(2,1)}, u32[]{:S(2)}, u32[]{:S(2)}) collective-permute-start(bf16[288,1664]{1,0:T(8,128)(2,1)} %get-tuple-element.207), channel_id=1, source_target_pairs={{0,4},{4,0},{8,12},{12,8},{16,20},{20,16},{24,28},{28,24},{1,5},{5... | collective-permute-start | bytes 2875400 | tf_op jit(solution)/shard_map/ppermute | solution.py:445
  313.5 23.9 %collective-permute-start.25 = (bf16[288,1664]{1,0:T(8,128)(2,1)}, bf16[288,1664]{1,0:T(8,128)(2,1)}, u32[]{:S(2)}, u32[]{:S(2)}) collective-permute-start(bf16[288,1664]{1,0:T(8,128)(2,1)} %add_convert_fusion.1), channel_id=1, source_target_pairs={{0,8},{4,12},{8,0},{12,4},{16,24},{20,28},{24,16},{28,20},{1,9},{5... | collective-permute-start | bytes 2875400 | tf_op jit(solution)/shard_map/ppermute | solution.py:445
  314.1 33.1 %collective-permute-start.28 = (bf16[4,768,640]{2,1,0:T(8,128)(2,1)}, bf16[4,768,640]{2,1,0:T(8,128)(2,1)}, u32[]{:S(2)}, u32[]{:S(2)}) collective-permute-start(bf16[4,768,640]{2,1,0:T(8,128)(2,1)} %bitcast.215), channel_id=1, source_target_pairs={{0,4},{4,0},{8,12},{12,8},{16,20},{20,16},{24,28},{28,24},{1,5},{5... | collective-permute-start | bytes 11796488 | tf_op jit(solution)/shard_map/ppermute | solution.py:445
  316.7 23.8 %collective-permute-start.27 = (bf16[288,1664]{1,0:T(8,128)(2,1)}, bf16[288,1664]{1,0:T(8,128)(2,1)}, u32[]{:S(2)}, u32[]{:S(2)}) collective-permute-start(bf16[288,1664]{1,0:T(8,128)(2,1)} %add_convert_fusion), channel_id=1, source_target_pairs={{0,16},{4,20},{8,24},{12,28},{16,0},{20,4},{24,8},{28,12},{1,17},{... | collective-permute-start | bytes 2875400 | tf_op jit(solution)/shard_map/ppermute | solution.py:445
  348.2 37.8 %all-to-all-start.1 = ((bf16[288,4,384]{2,0,1:T(8,128)(2,1)}), bf16[288,4,384]{2,0,1:T(8,128)(2,1)}, u32[]{:S(2)}, u32[]{:S(2)}) async-start(bf16[288,4,384]{2,0,1:T(8,128)(2,1)} %bitcast.220), calls=%async_computation.1 | async-start | bytes 1769472 | tf_op jit(solution)/shard_map/all_to_all | solution.py:880
  352.4 208.2 %reduce-scatter.11.cloned.1.call-start = ((), (), s32[]{:S(2)}) async-start(), calls=%async_computation.11 | async-start | bytes 3932160 | tf_op jit(solution)/shard_map/reduce_scatter | solution.py:886
  352.5 21.5 %collective-permute-start.29 = (bf16[288,1536]{1,0:T(8,128)(2,1)}, bf16[288,1536]{1,0:T(8,128)(2,1)}, u32[]{:S(2)}, u32[]{:S(2)}) collective-permute-start(bf16[288,1536]{1,0:T(8,128)(2,1)} %get-tuple-element.228), channel_id=1, source_target_pairs={{0,4},{4,0},{8,12},{12,8},{16,20},{20,16},{24,28},{28,24},{1,5},{5... | collective-permute-start | bytes 2654216 | tf_op jit(solution)/shard_map/ppermute | solution.py:445
  352.6 21.4 %collective-permute-start.30 = (bf16[288,1536]{1,0:T(8,128)(2,1)}, bf16[288,1536]{1,0:T(8,128)(2,1)}, u32[]{:S(2)}, u32[]{:S(2)}) collective-permute-start(bf16[288,1536]{1,0:T(8,128)(2,1)} %get-tuple-element.229), channel_id=1, source_target_pairs={{0,4},{4,0},{8,12},{12,8},{16,20},{20,16},{24,28},{28,24},{1,5},{5... | collective-permute-start | bytes 2654216 | tf_op jit(solution)/shard_map/ppermute | solution.py:445
  353.1 20.9 %collective-permute-start.31 = (bf16[288,1536]{1,0:T(8,128)(2,1)}, bf16[288,1536]{1,0:T(8,128)(2,1)}, u32[]{:S(2)}, u32[]{:S(2)}) collective-permute-start(bf16[288,1536]{1,0:T(8,128)(2,1)} %get-tuple-element.230), channel_id=1, source_target_pairs={{0,4},{4,0},{8,12},{12,8},{16,20},{20,16},{24,28},{28,24},{1,5},{5... | collective-permute-start | bytes 2654216 | tf_op jit(solution)/shard_map/ppermute | solution.py:445
  353.1 20.9 %collective-permute-start.32 = (bf16[288,1536]{1,0:T(8,128)(2,1)}, bf16[288,1536]{1,0:T(8,128)(2,1)}, u32[]{:S(2)}, u32[]{:S(2)}) collective-permute-start(bf16[288,1536]{1,0:T(8,128)(2,1)} %get-tuple-element.231), channel_id=1, source_target_pairs={{0,4},{4,0},{8,12},{12,8},{16,20},{20,16},{24,28},{28,24},{1,5},{5... | collective-permute-start | bytes 2654216 | tf_op jit(solution)/shard_map/ppermute | solution.py:445
  360.8 25.2 %collective-permute-start.33 = (bf16[4,192,1536]{2,1,0:T(8,128)(2,1)}, bf16[4,192,1536]{2,1,0:T(8,128)(2,1)}, u32[]{:S(2)}, u32[]{:S(2)}) collective-permute-start(bf16[4,192,1536]{2,1,0:T(8,128)(2,1)} %dynamic-slice_bitcast_fusion), channel_id=1, source_target_pairs={{0,4},{4,0},{8,12},{12,8},{16,20},{20,16},{24,28},{28,24},{1,5},{5... | collective-permute-start | bytes 7077896 | tf_op jit(solution)/shard_map/ppermute | solution.py:445
  390.3 37.8 %collective-permute-start.34 = (bf16[192,1536]{1,0:T(8,128)(2,1)S(1)}, bf16[192,1536]{1,0:T(8,128)(2,1)S(1)}, u32[]{:S(2)}, u32[]{:S(2)}) collective-permute-start(bf16[192,1536]{1,0:T(8,128)(2,1)S(1)} %get-tuple-element.353), channel_id=1, source_target_pairs={{0,16},{4,20},{8,24},{12,28},{16,0},{20,4},{24,8},{28,12},{1,17},{... | collective-permute-start | bytes 1769480 | tf_op jit(solution)/shard_map/ppermute | solution.py:445
  391.5 36.6 %collective-permute-start.35 = (bf16[288,1536]{1,0:T(8,128)(2,1)S(1)}, bf16[288,1536]{1,0:T(8,128)(2,1)S(1)}, u32[]{:S(2)}, u32[]{:S(2)}) collective-permute-start(bf16[288,1536]{1,0:T(8,128)(2,1)S(1)} %copy-done.33), channel_id=1, source_target_pairs={{0,16},{4,20},{8,24},{12,28},{16,0},{20,4},{24,8},{28,12},{1,17},{... | collective-permute-start | bytes 2654216 | tf_op jit(solution)/shard_map/ppermute | solution.py:445
  429.4 1.6 collective-permute-start.36
  432.7 4.7 collective-permute-start.37
  433.9 8.4 %collective-permute-start.39 = (bf16[128,256]{1,0:T(8,128)(2,1)}, bf16[128,256]{1,0:T(8,128)(2,1)}, u32[]{:S(2)}, u32[]{:S(2)}) collective-permute-start(bf16[128,256]{1,0:T(8,128)(2,1)} %get-tuple-element.373), channel_id=1, source_target_pairs={{0,16},{4,20},{8,24},{12,28},{16,0},{20,4},{24,8},{28,12},{1,17},{... | collective-permute-start | bytes 196616 | tf_op jit(solution)/shard_map/ppermute | solution.py:445
  438.0 4.6 collective-permute-start.38
  452.6 18.7 %collective-permute-start.47 = (bf16[192,1536]{1,0:T(8,128)(2,1)}, bf16[192,1536]{1,0:T(8,128)(2,1)}, u32[]{:S(2)}, u32[]{:S(2)}) collective-permute-start(bf16[192,1536]{1,0:T(8,128)(2,1)} %get-tuple-element.264), channel_id=1, source_target_pairs={{0,16},{4,20},{8,24},{12,28},{16,0},{20,4},{24,8},{28,12},{1,17},{... | collective-permute-start | bytes 1769480 | tf_op jit(solution)/shard_map/ppermute | solution.py:445
  456.5 14.8 %collective-permute-start.46 = (bf16[192,1536]{1,0:T(8,128)(2,1)}, bf16[192,1536]{1,0:T(8,128)(2,1)}, u32[]{:S(2)}, u32[]{:S(2)}) collective-permute-start(bf16[192,1536]{1,0:T(8,128)(2,1)} %add_convert_fusion.12), channel_id=1, source_target_pairs={{0,8},{4,12},{8,0},{12,4},{16,24},{20,28},{24,16},{28,20},{1,9},{5... | collective-permute-start | bytes 1769480 | tf_op jit(solution)/shard_map/ppermute | solution.py:445
  463.8 10.0 %collective-permute-start.40 = (bf16[4,192,640]{2,1,0:T(8,128)(2,1)}, bf16[4,192,640]{2,1,0:T(8,128)(2,1)}, u32[]{:S(2)}, u32[]{:S(2)}) collective-permute-start(bf16[4,192,640]{2,1,0:T(8,128)(2,1)} %dynamic-slice_bitcast_fusion.1), channel_id=1, source_target_pairs={{0,4},{4,0},{8,12},{12,8},{16,20},{20,16},{24,28},{28,24},{1,5},{5... | collective-permute-start | bytes 2949128 | tf_op jit(solution)/shard_map/ppermute | solution.py:445
  465.3 71.3 %all-to-all-start.2 = ((bf16[4,288,640]{2,1,0:T(8,128)(2,1)}), bf16[4,288,640]{2,1,0:T(8,128)(2,1)}, u32[]{:S(2)}, u32[]{:S(2)}) async-start(bf16[4,288,640]{2,1,0:T(8,128)(2,1)} %bitcast.212), calls=%async_computation.2 | async-start | bytes 2949120 | tf_op jit(solution)/shard_map/all_to_all | solution.py:943
  471.1 94.0 %reduce-scatter.13.cloned.1.call-start = ((), (), s32[]{:S(2)}) async-start(), calls=%async_computation.13 | async-start | bytes 983040
  476.0 4.4 collective-permute-start.48
  478.9 9.5 %collective-permute-start.43 = (bf16[192,640]{1,0:T(8,128)(2,1)S(1)}, bf16[192,640]{1,0:T(8,128)(2,1)S(1)}, u32[]{:S(2)}, u32[]{:S(2)}) collective-permute-start(bf16[192,640]{1,0:T(8,128)(2,1)S(1)} %get-tuple-element.362), channel_id=1, source_target_pairs={{0,16},{4,20},{8,24},{12,28},{16,0},{20,4},{24,8},{28,12},{1,17},{... | collective-permute-start | bytes 737288 | tf_op jit(solution)/shard_map/ppermute | solution.py:445
  480.6 7.4 %collective-permute-start.49 = (bf16[192,17]{0,1:T(8,128)(2,1)S(1)}, bf16[192,17]{0,1:T(8,128)(2,1)S(1)}, u32[]{:S(2)}, u32[]{:S(2)}) collective-permute-start(bf16[192,17]{0,1:T(8,128)(2,1)S(1)} %bitcast.241), channel_id=1, source_target_pairs={{0,16},{4,20},{8,24},{12,28},{16,0},{20,4},{24,8},{28,12},{1,17},{... | collective-permute-start | bytes 19592 | tf_op jit(solution)/shard_map/ppermute | solution.py:445
  483.4 35.7 %collective-permute-start.42 = (bf16[288,1536]{1,0:T(8,128)(2,1)}, bf16[288,1536]{1,0:T(8,128)(2,1)}, u32[]{:S(2)}, u32[]{:S(2)}) collective-permute-start(bf16[288,1536]{1,0:T(8,128)(2,1)} %add_convert_fusion.6), channel_id=1, source_target_pairs={{0,16},{4,20},{8,24},{12,28},{16,0},{20,4},{24,8},{28,12},{1,17},{... | collective-permute-start | bytes 2654216 | tf_op jit(solution)/shard_map/ppermute | solution.py:445
  484.9 27.4 %collective-permute-start.45 = (bf16[192,640]{1,0:T(8,128)(2,1)}, bf16[192,640]{1,0:T(8,128)(2,1)S(1)}, u32[]{:S(2)}, u32[]{:S(2)}) collective-permute-start(bf16[192,640]{1,0:T(8,128)(2,1)} %get-tuple-element.363), channel_id=1, source_target_pairs={{0,16},{4,20},{8,24},{12,28},{16,0},{20,4},{24,8},{28,12},{1,17},{... | collective-permute-start | bytes 737288 | tf_op jit(solution)/shard_map/ppermute | solution.py:445
  485.5 26.3 %collective-permute-start.51 = (bf16[192,17]{0,1:T(8,128)(2,1)S(1)}, bf16[192,17]{0,1:T(8,128)(2,1)S(1)}, u32[]{:S(2)}, u32[]{:S(2)}) collective-permute-start(bf16[192,17]{0,1:T(8,128)(2,1)S(1)} %bitcast.240), channel_id=1, source_target_pairs={{0,16},{4,20},{8,24},{12,28},{16,0},{20,4},{24,8},{28,12},{1,17},{... | collective-permute-start | bytes 19592 | tf_op jit(solution)/shard_map/ppermute | solution.py:445
  488.0 24.2 %collective-permute-start.50 = (bf16[192,17]{0,1:T(8,128)(2,1)S(1)}, bf16[192,17]{0,1:T(8,128)(2,1)S(1)}, u32[]{:S(2)}, u32[]{:S(2)}) collective-permute-start(bf16[192,17]{0,1:T(8,128)(2,1)S(1)} %fusion.74), channel_id=1, source_target_pairs={{0,8},{4,12},{8,0},{12,4},{16,24},{20,28},{24,16},{28,20},{1,9},{5... | collective-permute-start | bytes 19592 | tf_op jit(solution)/shard_map/ppermute | solution.py:445
  489.2 23.1 %collective-permute-start.44 = (bf16[192,640]{1,0:T(8,128)(2,1)}, bf16[192,640]{1,0:T(8,128)(2,1)S(1)}, u32[]{:S(2)}, u32[]{:S(2)}) collective-permute-start(bf16[192,640]{1,0:T(8,128)(2,1)} %fusion.46), channel_id=1, source_target_pairs={{0,8},{4,12},{8,0},{12,4},{16,24},{20,28},{24,16},{28,20},{1,9},{5... | collective-permute-start | bytes 737288 | tf_op jit(solution)/shard_map/ppermute | solution.py:445
  511.8 21.4 %collective-permute-start.41 = (bf16[288,1536]{1,0:T(8,128)(2,1)}, bf16[288,1536]{1,0:T(8,128)(2,1)}, u32[]{:S(2)}, u32[]{:S(2)}) collective-permute-start(bf16[288,1536]{1,0:T(8,128)(2,1)} %add_convert_fusion.7), channel_id=1, source_target_pairs={{0,8},{4,12},{8,0},{12,4},{16,24},{20,28},{24,16},{28,20},{1,9},{5... | collective-permute-start | bytes 2654216 | tf_op jit(solution)/shard_map/ppermute | solution.py:445
  (52 other events, 496.8 us)
Sparse Core Ops, SparseCore 0:
  9.6 82.2 all-gather.6
  112.8 44.6 all-gather.8
  207.1 73.9 all-gather.10
  300.8 57.1 reduce-scatter.6
  360.2 65.9 reduce-scatter.8
  439.6 84.9 reduce-scatter.10
  526.9 27.7 reduce-scatter.12

commit v9 on v8

--- a/solution.py
+++ b/solution.py
@@ -735,6 +735,16 @@
     block_rows = jnp.arange(block_len, dtype=jnp.int32)
     cos_table, sin_table = rotary_tables(
         place_of(block_rows, shard_index, prompt_len), HEAD_DIMENSION
+    )
+    back_tables = [
+        jnp.tile(cos_table[:, 0, :], (1, LANES // cos_table.shape[2])),
+        jnp.tile(
+            jnp.concatenate([sin_table, -sin_table], axis=2)[:, 0, :],
+            (1, LANES // HEAD_DIMENSION),
+        ),
+    ]
+    block_tokens, cos_table, sin_table, back_tables = lax.optimization_barrier(
+        (block_tokens, cos_table, sin_table, back_tables)
     )
     inputs = block_tokens.astype(jnp.float32)
     first_factor = rms_parts(inputs)
@@ -874,8 +884,10 @@
     residual_low = residual_grad.astype(bf16)
     mixed_grad_tokens = times_transposed(residual_low, out_weight).astype(bf16)
     other_half = exchange(wide_half, "shard", 1)
-    mixed_grad_tokens, out_parts, all_rows, other_half, mixed_late = lax.optimization_barrier(
-        (mixed_grad_tokens, out_parts, all_rows, other_half, mixed_tokens)
+    mixed_grad_tokens, out_parts, all_rows, other_half, mixed_late, logit_late = (
+        lax.optimization_barrier(
+            (mixed_grad_tokens, out_parts, all_rows, other_half, mixed_tokens, logit_grad)
+        )
     )
     mixed_grad = lax.all_to_all(mixed_grad_tokens, "seq", split_axis=1, concat_axis=0, tiled=True)
     odd = [exchange(out_parts[j + 1], "shard", 1) for j in order]
@@ -891,9 +903,15 @@
     whole_out = transposed_times(residual_low, mixed_late).astype(bf16)
     whole_keep, whole_give = halves_by_core(whole_out, "shard")
     whole_arrived = exchange(whole_give, "shard", 1)
-    mixed_grad, pre_sums, out_sums, whole_arrived, odd = lax.optimization_barrier(
-        (mixed_grad, pre_sums, out_sums, whole_arrived, odd)
-    )
+    grad_router = transposed_times(second_low.astype(jnp.float32), logit_late, highest)
+    small_grad = jnp.concatenate([grad_router, grad_gain_ffn[:, None]], axis=1)
+    small_keep, small_give = halves_by_core(small_grad.astype(bf16), "shard")
+    small_arrived = exchange(small_give, "shard", 1)
+    mixed_grad, pre_sums, out_sums, whole_arrived, odd, small_arrived = lax.optimization_barrier(
+        (mixed_grad, pre_sums, out_sums, whole_arrived, odd, small_arrived)
+    )
+    small_sums = chip_sums(small_keep, small_arrived, "shard")
+    small_pending = reduce_several(small_sums, "shard")
     out_pending = reduce_several(out_sums, "shard")
     whole_sums = chip_sums(whole_keep, whole_arrived, "shard")
     whole_pending = reduce_several(whole_sums, "shard")
@@ -904,29 +922,26 @@
         to_lanes(mixed_grad),
         mixed_own,
         levels,
-        [
-            jnp.tile(cos_table[:, 0, :], (1, LANES // cos_table.shape[2])),
-            jnp.tile(
-                jnp.concatenate([sin_table, -sin_table], axis=2)[:, 0, :],
-                (1, LANES // HEAD_DIMENSION),
-            ),
-        ],
+        back_tables,
         kv_prompt,
         kv_own,
         group,
         kv_heads,
     )
-    query_grad, prompt_grad, self_grad, arrived, out_arrived = lax.optimization_barrier(
+    query_grad, prompt_grad, self_grad, small_arrived, arrived, out_arrived = lax.optimization_barrier(
         (
             query_grad,
             prompt_grad,
             self_grad,
+            [piece for _, piece in small_pending],
             [piece for _, piece in whole_pending],
             [piece for _, piece in out_pending],
         )
     )
     whole_pending = [(j, piece) for (j, _), piece in zip(whole_pending, arrived)]
     out_pending = [(j, piece) for (j, _), piece in zip(out_pending, out_arrived)]
+    small_pending = [(j, piece) for (j, _), piece in zip(small_pending, small_arrived)]
+    small_grad = add_all(reduce_singles(small_sums, small_pending, "shard"))
     lin_query = query_grad[:, :query_width]
     own_prompt = reduce_rows(prompt_grad, "shard")
     key_grad = jnp.concatenate(
@@ -943,18 +958,15 @@
     lin_tokens = lax.all_to_all(lin_all, "seq", split_axis=0, concat_axis=1, tiled=True)
 
     keep, give = halves_by_core(transposed_times(normed_low, lin_all).astype(bf16), "shard")
-    arrived, odd, logit_grad = lax.optimization_barrier(
-        (exchange(give, "shard", 1), odd, logit_grad)
-    )
-    qkv_sums = chip_sums(keep, arrived, "shard")
-    grad_qkv = add_all(reduce_singles(qkv_sums, reduce_several(qkv_sums, "shard"), "shard"))
-    grad_router = transposed_times(second_low.astype(jnp.float32), logit_grad, highest)
-    small_grad = jnp.concatenate([grad_router, grad_gain_ffn[:, None]], axis=1)
-    small_grad = reduce_rows(small_grad.astype(bf16), "shard")
+    qkv_sums = chip_sums(keep, exchange(give, "shard", 1), "shard")
+    qkv_pending = reduce_several(qkv_sums, "shard")
+    arrived, odd = lax.optimization_barrier(([piece for _, piece in qkv_pending], odd))
+    qkv_pending = [(j, piece) for (j, _), piece in zip(qkv_pending, arrived)]
+    grad_qkv = add_all(reduce_singles(qkv_sums, qkv_pending, "shard"))
     for j in [0] + singles:
         out_sums[j] = add_rounded(out_parts[j], odd[j])
     out_sums = {j: out_sums[j] for j in [0] + singles}
-    output = (residual + add_all(reduce_singles(out_sums, out_pending, "shard"))).astype(bf16)
+    out_pieces = reduce_singles(out_sums, out_pending, "shard")
     grad_out = add_all(reduce_singles(whole_sums, whole_pending, "shard")).astype(bf16).T
     hidden_units = w_gate.shape[2]
     lin_tokens, grad_down, pre_grads[0] = lax.optimization_barrier(
@@ -973,6 +985,8 @@
         ],
         axis=1,
     )
+    normed_grad, out_pieces = lax.optimization_barrier((normed_grad, out_pieces))
+    output = (residual + add_all(out_pieces)).astype(bf16)
     own_features = own_weight.shape[0]
     gain_own = lax.dynamic_slice_in_dim(first_gain, shard_index * own_features, own_features)
     gain_part = (

time: 583 us -> 580 us (level)
  other arithmetic: 66 us -> 59.7 us
  waiting for transfers between devices: 99.8 us -> 106 us
    all_to_all x1, waiting for transfers between devices: 0.01 us -> 15.5 us  [on_device(): lax.all_to_all(lin_all, 'seq', split_axis=0, concat_axis=1, tiled=True)]
    ppermute x52, waiting for transfers between devices: 68 us -> 56.8 us  [exchange(): return lax.ppermute(values, axis_name, [(i, i ^ bit) for i in range(count)])]
    unnamed x135 -> x125, local copies, waits for them, and re-layouts: 20.6 us -> 25.4 us
    convert_element_type x16 -> x17, other arithmetic: 28.2 us -> 27.9 us  [add_rounded(): (left_side.astype(jnp.float32) + right_side.astype(jnp.float32)).astype(j...]
  transfers between devices with their start and end apart: 62 -> 62, of which waited for: 20 -> 21; matrix products, arithmetic and copies ran while one was open for 28% -> 27% of each run, Pallas kernels for 26% -> 26%
where the time goes in v9:
time: 580 us; the launch traced here: 571 us
  Pallas kernels  148 us (26%)
  waiting for transfers between devices  106 us (18%)
  matrix products  77.1 us (13%)
  blocking collectives  60.5 us (10%)
  other arithmetic  59.7 us (10%)
  local copies, waits for them, and re-layouts  57.4 us (10%)
  starting transfers between devices  46.2 us (8%)
  between operations  15.7 us (3%)
    pallas_call x4, Pallas kernels, expert_pair(): pl.pallas_call(partial(expert_body, experts_all), out_shape=out_shape, gr...  87.1 us
    ppermute x52, waiting for transfers between devices, exchange(): return lax.ppermute(values, axis_name, [(i, i ^ bit) for i in range(count)])  56.8 us
    dot_general x6, matrix products, transposed_times(): lax.dot_general(left_side, right_side, (((0,), (0,)), ((), ())), precisio...  49 us
    pallas_call x1, Pallas kernels, attend_backward(): pl.pallas_call(partial(attend_backward_body, group, kv_heads), out_shape=...  36.3 us
    ppermute x52, starting transfers between devices, exchange(): return lax.ppermute(values, axis_name, [(i, i ^ bit) for i in range(count)])  34.2 us
    convert_element_type x17, other arithmetic, add_rounded(): (left_side.astype(jnp.float32) + right_side.astype(jnp.float32)).astype(j...  27.9 us
    all_gather x1, blocking collectives, on_device(): out_weight = lax.all_gather(w_out, 'seq', axis=0, tiled=True)  25.8 us
    unnamed x125, local copies, waits for them, and re-layouts  25.4 us
  transfers between devices with their start and end apart: 62, of which 21 were waited for; matrix products, arithmetic and copies ran while one was open for 27% of the time, Pallas kernels for 26%

profile of v9, /device:TPU:0, one launch (start us, length us, event | category | flops | bytes accessed | tf_op | source)
XLA Modules:
  0.0 571.4 jit_solution(8931303941026440224)
XLA Ops:
  11.1 2.6 collective-permute-start.1
  15.8 25.8 %all_gather.28 = bf16[1536,192]{0,1:T(8,128)(2,1)} all-gather(bf16[384,192]{0,1:T(8,128)(2,1)} %param.18), channel_id=1, replica_groups=mesh['shard'=8,'seq'=4] {'seq'}, dimensions={0}, use_global_device_ids=true | all-gather | bytes 737280 | tf_op jit(solution)/shard_map/all_gather | solution.py:732
  42.3 14.3 %all-gather.1 = bf16[4,48,18]{1,2,0:T(8,128)(2,1)S(1)} all-gather(bf16[1,48,18]{1,2,0:T(8,128)(2,1)S(1)} %maximum_bitcast_fusion.1), channel_id=1, replica_groups=mesh['shard'=8,'seq'=4] {'seq'}, dimensions={0}, use_global_device_ids=true | all-gather | bytes 8640 | tf_op jit(solution)/shard_map/all_gather | solution.py:714
  56.7 9.3 %all-gather.2 = bf16[8,192,18]{1,2,0:T(8,128)(2,1)S(1)} all-gather(bf16[1,192,18]{1,2,0:T(8,128)(2,1)S(1)} %reshape.375), channel_id=1, replica_groups=mesh['shard'=8,'seq'=4] {'shard'}, dimensions={0}, use_global_device_ids=true | all-gather | bytes 62208 | tf_op jit(solution)/shard_map/all_gather | solution.py:715
  70.9 4.5 collective-permute-done.7
  82.7 6.8 %all-gather.7.cloned.1.call-done = bf16[1152,1536]{1,0:T(8,128)(2,1)} async-done(((bf16[288,1536]{1,0:T(8,128)(2,1)}), bf16[1152,1536]{1,0:T(8,128)(2,1)}) %all-gather.7.cloned.1.call-update) | async-done | bytes 3538960 | tf_op jit(solution)/shard_map/all_gather | solution.py:719
  91.3 2.9 fusion
  94.3 4.7 fusion.24
  101.1 11.1 %all_gather.27.kp_ref.vp_ref = bf16[1024,256]{1,0:T(8,128)(2,1)} all-gather(bf16[128,256]{1,0:T(8,128)(2,1)S(1)} %fusion.67), channel_id=1, replica_groups=mesh['shard'=8,'seq'=4] {'shard'}, dimensions={0}, use_global_device_ids=true | all-gather | bytes 589824 | tf_op jit(solution)/shard_map/all_gather | solution.py:762
  118.8 25.0 %attend_forward.1 = (bf16[1152,384]{1,0:T(8,128)(2,1)}, f32[6,1,1152]{2,1,0:T(1,128)}) custom-call(s32[1]{0:T(128)} %bitcast.9.index_ref, bf16[1152,384]{1,0:T(8,128)(2,1)} %copy.135.q_ref, bf16[1024,256]{1,0:T(8,128)(2,1)} %all_gather.27.kp_ref.vp_ref, bf16[1024,256]{1,0:T(8,128)(2,1)} %all_gather.27.kp_ref.vp_ref, ...), custom_call_target="tpu_custom_call" | custom-call | flops 9059696640 | bytes 3538944 | tf_op jit(solution)/shard_map/attend_forward/pallas_call | solution.py:376
  143.8 2.4 collective-permute-done.12.og_even
  146.2 3.5 all-to-all-start
  149.9 2.3 constant_dynamic-slice_fusion.4
  152.2 17.7 %all-to-all-done = bf16[4,288,384]{2,1,0:T(8,128)(2,1)S(1)} async-done(((bf16[4,288,384]{2,1,0:T(8,128)(2,1)}), bf16[4,288,384]{2,1,0:T(8,128)(2,1)S(1)}, u32[]{:S(2)}, u32[]{:S(2)}) %all-to-all-start) | async-done | bytes 884768 | tf_op jit(solution)/shard_map/all_to_all | solution.py:780
  171.0 4.3 multiply_reduce_fusion.2
  178.2 2.5 collective-permute-start.13
  181.1 21.4 %experts.4 = (bf16[2304,1536]{1,0:T(8,128)(2,1)}, bf16[2304,1536]{1,0:T(8,128)(2,1)}, bf16[2,2304,1024]{2,1,0:T(8,128)(2,1)}, bf16[2304,1024]{1,0:T(8,128)(2,1)}...) custom-call(s32[1]{0:T(128)} %bitcast.24.index_ref, ...), custom_call_target="tpu_custom_call" | custom-call | flops 10871635968 | bytes 27131904 | tf_op jit(solution)/shard_map/experts/pallas_call | solution.py:654
  207.3 22.2 %experts.5 = (bf16[2304,1536]{1,0:T(8,128)(2,1)}, bf16[2304,1536]{1,0:T(8,128)(2,1)}, bf16[2,2304,1024]{2,1,0:T(8,128)(2,1)}, bf16[2304,1024]{1,0:T(8,128)(2,1)}...) custom-call(s32[1]{0:T(128)} %bitcast.24.index_ref, ...), custom_call_target="tpu_custom_call", output_to_operand_aliasing={{0}: (8, {}), {1}: (9, {}), {2}: (10, {}), {3}: (11, {})} | custom-call | flops 10871635968 | bytes 27131904 | tf_op jit(solution)/shard_map/experts/pallas_call | solution.py:654
  230.6 3.0 collective-permute-done.22.og_odd
  233.7 21.9 %experts.6 = (bf16[2304,1536]{1,0:T(8,128)(2,1)}, bf16[2304,1536]{1,0:T(8,128)(2,1)}, bf16[2,2304,1024]{2,1,0:T(8,128)(2,1)}, bf16[2304,1024]{1,0:T(8,128)(2,1)}...) custom-call(s32[1]{0:T(128)} %bitcast.24.index_ref, ...), custom_call_target="tpu_custom_call", output_to_operand_aliasing={{0}: (8, {}), {1}: (9, {}), {2}: (10, {}), {3}: (11, {})} | custom-call | flops 10871635968 | bytes 27131904 | tf_op jit(solution)/shard_map/experts/pallas_call | solution.py:654
  255.8 2.7 add_convert_fusion.4
  258.5 2.5 add_convert_fusion.3
  262.2 21.6 %experts.7 = (bf16[2304,1536]{1,0:T(8,128)(2,1)}, bf16[2304,1536]{1,0:T(8,128)(2,1)}, bf16[2,2304,1024]{2,1,0:T(8,128)(2,1)}, bf16[2304,1024]{1,0:T(8,128)(2,1)}...) custom-call(s32[1]{0:T(128)} %bitcast.24.index_ref, ...), custom_call_target="tpu_custom_call", output_to_operand_aliasing={{0}: (8, {}), {1}: (9, {}), {2}: (10, {}), {3}: (11, {})} | custom-call | flops 10871635968 | bytes 27131904 | tf_op jit(solution)/shard_map/experts/pallas_call | solution.py:654
  283.9 2.1 collective-permute-done.24
  286.0 12.3 %convolution_convert_fusion.1 = bf16[1536,1024]{1,0:T(8,128)(2,1)} fusion(bf16[2304,1536]{1,0:T(8,128)(2,1)} %get-tuple-element.222, bf16[2304,1024]{1,0:T(8,128)(2,1)} %get-tuple-element.223), kind=kOutput, calls=%fused_computation.16 | convolution fusion | flops 7249330176 | bytes 14942208 | tf_op jit(solution)/shard_map/dot_general | solution.py:71
  300.4 2.3 copy.145.sin_ref
  302.7 2.7 add_convert_fusion.1
  305.8 2.4 add_convert_fusion
  308.8 12.9 %fusion.10 = bf16[1536,1024]{1,0:T(8,128)(2,1)} fusion(bf16[2304,1536]{1,0:T(8,128)(2,1)} %get-tuple-element.245, bf16[2,2304,1024]{2,1,0:T(8,128)(2,1)} %get-tuple-element.226), kind=kOutput, calls=%fused_computation.14 | convolution fusion | flops 7249330176 | bytes 14942208 | tf_op jit(solution)/shard_map/dot_general | solution.py:71
  321.8 6.5 %collective-permute-done.25 = bf16[288,1664]{1,0:T(8,128)(2,1)} collective-permute-done((bf16[288,1664]{1,0:T(8,128)(2,1)}, bf16[288,1664]{1,0:T(8,128)(2,1)}, u32[]{:S(2)}, u32[]{:S(2)}) %collective-permute-start.25) | collective-permute-done | bytes 958496 | tf_op jit(solution)/shard_map/ppermute | solution.py:445
  328.3 3.9 collective-permute-done.27
  332.1 2.1 convert_add_fusion.3
  334.6 2.4 multiply_reduce_fusion
  337.2 2.2 subtract_add_fusion
  339.4 4.5 convolution_convert_fusion.3
  345.0 4.2 all-to-all-start.1
  350.4 4.4 convolution_convert_fusion
  357.7 13.0 %fusion.13 = bf16[1536,1024]{1,0:T(8,128)(2,1)} fusion(bf16[2304,1536]{1,0:T(8,128)(2,1)} %get-tuple-element.245, bf16[2,2304,1024]{2,1,0:T(8,128)(2,1)} %get-tuple-element.226), kind=kOutput, calls=%fused_computation.15 | convolution fusion | flops 7249330176 | bytes 14942208 | tf_op jit(solution)/shard_map/dot_general | solution.py:71
  372.0 2.6 add_convert_fusion.10
  374.5 8.6 %all-to-all-done.1 = bf16[288,4,384]{2,0,1:T(8,128)(2,1)} async-done(((bf16[288,4,384]{2,0,1:T(8,128)(2,1)}), bf16[288,4,384]{2,0,1:T(8,128)(2,1)}, u32[]{:S(2)}, u32[]{:S(2)}) %all-to-all-start.1) | async-done | bytes 884768 | tf_op jit(solution)/shard_map/all_to_all | solution.py:892
  385.4 3.0 fusion.3
  391.6 36.3 %attend_backward.1 = (bf16[1152,384]{1,0:T(8,128)(2,1)}, bf16[1024,256]{1,0:T(8,128)(2,1)}, f32[1152,256]{1,0:T(8,128)}) custom-call(s32[1]{0:T(128)} %bitcast.9.index_ref, bf16[1152,384]{1,0:T(8,128)(2,1)} %copy.135.q_ref, bf16[1152,384]{1,0:T(8,128)(2,1)} %bitcast.28.grad_ref, bf16[1152,384]{1,0:T(8,128)(2,1)} %get-tuple-element.162.mixed_ref, ...), custom_call_target="tpu_custom_call" | custom-call | flops 22649241600 | bytes 3538944 | tf_op jit(solution)/shard_map/attend_backward/pallas_call | solution.py:406
  434.2 2.8 collective-permute-done.39
  439.3 1.8 slice.331
  444.6 2.5 maximum_maximum_fusion
  447.1 5.8 %convolution_convert_fusion.2 = bf16[1536,640]{1,0:T(8,128)(2,1)S(1)} fusion(bf16[1152,640]{1,0:T(8,128)(2,1)} %maximum_maximum_fusion, bf16[1152,1536]{1,0:T(8,128)(2,1)} %all-gather.7.cloned.1.call-done, f32[1536]{0:T(1024)S(1)} %get-tuple-element.367, f32[1152]{0:T(1024)S(1)} %copy-done.45), kind=kOutput, calls=%fused_computation.17 | convolution fusion | flops 2272985088 | bytes 6990336 | tf_op jit(solution)/shard_map/dot_general | solution.py:71
  456.3 2.0 collective-permute-start.49
  460.5 3.6 all-to-all-start.2
  464.4 1.8 fusion.16
  467.6 5.2 collective-permute-done.49
  474.4 2.3 fusion.44
  477.2 2.4 add_convert_fusion.7
  480.8 2.3 add_convert_fusion.6
  483.1 1.9 collective-permute-start.45
  486.0 2.3 add_convert_fusion.9
  488.3 17.8 %collective-permute-done.46 = bf16[192,640]{1,0:T(8,128)(2,1)S(1)} collective-permute-done((bf16[192,640]{1,0:T(8,128)(2,1)S(1)}, bf16[192,640]{1,0:T(8,128)(2,1)S(1)}, u32[]{:S(2)}, u32[]{:S(2)}) %collective-permute-start.46) | collective-permute-done | bytes 245792 | tf_op jit(solution)/shard_map/ppermute | solution.py:445
  508.0 2.0 pad_maximum_fusion.4
  510.0 2.2 copy.155
  513.9 15.5 %all-to-all-done.2 = bf16[4,288,640]{2,1,0:T(8,128)(2,1)S(1)} async-done(((bf16[4,288,640]{2,1,0:T(8,128)(2,1)}), bf16[4,288,640]{2,1,0:T(8,128)(2,1)S(1)}, u32[]{:S(2)}, u32[]{:S(2)}) %all-to-all-start.2) | async-done | bytes 1474592 | tf_op jit(solution)/shard_map/all_to_all | solution.py:958
  532.1 1.9 fusion.34
  542.1 1.8 broadcast_select_fusion.1
  549.0 3.0 copy.154
  552.0 4.8 fusion.20
  559.4 2.0 pad_maximum_fusion.1
  (335 shorter events, 104.7 us)
Async XLA Ops:
  7.2 82.3 %all-gather.7.cloned.1.call-start = ((), (), s32[]{:S(2)}) async-start(), calls=%async_computation.7 | async-start | bytes 4423680 | tf_op jit(solution)/shard_map/all_gather | solution.py:719
  7.9 163.1 %all-gather.9.cloned.1.call-start = ((), (), s32[]{:S(2)}) async-start(), calls=%async_computation.8 | async-start | bytes 5308416 | tf_op jit(solution)/shard_map/all_gather | solution.py:767
  10.6 60.3 %copy-start.15 = (bf16[192,640]{1,0:T(8,128)(2,1)}, bf16[192,640]{1,0:T(8,128)(2,1)S(1)}, u32[]{:S(2)}) copy-start(bf16[192,640]{1,0:T(8,128)(2,1)S(1)} %constant_dynamic-update-slice_fusion) | copy-start | bytes 737284
  10.6 58.2 %collective-permute-start = (bf16[192,640]{1,0:T(8,128)(2,1)S(1)}, bf16[192,640]{1,0:T(8,128)(2,1)}, u32[]{:S(2)}, u32[]{:S(2)}) collective-permute-start(bf16[192,640]{1,0:T(8,128)(2,1)S(1)} %constant_dynamic-update-slice_fusion), channel_id=1, source_target_pairs={{0,4},{4,0},{8,12},{12,8},{16,20},{20,16},{24,28},{28,24},{1,5},{5... | collective-permute-start | bytes 737288 | tf_op jit(solution)/shard_map/ppermute | solution.py:445
  11.1 55.7 %collective-permute-start.1 = (bf16[192,640]{1,0:T(8,128)(2,1)S(1)}, bf16[192,640]{1,0:T(8,128)(2,1)}, u32[]{:S(2)}, u32[]{:S(2)}) collective-permute-start(bf16[192,640]{1,0:T(8,128)(2,1)S(1)} %constant_dynamic-update-slice_fusion), channel_id=1, source_target_pairs={{0,8},{4,12},{8,0},{12,4},{16,24},{20,28},{24,16},{28,20},{1,9},{5... | collective-permute-start | bytes 737288 | tf_op jit(solution)/shard_map/ppermute | solution.py:445
  13.7 53.2 %collective-permute-start.2 = (bf16[192,640]{1,0:T(8,128)(2,1)S(1)}, bf16[192,640]{1,0:T(8,128)(2,1)S(1)}, u32[]{:S(2)}, u32[]{:S(2)}) collective-permute-start(bf16[192,640]{1,0:T(8,128)(2,1)S(1)} %constant_dynamic-update-slice_fusion), channel_id=1, source_target_pairs={{0,16},{4,20},{8,24},{12,28},{16,0},{20,4},{24,8},{28,12},{1,17},{... | collective-permute-start | bytes 737288 | tf_op jit(solution)/shard_map/ppermute | solution.py:445
  15.2 51.7 %collective-permute-start.3 = (bf16[288,1536]{1,0:T(8,128)(2,1)}, bf16[288,1536]{1,0:T(8,128)(2,1)}, u32[]{:S(2)}, u32[]{:S(2)}) collective-permute-start(bf16[288,1536]{1,0:T(8,128)(2,1)} %og_even.1), channel_id=1, source_target_pairs={{0,8},{4,12},{8,0},{12,4},{16,24},{20,28},{24,16},{28,20},{1,9},{5... | collective-permute-start | bytes 2654216 | tf_op jit(solution)/shard_map/ppermute | solution.py:445
  15.7 51.2 %collective-permute-start.4 = (bf16[288,1536]{1,0:T(8,128)(2,1)}, bf16[288,1536]{1,0:T(8,128)(2,1)}, u32[]{:S(2)}, u32[]{:S(2)}) collective-permute-start(bf16[288,1536]{1,0:T(8,128)(2,1)} %og_even.1), channel_id=1, source_target_pairs={{0,16},{4,20},{8,24},{12,28},{16,0},{20,4},{24,8},{28,12},{1,17},{... | collective-permute-start | bytes 2654216 | tf_op jit(solution)/shard_map/ppermute | solution.py:445
  66.7 49.5 %copy-start.12 = (f32[1152,1,32]{0,2,1:T(8,128)}, f32[1152,1,32]{0,2,1:T(8,128)S(1)}, u32[]{:S(2)}) copy-start(f32[1152,1,32]{0,2,1:T(8,128)S(1)} %get-tuple-element.154) | copy-start | bytes 442372
  66.9 8.4 %collective-permute-start.5 = (bf16[192,640]{1,0:T(8,128)(2,1)}, bf16[192,640]{1,0:T(8,128)(2,1)S(1)}, u32[]{:S(2)}, u32[]{:S(2)}) collective-permute-start(bf16[192,640]{1,0:T(8,128)(2,1)} %collective-permute-done.1), channel_id=1, source_target_pairs={{0,4},{4,0},{8,12},{12,8},{16,20},{20,16},{24,28},{28,24},{1,5},{5... | collective-permute-start | bytes 737288 | tf_op jit(solution)/shard_map/ppermute | solution.py:445
  67.3 8.0 %collective-permute-start.7 = (bf16[192,640]{1,0:T(8,128)(2,1)S(1)}, bf16[192,640]{1,0:T(8,128)(2,1)S(1)}, u32[]{:S(2)}, u32[]{:S(2)}) collective-permute-start(bf16[192,640]{1,0:T(8,128)(2,1)S(1)} %collective-permute-done.2), channel_id=1, source_target_pairs={{0,8},{4,12},{8,0},{12,4},{16,24},{20,28},{24,16},{28,20},{1,9},{5... | collective-permute-start | bytes 737288 | tf_op jit(solution)/shard_map/ppermute | solution.py:445
  69.8 5.6 collective-permute-start.6
  75.3 1.5 collective-permute-start.8
  112.2 31.6 %collective-permute-start.9 = (bf16[288,1536]{1,0:T(8,128)(2,1)}, bf16[288,1536]{1,0:T(8,128)(2,1)}, u32[]{:S(2)}, u32[]{:S(2)}) collective-permute-start(bf16[288,1536]{1,0:T(8,128)(2,1)} %og_even.1), channel_id=1, source_target_pairs={{0,4},{4,0},{8,12},{12,8},{16,20},{20,16},{24,28},{28,24},{1,5},{5... | collective-permute-start | bytes 2654216 | tf_op jit(solution)/shard_map/ppermute | solution.py:445
  112.6 31.2 %collective-permute-start.10 = (bf16[288,1536]{1,0:T(8,128)(2,1)}, bf16[288,1536]{1,0:T(8,128)(2,1)}, u32[]{:S(2)}, u32[]{:S(2)}) collective-permute-start(bf16[288,1536]{1,0:T(8,128)(2,1)} %collective-permute-done.3.og_even), channel_id=1, source_target_pairs={{0,4},{4,0},{8,12},{12,8},{16,20},{20,16},{24,28},{28,24},{1,5},{5... | collective-permute-start | bytes 2654216 | tf_op jit(solution)/shard_map/ppermute | solution.py:445
  112.8 31.0 %collective-permute-start.11 = (bf16[288,1536]{1,0:T(8,128)(2,1)}, bf16[288,1536]{1,0:T(8,128)(2,1)}, u32[]{:S(2)}, u32[]{:S(2)}) collective-permute-start(bf16[288,1536]{1,0:T(8,128)(2,1)} %collective-permute-done.4.og_even), channel_id=1, source_target_pairs={{0,4},{4,0},{8,12},{12,8},{16,20},{20,16},{24,28},{28,24},{1,5},{5... | collective-permute-start | bytes 2654216 | tf_op jit(solution)/shard_map/ppermute | solution.py:445
  114.7 31.5 %collective-permute-start.12 = (bf16[288,1536]{1,0:T(8,128)(2,1)}, bf16[288,1536]{1,0:T(8,128)(2,1)}, u32[]{:S(2)}, u32[]{:S(2)}) collective-permute-start(bf16[288,1536]{1,0:T(8,128)(2,1)} %collective-permute-done.4.og_even), channel_id=1, source_target_pairs={{0,8},{4,12},{8,0},{12,4},{16,24},{20,28},{24,16},{28,20},{1,9},{5... | collective-permute-start | bytes 2654216 | tf_op jit(solution)/shard_map/ppermute | solution.py:445
  146.2 23.8 %all-to-all-start = ((bf16[4,288,384]{2,1,0:T(8,128)(2,1)}), bf16[4,288,384]{2,1,0:T(8,128)(2,1)S(1)}, u32[]{:S(2)}, u32[]{:S(2)}) async-start(bf16[4,288,384]{2,1,0:T(8,128)(2,1)} %bitcast.241), calls=%async_computation | async-start | bytes 1769472 | tf_op jit(solution)/shard_map/all_to_all | solution.py:780
  149.7 136.2 %all-gather.11.cloned.1.call-start = ((), (), s32[]{:S(2)}) async-start(), calls=%async_computation.12 | async-start | bytes 4915200 | tf_op jit(solution)/shard_map/all_gather | solution.py:790
  178.2 2.9 collective-permute-start.15
  178.2 24.7 %collective-permute-start.13 = (bf16[288,1664]{1,0:T(8,128)(2,1)}, bf16[288,1664]{1,0:T(8,128)(2,1)}, u32[]{:S(2)}, u32[]{:S(2)}) collective-permute-start(bf16[288,1664]{1,0:T(8,128)(2,1)} %concatenate.70.x_even), channel_id=1, source_target_pairs={{0,8},{4,12},{8,0},{12,4},{16,24},{20,28},{24,16},{28,20},{1,9},{5... | collective-permute-start | bytes 2875400 | tf_op jit(solution)/shard_map/ppermute | solution.py:445
  180.7 23.7 %collective-permute-start.14 = (bf16[288,1664]{1,0:T(8,128)(2,1)}, bf16[288,1664]{1,0:T(8,128)(2,1)}, u32[]{:S(2)}, u32[]{:S(2)}) collective-permute-start(bf16[288,1664]{1,0:T(8,128)(2,1)} %concatenate.70.x_even), channel_id=1, source_target_pairs={{0,16},{4,20},{8,24},{12,28},{16,0},{20,4},{24,8},{28,12},{1,17},{... | collective-permute-start | bytes 2875400 | tf_op jit(solution)/shard_map/ppermute | solution.py:445
  204.4 2.9 collective-permute-start.19
  204.4 327.6 %reduce-scatter.7.cloned.1.call-start = ((), (), s32[]{:S(2)}) async-start(), calls=%async_computation.9 | async-start | bytes 3932160 | tf_op jit(solution)/shard_map/reduce_scatter | solution.py:864
  204.7 24.8 %collective-permute-start.18 = (bf16[288,1664]{1,0:T(8,128)(2,1)}, bf16[288,1664]{1,0:T(8,128)(2,1)}, u32[]{:S(2)}, u32[]{:S(2)}) collective-permute-start(bf16[288,1664]{1,0:T(8,128)(2,1)} %collective-permute-done.14.x_even), channel_id=1, source_target_pairs={{0,8},{4,12},{8,0},{12,4},{16,24},{20,28},{24,16},{28,20},{1,9},{5... | collective-permute-start | bytes 2875400 | tf_op jit(solution)/shard_map/ppermute | solution.py:445
  229.4 4.2 collective-permute-start.21
  229.6 4.1 collective-permute-start.22
  230.0 32.2 %collective-permute-start.16 = (bf16[288,1664]{1,0:T(8,128)(2,1)}, bf16[288,1664]{1,0:T(8,128)(2,1)}, u32[]{:S(2)}, u32[]{:S(2)}) collective-permute-start(bf16[288,1664]{1,0:T(8,128)(2,1)} %collective-permute-done.14.x_even), channel_id=1, source_target_pairs={{0,4},{4,0},{8,12},{12,8},{16,20},{20,16},{24,28},{28,24},{1,5},{5... | collective-permute-start | bytes 2875400 | tf_op jit(solution)/shard_map/ppermute | solution.py:445
  230.1 25.7 %collective-permute-start.17 = (bf16[288,1664]{1,0:T(8,128)(2,1)}, bf16[288,1664]{1,0:T(8,128)(2,1)}, u32[]{:S(2)}, u32[]{:S(2)}) collective-permute-start(bf16[288,1664]{1,0:T(8,128)(2,1)} %get-tuple-element.172), channel_id=1, source_target_pairs={{0,4},{4,0},{8,12},{12,8},{16,20},{20,16},{24,28},{28,24},{1,5},{5... | collective-permute-start | bytes 2875400 | tf_op jit(solution)/shard_map/ppermute | solution.py:445
  230.5 28.0 %collective-permute-start.20 = (bf16[288,1664]{1,0:T(8,128)(2,1)}, bf16[288,1664]{1,0:T(8,128)(2,1)}, u32[]{:S(2)}, u32[]{:S(2)}) collective-permute-start(bf16[288,1664]{1,0:T(8,128)(2,1)} %get-tuple-element.185), channel_id=1, source_target_pairs={{0,4},{4,0},{8,12},{12,8},{16,20},{20,16},{24,28},{28,24},{1,5},{5... | collective-permute-start | bytes 2875400 | tf_op jit(solution)/shard_map/ppermute | solution.py:445
  255.6 5.4 collective-permute-start.23
  262.2 23.7 %collective-permute-start.24 = (bf16[288,1664]{1,0:T(8,128)(2,1)}, bf16[288,1664]{1,0:T(8,128)(2,1)}, u32[]{:S(2)}, u32[]{:S(2)}) collective-permute-start(bf16[288,1664]{1,0:T(8,128)(2,1)} %add_convert_fusion.2), channel_id=1, source_target_pairs={{0,16},{4,20},{8,24},{12,28},{16,0},{20,4},{24,8},{28,12},{1,17},{... | collective-permute-start | bytes 2875400 | tf_op jit(solution)/shard_map/ppermute | solution.py:445
  298.3 233.8 %reduce-scatter.9.cloned.1.call-start = ((), (), s32[]{:S(2)}) async-start(), calls=%async_computation.10 | async-start | bytes 3932160 | tf_op jit(solution)/shard_map/reduce_scatter | solution.py:868
  298.3 7.4 %collective-permute-start.26 = (bf16[288,1664]{1,0:T(8,128)(2,1)}, bf16[288,1664]{1,0:T(8,128)(2,1)}, u32[]{:S(2)}, u32[]{:S(2)}) collective-permute-start(bf16[288,1664]{1,0:T(8,128)(2,1)} %get-tuple-element.221), channel_id=1, source_target_pairs={{0,4},{4,0},{8,12},{12,8},{16,20},{20,16},{24,28},{28,24},{1,5},{5... | collective-permute-start | bytes 2875400 | tf_op jit(solution)/shard_map/ppermute | solution.py:445
  305.4 22.9 %collective-permute-start.25 = (bf16[288,1664]{1,0:T(8,128)(2,1)}, bf16[288,1664]{1,0:T(8,128)(2,1)}, u32[]{:S(2)}, u32[]{:S(2)}) collective-permute-start(bf16[288,1664]{1,0:T(8,128)(2,1)} %add_convert_fusion.1), channel_id=1, source_target_pairs={{0,8},{4,12},{8,0},{12,4},{16,24},{20,28},{24,16},{28,20},{1,9},{5... | collective-permute-start | bytes 2875400 | tf_op jit(solution)/shard_map/ppermute | solution.py:445
  305.8 38.2 %collective-permute-start.28 = (bf16[4,768,640]{2,1,0:T(8,128)(2,1)}, bf16[4,768,640]{2,1,0:T(8,128)(2,1)}, u32[]{:S(2)}, u32[]{:S(2)}) collective-permute-start(bf16[4,768,640]{2,1,0:T(8,128)(2,1)} %bitcast.219), channel_id=1, source_target_pairs={{0,4},{4,0},{8,12},{12,8},{16,20},{20,16},{24,28},{28,24},{1,5},{5... | collective-permute-start | bytes 11796488 | tf_op jit(solution)/shard_map/ppermute | solution.py:445
  308.2 24.0 %collective-permute-start.27 = (bf16[288,1664]{1,0:T(8,128)(2,1)}, bf16[288,1664]{1,0:T(8,128)(2,1)}, u32[]{:S(2)}, u32[]{:S(2)}) collective-permute-start(bf16[288,1664]{1,0:T(8,128)(2,1)} %add_convert_fusion), channel_id=1, source_target_pairs={{0,16},{4,20},{8,24},{12,28},{16,0},{20,4},{24,8},{28,12},{1,17},{... | collective-permute-start | bytes 2875400 | tf_op jit(solution)/shard_map/ppermute | solution.py:445
  345.0 38.1 %all-to-all-start.1 = ((bf16[288,4,384]{2,0,1:T(8,128)(2,1)}), bf16[288,4,384]{2,0,1:T(8,128)(2,1)}, u32[]{:S(2)}, u32[]{:S(2)}) async-start(bf16[288,4,384]{2,0,1:T(8,128)(2,1)} %bitcast.226), calls=%async_computation.1 | async-start | bytes 1769472 | tf_op jit(solution)/shard_map/all_to_all | solution.py:892
  349.2 207.5 %reduce-scatter.11.cloned.1.call-start = ((), (), s32[]{:S(2)}) async-start(), calls=%async_computation.11 | async-start | bytes 3932160 | tf_op jit(solution)/shard_map/reduce_scatter | solution.py:898
  349.3 22.1 %collective-permute-start.29 = (bf16[288,1536]{1,0:T(8,128)(2,1)}, bf16[288,1536]{1,0:T(8,128)(2,1)}, u32[]{:S(2)}, u32[]{:S(2)}) collective-permute-start(bf16[288,1536]{1,0:T(8,128)(2,1)} %get-tuple-element.241), channel_id=1, source_target_pairs={{0,4},{4,0},{8,12},{12,8},{16,20},{20,16},{24,28},{28,24},{1,5},{5... | collective-permute-start | bytes 2654216 | tf_op jit(solution)/shard_map/ppermute | solution.py:445
  349.3 22.6 %collective-permute-start.30 = (bf16[288,1536]{1,0:T(8,128)(2,1)}, bf16[288,1536]{1,0:T(8,128)(2,1)}, u32[]{:S(2)}, u32[]{:S(2)}) collective-permute-start(bf16[288,1536]{1,0:T(8,128)(2,1)} %get-tuple-element.242), channel_id=1, source_target_pairs={{0,4},{4,0},{8,12},{12,8},{16,20},{20,16},{24,28},{28,24},{1,5},{5... | collective-permute-start | bytes 2654216 | tf_op jit(solution)/shard_map/ppermute | solution.py:445
  349.8 22.1 %collective-permute-start.31 = (bf16[288,1536]{1,0:T(8,128)(2,1)}, bf16[288,1536]{1,0:T(8,128)(2,1)}, u32[]{:S(2)}, u32[]{:S(2)}) collective-permute-start(bf16[288,1536]{1,0:T(8,128)(2,1)} %get-tuple-element.243), channel_id=1, source_target_pairs={{0,4},{4,0},{8,12},{12,8},{16,20},{20,16},{24,28},{28,24},{1,5},{5... | collective-permute-start | bytes 2654216 | tf_op jit(solution)/shard_map/ppermute | solution.py:445
  349.9 22.0 %collective-permute-start.32 = (bf16[288,1536]{1,0:T(8,128)(2,1)}, bf16[288,1536]{1,0:T(8,128)(2,1)}, u32[]{:S(2)}, u32[]{:S(2)}) collective-permute-start(bf16[288,1536]{1,0:T(8,128)(2,1)} %get-tuple-element.244), channel_id=1, source_target_pairs={{0,4},{4,0},{8,12},{12,8},{16,20},{20,16},{24,28},{28,24},{1,5},{5... | collective-permute-start | bytes 2654216 | tf_op jit(solution)/shard_map/ppermute | solution.py:445
  357.7 25.4 %collective-permute-start.33 = (bf16[4,192,1536]{2,1,0:T(8,128)(2,1)}, bf16[4,192,1536]{2,1,0:T(8,128)(2,1)}, u32[]{:S(2)}, u32[]{:S(2)}) collective-permute-start(bf16[4,192,1536]{2,1,0:T(8,128)(2,1)} %dynamic-slice_bitcast_fusion), channel_id=1, source_target_pairs={{0,4},{4,0},{8,12},{12,8},{16,20},{20,16},{24,28},{28,24},{1,5},{5... | collective-permute-start | bytes 7077896 | tf_op jit(solution)/shard_map/ppermute | solution.py:445
  371.4 3.1 collective-permute-start.34
  383.8 44.1 %collective-permute-start.35 = (bf16[192,17]{0,1:T(8,128)(2,1)S(1)}, bf16[192,17]{0,1:T(8,128)(2,1)S(1)}, u32[]{:S(2)}, u32[]{:S(2)}) collective-permute-start(bf16[192,17]{0,1:T(8,128)(2,1)S(1)} %bitcast.249), channel_id=1, source_target_pairs={{0,16},{4,20},{8,24},{12,28},{16,0},{20,4},{24,8},{28,12},{1,17},{... | collective-permute-start | bytes 19592 | tf_op jit(solution)/shard_map/ppermute | solution.py:445
  389.6 38.3 %collective-permute-start.36 = (bf16[192,1536]{1,0:T(8,128)(2,1)S(1)}, bf16[192,1536]{1,0:T(8,128)(2,1)S(1)}, u32[]{:S(2)}, u32[]{:S(2)}) collective-permute-start(bf16[192,1536]{1,0:T(8,128)(2,1)S(1)} %get-tuple-element.375), channel_id=1, source_target_pairs={{0,16},{4,20},{8,24},{12,28},{16,0},{20,4},{24,8},{28,12},{1,17},{... | collective-permute-start | bytes 1769480 | tf_op jit(solution)/shard_map/ppermute | solution.py:445
  390.1 37.8 %collective-permute-start.37 = (bf16[288,1536]{1,0:T(8,128)(2,1)S(1)}, bf16[288,1536]{1,0:T(8,128)(2,1)S(1)}, u32[]{:S(2)}, u32[]{:S(2)}) collective-permute-start(bf16[288,1536]{1,0:T(8,128)(2,1)S(1)} %copy-done.26), channel_id=1, source_target_pairs={{0,16},{4,20},{8,24},{12,28},{16,0},{20,4},{24,8},{28,12},{1,17},{... | collective-permute-start | bytes 2654216 | tf_op jit(solution)/shard_map/ppermute | solution.py:445
  429.5 1.6 collective-permute-start.38
  432.1 4.9 collective-permute-start.39
  432.7 9.5 %collective-permute-start.41 = (bf16[128,256]{1,0:T(8,128)(2,1)S(1)}, bf16[128,256]{1,0:T(8,128)(2,1)S(1)}, u32[]{:S(2)}, u32[]{:S(2)}) collective-permute-start(bf16[128,256]{1,0:T(8,128)(2,1)S(1)} %get-tuple-element.395), channel_id=1, source_target_pairs={{0,16},{4,20},{8,24},{12,28},{16,0},{20,4},{24,8},{28,12},{1,17},{... | collective-permute-start | bytes 196616 | tf_op jit(solution)/shard_map/ppermute | solution.py:445
  437.1 5.1 collective-permute-start.40
  455.2 9.2 %collective-permute-start.42 = (bf16[4,192,640]{2,1,0:T(8,128)(2,1)}, bf16[4,192,640]{2,1,0:T(8,128)(2,1)}, u32[]{:S(2)}, u32[]{:S(2)}) collective-permute-start(bf16[4,192,640]{2,1,0:T(8,128)(2,1)} %dynamic-slice_bitcast_fusion.1), channel_id=1, source_target_pairs={{0,4},{4,0},{8,12},{12,8},{16,20},{20,16},{24,28},{28,24},{1,5},{5... | collective-permute-start | bytes 2949128 | tf_op jit(solution)/shard_map/ppermute | solution.py:445
  455.3 5.2 collective-permute-start.51
  455.4 5.1 collective-permute-start.50
  456.3 16.5 %collective-permute-start.49 = (bf16[192,1536]{1,0:T(8,128)(2,1)}, bf16[192,1536]{1,0:T(8,128)(2,1)}, u32[]{:S(2)}, u32[]{:S(2)}) collective-permute-start(bf16[192,1536]{1,0:T(8,128)(2,1)} %get-tuple-element.286), channel_id=1, source_target_pairs={{0,16},{4,20},{8,24},{12,28},{16,0},{20,4},{24,8},{28,12},{1,17},{... | collective-permute-start | bytes 1769480 | tf_op jit(solution)/shard_map/ppermute | solution.py:445
  459.2 15.2 %collective-permute-start.48 = (bf16[192,1536]{1,0:T(8,128)(2,1)}, bf16[192,1536]{1,0:T(8,128)(2,1)}, u32[]{:S(2)}, u32[]{:S(2)}) collective-permute-start(bf16[192,1536]{1,0:T(8,128)(2,1)} %add_convert_fusion.12), channel_id=1, source_target_pairs={{0,8},{4,12},{8,0},{12,4},{16,24},{20,28},{24,16},{28,20},{1,9},{5... | collective-permute-start | bytes 1769480 | tf_op jit(solution)/shard_map/ppermute | solution.py:445
  460.5 68.8 %all-to-all-start.2 = ((bf16[4,288,640]{2,1,0:T(8,128)(2,1)}), bf16[4,288,640]{2,1,0:T(8,128)(2,1)S(1)}, u32[]{:S(2)}, u32[]{:S(2)}) async-start(bf16[4,288,640]{2,1,0:T(8,128)(2,1)} %bitcast.49), calls=%async_computation.2 | async-start | bytes 2949120 | tf_op jit(solution)/shard_map/all_to_all | solution.py:958
  464.1 97.3 %reduce-scatter.13.cloned.1.call-start = ((), (), s32[]{:S(2)}) async-start(), calls=%async_computation.13 | async-start | bytes 983040
  466.2 11.0 %collective-permute-start.43 = (bf16[192,640]{1,0:T(8,128)(2,1)S(1)}, bf16[192,640]{1,0:T(8,128)(2,1)S(1)}, u32[]{:S(2)}, u32[]{:S(2)}) collective-permute-start(bf16[192,640]{1,0:T(8,128)(2,1)S(1)} %get-tuple-element.385), channel_id=1, source_target_pairs={{0,16},{4,20},{8,24},{12,28},{16,0},{20,4},{24,8},{28,12},{1,17},{... | collective-permute-start | bytes 737288 | tf_op jit(solution)/shard_map/ppermute | solution.py:445
  476.7 11.6 %collective-permute-start.47 = (bf16[192,640]{1,0:T(8,128)(2,1)S(1)}, bf16[192,640]{1,0:T(8,128)(2,1)S(1)}, u32[]{:S(2)}, u32[]{:S(2)}) collective-permute-start(bf16[192,640]{1,0:T(8,128)(2,1)S(1)} %get-tuple-element.384), channel_id=1, source_target_pairs={{0,16},{4,20},{8,24},{12,28},{16,0},{20,4},{24,8},{28,12},{1,17},{... | collective-permute-start | bytes 737288 | tf_op jit(solution)/shard_map/ppermute | solution.py:445
  479.6 64.5 %collective-permute-start.44 = (bf16[288,1536]{1,0:T(8,128)(2,1)}, bf16[288,1536]{1,0:T(8,128)(2,1)}, u32[]{:S(2)}, u32[]{:S(2)}) collective-permute-start(bf16[288,1536]{1,0:T(8,128)(2,1)} %add_convert_fusion.7), channel_id=1, source_target_pairs={{0,8},{4,12},{8,0},{12,4},{16,24},{20,28},{24,16},{28,20},{1,9},{5... | collective-permute-start | bytes 2654216 | tf_op jit(solution)/shard_map/ppermute | solution.py:445
  483.1 61.0 %collective-permute-start.45 = (bf16[288,1536]{1,0:T(8,128)(2,1)}, bf16[288,1536]{1,0:T(8,128)(2,1)}, u32[]{:S(2)}, u32[]{:S(2)}) collective-permute-start(bf16[288,1536]{1,0:T(8,128)(2,1)} %add_convert_fusion.6), channel_id=1, source_target_pairs={{0,16},{4,20},{8,24},{12,28},{16,0},{20,4},{24,8},{28,12},{1,17},{... | collective-permute-start | bytes 2654216 | tf_op jit(solution)/shard_map/ppermute | solution.py:445
  485.1 21.0 %collective-permute-start.46 = (bf16[192,640]{1,0:T(8,128)(2,1)S(1)}, bf16[192,640]{1,0:T(8,128)(2,1)S(1)}, u32[]{:S(2)}, u32[]{:S(2)}) collective-permute-start(bf16[192,640]{1,0:T(8,128)(2,1)S(1)} %fusion.46), channel_id=1, source_target_pairs={{0,8},{4,12},{8,0},{12,4},{16,24},{20,28},{24,16},{28,20},{1,9},{5... | collective-permute-start | bytes 737288 | tf_op jit(solution)/shard_map/ppermute | solution.py:445
  (47 other events, 326.9 us)
Sparse Core Ops, SparseCore 0:
  9.6 79.8 all-gather.6
  112.3 44.8 all-gather.8
  204.5 73.9 all-gather.10
  298.4 57.3 reduce-scatter.6
  358.0 66.0 reduce-scatter.8
  439.5 82.6 reduce-scatter.10
  524.5 29.7 reduce-scatter.12

commit v10 on v9

--- a/solution.py
+++ b/solution.py
@@ -960,9 +960,9 @@
     keep, give = halves_by_core(transposed_times(normed_low, lin_all).astype(bf16), "shard")
     qkv_sums = chip_sums(keep, exchange(give, "shard", 1), "shard")
     qkv_pending = reduce_several(qkv_sums, "shard")
-    arrived, odd = lax.optimization_barrier(([piece for _, piece in qkv_pending], odd))
-    qkv_pending = [(j, piece) for (j, _), piece in zip(qkv_pending, arrived)]
-    grad_qkv = add_all(reduce_singles(qkv_sums, qkv_pending, "shard"))
+    qkv_pieces = reduce_singles(qkv_sums, qkv_pending, "shard")
+    qkv_pieces, odd = lax.optimization_barrier((qkv_pieces, odd))
+    grad_qkv = add_all(qkv_pieces)
     for j in [0] + singles:
         out_sums[j] = add_rounded(out_parts[j], odd[j])
     out_sums = {j: out_sums[j] for j in [0] + singles}

time: 580 us -> 583 us (level)
    ppermute x52, waiting for transfers between devices: 56.8 us -> 43.7 us  [exchange(): return lax.ppermute(values, axis_name, [(i, i ^ bit) for i in range(count)])]
    all_to_all x1, waiting for transfers between devices: 15.5 us -> 27.2 us  [on_device(): lax.all_to_all(lin_all, 'seq', split_axis=0, concat_axis=1, tiled=True)]
    unnamed x125 -> x131, local copies, waits for them, and re-layouts: 25.4 us -> 25.5 us
  transfers between devices with their start and end apart: 62 -> 62, of which waited for: 21 -> 19; matrix products, arithmetic and copies ran while one was open for 27% -> 27% of each run, Pallas kernels for 26% -> 26%
where the time goes in v10:
time: 583 us; the launch traced here: 575 us
  Pallas kernels  148 us (25%)
  waiting for transfers between devices  105 us (18%)
  matrix products  79.1 us (14%)
  blocking collectives  60.5 us (10%)
  other arithmetic  59.9 us (10%)
  local copies, waits for them, and re-layouts  59.4 us (10%)
  starting transfers between devices  47.1 us (8%)
  between operations  15.7 us (3%)
    pallas_call x4, Pallas kernels, expert_pair(): pl.pallas_call(partial(expert_body, experts_all), out_shape=out_shape, gr...  87.2 us
    dot_general x6, matrix products, transposed_times(): lax.dot_general(left_side, right_side, (((0,), (0,)), ((), ())), precisio...  48.9 us
    ppermute x52, waiting for transfers between devices, exchange(): return lax.ppermute(values, axis_name, [(i, i ^ bit) for i in range(count)])  43.7 us
    pallas_call x1, Pallas kernels, attend_backward(): pl.pallas_call(partial(attend_backward_body, group, kv_heads), out_shape=...  36.3 us
    ppermute x52, starting transfers between devices, exchange(): return lax.ppermute(values, axis_name, [(i, i ^ bit) for i in range(count)])  33.7 us
    convert_element_type x17, other arithmetic, add_rounded(): (left_side.astype(jnp.float32) + right_side.astype(jnp.float32)).astype(j...  27.7 us
    all_to_all x1, waiting for transfers between devices, on_device(): lax.all_to_all(lin_all, 'seq', split_axis=0, concat_axis=1, tiled=True)  27.2 us
    all_gather x1, blocking collectives, on_device(): out_weight = lax.all_gather(w_out, 'seq', axis=0, tiled=True)  25.8 us
  transfers between devices with their start and end apart: 62, of which 19 were waited for; matrix products, arithmetic and copies ran while one was open for 27% of the time, Pallas kernels for 26%

profile of v10, /device:TPU:0, one launch (start us, length us, event | category | flops | bytes accessed | tf_op | source)
XLA Modules:
  0.0 575.0 jit_solution(16645296131291609011)
XLA Ops:
  11.1 2.6 collective-permute-start.1
  15.8 25.8 %all_gather.28 = bf16[1536,192]{0,1:T(8,128)(2,1)} all-gather(bf16[384,192]{0,1:T(8,128)(2,1)} %param.18), channel_id=1, replica_groups=mesh['shard'=8,'seq'=4] {'seq'}, dimensions={0}, use_global_device_ids=true | all-gather | bytes 737280 | tf_op jit(solution)/shard_map/all_gather | solution.py:732
  42.2 14.3 %all-gather.1 = bf16[4,48,18]{1,2,0:T(8,128)(2,1)S(1)} all-gather(bf16[1,48,18]{1,2,0:T(8,128)(2,1)S(1)} %maximum_bitcast_fusion.1), channel_id=1, replica_groups=mesh['shard'=8,'seq'=4] {'seq'}, dimensions={0}, use_global_device_ids=true | all-gather | bytes 8640 | tf_op jit(solution)/shard_map/all_gather | solution.py:714
  56.7 9.3 %all-gather.2 = bf16[8,192,18]{1,2,0:T(8,128)(2,1)S(1)} all-gather(bf16[1,192,18]{1,2,0:T(8,128)(2,1)S(1)} %reshape.372), channel_id=1, replica_groups=mesh['shard'=8,'seq'=4] {'shard'}, dimensions={0}, use_global_device_ids=true | all-gather | bytes 62208 | tf_op jit(solution)/shard_map/all_gather | solution.py:715
  70.8 4.5 collective-permute-done.7
  82.6 6.9 %all-gather.7.cloned.1.call-done = bf16[1152,1536]{1,0:T(8,128)(2,1)} async-done(((bf16[288,1536]{1,0:T(8,128)(2,1)}), bf16[1152,1536]{1,0:T(8,128)(2,1)}) %all-gather.7.cloned.1.call-update) | async-done | bytes 3538960 | tf_op jit(solution)/shard_map/all_gather | solution.py:719
  91.2 2.9 fusion
  94.3 4.7 fusion.24
  101.1 11.1 %all_gather.27.kp_ref.vp_ref = bf16[1024,256]{1,0:T(8,128)(2,1)} all-gather(bf16[128,256]{1,0:T(8,128)(2,1)S(1)} %fusion.66), channel_id=1, replica_groups=mesh['shard'=8,'seq'=4] {'shard'}, dimensions={0}, use_global_device_ids=true | all-gather | bytes 589824 | tf_op jit(solution)/shard_map/all_gather | solution.py:762
  118.8 25.0 %attend_forward.1 = (bf16[1152,384]{1,0:T(8,128)(2,1)}, f32[6,1,1152]{2,1,0:T(1,128)}) custom-call(s32[1]{0:T(128)} %bitcast.9.index_ref, bf16[1152,384]{1,0:T(8,128)(2,1)} %copy.135.q_ref, bf16[1024,256]{1,0:T(8,128)(2,1)} %all_gather.27.kp_ref.vp_ref, bf16[1024,256]{1,0:T(8,128)(2,1)} %all_gather.27.kp_ref.vp_ref, ...), custom_call_target="tpu_custom_call" | custom-call | flops 9059696640 | bytes 3538944 | tf_op jit(solution)/shard_map/attend_forward/pallas_call | solution.py:376
  143.8 2.5 collective-permute-done.12.og_even
  146.3 3.5 all-to-all-start
  150.1 2.3 constant_dynamic-slice_fusion.4
  152.3 17.8 %all-to-all-done = bf16[4,288,384]{2,1,0:T(8,128)(2,1)S(1)} async-done(((bf16[4,288,384]{2,1,0:T(8,128)(2,1)}), bf16[4,288,384]{2,1,0:T(8,128)(2,1)S(1)}, u32[]{:S(2)}, u32[]{:S(2)}) %all-to-all-start) | async-done | bytes 884768 | tf_op jit(solution)/shard_map/all_to_all | solution.py:780
  171.2 4.3 multiply_reduce_fusion.2
  178.4 2.5 collective-permute-start.13
  181.2 21.4 %experts.4 = (bf16[2304,1536]{1,0:T(8,128)(2,1)}, bf16[2304,1536]{1,0:T(8,128)(2,1)}, bf16[2,2304,1024]{2,1,0:T(8,128)(2,1)}, bf16[2304,1024]{1,0:T(8,128)(2,1)}...) custom-call(s32[1]{0:T(128)} %bitcast.24.index_ref, ...), custom_call_target="tpu_custom_call" | custom-call | flops 10871635968 | bytes 27131904 | tf_op jit(solution)/shard_map/experts/pallas_call | solution.py:654
  207.4 22.2 %experts.5 = (bf16[2304,1536]{1,0:T(8,128)(2,1)}, bf16[2304,1536]{1,0:T(8,128)(2,1)}, bf16[2,2304,1024]{2,1,0:T(8,128)(2,1)}, bf16[2304,1024]{1,0:T(8,128)(2,1)}...) custom-call(s32[1]{0:T(128)} %bitcast.24.index_ref, ...), custom_call_target="tpu_custom_call", output_to_operand_aliasing={{0}: (8, {}), {1}: (9, {}), {2}: (10, {}), {3}: (11, {})} | custom-call | flops 10871635968 | bytes 27131904 | tf_op jit(solution)/shard_map/experts/pallas_call | solution.py:654
  230.8 3.0 collective-permute-done.22.og_odd
  233.8 21.9 %experts.6 = (bf16[2304,1536]{1,0:T(8,128)(2,1)}, bf16[2304,1536]{1,0:T(8,128)(2,1)}, bf16[2,2304,1024]{2,1,0:T(8,128)(2,1)}, bf16[2304,1024]{1,0:T(8,128)(2,1)}...) custom-call(s32[1]{0:T(128)} %bitcast.24.index_ref, ...), custom_call_target="tpu_custom_call", output_to_operand_aliasing={{0}: (8, {}), {1}: (9, {}), {2}: (10, {}), {3}: (11, {})} | custom-call | flops 10871635968 | bytes 27131904 | tf_op jit(solution)/shard_map/experts/pallas_call | solution.py:654
  256.0 2.7 add_convert_fusion.4
  258.7 2.5 add_convert_fusion.3
  262.4 21.6 %experts.7 = (bf16[2304,1536]{1,0:T(8,128)(2,1)}, bf16[2304,1536]{1,0:T(8,128)(2,1)}, bf16[2,2304,1024]{2,1,0:T(8,128)(2,1)}, bf16[2304,1024]{1,0:T(8,128)(2,1)}...) custom-call(s32[1]{0:T(128)} %bitcast.24.index_ref, ...), custom_call_target="tpu_custom_call", output_to_operand_aliasing={{0}: (8, {}), {1}: (9, {}), {2}: (10, {}), {3}: (11, {})} | custom-call | flops 10871635968 | bytes 27131904 | tf_op jit(solution)/shard_map/experts/pallas_call | solution.py:654
  284.1 2.1 collective-permute-done.24
  286.2 12.3 %convolution_convert_fusion.1 = bf16[1536,1024]{1,0:T(8,128)(2,1)} fusion(bf16[2304,1536]{1,0:T(8,128)(2,1)} %get-tuple-element.224, bf16[2304,1024]{1,0:T(8,128)(2,1)} %get-tuple-element.225), kind=kOutput, calls=%fused_computation.16 | convolution fusion | flops 7249330176 | bytes 14942208 | tf_op jit(solution)/shard_map/dot_general | solution.py:71
  300.6 2.3 copy.145.sin_ref
  302.9 2.7 add_convert_fusion.1
  306.0 2.4 add_convert_fusion
  309.0 12.9 %fusion.10 = bf16[1536,1024]{1,0:T(8,128)(2,1)} fusion(bf16[2304,1536]{1,0:T(8,128)(2,1)} %get-tuple-element.247, bf16[2,2304,1024]{2,1,0:T(8,128)(2,1)} %get-tuple-element.228), kind=kOutput, calls=%fused_computation.14 | convolution fusion | flops 7249330176 | bytes 14942208 | tf_op jit(solution)/shard_map/dot_general | solution.py:71
  322.0 6.5 %collective-permute-done.25 = bf16[288,1664]{1,0:T(8,128)(2,1)} collective-permute-done((bf16[288,1664]{1,0:T(8,128)(2,1)}, bf16[288,1664]{1,0:T(8,128)(2,1)}, u32[]{:S(2)}, u32[]{:S(2)}) %collective-permute-start.25) | collective-permute-done | bytes 958496 | tf_op jit(solution)/shard_map/ppermute | solution.py:445
  328.5 3.8 collective-permute-done.27
  332.3 2.1 convert_add_fusion.3
  334.8 2.5 multiply_reduce_fusion
  337.4 2.2 subtract_add_fusion
  339.6 4.5 convolution_convert_fusion.3
  345.2 4.2 all-to-all-start.1
  350.5 4.4 convolution_convert_fusion
  357.9 13.0 %fusion.13 = bf16[1536,1024]{1,0:T(8,128)(2,1)} fusion(bf16[2304,1536]{1,0:T(8,128)(2,1)} %get-tuple-element.247, bf16[2,2304,1024]{2,1,0:T(8,128)(2,1)} %get-tuple-element.228), kind=kOutput, calls=%fused_computation.15 | convolution fusion | flops 7249330176 | bytes 14942208 | tf_op jit(solution)/shard_map/dot_general | solution.py:71
  372.2 2.6 add_convert_fusion.10
  374.7 8.6 %all-to-all-done.1 = bf16[288,4,384]{2,0,1:T(8,128)(2,1)} async-done(((bf16[288,4,384]{2,0,1:T(8,128)(2,1)}), bf16[288,4,384]{2,0,1:T(8,128)(2,1)}, u32[]{:S(2)}, u32[]{:S(2)}) %all-to-all-start.1) | async-done | bytes 884768 | tf_op jit(solution)/shard_map/all_to_all | solution.py:892
  385.5 3.0 fusion.3
  391.8 36.3 %attend_backward.1 = (bf16[1152,384]{1,0:T(8,128)(2,1)}, bf16[1024,256]{1,0:T(8,128)(2,1)}, f32[1152,256]{1,0:T(8,128)}) custom-call(s32[1]{0:T(128)} %bitcast.9.index_ref, bf16[1152,384]{1,0:T(8,128)(2,1)} %copy.135.q_ref, bf16[1152,384]{1,0:T(8,128)(2,1)} %bitcast.28.grad_ref, bf16[1152,384]{1,0:T(8,128)(2,1)} %get-tuple-element.164.mixed_ref, ...), custom_call_target="tpu_custom_call" | custom-call | flops 22649241600 | bytes 3538944 | tf_op jit(solution)/shard_map/attend_backward/pallas_call | solution.py:406
  434.4 2.8 collective-permute-done.39
  439.5 1.8 slice.331
  444.7 2.5 maximum_maximum_fusion
  447.2 5.8 %convolution_convert_fusion.2 = bf16[1536,640]{1,0:T(8,128)(2,1)S(1)} fusion(bf16[1152,640]{1,0:T(8,128)(2,1)} %maximum_maximum_fusion, bf16[1152,1536]{1,0:T(8,128)(2,1)} %all-gather.7.cloned.1.call-done, f32[1536]{0:T(1024)S(1)} %get-tuple-element.371, f32[1152]{0:T(1024)S(1)} %copy-done.47), kind=kOutput, calls=%fused_computation.17 | convolution fusion | flops 2272985088 | bytes 6990336 | tf_op jit(solution)/shard_map/dot_general | solution.py:71
  455.0 2.0 collective-permute-start.49
  462.1 5.0 all-to-all-start.2
  467.9 8.9 %collective-permute-done.43 = bf16[192,640]{1,0:T(8,128)(2,1)} collective-permute-done((bf16[192,640]{1,0:T(8,128)(2,1)}, bf16[192,640]{1,0:T(8,128)(2,1)}, u32[]{:S(2)}, u32[]{:S(2)}) %collective-permute-start.43) | collective-permute-done | bytes 245792 | tf_op jit(solution)/shard_map/ppermute | solution.py:445
  479.2 2.4 fusion.44
  481.7 2.7 collective-permute-done.44
  484.4 2.4 add_convert_fusion.7
  488.0 2.3 add_convert_fusion.6
  490.3 1.8 collective-permute-start.47
  494.0 1.9 pad_maximum_fusion.4
  496.0 2.3 copy.155
  499.9 2.6 add_convert_fusion.9
  502.5 27.2 %all-to-all-done.2 = bf16[4,288,640]{2,1,0:T(8,128)(2,1)S(1)} async-done(((bf16[4,288,640]{2,1,0:T(8,128)(2,1)}), bf16[4,288,640]{2,1,0:T(8,128)(2,1)S(1)}, u32[]{:S(2)}, u32[]{:S(2)}) %all-to-all-start.2) | async-done | bytes 1474592 | tf_op jit(solution)/shard_map/all_to_all | solution.py:958
  532.4 1.9 fusion.34
  541.6 2.8 convolution_add_fusion.2
  547.1 3.0 copy.154
  550.1 2.8 slice_bitcast_fusion.1
  556.7 3.6 fusion.20
  563.0 2.0 pad_maximum_fusion.1
  (341 shorter events, 105.2 us)
Async XLA Ops:
  7.2 82.3 %all-gather.7.cloned.1.call-start = ((), (), s32[]{:S(2)}) async-start(), calls=%async_computation.7 | async-start | bytes 4423680 | tf_op jit(solution)/shard_map/all_gather | solution.py:719
  7.9 163.2 %all-gather.9.cloned.1.call-start = ((), (), s32[]{:S(2)}) async-start(), calls=%async_computation.8 | async-start | bytes 5308416 | tf_op jit(solution)/shard_map/all_gather | solution.py:767
  10.6 60.3 %copy-start.18 = (bf16[192,640]{1,0:T(8,128)(2,1)}, bf16[192,640]{1,0:T(8,128)(2,1)S(1)}, u32[]{:S(2)}) copy-start(bf16[192,640]{1,0:T(8,128)(2,1)S(1)} %constant_dynamic-update-slice_fusion) | copy-start | bytes 737284
  10.6 58.2 %collective-permute-start = (bf16[192,640]{1,0:T(8,128)(2,1)S(1)}, bf16[192,640]{1,0:T(8,128)(2,1)}, u32[]{:S(2)}, u32[]{:S(2)}) collective-permute-start(bf16[192,640]{1,0:T(8,128)(2,1)S(1)} %constant_dynamic-update-slice_fusion), channel_id=1, source_target_pairs={{0,4},{4,0},{8,12},{12,8},{16,20},{20,16},{24,28},{28,24},{1,5},{5... | collective-permute-start | bytes 737288 | tf_op jit(solution)/shard_map/ppermute | solution.py:445
  11.1 55.7 %collective-permute-start.1 = (bf16[192,640]{1,0:T(8,128)(2,1)S(1)}, bf16[192,640]{1,0:T(8,128)(2,1)}, u32[]{:S(2)}, u32[]{:S(2)}) collective-permute-start(bf16[192,640]{1,0:T(8,128)(2,1)S(1)} %constant_dynamic-update-slice_fusion), channel_id=1, source_target_pairs={{0,8},{4,12},{8,0},{12,4},{16,24},{20,28},{24,16},{28,20},{1,9},{5... | collective-permute-start | bytes 737288 | tf_op jit(solution)/shard_map/ppermute | solution.py:445
  13.7 53.2 %collective-permute-start.2 = (bf16[192,640]{1,0:T(8,128)(2,1)S(1)}, bf16[192,640]{1,0:T(8,128)(2,1)S(1)}, u32[]{:S(2)}, u32[]{:S(2)}) collective-permute-start(bf16[192,640]{1,0:T(8,128)(2,1)S(1)} %constant_dynamic-update-slice_fusion), channel_id=1, source_target_pairs={{0,16},{4,20},{8,24},{12,28},{16,0},{20,4},{24,8},{28,12},{1,17},{... | collective-permute-start | bytes 737288 | tf_op jit(solution)/shard_map/ppermute | solution.py:445
  15.2 51.7 %collective-permute-start.3 = (bf16[288,1536]{1,0:T(8,128)(2,1)}, bf16[288,1536]{1,0:T(8,128)(2,1)}, u32[]{:S(2)}, u32[]{:S(2)}) collective-permute-start(bf16[288,1536]{1,0:T(8,128)(2,1)} %og_even.1), channel_id=1, source_target_pairs={{0,8},{4,12},{8,0},{12,4},{16,24},{20,28},{24,16},{28,20},{1,9},{5... | collective-permute-start | bytes 2654216 | tf_op jit(solution)/shard_map/ppermute | solution.py:445
  15.7 51.1 %collective-permute-start.4 = (bf16[288,1536]{1,0:T(8,128)(2,1)}, bf16[288,1536]{1,0:T(8,128)(2,1)}, u32[]{:S(2)}, u32[]{:S(2)}) collective-permute-start(bf16[288,1536]{1,0:T(8,128)(2,1)} %og_even.1), channel_id=1, source_target_pairs={{0,16},{4,20},{8,24},{12,28},{16,0},{20,4},{24,8},{28,12},{1,17},{... | collective-permute-start | bytes 2654216 | tf_op jit(solution)/shard_map/ppermute | solution.py:445
  66.7 49.5 %copy-start.16 = (f32[1152,1,32]{0,2,1:T(8,128)}, f32[1152,1,32]{0,2,1:T(8,128)S(1)}, u32[]{:S(2)}) copy-start(f32[1152,1,32]{0,2,1:T(8,128)S(1)} %get-tuple-element.156) | copy-start | bytes 442372
  66.9 8.4 %collective-permute-start.5 = (bf16[192,640]{1,0:T(8,128)(2,1)}, bf16[192,640]{1,0:T(8,128)(2,1)S(1)}, u32[]{:S(2)}, u32[]{:S(2)}) collective-permute-start(bf16[192,640]{1,0:T(8,128)(2,1)} %collective-permute-done.1), channel_id=1, source_target_pairs={{0,4},{4,0},{8,12},{12,8},{16,20},{20,16},{24,28},{28,24},{1,5},{5... | collective-permute-start | bytes 737288 | tf_op jit(solution)/shard_map/ppermute | solution.py:445
  67.3 8.0 %collective-permute-start.7 = (bf16[192,640]{1,0:T(8,128)(2,1)S(1)}, bf16[192,640]{1,0:T(8,128)(2,1)S(1)}, u32[]{:S(2)}, u32[]{:S(2)}) collective-permute-start(bf16[192,640]{1,0:T(8,128)(2,1)S(1)} %collective-permute-done.2), channel_id=1, source_target_pairs={{0,8},{4,12},{8,0},{12,4},{16,24},{20,28},{24,16},{28,20},{1,9},{5... | collective-permute-start | bytes 737288 | tf_op jit(solution)/shard_map/ppermute | solution.py:445
  69.8 5.6 collective-permute-start.6
  75.3 1.5 collective-permute-start.8
  112.2 31.6 %collective-permute-start.9 = (bf16[288,1536]{1,0:T(8,128)(2,1)}, bf16[288,1536]{1,0:T(8,128)(2,1)}, u32[]{:S(2)}, u32[]{:S(2)}) collective-permute-start(bf16[288,1536]{1,0:T(8,128)(2,1)} %og_even.1), channel_id=1, source_target_pairs={{0,4},{4,0},{8,12},{12,8},{16,20},{20,16},{24,28},{28,24},{1,5},{5... | collective-permute-start | bytes 2654216 | tf_op jit(solution)/shard_map/ppermute | solution.py:445
  112.6 31.2 %collective-permute-start.10 = (bf16[288,1536]{1,0:T(8,128)(2,1)}, bf16[288,1536]{1,0:T(8,128)(2,1)}, u32[]{:S(2)}, u32[]{:S(2)}) collective-permute-start(bf16[288,1536]{1,0:T(8,128)(2,1)} %collective-permute-done.3.og_even), channel_id=1, source_target_pairs={{0,4},{4,0},{8,12},{12,8},{16,20},{20,16},{24,28},{28,24},{1,5},{5... | collective-permute-start | bytes 2654216 | tf_op jit(solution)/shard_map/ppermute | solution.py:445
  112.8 31.0 %collective-permute-start.11 = (bf16[288,1536]{1,0:T(8,128)(2,1)}, bf16[288,1536]{1,0:T(8,128)(2,1)}, u32[]{:S(2)}, u32[]{:S(2)}) collective-permute-start(bf16[288,1536]{1,0:T(8,128)(2,1)} %collective-permute-done.4.og_even), channel_id=1, source_target_pairs={{0,4},{4,0},{8,12},{12,8},{16,20},{20,16},{24,28},{28,24},{1,5},{5... | collective-permute-start | bytes 2654216 | tf_op jit(solution)/shard_map/ppermute | solution.py:445
  114.7 31.6 %collective-permute-start.12 = (bf16[288,1536]{1,0:T(8,128)(2,1)}, bf16[288,1536]{1,0:T(8,128)(2,1)}, u32[]{:S(2)}, u32[]{:S(2)}) collective-permute-start(bf16[288,1536]{1,0:T(8,128)(2,1)} %collective-permute-done.4.og_even), channel_id=1, source_target_pairs={{0,8},{4,12},{8,0},{12,4},{16,24},{20,28},{24,16},{28,20},{1,9},{5... | collective-permute-start | bytes 2654216 | tf_op jit(solution)/shard_map/ppermute | solution.py:445
  146.3 23.8 %all-to-all-start = ((bf16[4,288,384]{2,1,0:T(8,128)(2,1)}), bf16[4,288,384]{2,1,0:T(8,128)(2,1)S(1)}, u32[]{:S(2)}, u32[]{:S(2)}) async-start(bf16[4,288,384]{2,1,0:T(8,128)(2,1)} %bitcast.239), calls=%async_computation | async-start | bytes 1769472 | tf_op jit(solution)/shard_map/all_to_all | solution.py:780
  149.8 136.3 %all-gather.11.cloned.1.call-start = ((), (), s32[]{:S(2)}) async-start(), calls=%async_computation.12 | async-start | bytes 4915200 | tf_op jit(solution)/shard_map/all_gather | solution.py:790
  178.4 2.9 collective-permute-start.15
  178.4 24.7 %collective-permute-start.13 = (bf16[288,1664]{1,0:T(8,128)(2,1)}, bf16[288,1664]{1,0:T(8,128)(2,1)}, u32[]{:S(2)}, u32[]{:S(2)}) collective-permute-start(bf16[288,1664]{1,0:T(8,128)(2,1)} %concatenate.70.x_even), channel_id=1, source_target_pairs={{0,8},{4,12},{8,0},{12,4},{16,24},{20,28},{24,16},{28,20},{1,9},{5... | collective-permute-start | bytes 2875400 | tf_op jit(solution)/shard_map/ppermute | solution.py:445
  180.9 23.7 %collective-permute-start.14 = (bf16[288,1664]{1,0:T(8,128)(2,1)}, bf16[288,1664]{1,0:T(8,128)(2,1)}, u32[]{:S(2)}, u32[]{:S(2)}) collective-permute-start(bf16[288,1664]{1,0:T(8,128)(2,1)} %concatenate.70.x_even), channel_id=1, source_target_pairs={{0,16},{4,20},{8,24},{12,28},{16,0},{20,4},{24,8},{28,12},{1,17},{... | collective-permute-start | bytes 2875400 | tf_op jit(solution)/shard_map/ppermute | solution.py:445
  204.5 2.9 collective-permute-start.19
  204.6 327.8 %reduce-scatter.7.cloned.1.call-start = ((), (), s32[]{:S(2)}) async-start(), calls=%async_computation.9 | async-start | bytes 3932160 | tf_op jit(solution)/shard_map/reduce_scatter | solution.py:864
  204.8 24.8 %collective-permute-start.18 = (bf16[288,1664]{1,0:T(8,128)(2,1)}, bf16[288,1664]{1,0:T(8,128)(2,1)}, u32[]{:S(2)}, u32[]{:S(2)}) collective-permute-start(bf16[288,1664]{1,0:T(8,128)(2,1)} %collective-permute-done.14.x_even), channel_id=1, source_target_pairs={{0,8},{4,12},{8,0},{12,4},{16,24},{20,28},{24,16},{28,20},{1,9},{5... | collective-permute-start | bytes 2875400 | tf_op jit(solution)/shard_map/ppermute | solution.py:445
  229.6 4.2 collective-permute-start.21
  229.7 4.1 collective-permute-start.22
  230.2 32.2 %collective-permute-start.16 = (bf16[288,1664]{1,0:T(8,128)(2,1)}, bf16[288,1664]{1,0:T(8,128)(2,1)}, u32[]{:S(2)}, u32[]{:S(2)}) collective-permute-start(bf16[288,1664]{1,0:T(8,128)(2,1)} %collective-permute-done.14.x_even), channel_id=1, source_target_pairs={{0,4},{4,0},{8,12},{12,8},{16,20},{20,16},{24,28},{28,24},{1,5},{5... | collective-permute-start | bytes 2875400 | tf_op jit(solution)/shard_map/ppermute | solution.py:445
  230.3 25.7 %collective-permute-start.17 = (bf16[288,1664]{1,0:T(8,128)(2,1)}, bf16[288,1664]{1,0:T(8,128)(2,1)}, u32[]{:S(2)}, u32[]{:S(2)}) collective-permute-start(bf16[288,1664]{1,0:T(8,128)(2,1)} %get-tuple-element.174), channel_id=1, source_target_pairs={{0,4},{4,0},{8,12},{12,8},{16,20},{20,16},{24,28},{28,24},{1,5},{5... | collective-permute-start | bytes 2875400 | tf_op jit(solution)/shard_map/ppermute | solution.py:445
  230.7 28.0 %collective-permute-start.20 = (bf16[288,1664]{1,0:T(8,128)(2,1)}, bf16[288,1664]{1,0:T(8,128)(2,1)}, u32[]{:S(2)}, u32[]{:S(2)}) collective-permute-start(bf16[288,1664]{1,0:T(8,128)(2,1)} %get-tuple-element.187), channel_id=1, source_target_pairs={{0,4},{4,0},{8,12},{12,8},{16,20},{20,16},{24,28},{28,24},{1,5},{5... | collective-permute-start | bytes 2875400 | tf_op jit(solution)/shard_map/ppermute | solution.py:445
  255.8 5.4 collective-permute-start.23
  262.4 23.7 %collective-permute-start.24 = (bf16[288,1664]{1,0:T(8,128)(2,1)}, bf16[288,1664]{1,0:T(8,128)(2,1)}, u32[]{:S(2)}, u32[]{:S(2)}) collective-permute-start(bf16[288,1664]{1,0:T(8,128)(2,1)} %add_convert_fusion.2), channel_id=1, source_target_pairs={{0,16},{4,20},{8,24},{12,28},{16,0},{20,4},{24,8},{28,12},{1,17},{... | collective-permute-start | bytes 2875400 | tf_op jit(solution)/shard_map/ppermute | solution.py:445
  298.5 233.9 %reduce-scatter.9.cloned.1.call-start = ((), (), s32[]{:S(2)}) async-start(), calls=%async_computation.10 | async-start | bytes 3932160 | tf_op jit(solution)/shard_map/reduce_scatter | solution.py:868
  298.5 7.4 %collective-permute-start.26 = (bf16[288,1664]{1,0:T(8,128)(2,1)}, bf16[288,1664]{1,0:T(8,128)(2,1)}, u32[]{:S(2)}, u32[]{:S(2)}) collective-permute-start(bf16[288,1664]{1,0:T(8,128)(2,1)} %get-tuple-element.223), channel_id=1, source_target_pairs={{0,4},{4,0},{8,12},{12,8},{16,20},{20,16},{24,28},{28,24},{1,5},{5... | collective-permute-start | bytes 2875400 | tf_op jit(solution)/shard_map/ppermute | solution.py:445
  305.6 22.9 %collective-permute-start.25 = (bf16[288,1664]{1,0:T(8,128)(2,1)}, bf16[288,1664]{1,0:T(8,128)(2,1)}, u32[]{:S(2)}, u32[]{:S(2)}) collective-permute-start(bf16[288,1664]{1,0:T(8,128)(2,1)} %add_convert_fusion.1), channel_id=1, source_target_pairs={{0,8},{4,12},{8,0},{12,4},{16,24},{20,28},{24,16},{28,20},{1,9},{5... | collective-permute-start | bytes 2875400 | tf_op jit(solution)/shard_map/ppermute | solution.py:445
  306.0 38.2 %collective-permute-start.28 = (bf16[4,768,640]{2,1,0:T(8,128)(2,1)}, bf16[4,768,640]{2,1,0:T(8,128)(2,1)}, u32[]{:S(2)}, u32[]{:S(2)}) collective-permute-start(bf16[4,768,640]{2,1,0:T(8,128)(2,1)} %bitcast.217), channel_id=1, source_target_pairs={{0,4},{4,0},{8,12},{12,8},{16,20},{20,16},{24,28},{28,24},{1,5},{5... | collective-permute-start | bytes 11796488 | tf_op jit(solution)/shard_map/ppermute | solution.py:445
  308.4 24.0 %collective-permute-start.27 = (bf16[288,1664]{1,0:T(8,128)(2,1)}, bf16[288,1664]{1,0:T(8,128)(2,1)}, u32[]{:S(2)}, u32[]{:S(2)}) collective-permute-start(bf16[288,1664]{1,0:T(8,128)(2,1)} %add_convert_fusion), channel_id=1, source_target_pairs={{0,16},{4,20},{8,24},{12,28},{16,0},{20,4},{24,8},{28,12},{1,17},{... | collective-permute-start | bytes 2875400 | tf_op jit(solution)/shard_map/ppermute | solution.py:445
  345.2 38.1 %all-to-all-start.1 = ((bf16[288,4,384]{2,0,1:T(8,128)(2,1)}), bf16[288,4,384]{2,0,1:T(8,128)(2,1)}, u32[]{:S(2)}, u32[]{:S(2)}) async-start(bf16[288,4,384]{2,0,1:T(8,128)(2,1)} %bitcast.224), calls=%async_computation.1 | async-start | bytes 1769472 | tf_op jit(solution)/shard_map/all_to_all | solution.py:892
  349.4 210.9 %reduce-scatter.11.cloned.1.call-start = ((), (), s32[]{:S(2)}) async-start(), calls=%async_computation.11 | async-start | bytes 3932160 | tf_op jit(solution)/shard_map/reduce_scatter | solution.py:898
  349.5 22.1 %collective-permute-start.29 = (bf16[288,1536]{1,0:T(8,128)(2,1)}, bf16[288,1536]{1,0:T(8,128)(2,1)}, u32[]{:S(2)}, u32[]{:S(2)}) collective-permute-start(bf16[288,1536]{1,0:T(8,128)(2,1)} %get-tuple-element.243), channel_id=1, source_target_pairs={{0,4},{4,0},{8,12},{12,8},{16,20},{20,16},{24,28},{28,24},{1,5},{5... | collective-permute-start | bytes 2654216 | tf_op jit(solution)/shard_map/ppermute | solution.py:445
  349.5 22.6 %collective-permute-start.30 = (bf16[288,1536]{1,0:T(8,128)(2,1)}, bf16[288,1536]{1,0:T(8,128)(2,1)}, u32[]{:S(2)}, u32[]{:S(2)}) collective-permute-start(bf16[288,1536]{1,0:T(8,128)(2,1)} %get-tuple-element.244), channel_id=1, source_target_pairs={{0,4},{4,0},{8,12},{12,8},{16,20},{20,16},{24,28},{28,24},{1,5},{5... | collective-permute-start | bytes 2654216 | tf_op jit(solution)/shard_map/ppermute | solution.py:445
  350.0 22.1 %collective-permute-start.31 = (bf16[288,1536]{1,0:T(8,128)(2,1)}, bf16[288,1536]{1,0:T(8,128)(2,1)}, u32[]{:S(2)}, u32[]{:S(2)}) collective-permute-start(bf16[288,1536]{1,0:T(8,128)(2,1)} %get-tuple-element.245), channel_id=1, source_target_pairs={{0,4},{4,0},{8,12},{12,8},{16,20},{20,16},{24,28},{28,24},{1,5},{5... | collective-permute-start | bytes 2654216 | tf_op jit(solution)/shard_map/ppermute | solution.py:445
  350.1 22.0 %collective-permute-start.32 = (bf16[288,1536]{1,0:T(8,128)(2,1)}, bf16[288,1536]{1,0:T(8,128)(2,1)}, u32[]{:S(2)}, u32[]{:S(2)}) collective-permute-start(bf16[288,1536]{1,0:T(8,128)(2,1)} %get-tuple-element.246), channel_id=1, source_target_pairs={{0,4},{4,0},{8,12},{12,8},{16,20},{20,16},{24,28},{28,24},{1,5},{5... | collective-permute-start | bytes 2654216 | tf_op jit(solution)/shard_map/ppermute | solution.py:445
  357.8 25.5 %collective-permute-start.33 = (bf16[4,192,1536]{2,1,0:T(8,128)(2,1)}, bf16[4,192,1536]{2,1,0:T(8,128)(2,1)}, u32[]{:S(2)}, u32[]{:S(2)}) collective-permute-start(bf16[4,192,1536]{2,1,0:T(8,128)(2,1)} %dynamic-slice_bitcast_fusion), channel_id=1, source_target_pairs={{0,4},{4,0},{8,12},{12,8},{16,20},{20,16},{24,28},{28,24},{1,5},{5... | collective-permute-start | bytes 7077896 | tf_op jit(solution)/shard_map/ppermute | solution.py:445
  371.6 3.1 collective-permute-start.34
  384.0 44.1 %collective-permute-start.35 = (bf16[192,17]{0,1:T(8,128)(2,1)S(1)}, bf16[192,17]{0,1:T(8,128)(2,1)S(1)}, u32[]{:S(2)}, u32[]{:S(2)}) collective-permute-start(bf16[192,17]{0,1:T(8,128)(2,1)S(1)} %bitcast.248), channel_id=1, source_target_pairs={{0,16},{4,20},{8,24},{12,28},{16,0},{20,4},{24,8},{28,12},{1,17},{... | collective-permute-start | bytes 19592 | tf_op jit(solution)/shard_map/ppermute | solution.py:445
  389.8 38.3 %collective-permute-start.36 = (bf16[192,1536]{1,0:T(8,128)(2,1)S(1)}, bf16[192,1536]{1,0:T(8,128)(2,1)S(1)}, u32[]{:S(2)}, u32[]{:S(2)}) collective-permute-start(bf16[192,1536]{1,0:T(8,128)(2,1)S(1)} %get-tuple-element.379), channel_id=1, source_target_pairs={{0,16},{4,20},{8,24},{12,28},{16,0},{20,4},{24,8},{28,12},{1,17},{... | collective-permute-start | bytes 1769480 | tf_op jit(solution)/shard_map/ppermute | solution.py:445
  390.3 37.8 %collective-permute-start.37 = (bf16[288,1536]{1,0:T(8,128)(2,1)S(1)}, bf16[288,1536]{1,0:T(8,128)(2,1)S(1)}, u32[]{:S(2)}, u32[]{:S(2)}) collective-permute-start(bf16[288,1536]{1,0:T(8,128)(2,1)S(1)} %copy-done.28), channel_id=1, source_target_pairs={{0,16},{4,20},{8,24},{12,28},{16,0},{20,4},{24,8},{28,12},{1,17},{... | collective-permute-start | bytes 2654216 | tf_op jit(solution)/shard_map/ppermute | solution.py:445
  429.7 1.6 collective-permute-start.38
  432.3 4.9 collective-permute-start.39
  432.9 9.5 %collective-permute-start.41 = (bf16[128,256]{1,0:T(8,128)(2,1)S(1)}, bf16[128,256]{1,0:T(8,128)(2,1)S(1)}, u32[]{:S(2)}, u32[]{:S(2)}) collective-permute-start(bf16[128,256]{1,0:T(8,128)(2,1)S(1)} %get-tuple-element.400), channel_id=1, source_target_pairs={{0,16},{4,20},{8,24},{12,28},{16,0},{20,4},{24,8},{28,12},{1,17},{... | collective-permute-start | bytes 196616 | tf_op jit(solution)/shard_map/ppermute | solution.py:445
  437.3 5.1 collective-permute-start.40
  453.2 6.0 %collective-permute-start.42 = (bf16[4,192,640]{2,1,0:T(8,128)(2,1)S(1)}, bf16[4,192,640]{2,1,0:T(8,128)(2,1)S(1)}, u32[]{:S(2)}, u32[]{:S(2)}) collective-permute-start(bf16[4,192,640]{2,1,0:T(8,128)(2,1)S(1)} %dynamic-slice_bitcast_fusion.1), channel_id=1, source_target_pairs={{0,4},{4,0},{8,12},{12,8},{16,20},{20,16},{24,28},{28,24},{1,5},{5... | collective-permute-start | bytes 2949128 | tf_op jit(solution)/shard_map/ppermute | solution.py:445
  454.1 7.9 %collective-permute-start.51 = (bf16[192,17]{0,1:T(8,128)(2,1)S(1)}, bf16[192,17]{0,1:T(8,128)(2,1)S(1)}, u32[]{:S(2)}, u32[]{:S(2)}) collective-permute-start(bf16[192,17]{0,1:T(8,128)(2,1)S(1)} %bitcast.247), channel_id=1, source_target_pairs={{0,16},{4,20},{8,24},{12,28},{16,0},{20,4},{24,8},{28,12},{1,17},{... | collective-permute-start | bytes 19592 | tf_op jit(solution)/shard_map/ppermute | solution.py:445
  454.2 7.8 %collective-permute-start.50 = (bf16[192,17]{0,1:T(8,128)(2,1)S(1)}, bf16[192,17]{0,1:T(8,128)(2,1)S(1)}, u32[]{:S(2)}, u32[]{:S(2)}) collective-permute-start(bf16[192,17]{0,1:T(8,128)(2,1)S(1)} %fusion.72), channel_id=1, source_target_pairs={{0,8},{4,12},{8,0},{12,4},{16,24},{20,28},{24,16},{28,20},{1,9},{5... | collective-permute-start | bytes 19592 | tf_op jit(solution)/shard_map/ppermute | solution.py:445
  455.0 24.2 %collective-permute-start.49 = (bf16[192,1536]{1,0:T(8,128)(2,1)}, bf16[192,1536]{1,0:T(8,128)(2,1)}, u32[]{:S(2)}, u32[]{:S(2)}) collective-permute-start(bf16[192,1536]{1,0:T(8,128)(2,1)} %get-tuple-element.290), channel_id=1, source_target_pairs={{0,16},{4,20},{8,24},{12,28},{16,0},{20,4},{24,8},{28,12},{1,17},{... | collective-permute-start | bytes 1769480 | tf_op jit(solution)/shard_map/ppermute | solution.py:445
  458.0 21.3 %collective-permute-start.48 = (bf16[192,1536]{1,0:T(8,128)(2,1)}, bf16[192,1536]{1,0:T(8,128)(2,1)}, u32[]{:S(2)}, u32[]{:S(2)}) collective-permute-start(bf16[192,1536]{1,0:T(8,128)(2,1)} %add_convert_fusion.12), channel_id=1, source_target_pairs={{0,8},{4,12},{8,0},{12,4},{16,24},{20,28},{24,16},{28,20},{1,9},{5... | collective-permute-start | bytes 1769480 | tf_op jit(solution)/shard_map/ppermute | solution.py:445
  461.3 15.5 %collective-permute-start.43 = (bf16[192,640]{1,0:T(8,128)(2,1)}, bf16[192,640]{1,0:T(8,128)(2,1)}, u32[]{:S(2)}, u32[]{:S(2)}) collective-permute-start(bf16[192,640]{1,0:T(8,128)(2,1)} %get-tuple-element.389), channel_id=1, source_target_pairs={{0,16},{4,20},{8,24},{12,28},{16,0},{20,4},{24,8},{28,12},{1,17},{... | collective-permute-start | bytes 737288 | tf_op jit(solution)/shard_map/ppermute | solution.py:445
  462.1 67.6 %all-to-all-start.2 = ((bf16[4,288,640]{2,1,0:T(8,128)(2,1)}), bf16[4,288,640]{2,1,0:T(8,128)(2,1)S(1)}, u32[]{:S(2)}, u32[]{:S(2)}) async-start(bf16[4,288,640]{2,1,0:T(8,128)(2,1)} %bitcast.49), calls=%async_computation.2 | async-start | bytes 2949120 | tf_op jit(solution)/shard_map/all_to_all | solution.py:958
  467.1 97.9 %reduce-scatter.13.cloned.1.call-start = ((), (), s32[]{:S(2)}) async-start(), calls=%async_computation.13 | async-start | bytes 983040
  467.3 14.4 %collective-permute-start.45 = (bf16[192,640]{1,0:T(8,128)(2,1)}, bf16[192,640]{1,0:T(8,128)(2,1)S(1)}, u32[]{:S(2)}, u32[]{:S(2)}) collective-permute-start(bf16[192,640]{1,0:T(8,128)(2,1)} %get-tuple-element.388), channel_id=1, source_target_pairs={{0,16},{4,20},{8,24},{12,28},{16,0},{20,4},{24,8},{28,12},{1,17},{... | collective-permute-start | bytes 737288 | tf_op jit(solution)/shard_map/ppermute | solution.py:445
  477.9 6.4 %collective-permute-start.44 = (bf16[192,640]{1,0:T(8,128)(2,1)S(1)}, bf16[192,640]{1,0:T(8,128)(2,1)S(1)}, u32[]{:S(2)}, u32[]{:S(2)}) collective-permute-start(bf16[192,640]{1,0:T(8,128)(2,1)S(1)} %fusion.46), channel_id=1, source_target_pairs={{0,8},{4,12},{8,0},{12,4},{16,24},{20,28},{24,16},{28,20},{1,9},{5... | collective-permute-start | bytes 737288 | tf_op jit(solution)/shard_map/ppermute | solution.py:445
  486.8 68.2 %collective-permute-start.46 = (bf16[288,1536]{1,0:T(8,128)(2,1)}, bf16[288,1536]{1,0:T(8,128)(2,1)}, u32[]{:S(2)}, u32[]{:S(2)}) collective-permute-start(bf16[288,1536]{1,0:T(8,128)(2,1)} %add_convert_fusion.7), channel_id=1, source_target_pairs={{0,8},{4,12},{8,0},{12,4},{16,24},{20,28},{24,16},{28,20},{1,9},{5... | collective-permute-start | bytes 2654216 | tf_op jit(solution)/shard_map/ppermute | solution.py:445
  490.3 64.6 %collective-permute-start.47 = (bf16[288,1536]{1,0:T(8,128)(2,1)}, bf16[288,1536]{1,0:T(8,128)(2,1)}, u32[]{:S(2)}, u32[]{:S(2)}) collective-permute-start(bf16[288,1536]{1,0:T(8,128)(2,1)} %add_convert_fusion.6), channel_id=1, source_target_pairs={{0,16},{4,20},{8,24},{12,28},{16,0},{20,4},{24,8},{28,12},{1,17},{... | collective-permute-start | bytes 2654216 | tf_op jit(solution)/shard_map/ppermute | solution.py:445
  (50 other events, 317.6 us)
Sparse Core Ops, SparseCore 0:
  9.6 79.8 all-gather.6
  112.3 44.8 all-gather.8
  204.7 73.9 all-gather.10
  298.6 57.3 reduce-scatter.6
  358.2 65.9 reduce-scatter.8
  439.6 82.8 reduce-scatter.10
  524.8 28.9 reduce-scatter.12

commit v11 on v9

--- a/solution.py
+++ b/solution.py
@@ -969,10 +969,12 @@
     out_pieces = reduce_singles(out_sums, out_pending, "shard")
     grad_out = add_all(reduce_singles(whole_sums, whole_pending, "shard")).astype(bf16).T
     hidden_units = w_gate.shape[2]
+    grad_down, first_sums = lax.optimization_barrier((grad_down, pre_grads[0], grad_qkv))[:2]
+    grad_down = grad_down.T.reshape(local_experts, hidden_units, -1).astype(jnp.float32)
+    pre_grads[0] = first_sums.astype(jnp.float32)
     lin_tokens, grad_down, pre_grads[0] = lax.optimization_barrier(
         (lin_tokens, grad_down, pre_grads[0])
     )
-    grad_down = grad_down.T.reshape(local_experts, hidden_units, -1).astype(jnp.float32)
     parts = [0.0, 0.0]
     for k, weight in enumerate((wide_half, other_half)):
         for group_index in range(seq_count):

time: 580 us -> 576 us (level)
    ppermute x52, waiting for transfers between devices: 56.8 us -> 39.4 us  [exchange(): return lax.ppermute(values, axis_name, [(i, i ^ bit) for i in range(count)])]
    all_to_all x1, waiting for transfers between devices: 15.5 us -> 29.3 us  [on_device(): lax.all_to_all(lin_all, 'seq', split_axis=0, concat_axis=1, tiled=True)]
    unnamed x125 -> x121, local copies, waits for them, and re-layouts: 25.4 us -> 23.9 us
  transfers between devices with their start and end apart: 62 -> 62, of which waited for: 21 -> 19; matrix products, arithmetic and copies ran while one was open for 27% -> 27% of each run, Pallas kernels for 26% -> 26%
where the time goes in v11:
time: 576 us; the launch traced here: 568 us
  Pallas kernels  148 us (26%)
  waiting for transfers between devices  102 us (18%)
  matrix products  76 us (13%)
  other arithmetic  60.8 us (11%)
  blocking collectives  60.5 us (11%)
  local copies, waits for them, and re-layouts  58.5 us (10%)
  starting transfers between devices  45.9 us (8%)
  between operations  15.7 us (3%)
    pallas_call x4, Pallas kernels, expert_pair(): pl.pallas_call(partial(expert_body, experts_all), out_shape=out_shape, gr...  87.1 us
    dot_general x6, matrix products, transposed_times(): lax.dot_general(left_side, right_side, (((0,), (0,)), ((), ())), precisio...  49.1 us
    ppermute x52, waiting for transfers between devices, exchange(): return lax.ppermute(values, axis_name, [(i, i ^ bit) for i in range(count)])  39.4 us
    pallas_call x1, Pallas kernels, attend_backward(): pl.pallas_call(partial(attend_backward_body, group, kv_heads), out_shape=...  35.8 us
    ppermute x52, starting transfers between devices, exchange(): return lax.ppermute(values, axis_name, [(i, i ^ bit) for i in range(count)])  33.2 us
    all_to_all x1, waiting for transfers between devices, on_device(): lax.all_to_all(lin_all, 'seq', split_axis=0, concat_axis=1, tiled=True)  29.3 us
    convert_element_type x17, other arithmetic, add_rounded(): (left_side.astype(jnp.float32) + right_side.astype(jnp.float32)).astype(j...  28.7 us
    all_gather x1, blocking collectives, on_device(): out_weight = lax.all_gather(w_out, 'seq', axis=0, tiled=True)  25.8 us
  transfers between devices with their start and end apart: 62, of which 19 were waited for; matrix products, arithmetic and copies ran while one was open for 27% of the time, Pallas kernels for 26%

profile of v11, /device:TPU:0, one launch (start us, length us, event | category | flops | bytes accessed | tf_op | source)
XLA Modules:
  0.0 567.8 jit_solution(14328892088438636063)
XLA Ops:
  11.1 2.6 collective-permute-start.1
  15.8 25.8 %all_gather.28 = bf16[1536,192]{0,1:T(8,128)(2,1)} all-gather(bf16[384,192]{0,1:T(8,128)(2,1)} %param.18), channel_id=1, replica_groups=mesh['shard'=8,'seq'=4] {'seq'}, dimensions={0}, use_global_device_ids=true | all-gather | bytes 737280 | tf_op jit(solution)/shard_map/all_gather | solution.py:732
  42.2 14.3 %all-gather.1 = bf16[4,48,18]{1,2,0:T(8,128)(2,1)S(1)} all-gather(bf16[1,48,18]{1,2,0:T(8,128)(2,1)S(1)} %maximum_bitcast_fusion.1), channel_id=1, replica_groups=mesh['shard'=8,'seq'=4] {'seq'}, dimensions={0}, use_global_device_ids=true | all-gather | bytes 8640 | tf_op jit(solution)/shard_map/all_gather | solution.py:714
  56.7 9.3 %all-gather.2 = bf16[8,192,18]{1,2,0:T(8,128)(2,1)S(1)} all-gather(bf16[1,192,18]{1,2,0:T(8,128)(2,1)S(1)} %reshape.375), channel_id=1, replica_groups=mesh['shard'=8,'seq'=4] {'shard'}, dimensions={0}, use_global_device_ids=true | all-gather | bytes 62208 | tf_op jit(solution)/shard_map/all_gather | solution.py:715
  70.8 4.5 collective-permute-done.7
  82.6 6.9 %all-gather.7.cloned.1.call-done = bf16[1152,1536]{1,0:T(8,128)(2,1)} async-done(((bf16[288,1536]{1,0:T(8,128)(2,1)}), bf16[1152,1536]{1,0:T(8,128)(2,1)}) %all-gather.7.cloned.1.call-update) | async-done | bytes 3538960 | tf_op jit(solution)/shard_map/all_gather | solution.py:719
  91.2 2.9 fusion
  94.3 4.7 fusion.24
  101.0 11.1 %all_gather.27.kp_ref.vp_ref = bf16[1024,256]{1,0:T(8,128)(2,1)} all-gather(bf16[128,256]{1,0:T(8,128)(2,1)S(1)} %fusion.67), channel_id=1, replica_groups=mesh['shard'=8,'seq'=4] {'shard'}, dimensions={0}, use_global_device_ids=true | all-gather | bytes 589824 | tf_op jit(solution)/shard_map/all_gather | solution.py:762
  118.7 25.0 %attend_forward.1 = (bf16[1152,384]{1,0:T(8,128)(2,1)}, f32[6,1,1152]{2,1,0:T(1,128)}) custom-call(s32[1]{0:T(128)} %bitcast.9.index_ref, bf16[1152,384]{1,0:T(8,128)(2,1)} %copy.135.q_ref, bf16[1024,256]{1,0:T(8,128)(2,1)} %all_gather.27.kp_ref.vp_ref, bf16[1024,256]{1,0:T(8,128)(2,1)} %all_gather.27.kp_ref.vp_ref, ...), custom_call_target="tpu_custom_call" | custom-call | flops 9059696640 | bytes 3538944 | tf_op jit(solution)/shard_map/attend_forward/pallas_call | solution.py:376
  143.7 2.5 collective-permute-done.12.og_even
  146.2 3.5 all-to-all-start
  149.9 2.3 constant_dynamic-slice_fusion.4
  152.2 17.7 %all-to-all-done = bf16[4,288,384]{2,1,0:T(8,128)(2,1)S(1)} async-done(((bf16[4,288,384]{2,1,0:T(8,128)(2,1)}), bf16[4,288,384]{2,1,0:T(8,128)(2,1)S(1)}, u32[]{:S(2)}, u32[]{:S(2)}) %all-to-all-start) | async-done | bytes 884768 | tf_op jit(solution)/shard_map/all_to_all | solution.py:780
  171.0 4.3 multiply_reduce_fusion.2
  178.2 2.5 collective-permute-start.13
  181.1 21.4 %experts.4 = (bf16[2304,1536]{1,0:T(8,128)(2,1)}, bf16[2304,1536]{1,0:T(8,128)(2,1)}, bf16[2,2304,1024]{2,1,0:T(8,128)(2,1)}, bf16[2304,1024]{1,0:T(8,128)(2,1)}...) custom-call(s32[1]{0:T(128)} %bitcast.24.index_ref, ...), custom_call_target="tpu_custom_call" | custom-call | flops 10871635968 | bytes 27131904 | tf_op jit(solution)/shard_map/experts/pallas_call | solution.py:654
  207.3 22.2 %experts.5 = (bf16[2304,1536]{1,0:T(8,128)(2,1)}, bf16[2304,1536]{1,0:T(8,128)(2,1)}, bf16[2,2304,1024]{2,1,0:T(8,128)(2,1)}, bf16[2304,1024]{1,0:T(8,128)(2,1)}...) custom-call(s32[1]{0:T(128)} %bitcast.24.index_ref, ...), custom_call_target="tpu_custom_call", output_to_operand_aliasing={{0}: (8, {}), {1}: (9, {}), {2}: (10, {}), {3}: (11, {})} | custom-call | flops 10871635968 | bytes 27131904 | tf_op jit(solution)/shard_map/experts/pallas_call | solution.py:654
  230.6 3.0 collective-permute-done.22.og_odd
  233.7 21.9 %experts.6 = (bf16[2304,1536]{1,0:T(8,128)(2,1)}, bf16[2304,1536]{1,0:T(8,128)(2,1)}, bf16[2,2304,1024]{2,1,0:T(8,128)(2,1)}, bf16[2304,1024]{1,0:T(8,128)(2,1)}...) custom-call(s32[1]{0:T(128)} %bitcast.24.index_ref, ...), custom_call_target="tpu_custom_call", output_to_operand_aliasing={{0}: (8, {}), {1}: (9, {}), {2}: (10, {}), {3}: (11, {})} | custom-call | flops 10871635968 | bytes 27131904 | tf_op jit(solution)/shard_map/experts/pallas_call | solution.py:654
  255.8 2.7 add_convert_fusion.4
  258.5 2.5 add_convert_fusion.3
  262.2 21.6 %experts.7 = (bf16[2304,1536]{1,0:T(8,128)(2,1)}, bf16[2304,1536]{1,0:T(8,128)(2,1)}, bf16[2,2304,1024]{2,1,0:T(8,128)(2,1)}, bf16[2304,1024]{1,0:T(8,128)(2,1)}...) custom-call(s32[1]{0:T(128)} %bitcast.24.index_ref, ...), custom_call_target="tpu_custom_call", output_to_operand_aliasing={{0}: (8, {}), {1}: (9, {}), {2}: (10, {}), {3}: (11, {})} | custom-call | flops 10871635968 | bytes 27131904 | tf_op jit(solution)/shard_map/experts/pallas_call | solution.py:654
  283.8 2.1 collective-permute-done.24
  285.9 12.3 %convolution_convert_fusion.1 = bf16[1536,1024]{1,0:T(8,128)(2,1)} fusion(bf16[2304,1536]{1,0:T(8,128)(2,1)} %get-tuple-element.224, bf16[2304,1024]{1,0:T(8,128)(2,1)} %get-tuple-element.225), kind=kOutput, calls=%fused_computation.16 | convolution fusion | flops 7249330176 | bytes 14942208 | tf_op jit(solution)/shard_map/dot_general | solution.py:71
  300.4 2.3 copy.145.sin_ref
  302.6 2.7 add_convert_fusion.1
  305.8 2.4 add_convert_fusion
  308.8 12.9 %fusion.10 = bf16[1536,1024]{1,0:T(8,128)(2,1)} fusion(bf16[2304,1536]{1,0:T(8,128)(2,1)} %get-tuple-element.247, bf16[2,2304,1024]{2,1,0:T(8,128)(2,1)} %get-tuple-element.228), kind=kOutput, calls=%fused_computation.14 | convolution fusion | flops 7249330176 | bytes 14942208 | tf_op jit(solution)/shard_map/dot_general | solution.py:71
  321.8 6.4 %collective-permute-done.25 = bf16[288,1664]{1,0:T(8,128)(2,1)} collective-permute-done((bf16[288,1664]{1,0:T(8,128)(2,1)}, bf16[288,1664]{1,0:T(8,128)(2,1)}, u32[]{:S(2)}, u32[]{:S(2)}) %collective-permute-start.25) | collective-permute-done | bytes 958496 | tf_op jit(solution)/shard_map/ppermute | solution.py:445
  328.3 3.9 collective-permute-done.27
  332.1 2.1 convert_add_fusion.3
  334.6 2.4 multiply_reduce_fusion
  337.2 2.2 subtract_add_fusion
  339.4 4.5 convolution_convert_fusion.3
  345.0 4.2 all-to-all-start.1
  350.4 4.4 convolution_convert_fusion
  357.7 13.1 %fusion.13 = bf16[1536,1024]{1,0:T(8,128)(2,1)} fusion(bf16[2304,1536]{1,0:T(8,128)(2,1)} %get-tuple-element.247, bf16[2,2304,1024]{2,1,0:T(8,128)(2,1)} %get-tuple-element.228), kind=kOutput, calls=%fused_computation.15 | convolution fusion | flops 7249330176 | bytes 14942208 | tf_op jit(solution)/shard_map/dot_general | solution.py:71
  372.1 2.6 add_convert_fusion.10
  374.7 8.4 %all-to-all-done.1 = bf16[288,4,384]{2,0,1:T(8,128)(2,1)} async-done(((bf16[288,4,384]{2,0,1:T(8,128)(2,1)}), bf16[288,4,384]{2,0,1:T(8,128)(2,1)}, u32[]{:S(2)}, u32[]{:S(2)}) %all-to-all-start.1) | async-done | bytes 884768 | tf_op jit(solution)/shard_map/all_to_all | solution.py:892
  385.4 3.0 fusion.3
  391.7 35.8 %attend_backward.1 = (bf16[1152,384]{1,0:T(8,128)(2,1)}, bf16[1024,256]{1,0:T(8,128)(2,1)}, f32[1152,256]{1,0:T(8,128)}) custom-call(s32[1]{0:T(128)} %bitcast.9.index_ref, bf16[1152,384]{1,0:T(8,128)(2,1)} %copy.135.q_ref, bf16[1152,384]{1,0:T(8,128)(2,1)} %bitcast.28.grad_ref, bf16[1152,384]{1,0:T(8,128)(2,1)} %get-tuple-element.164.mixed_ref, ...), custom_call_target="tpu_custom_call" | custom-call | flops 22649241600 | bytes 3538944 | tf_op jit(solution)/shard_map/attend_backward/pallas_call | solution.py:406
  433.8 2.8 collective-permute-done.39
  438.9 1.8 slice.329
  444.2 2.5 maximum_maximum_fusion
  446.6 5.8 %convolution_convert_fusion.2 = bf16[1536,640]{1,0:T(8,128)(2,1)S(1)} fusion(bf16[1152,640]{1,0:T(8,128)(2,1)} %maximum_maximum_fusion, bf16[1152,1536]{1,0:T(8,128)(2,1)} %all-gather.7.cloned.1.call-done, f32[1536]{0:T(1024)S(1)} %get-tuple-element.371, f32[1152]{0:T(1024)S(1)} %copy-done.43), kind=kOutput, calls=%fused_computation.17 | convolution fusion | flops 2272985088 | bytes 6990336 | tf_op jit(solution)/shard_map/dot_general | solution.py:71
  455.9 2.0 collective-permute-start.49
  457.9 2.0 add_convert_fusion.12
  461.2 4.3 all-to-all-start.2
  467.8 4.6 collective-permute-done.49
  472.4 2.7 collective-permute-done.48
  475.1 2.3 fusion.44
  479.0 2.4 add_convert_fusion.7
  482.3 2.3 add_convert_fusion.6
  486.3 2.3 add_convert_fusion.9
  491.7 2.5 reshape.369
  494.1 2.5 convert_element_type.444
  499.8 29.3 %all-to-all-done.2 = bf16[4,288,640]{2,1,0:T(8,128)(2,1)} async-done(((bf16[4,288,640]{2,1,0:T(8,128)(2,1)}), bf16[4,288,640]{2,1,0:T(8,128)(2,1)}, u32[]{:S(2)}, u32[]{:S(2)}) %all-to-all-start.2) | async-done | bytes 1474592 | tf_op jit(solution)/shard_map/all_to_all | solution.py:958
  535.9 1.8 convolution_add_fusion.3
  537.7 1.8 convolution_add_fusion.2
  539.5 1.8 broadcast_select_fusion.1
  544.8 3.7 copy.152
  548.4 4.7 fusion.20
  555.9 2.0 pad_maximum_fusion.1
  (332 shorter events, 101.5 us)
Async XLA Ops:
  7.2 82.3 %all-gather.7.cloned.1.call-start = ((), (), s32[]{:S(2)}) async-start(), calls=%async_computation.7 | async-start | bytes 4423680 | tf_op jit(solution)/shard_map/all_gather | solution.py:719
  7.9 163.1 %all-gather.9.cloned.1.call-start = ((), (), s32[]{:S(2)}) async-start(), calls=%async_computation.8 | async-start | bytes 5308416 | tf_op jit(solution)/shard_map/all_gather | solution.py:767
  10.6 60.3 %copy-start.16 = (bf16[192,640]{1,0:T(8,128)(2,1)}, bf16[192,640]{1,0:T(8,128)(2,1)S(1)}, u32[]{:S(2)}) copy-start(bf16[192,640]{1,0:T(8,128)(2,1)S(1)} %constant_dynamic-update-slice_fusion) | copy-start | bytes 737284
  10.6 58.2 %collective-permute-start = (bf16[192,640]{1,0:T(8,128)(2,1)S(1)}, bf16[192,640]{1,0:T(8,128)(2,1)}, u32[]{:S(2)}, u32[]{:S(2)}) collective-permute-start(bf16[192,640]{1,0:T(8,128)(2,1)S(1)} %constant_dynamic-update-slice_fusion), channel_id=1, source_target_pairs={{0,4},{4,0},{8,12},{12,8},{16,20},{20,16},{24,28},{28,24},{1,5},{5... | collective-permute-start | bytes 737288 | tf_op jit(solution)/shard_map/ppermute | solution.py:445
  11.1 55.7 %collective-permute-start.1 = (bf16[192,640]{1,0:T(8,128)(2,1)S(1)}, bf16[192,640]{1,0:T(8,128)(2,1)}, u32[]{:S(2)}, u32[]{:S(2)}) collective-permute-start(bf16[192,640]{1,0:T(8,128)(2,1)S(1)} %constant_dynamic-update-slice_fusion), channel_id=1, source_target_pairs={{0,8},{4,12},{8,0},{12,4},{16,24},{20,28},{24,16},{28,20},{1,9},{5... | collective-permute-start | bytes 737288 | tf_op jit(solution)/shard_map/ppermute | solution.py:445
  13.7 53.2 %collective-permute-start.2 = (bf16[192,640]{1,0:T(8,128)(2,1)S(1)}, bf16[192,640]{1,0:T(8,128)(2,1)S(1)}, u32[]{:S(2)}, u32[]{:S(2)}) collective-permute-start(bf16[192,640]{1,0:T(8,128)(2,1)S(1)} %constant_dynamic-update-slice_fusion), channel_id=1, source_target_pairs={{0,16},{4,20},{8,24},{12,28},{16,0},{20,4},{24,8},{28,12},{1,17},{... | collective-permute-start | bytes 737288 | tf_op jit(solution)/shard_map/ppermute | solution.py:445
  15.2 51.6 %collective-permute-start.3 = (bf16[288,1536]{1,0:T(8,128)(2,1)}, bf16[288,1536]{1,0:T(8,128)(2,1)}, u32[]{:S(2)}, u32[]{:S(2)}) collective-permute-start(bf16[288,1536]{1,0:T(8,128)(2,1)} %og_even.1), channel_id=1, source_target_pairs={{0,8},{4,12},{8,0},{12,4},{16,24},{20,28},{24,16},{28,20},{1,9},{5... | collective-permute-start | bytes 2654216 | tf_op jit(solution)/shard_map/ppermute | solution.py:445
  15.7 51.1 %collective-permute-start.4 = (bf16[288,1536]{1,0:T(8,128)(2,1)}, bf16[288,1536]{1,0:T(8,128)(2,1)}, u32[]{:S(2)}, u32[]{:S(2)}) collective-permute-start(bf16[288,1536]{1,0:T(8,128)(2,1)} %og_even.1), channel_id=1, source_target_pairs={{0,16},{4,20},{8,24},{12,28},{16,0},{20,4},{24,8},{28,12},{1,17},{... | collective-permute-start | bytes 2654216 | tf_op jit(solution)/shard_map/ppermute | solution.py:445
  66.7 49.5 %copy-start.13 = (f32[1152,1,32]{0,2,1:T(8,128)}, f32[1152,1,32]{0,2,1:T(8,128)S(1)}, u32[]{:S(2)}) copy-start(f32[1152,1,32]{0,2,1:T(8,128)S(1)} %get-tuple-element.156) | copy-start | bytes 442372
  66.9 8.4 %collective-permute-start.5 = (bf16[192,640]{1,0:T(8,128)(2,1)}, bf16[192,640]{1,0:T(8,128)(2,1)S(1)}, u32[]{:S(2)}, u32[]{:S(2)}) collective-permute-start(bf16[192,640]{1,0:T(8,128)(2,1)} %collective-permute-done.1), channel_id=1, source_target_pairs={{0,4},{4,0},{8,12},{12,8},{16,20},{20,16},{24,28},{28,24},{1,5},{5... | collective-permute-start | bytes 737288 | tf_op jit(solution)/shard_map/ppermute | solution.py:445
  67.3 8.0 %collective-permute-start.7 = (bf16[192,640]{1,0:T(8,128)(2,1)S(1)}, bf16[192,640]{1,0:T(8,128)(2,1)S(1)}, u32[]{:S(2)}, u32[]{:S(2)}) collective-permute-start(bf16[192,640]{1,0:T(8,128)(2,1)S(1)} %collective-permute-done.2), channel_id=1, source_target_pairs={{0,8},{4,12},{8,0},{12,4},{16,24},{20,28},{24,16},{28,20},{1,9},{5... | collective-permute-start | bytes 737288 | tf_op jit(solution)/shard_map/ppermute | solution.py:445
  69.8 5.6 collective-permute-start.6
  75.3 1.5 collective-permute-start.8
  112.2 31.5 %collective-permute-start.9 = (bf16[288,1536]{1,0:T(8,128)(2,1)}, bf16[288,1536]{1,0:T(8,128)(2,1)}, u32[]{:S(2)}, u32[]{:S(2)}) collective-permute-start(bf16[288,1536]{1,0:T(8,128)(2,1)} %og_even.1), channel_id=1, source_target_pairs={{0,4},{4,0},{8,12},{12,8},{16,20},{20,16},{24,28},{28,24},{1,5},{5... | collective-permute-start | bytes 2654216 | tf_op jit(solution)/shard_map/ppermute | solution.py:445
  112.6 31.1 %collective-permute-start.10 = (bf16[288,1536]{1,0:T(8,128)(2,1)}, bf16[288,1536]{1,0:T(8,128)(2,1)}, u32[]{:S(2)}, u32[]{:S(2)}) collective-permute-start(bf16[288,1536]{1,0:T(8,128)(2,1)} %collective-permute-done.3.og_even), channel_id=1, source_target_pairs={{0,4},{4,0},{8,12},{12,8},{16,20},{20,16},{24,28},{28,24},{1,5},{5... | collective-permute-start | bytes 2654216 | tf_op jit(solution)/shard_map/ppermute | solution.py:445
  112.7 31.0 %collective-permute-start.11 = (bf16[288,1536]{1,0:T(8,128)(2,1)}, bf16[288,1536]{1,0:T(8,128)(2,1)}, u32[]{:S(2)}, u32[]{:S(2)}) collective-permute-start(bf16[288,1536]{1,0:T(8,128)(2,1)} %collective-permute-done.4.og_even), channel_id=1, source_target_pairs={{0,4},{4,0},{8,12},{12,8},{16,20},{20,16},{24,28},{28,24},{1,5},{5... | collective-permute-start | bytes 2654216 | tf_op jit(solution)/shard_map/ppermute | solution.py:445
  114.7 31.5 %collective-permute-start.12 = (bf16[288,1536]{1,0:T(8,128)(2,1)}, bf16[288,1536]{1,0:T(8,128)(2,1)}, u32[]{:S(2)}, u32[]{:S(2)}) collective-permute-start(bf16[288,1536]{1,0:T(8,128)(2,1)} %collective-permute-done.4.og_even), channel_id=1, source_target_pairs={{0,8},{4,12},{8,0},{12,4},{16,24},{20,28},{24,16},{28,20},{1,9},{5... | collective-permute-start | bytes 2654216 | tf_op jit(solution)/shard_map/ppermute | solution.py:445
  146.2 23.8 %all-to-all-start = ((bf16[4,288,384]{2,1,0:T(8,128)(2,1)}), bf16[4,288,384]{2,1,0:T(8,128)(2,1)S(1)}, u32[]{:S(2)}, u32[]{:S(2)}) async-start(bf16[4,288,384]{2,1,0:T(8,128)(2,1)} %bitcast.240), calls=%async_computation | async-start | bytes 1769472 | tf_op jit(solution)/shard_map/all_to_all | solution.py:780
  149.7 136.2 %all-gather.11.cloned.1.call-start = ((), (), s32[]{:S(2)}) async-start(), calls=%async_computation.12 | async-start | bytes 4915200 | tf_op jit(solution)/shard_map/all_gather | solution.py:790
  178.2 2.9 collective-permute-start.15
  178.2 24.7 %collective-permute-start.13 = (bf16[288,1664]{1,0:T(8,128)(2,1)}, bf16[288,1664]{1,0:T(8,128)(2,1)}, u32[]{:S(2)}, u32[]{:S(2)}) collective-permute-start(bf16[288,1664]{1,0:T(8,128)(2,1)} %concatenate.70.x_even), channel_id=1, source_target_pairs={{0,8},{4,12},{8,0},{12,4},{16,24},{20,28},{24,16},{28,20},{1,9},{5... | collective-permute-start | bytes 2875400 | tf_op jit(solution)/shard_map/ppermute | solution.py:445
  180.7 23.7 %collective-permute-start.14 = (bf16[288,1664]{1,0:T(8,128)(2,1)}, bf16[288,1664]{1,0:T(8,128)(2,1)}, u32[]{:S(2)}, u32[]{:S(2)}) collective-permute-start(bf16[288,1664]{1,0:T(8,128)(2,1)} %concatenate.70.x_even), channel_id=1, source_target_pairs={{0,16},{4,20},{8,24},{12,28},{16,0},{20,4},{24,8},{28,12},{1,17},{... | collective-permute-start | bytes 2875400 | tf_op jit(solution)/shard_map/ppermute | solution.py:445
  204.4 2.9 collective-permute-start.19
  204.4 285.9 %reduce-scatter.7.cloned.1.call-start = ((), (), s32[]{:S(2)}) async-start(), calls=%async_computation.9 | async-start | bytes 3932160 | tf_op jit(solution)/shard_map/reduce_scatter | solution.py:864
  204.7 24.8 %collective-permute-start.18 = (bf16[288,1664]{1,0:T(8,128)(2,1)}, bf16[288,1664]{1,0:T(8,128)(2,1)}, u32[]{:S(2)}, u32[]{:S(2)}) collective-permute-start(bf16[288,1664]{1,0:T(8,128)(2,1)} %collective-permute-done.14.x_even), channel_id=1, source_target_pairs={{0,8},{4,12},{8,0},{12,4},{16,24},{20,28},{24,16},{28,20},{1,9},{5... | collective-permute-start | bytes 2875400 | tf_op jit(solution)/shard_map/ppermute | solution.py:445
  229.5 4.2 collective-permute-start.21
  229.6 4.1 collective-permute-start.22
  230.0 32.2 %collective-permute-start.16 = (bf16[288,1664]{1,0:T(8,128)(2,1)}, bf16[288,1664]{1,0:T(8,128)(2,1)}, u32[]{:S(2)}, u32[]{:S(2)}) collective-permute-start(bf16[288,1664]{1,0:T(8,128)(2,1)} %collective-permute-done.14.x_even), channel_id=1, source_target_pairs={{0,4},{4,0},{8,12},{12,8},{16,20},{20,16},{24,28},{28,24},{1,5},{5... | collective-permute-start | bytes 2875400 | tf_op jit(solution)/shard_map/ppermute | solution.py:445
  230.1 25.7 %collective-permute-start.17 = (bf16[288,1664]{1,0:T(8,128)(2,1)}, bf16[288,1664]{1,0:T(8,128)(2,1)}, u32[]{:S(2)}, u32[]{:S(2)}) collective-permute-start(bf16[288,1664]{1,0:T(8,128)(2,1)} %get-tuple-element.174), channel_id=1, source_target_pairs={{0,4},{4,0},{8,12},{12,8},{16,20},{20,16},{24,28},{28,24},{1,5},{5... | collective-permute-start | bytes 2875400 | tf_op jit(solution)/shard_map/ppermute | solution.py:445
  230.5 27.9 %collective-permute-start.20 = (bf16[288,1664]{1,0:T(8,128)(2,1)}, bf16[288,1664]{1,0:T(8,128)(2,1)}, u32[]{:S(2)}, u32[]{:S(2)}) collective-permute-start(bf16[288,1664]{1,0:T(8,128)(2,1)} %get-tuple-element.187), channel_id=1, source_target_pairs={{0,4},{4,0},{8,12},{12,8},{16,20},{20,16},{24,28},{28,24},{1,5},{5... | collective-permute-start | bytes 2875400 | tf_op jit(solution)/shard_map/ppermute | solution.py:445
  255.6 5.4 collective-permute-start.23
  262.2 23.7 %collective-permute-start.24 = (bf16[288,1664]{1,0:T(8,128)(2,1)}, bf16[288,1664]{1,0:T(8,128)(2,1)}, u32[]{:S(2)}, u32[]{:S(2)}) collective-permute-start(bf16[288,1664]{1,0:T(8,128)(2,1)} %add_convert_fusion.2), channel_id=1, source_target_pairs={{0,16},{4,20},{8,24},{12,28},{16,0},{20,4},{24,8},{28,12},{1,17},{... | collective-permute-start | bytes 2875400 | tf_op jit(solution)/shard_map/ppermute | solution.py:445
  298.3 192.0 %reduce-scatter.9.cloned.1.call-start = ((), (), s32[]{:S(2)}) async-start(), calls=%async_computation.10 | async-start | bytes 3932160 | tf_op jit(solution)/shard_map/reduce_scatter | solution.py:868
  298.3 7.4 %collective-permute-start.26 = (bf16[288,1664]{1,0:T(8,128)(2,1)}, bf16[288,1664]{1,0:T(8,128)(2,1)}, u32[]{:S(2)}, u32[]{:S(2)}) collective-permute-start(bf16[288,1664]{1,0:T(8,128)(2,1)} %get-tuple-element.223), channel_id=1, source_target_pairs={{0,4},{4,0},{8,12},{12,8},{16,20},{20,16},{24,28},{28,24},{1,5},{5... | collective-permute-start | bytes 2875400 | tf_op jit(solution)/shard_map/ppermute | solution.py:445
  305.4 22.9 %collective-permute-start.25 = (bf16[288,1664]{1,0:T(8,128)(2,1)}, bf16[288,1664]{1,0:T(8,128)(2,1)}, u32[]{:S(2)}, u32[]{:S(2)}) collective-permute-start(bf16[288,1664]{1,0:T(8,128)(2,1)} %add_convert_fusion.1), channel_id=1, source_target_pairs={{0,8},{4,12},{8,0},{12,4},{16,24},{20,28},{24,16},{28,20},{1,9},{5... | collective-permute-start | bytes 2875400 | tf_op jit(solution)/shard_map/ppermute | solution.py:445
  305.8 38.2 %collective-permute-start.28 = (bf16[4,768,640]{2,1,0:T(8,128)(2,1)}, bf16[4,768,640]{2,1,0:T(8,128)(2,1)}, u32[]{:S(2)}, u32[]{:S(2)}) collective-permute-start(bf16[4,768,640]{2,1,0:T(8,128)(2,1)} %bitcast.219), channel_id=1, source_target_pairs={{0,4},{4,0},{8,12},{12,8},{16,20},{20,16},{24,28},{28,24},{1,5},{5... | collective-permute-start | bytes 11796488 | tf_op jit(solution)/shard_map/ppermute | solution.py:445
  308.2 24.0 %collective-permute-start.27 = (bf16[288,1664]{1,0:T(8,128)(2,1)}, bf16[288,1664]{1,0:T(8,128)(2,1)}, u32[]{:S(2)}, u32[]{:S(2)}) collective-permute-start(bf16[288,1664]{1,0:T(8,128)(2,1)} %add_convert_fusion), channel_id=1, source_target_pairs={{0,16},{4,20},{8,24},{12,28},{16,0},{20,4},{24,8},{28,12},{1,17},{... | collective-permute-start | bytes 2875400 | tf_op jit(solution)/shard_map/ppermute | solution.py:445
  345.0 38.1 %all-to-all-start.1 = ((bf16[288,4,384]{2,0,1:T(8,128)(2,1)}), bf16[288,4,384]{2,0,1:T(8,128)(2,1)}, u32[]{:S(2)}, u32[]{:S(2)}) async-start(bf16[288,4,384]{2,0,1:T(8,128)(2,1)} %bitcast.226), calls=%async_computation.1 | async-start | bytes 1769472 | tf_op jit(solution)/shard_map/all_to_all | solution.py:892
  349.2 204.0 %reduce-scatter.11.cloned.1.call-start = ((), (), s32[]{:S(2)}) async-start(), calls=%async_computation.11 | async-start | bytes 3932160 | tf_op jit(solution)/shard_map/reduce_scatter | solution.py:898
  349.3 22.3 %collective-permute-start.29 = (bf16[288,1536]{1,0:T(8,128)(2,1)}, bf16[288,1536]{1,0:T(8,128)(2,1)}, u32[]{:S(2)}, u32[]{:S(2)}) collective-permute-start(bf16[288,1536]{1,0:T(8,128)(2,1)} %get-tuple-element.243), channel_id=1, source_target_pairs={{0,4},{4,0},{8,12},{12,8},{16,20},{20,16},{24,28},{28,24},{1,5},{5... | collective-permute-start | bytes 2654216 | tf_op jit(solution)/shard_map/ppermute | solution.py:445
  349.3 22.8 %collective-permute-start.30 = (bf16[288,1536]{1,0:T(8,128)(2,1)}, bf16[288,1536]{1,0:T(8,128)(2,1)}, u32[]{:S(2)}, u32[]{:S(2)}) collective-permute-start(bf16[288,1536]{1,0:T(8,128)(2,1)} %get-tuple-element.244), channel_id=1, source_target_pairs={{0,4},{4,0},{8,12},{12,8},{16,20},{20,16},{24,28},{28,24},{1,5},{5... | collective-permute-start | bytes 2654216 | tf_op jit(solution)/shard_map/ppermute | solution.py:445
  349.8 22.3 %collective-permute-start.31 = (bf16[288,1536]{1,0:T(8,128)(2,1)}, bf16[288,1536]{1,0:T(8,128)(2,1)}, u32[]{:S(2)}, u32[]{:S(2)}) collective-permute-start(bf16[288,1536]{1,0:T(8,128)(2,1)} %get-tuple-element.245), channel_id=1, source_target_pairs={{0,4},{4,0},{8,12},{12,8},{16,20},{20,16},{24,28},{28,24},{1,5},{5... | collective-permute-start | bytes 2654216 | tf_op jit(solution)/shard_map/ppermute | solution.py:445
  349.9 22.2 %collective-permute-start.32 = (bf16[288,1536]{1,0:T(8,128)(2,1)}, bf16[288,1536]{1,0:T(8,128)(2,1)}, u32[]{:S(2)}, u32[]{:S(2)}) collective-permute-start(bf16[288,1536]{1,0:T(8,128)(2,1)} %get-tuple-element.246), channel_id=1, source_target_pairs={{0,4},{4,0},{8,12},{12,8},{16,20},{20,16},{24,28},{28,24},{1,5},{5... | collective-permute-start | bytes 2654216 | tf_op jit(solution)/shard_map/ppermute | solution.py:445
  357.7 25.4 %collective-permute-start.33 = (bf16[4,192,1536]{2,1,0:T(8,128)(2,1)}, bf16[4,192,1536]{2,1,0:T(8,128)(2,1)}, u32[]{:S(2)}, u32[]{:S(2)}) collective-permute-start(bf16[4,192,1536]{2,1,0:T(8,128)(2,1)} %dynamic-slice_bitcast_fusion), channel_id=1, source_target_pairs={{0,4},{4,0},{8,12},{12,8},{16,20},{20,16},{24,28},{28,24},{1,5},{5... | collective-permute-start | bytes 7077896 | tf_op jit(solution)/shard_map/ppermute | solution.py:445
  371.6 3.1 collective-permute-start.34
  383.8 43.7 %collective-permute-start.35 = (bf16[192,17]{0,1:T(8,128)(2,1)S(1)}, bf16[192,17]{0,1:T(8,128)(2,1)S(1)}, u32[]{:S(2)}, u32[]{:S(2)}) collective-permute-start(bf16[192,17]{0,1:T(8,128)(2,1)S(1)} %bitcast.248), channel_id=1, source_target_pairs={{0,16},{4,20},{8,24},{12,28},{16,0},{20,4},{24,8},{28,12},{1,17},{... | collective-permute-start | bytes 19592 | tf_op jit(solution)/shard_map/ppermute | solution.py:445
  389.6 37.9 %collective-permute-start.36 = (bf16[192,1536]{1,0:T(8,128)(2,1)S(1)}, bf16[192,1536]{1,0:T(8,128)(2,1)S(1)}, u32[]{:S(2)}, u32[]{:S(2)}) collective-permute-start(bf16[192,1536]{1,0:T(8,128)(2,1)S(1)} %get-tuple-element.379), channel_id=1, source_target_pairs={{0,16},{4,20},{8,24},{12,28},{16,0},{20,4},{24,8},{28,12},{1,17},{... | collective-permute-start | bytes 1769480 | tf_op jit(solution)/shard_map/ppermute | solution.py:445
  390.2 37.4 %collective-permute-start.37 = (bf16[288,1536]{1,0:T(8,128)(2,1)S(1)}, bf16[288,1536]{1,0:T(8,128)(2,1)S(1)}, u32[]{:S(2)}, u32[]{:S(2)}) collective-permute-start(bf16[288,1536]{1,0:T(8,128)(2,1)S(1)} %copy-done.27), channel_id=1, source_target_pairs={{0,16},{4,20},{8,24},{12,28},{16,0},{20,4},{24,8},{28,12},{1,17},{... | collective-permute-start | bytes 2654216 | tf_op jit(solution)/shard_map/ppermute | solution.py:445
  429.1 1.6 collective-permute-start.38
  431.7 4.9 collective-permute-start.39
  432.3 9.5 %collective-permute-start.41 = (bf16[128,256]{1,0:T(8,128)(2,1)S(1)}, bf16[128,256]{1,0:T(8,128)(2,1)S(1)}, u32[]{:S(2)}, u32[]{:S(2)}) collective-permute-start(bf16[128,256]{1,0:T(8,128)(2,1)S(1)} %get-tuple-element.399), channel_id=1, source_target_pairs={{0,16},{4,20},{8,24},{12,28},{16,0},{20,4},{24,8},{28,12},{1,17},{... | collective-permute-start | bytes 196616 | tf_op jit(solution)/shard_map/ppermute | solution.py:445
  436.7 5.1 collective-permute-start.40
  454.7 11.0 %collective-permute-start.42 = (bf16[4,192,640]{2,1,0:T(8,128)(2,1)}, bf16[4,192,640]{2,1,0:T(8,128)(2,1)S(1)}, u32[]{:S(2)}, u32[]{:S(2)}) collective-permute-start(bf16[4,192,640]{2,1,0:T(8,128)(2,1)} %dynamic-slice_bitcast_fusion.1), channel_id=1, source_target_pairs={{0,4},{4,0},{8,12},{12,8},{16,20},{20,16},{24,28},{28,24},{1,5},{5... | collective-permute-start | bytes 2949128 | tf_op jit(solution)/shard_map/ppermute | solution.py:445
  454.8 6.2 %collective-permute-start.51 = (bf16[192,17]{0,1:T(8,128)(2,1)S(1)}, bf16[192,17]{0,1:T(8,128)(2,1)S(1)}, u32[]{:S(2)}, u32[]{:S(2)}) collective-permute-start(bf16[192,17]{0,1:T(8,128)(2,1)S(1)} %bitcast.249), channel_id=1, source_target_pairs={{0,16},{4,20},{8,24},{12,28},{16,0},{20,4},{24,8},{28,12},{1,17},{... | collective-permute-start | bytes 19592 | tf_op jit(solution)/shard_map/ppermute | solution.py:445
  455.0 6.1 %collective-permute-start.50 = (bf16[192,17]{0,1:T(8,128)(2,1)S(1)}, bf16[192,17]{0,1:T(8,128)(2,1)S(1)}, u32[]{:S(2)}, u32[]{:S(2)}) collective-permute-start(bf16[192,17]{0,1:T(8,128)(2,1)S(1)} %fusion.73), channel_id=1, source_target_pairs={{0,8},{4,12},{8,0},{12,4},{16,24},{20,28},{24,16},{28,20},{1,9},{5... | collective-permute-start | bytes 19592 | tf_op jit(solution)/shard_map/ppermute | solution.py:445
  455.9 16.5 %collective-permute-start.49 = (bf16[192,1536]{1,0:T(8,128)(2,1)}, bf16[192,1536]{1,0:T(8,128)(2,1)}, u32[]{:S(2)}, u32[]{:S(2)}) collective-permute-start(bf16[192,1536]{1,0:T(8,128)(2,1)} %get-tuple-element.290), channel_id=1, source_target_pairs={{0,16},{4,20},{8,24},{12,28},{16,0},{20,4},{24,8},{28,12},{1,17},{... | collective-permute-start | bytes 1769480 | tf_op jit(solution)/shard_map/ppermute | solution.py:445
  459.9 15.2 %collective-permute-start.48 = (bf16[192,1536]{1,0:T(8,128)(2,1)}, bf16[192,1536]{1,0:T(8,128)(2,1)}, u32[]{:S(2)}, u32[]{:S(2)}) collective-permute-start(bf16[192,1536]{1,0:T(8,128)(2,1)} %add_convert_fusion.12), channel_id=1, source_target_pairs={{0,8},{4,12},{8,0},{12,4},{16,24},{20,28},{24,16},{28,20},{1,9},{5... | collective-permute-start | bytes 1769480 | tf_op jit(solution)/shard_map/ppermute | solution.py:445
  461.2 67.9 %all-to-all-start.2 = ((bf16[4,288,640]{2,1,0:T(8,128)(2,1)}), bf16[4,288,640]{2,1,0:T(8,128)(2,1)}, u32[]{:S(2)}, u32[]{:S(2)}) async-start(bf16[4,288,640]{2,1,0:T(8,128)(2,1)} %bitcast.49), calls=%async_computation.2 | async-start | bytes 2949120 | tf_op jit(solution)/shard_map/all_to_all | solution.py:958
  465.5 92.3 %reduce-scatter.13.cloned.1.call-start = ((), (), s32[]{:S(2)}) async-start(), calls=%async_computation.13 | async-start | bytes 983040
  467.3 10.4 %collective-permute-start.43 = (bf16[192,640]{1,0:T(8,128)(2,1)S(1)}, bf16[192,640]{1,0:T(8,128)(2,1)S(1)}, u32[]{:S(2)}, u32[]{:S(2)}) collective-permute-start(bf16[192,640]{1,0:T(8,128)(2,1)S(1)} %get-tuple-element.388), channel_id=1, source_target_pairs={{0,16},{4,20},{8,24},{12,28},{16,0},{20,4},{24,8},{28,12},{1,17},{... | collective-permute-start | bytes 737288 | tf_op jit(solution)/shard_map/ppermute | solution.py:445
  477.4 11.2 %collective-permute-start.45 = (bf16[192,640]{1,0:T(8,128)(2,1)S(1)}, bf16[192,640]{1,0:T(8,128)(2,1)S(1)}, u32[]{:S(2)}, u32[]{:S(2)}) collective-permute-start(bf16[192,640]{1,0:T(8,128)(2,1)S(1)} %get-tuple-element.389), channel_id=1, source_target_pairs={{0,16},{4,20},{8,24},{12,28},{16,0},{20,4},{24,8},{28,12},{1,17},{... | collective-permute-start | bytes 737288 | tf_op jit(solution)/shard_map/ppermute | solution.py:445
  477.8 10.8 %collective-permute-start.44 = (bf16[192,640]{1,0:T(8,128)(2,1)S(1)}, bf16[192,640]{1,0:T(8,128)(2,1)S(1)}, u32[]{:S(2)}, u32[]{:S(2)}) collective-permute-start(bf16[192,640]{1,0:T(8,128)(2,1)S(1)} %fusion.46), channel_id=1, source_target_pairs={{0,8},{4,12},{8,0},{12,4},{16,24},{20,28},{24,16},{28,20},{1,9},{5... | collective-permute-start | bytes 737288 | tf_op jit(solution)/shard_map/ppermute | solution.py:445
  481.4 60.1 %collective-permute-start.46 = (bf16[288,1536]{1,0:T(8,128)(2,1)}, bf16[288,1536]{1,0:T(8,128)(2,1)}, u32[]{:S(2)}, u32[]{:S(2)}) collective-permute-start(bf16[288,1536]{1,0:T(8,128)(2,1)} %add_convert_fusion.7), channel_id=1, source_target_pairs={{0,8},{4,12},{8,0},{12,4},{16,24},{20,28},{24,16},{28,20},{1,9},{5... | collective-permute-start | bytes 2654216 | tf_op jit(solution)/shard_map/ppermute | solution.py:445
  484.6 56.9 %collective-permute-start.47 = (bf16[288,1536]{1,0:T(8,128)(2,1)}, bf16[288,1536]{1,0:T(8,128)(2,1)}, u32[]{:S(2)}, u32[]{:S(2)}) collective-permute-start(bf16[288,1536]{1,0:T(8,128)(2,1)} %add_convert_fusion.6), channel_id=1, source_target_pairs={{0,16},{4,20},{8,24},{12,28},{16,0},{20,4},{24,8},{28,12},{1,17},{... | collective-permute-start | bytes 2654216 | tf_op jit(solution)/shard_map/ppermute | solution.py:445
  (45 other events, 303.9 us)
Sparse Core Ops, SparseCore 0:
  9.6 79.8 all-gather.6
  112.3 44.8 all-gather.8
  204.5 73.9 all-gather.10
  298.4 57.3 reduce-scatter.6
  358.0 66.0 reduce-scatter.8
  439.1 82.6 reduce-scatter.10
  524.0 29.3 reduce-scatter.12

commit v12 on v11

--- a/solution.py
+++ b/solution.py
@@ -969,7 +969,9 @@
     out_pieces = reduce_singles(out_sums, out_pending, "shard")
     grad_out = add_all(reduce_singles(whole_sums, whole_pending, "shard")).astype(bf16).T
     hidden_units = w_gate.shape[2]
-    grad_down, first_sums = lax.optimization_barrier((grad_down, pre_grads[0], grad_qkv))[:2]
+    grad_down, first_sums, grad_qkv = lax.optimization_barrier(
+        (grad_down, pre_grads[0], grad_qkv)
+    )
     grad_down = grad_down.T.reshape(local_experts, hidden_units, -1).astype(jnp.float32)
     pre_grads[0] = first_sums.astype(jnp.float32)
     lin_tokens, grad_down, pre_grads[0] = lax.optimization_barrier(

time: 576 us -> 576 us (level)
    unnamed x121 -> x123, local copies, waits for them, and re-layouts: 23.9 us -> 23.7 us
where the time goes in v12:
time: 576 us; the launch traced here: 568 us
  Pallas kernels  148 us (26%)
  waiting for transfers between devices  102 us (18%)
  matrix products  76 us (13%)
  other arithmetic  61.6 us (11%)
  blocking collectives  60.5 us (11%)
  local copies, waits for them, and re-layouts  58.2 us (10%)
  starting transfers between devices  46.2 us (8%)
  between operations  15.7 us (3%)
    pallas_call x4, Pallas kernels, expert_pair(): pl.pallas_call(partial(expert_body, experts_all), out_shape=out_shape, gr...  87.1 us
    dot_general x6, matrix products, transposed_times(): lax.dot_general(left_side, right_side, (((0,), (0,)), ((), ())), precisio...  49.1 us
    ppermute x52, waiting for transfers between devices, exchange(): return lax.ppermute(values, axis_name, [(i, i ^ bit) for i in range(count)])  39.1 us
    pallas_call x1, Pallas kernels, attend_backward(): pl.pallas_call(partial(attend_backward_body, group, kv_heads), out_shape=...  35.8 us
    ppermute x52, starting transfers between devices, exchange(): return lax.ppermute(values, axis_name, [(i, i ^ bit) for i in range(count)])  33.5 us
    all_to_all x1, waiting for transfers between devices, on_device(): lax.all_to_all(lin_all, 'seq', split_axis=0, concat_axis=1, tiled=True)  28.8 us
    convert_element_type x17, other arithmetic, add_rounded(): (left_side.astype(jnp.float32) + right_side.astype(jnp.float32)).astype(j...  28.7 us
    all_gather x1, blocking collectives, on_device(): out_weight = lax.all_gather(w_out, 'seq', axis=0, tiled=True)  25.8 us
  transfers between devices with their start and end apart: 62, of which 19 were waited for; matrix products, arithmetic and copies ran while one was open for 27% of the time, Pallas kernels for 26%

profile of v12, /device:TPU:0, one launch (start us, length us, event | category | flops | bytes accessed | tf_op | source)
XLA Modules:
  0.0 568.1 jit_solution(9121473810974116621)
XLA Ops:
  11.1 2.6 collective-permute-start.1
  15.8 25.8 %all_gather.28 = bf16[1536,192]{0,1:T(8,128)(2,1)} all-gather(bf16[384,192]{0,1:T(8,128)(2,1)} %param.18), channel_id=1, replica_groups=mesh['shard'=8,'seq'=4] {'seq'}, dimensions={0}, use_global_device_ids=true | all-gather | bytes 737280 | tf_op jit(solution)/shard_map/all_gather | solution.py:732
  42.2 14.3 %all-gather.1 = bf16[4,48,18]{1,2,0:T(8,128)(2,1)S(1)} all-gather(bf16[1,48,18]{1,2,0:T(8,128)(2,1)S(1)} %maximum_bitcast_fusion.1), channel_id=1, replica_groups=mesh['shard'=8,'seq'=4] {'seq'}, dimensions={0}, use_global_device_ids=true | all-gather | bytes 8640 | tf_op jit(solution)/shard_map/all_gather | solution.py:714
  56.7 9.3 %all-gather.2 = bf16[8,192,18]{1,2,0:T(8,128)(2,1)S(1)} all-gather(bf16[1,192,18]{1,2,0:T(8,128)(2,1)S(1)} %reshape.375), channel_id=1, replica_groups=mesh['shard'=8,'seq'=4] {'shard'}, dimensions={0}, use_global_device_ids=true | all-gather | bytes 62208 | tf_op jit(solution)/shard_map/all_gather | solution.py:715
  70.8 4.5 collective-permute-done.7
  82.6 6.9 %all-gather.7.cloned.1.call-done = bf16[1152,1536]{1,0:T(8,128)(2,1)} async-done(((bf16[288,1536]{1,0:T(8,128)(2,1)}), bf16[1152,1536]{1,0:T(8,128)(2,1)}) %all-gather.7.cloned.1.call-update) | async-done | bytes 3538960 | tf_op jit(solution)/shard_map/all_gather | solution.py:719
  91.2 2.9 fusion
  94.3 4.7 fusion.24
  101.1 11.1 %all_gather.27.kp_ref.vp_ref = bf16[1024,256]{1,0:T(8,128)(2,1)} all-gather(bf16[128,256]{1,0:T(8,128)(2,1)S(1)} %fusion.67), channel_id=1, replica_groups=mesh['shard'=8,'seq'=4] {'shard'}, dimensions={0}, use_global_device_ids=true | all-gather | bytes 589824 | tf_op jit(solution)/shard_map/all_gather | solution.py:762
  118.8 24.9 %attend_forward.1 = (bf16[1152,384]{1,0:T(8,128)(2,1)}, f32[6,1,1152]{2,1,0:T(1,128)}) custom-call(s32[1]{0:T(128)} %bitcast.9.index_ref, bf16[1152,384]{1,0:T(8,128)(2,1)} %copy.135.q_ref, bf16[1024,256]{1,0:T(8,128)(2,1)} %all_gather.27.kp_ref.vp_ref, bf16[1024,256]{1,0:T(8,128)(2,1)} %all_gather.27.kp_ref.vp_ref, ...), custom_call_target="tpu_custom_call" | custom-call | flops 9059696640 | bytes 3538944 | tf_op jit(solution)/shard_map/attend_forward/pallas_call | solution.py:376
  143.7 2.5 collective-permute-done.12.og_even
  146.2 3.5 all-to-all-start
  150.0 2.3 constant_dynamic-slice_fusion.4
  152.3 17.7 %all-to-all-done = bf16[4,288,384]{2,1,0:T(8,128)(2,1)S(1)} async-done(((bf16[4,288,384]{2,1,0:T(8,128)(2,1)}), bf16[4,288,384]{2,1,0:T(8,128)(2,1)S(1)}, u32[]{:S(2)}, u32[]{:S(2)}) %all-to-all-start) | async-done | bytes 884768 | tf_op jit(solution)/shard_map/all_to_all | solution.py:780
  171.1 4.3 multiply_reduce_fusion.2
  178.3 2.5 collective-permute-start.13
  181.2 21.4 %experts.4 = (bf16[2304,1536]{1,0:T(8,128)(2,1)}, bf16[2304,1536]{1,0:T(8,128)(2,1)}, bf16[2,2304,1024]{2,1,0:T(8,128)(2,1)}, bf16[2304,1024]{1,0:T(8,128)(2,1)}...) custom-call(s32[1]{0:T(128)} %bitcast.24.index_ref, ...), custom_call_target="tpu_custom_call" | custom-call | flops 10871635968 | bytes 27131904 | tf_op jit(solution)/shard_map/experts/pallas_call | solution.py:654
  207.3 22.2 %experts.5 = (bf16[2304,1536]{1,0:T(8,128)(2,1)}, bf16[2304,1536]{1,0:T(8,128)(2,1)}, bf16[2,2304,1024]{2,1,0:T(8,128)(2,1)}, bf16[2304,1024]{1,0:T(8,128)(2,1)}...) custom-call(s32[1]{0:T(128)} %bitcast.24.index_ref, ...), custom_call_target="tpu_custom_call", output_to_operand_aliasing={{0}: (8, {}), {1}: (9, {}), {2}: (10, {}), {3}: (11, {})} | custom-call | flops 10871635968 | bytes 27131904 | tf_op jit(solution)/shard_map/experts/pallas_call | solution.py:654
  230.7 3.0 collective-permute-done.22.og_odd
  233.7 21.9 %experts.6 = (bf16[2304,1536]{1,0:T(8,128)(2,1)}, bf16[2304,1536]{1,0:T(8,128)(2,1)}, bf16[2,2304,1024]{2,1,0:T(8,128)(2,1)}, bf16[2304,1024]{1,0:T(8,128)(2,1)}...) custom-call(s32[1]{0:T(128)} %bitcast.24.index_ref, ...), custom_call_target="tpu_custom_call", output_to_operand_aliasing={{0}: (8, {}), {1}: (9, {}), {2}: (10, {}), {3}: (11, {})} | custom-call | flops 10871635968 | bytes 27131904 | tf_op jit(solution)/shard_map/experts/pallas_call | solution.py:654
  255.9 2.7 add_convert_fusion.4
  258.6 2.5 add_convert_fusion.3
  262.4 21.6 %experts.7 = (bf16[2304,1536]{1,0:T(8,128)(2,1)}, bf16[2304,1536]{1,0:T(8,128)(2,1)}, bf16[2,2304,1024]{2,1,0:T(8,128)(2,1)}, bf16[2304,1024]{1,0:T(8,128)(2,1)}...) custom-call(s32[1]{0:T(128)} %bitcast.24.index_ref, ...), custom_call_target="tpu_custom_call", output_to_operand_aliasing={{0}: (8, {}), {1}: (9, {}), {2}: (10, {}), {3}: (11, {})} | custom-call | flops 10871635968 | bytes 27131904 | tf_op jit(solution)/shard_map/experts/pallas_call | solution.py:654
  284.0 2.1 collective-permute-done.24
  286.1 12.3 %convolution_convert_fusion.1 = bf16[1536,1024]{1,0:T(8,128)(2,1)} fusion(bf16[2304,1536]{1,0:T(8,128)(2,1)} %get-tuple-element.225, bf16[2304,1024]{1,0:T(8,128)(2,1)} %get-tuple-element.226), kind=kOutput, calls=%fused_computation.16 | convolution fusion | flops 7249330176 | bytes 14942208 | tf_op jit(solution)/shard_map/dot_general | solution.py:71
  300.6 2.3 copy.145.sin_ref
  302.8 2.7 add_convert_fusion.1
  305.9 2.4 add_convert_fusion
  309.0 12.9 %fusion.10 = bf16[1536,1024]{1,0:T(8,128)(2,1)} fusion(bf16[2304,1536]{1,0:T(8,128)(2,1)} %get-tuple-element.248, bf16[2,2304,1024]{2,1,0:T(8,128)(2,1)} %get-tuple-element.229), kind=kOutput, calls=%fused_computation.14 | convolution fusion | flops 7249330176 | bytes 14942208 | tf_op jit(solution)/shard_map/dot_general | solution.py:71
  321.9 6.5 %collective-permute-done.25 = bf16[288,1664]{1,0:T(8,128)(2,1)} collective-permute-done((bf16[288,1664]{1,0:T(8,128)(2,1)}, bf16[288,1664]{1,0:T(8,128)(2,1)}, u32[]{:S(2)}, u32[]{:S(2)}) %collective-permute-start.25) | collective-permute-done | bytes 958496 | tf_op jit(solution)/shard_map/ppermute | solution.py:445
  328.4 3.8 collective-permute-done.27
  332.3 2.1 convert_add_fusion.3
  334.8 2.4 multiply_reduce_fusion
  337.3 2.2 subtract_add_fusion
  339.6 4.5 convolution_convert_fusion.3
  345.2 4.2 all-to-all-start.1
  350.5 4.4 convolution_convert_fusion
  357.8 13.1 %fusion.13 = bf16[1536,1024]{1,0:T(8,128)(2,1)} fusion(bf16[2304,1536]{1,0:T(8,128)(2,1)} %get-tuple-element.248, bf16[2,2304,1024]{2,1,0:T(8,128)(2,1)} %get-tuple-element.229), kind=kOutput, calls=%fused_computation.15 | convolution fusion | flops 7249330176 | bytes 14942208 | tf_op jit(solution)/shard_map/dot_general | solution.py:71
  372.2 2.6 add_convert_fusion.10
  374.8 8.5 %all-to-all-done.1 = bf16[288,4,384]{2,0,1:T(8,128)(2,1)} async-done(((bf16[288,4,384]{2,0,1:T(8,128)(2,1)}), bf16[288,4,384]{2,0,1:T(8,128)(2,1)}, u32[]{:S(2)}, u32[]{:S(2)}) %all-to-all-start.1) | async-done | bytes 884768 | tf_op jit(solution)/shard_map/all_to_all | solution.py:892
  385.5 3.0 fusion.3
  391.8 35.8 %attend_backward.1 = (bf16[1152,384]{1,0:T(8,128)(2,1)}, bf16[1024,256]{1,0:T(8,128)(2,1)}, f32[1152,256]{1,0:T(8,128)}) custom-call(s32[1]{0:T(128)} %bitcast.9.index_ref, bf16[1152,384]{1,0:T(8,128)(2,1)} %copy.135.q_ref, bf16[1152,384]{1,0:T(8,128)(2,1)} %bitcast.28.grad_ref, bf16[1152,384]{1,0:T(8,128)(2,1)} %get-tuple-element.165.mixed_ref, ...), custom_call_target="tpu_custom_call" | custom-call | flops 22649241600 | bytes 3538944 | tf_op jit(solution)/shard_map/attend_backward/pallas_call | solution.py:406
  434.0 2.8 collective-permute-done.39
  439.1 1.8 slice.326
  445.2 2.4 maximum_maximum_fusion
  447.6 5.8 %convolution_convert_fusion.2 = bf16[1536,640]{1,0:T(8,128)(2,1)S(1)} fusion(bf16[1152,640]{1,0:T(8,128)(2,1)} %maximum_maximum_fusion, bf16[1152,1536]{1,0:T(8,128)(2,1)} %all-gather.7.cloned.1.call-done, f32[1536]{0:T(1024)S(1)} %get-tuple-element.373, f32[1152]{0:T(1024)S(1)} %copy-done.43), kind=kOutput, calls=%fused_computation.17 | convolution fusion | flops 2272985088 | bytes 6990336 | tf_op jit(solution)/shard_map/dot_general | solution.py:71
  457.4 2.0 collective-permute-start.49
  459.4 2.0 add_convert_fusion.12
  462.8 4.4 all-to-all-start.2
  469.7 4.2 collective-permute-done.49
  473.9 2.7 collective-permute-done.48
  476.6 2.3 fusion.44
  480.6 2.4 add_convert_fusion.7
  483.8 2.3 add_convert_fusion.6
  487.8 2.3 add_convert_fusion.9
  492.3 2.5 reshape.369
  494.8 2.6 convert_element_type.444
  500.4 28.8 %all-to-all-done.2 = bf16[4,288,640]{2,1,0:T(8,128)(2,1)} async-done(((bf16[4,288,640]{2,1,0:T(8,128)(2,1)}), bf16[4,288,640]{2,1,0:T(8,128)(2,1)}, u32[]{:S(2)}, u32[]{:S(2)}) %all-to-all-start.2) | async-done | bytes 1474592 | tf_op jit(solution)/shard_map/all_to_all | solution.py:958
  534.4 1.8 fusion.29
  538.0 1.8 convolution_add_fusion.2
  539.8 1.8 broadcast_select_fusion.1
  545.0 3.7 copy.152
  548.7 4.7 fusion.20
  556.1 2.0 pad_maximum_fusion.1
  (335 shorter events, 102.2 us)
Async XLA Ops:
  7.2 82.3 %all-gather.7.cloned.1.call-start = ((), (), s32[]{:S(2)}) async-start(), calls=%async_computation.7 | async-start | bytes 4423680 | tf_op jit(solution)/shard_map/all_gather | solution.py:719
  7.9 163.1 %all-gather.9.cloned.1.call-start = ((), (), s32[]{:S(2)}) async-start(), calls=%async_computation.8 | async-start | bytes 5308416 | tf_op jit(solution)/shard_map/all_gather | solution.py:767
  10.6 60.3 %copy-start.16 = (bf16[192,640]{1,0:T(8,128)(2,1)}, bf16[192,640]{1,0:T(8,128)(2,1)S(1)}, u32[]{:S(2)}) copy-start(bf16[192,640]{1,0:T(8,128)(2,1)S(1)} %constant_dynamic-update-slice_fusion) | copy-start | bytes 737284
  10.6 58.2 %collective-permute-start = (bf16[192,640]{1,0:T(8,128)(2,1)S(1)}, bf16[192,640]{1,0:T(8,128)(2,1)}, u32[]{:S(2)}, u32[]{:S(2)}) collective-permute-start(bf16[192,640]{1,0:T(8,128)(2,1)S(1)} %constant_dynamic-update-slice_fusion), channel_id=1, source_target_pairs={{0,4},{4,0},{8,12},{12,8},{16,20},{20,16},{24,28},{28,24},{1,5},{5... | collective-permute-start | bytes 737288 | tf_op jit(solution)/shard_map/ppermute | solution.py:445
  11.1 55.7 %collective-permute-start.1 = (bf16[192,640]{1,0:T(8,128)(2,1)S(1)}, bf16[192,640]{1,0:T(8,128)(2,1)}, u32[]{:S(2)}, u32[]{:S(2)}) collective-permute-start(bf16[192,640]{1,0:T(8,128)(2,1)S(1)} %constant_dynamic-update-slice_fusion), channel_id=1, source_target_pairs={{0,8},{4,12},{8,0},{12,4},{16,24},{20,28},{24,16},{28,20},{1,9},{5... | collective-permute-start | bytes 737288 | tf_op jit(solution)/shard_map/ppermute | solution.py:445
  13.7 53.2 %collective-permute-start.2 = (bf16[192,640]{1,0:T(8,128)(2,1)S(1)}, bf16[192,640]{1,0:T(8,128)(2,1)S(1)}, u32[]{:S(2)}, u32[]{:S(2)}) collective-permute-start(bf16[192,640]{1,0:T(8,128)(2,1)S(1)} %constant_dynamic-update-slice_fusion), channel_id=1, source_target_pairs={{0,16},{4,20},{8,24},{12,28},{16,0},{20,4},{24,8},{28,12},{1,17},{... | collective-permute-start | bytes 737288 | tf_op jit(solution)/shard_map/ppermute | solution.py:445
  15.2 51.7 %collective-permute-start.3 = (bf16[288,1536]{1,0:T(8,128)(2,1)}, bf16[288,1536]{1,0:T(8,128)(2,1)}, u32[]{:S(2)}, u32[]{:S(2)}) collective-permute-start(bf16[288,1536]{1,0:T(8,128)(2,1)} %og_even.1), channel_id=1, source_target_pairs={{0,8},{4,12},{8,0},{12,4},{16,24},{20,28},{24,16},{28,20},{1,9},{5... | collective-permute-start | bytes 2654216 | tf_op jit(solution)/shard_map/ppermute | solution.py:445
  15.7 51.1 %collective-permute-start.4 = (bf16[288,1536]{1,0:T(8,128)(2,1)}, bf16[288,1536]{1,0:T(8,128)(2,1)}, u32[]{:S(2)}, u32[]{:S(2)}) collective-permute-start(bf16[288,1536]{1,0:T(8,128)(2,1)} %og_even.1), channel_id=1, source_target_pairs={{0,16},{4,20},{8,24},{12,28},{16,0},{20,4},{24,8},{28,12},{1,17},{... | collective-permute-start | bytes 2654216 | tf_op jit(solution)/shard_map/ppermute | solution.py:445
  66.7 49.5 %copy-start.14 = (f32[1152,1,32]{0,2,1:T(8,128)}, f32[1152,1,32]{0,2,1:T(8,128)S(1)}, u32[]{:S(2)}) copy-start(f32[1152,1,32]{0,2,1:T(8,128)S(1)} %get-tuple-element.157) | copy-start | bytes 442372
  66.9 8.4 %collective-permute-start.5 = (bf16[192,640]{1,0:T(8,128)(2,1)}, bf16[192,640]{1,0:T(8,128)(2,1)S(1)}, u32[]{:S(2)}, u32[]{:S(2)}) collective-permute-start(bf16[192,640]{1,0:T(8,128)(2,1)} %collective-permute-done.1), channel_id=1, source_target_pairs={{0,4},{4,0},{8,12},{12,8},{16,20},{20,16},{24,28},{28,24},{1,5},{5... | collective-permute-start | bytes 737288 | tf_op jit(solution)/shard_map/ppermute | solution.py:445
  67.3 8.0 %collective-permute-start.7 = (bf16[192,640]{1,0:T(8,128)(2,1)S(1)}, bf16[192,640]{1,0:T(8,128)(2,1)S(1)}, u32[]{:S(2)}, u32[]{:S(2)}) collective-permute-start(bf16[192,640]{1,0:T(8,128)(2,1)S(1)} %collective-permute-done.2), channel_id=1, source_target_pairs={{0,8},{4,12},{8,0},{12,4},{16,24},{20,28},{24,16},{28,20},{1,9},{5... | collective-permute-start | bytes 737288 | tf_op jit(solution)/shard_map/ppermute | solution.py:445
  69.8 5.6 collective-permute-start.6
  75.3 1.5 collective-permute-start.8
  112.2 31.5 %collective-permute-start.9 = (bf16[288,1536]{1,0:T(8,128)(2,1)}, bf16[288,1536]{1,0:T(8,128)(2,1)}, u32[]{:S(2)}, u32[]{:S(2)}) collective-permute-start(bf16[288,1536]{1,0:T(8,128)(2,1)} %og_even.1), channel_id=1, source_target_pairs={{0,4},{4,0},{8,12},{12,8},{16,20},{20,16},{24,28},{28,24},{1,5},{5... | collective-permute-start | bytes 2654216 | tf_op jit(solution)/shard_map/ppermute | solution.py:445
  112.6 31.1 %collective-permute-start.10 = (bf16[288,1536]{1,0:T(8,128)(2,1)}, bf16[288,1536]{1,0:T(8,128)(2,1)}, u32[]{:S(2)}, u32[]{:S(2)}) collective-permute-start(bf16[288,1536]{1,0:T(8,128)(2,1)} %collective-permute-done.3.og_even), channel_id=1, source_target_pairs={{0,4},{4,0},{8,12},{12,8},{16,20},{20,16},{24,28},{28,24},{1,5},{5... | collective-permute-start | bytes 2654216 | tf_op jit(solution)/shard_map/ppermute | solution.py:445
  112.8 31.0 %collective-permute-start.11 = (bf16[288,1536]{1,0:T(8,128)(2,1)}, bf16[288,1536]{1,0:T(8,128)(2,1)}, u32[]{:S(2)}, u32[]{:S(2)}) collective-permute-start(bf16[288,1536]{1,0:T(8,128)(2,1)} %collective-permute-done.4.og_even), channel_id=1, source_target_pairs={{0,4},{4,0},{8,12},{12,8},{16,20},{20,16},{24,28},{28,24},{1,5},{5... | collective-permute-start | bytes 2654216 | tf_op jit(solution)/shard_map/ppermute | solution.py:445
  114.7 31.5 %collective-permute-start.12 = (bf16[288,1536]{1,0:T(8,128)(2,1)}, bf16[288,1536]{1,0:T(8,128)(2,1)}, u32[]{:S(2)}, u32[]{:S(2)}) collective-permute-start(bf16[288,1536]{1,0:T(8,128)(2,1)} %collective-permute-done.4.og_even), channel_id=1, source_target_pairs={{0,8},{4,12},{8,0},{12,4},{16,24},{20,28},{24,16},{28,20},{1,9},{5... | collective-permute-start | bytes 2654216 | tf_op jit(solution)/shard_map/ppermute | solution.py:445
  146.2 23.8 %all-to-all-start = ((bf16[4,288,384]{2,1,0:T(8,128)(2,1)}), bf16[4,288,384]{2,1,0:T(8,128)(2,1)S(1)}, u32[]{:S(2)}, u32[]{:S(2)}) async-start(bf16[4,288,384]{2,1,0:T(8,128)(2,1)} %bitcast.239), calls=%async_computation | async-start | bytes 1769472 | tf_op jit(solution)/shard_map/all_to_all | solution.py:780
  149.7 136.4 %all-gather.11.cloned.1.call-start = ((), (), s32[]{:S(2)}) async-start(), calls=%async_computation.12 | async-start | bytes 4915200 | tf_op jit(solution)/shard_map/all_gather | solution.py:790
  178.3 2.9 collective-permute-start.15
  178.3 24.7 %collective-permute-start.13 = (bf16[288,1664]{1,0:T(8,128)(2,1)}, bf16[288,1664]{1,0:T(8,128)(2,1)}, u32[]{:S(2)}, u32[]{:S(2)}) collective-permute-start(bf16[288,1664]{1,0:T(8,128)(2,1)} %concatenate.70.x_even), channel_id=1, source_target_pairs={{0,8},{4,12},{8,0},{12,4},{16,24},{20,28},{24,16},{28,20},{1,9},{5... | collective-permute-start | bytes 2875400 | tf_op jit(solution)/shard_map/ppermute | solution.py:445
  180.8 23.7 %collective-permute-start.14 = (bf16[288,1664]{1,0:T(8,128)(2,1)}, bf16[288,1664]{1,0:T(8,128)(2,1)}, u32[]{:S(2)}, u32[]{:S(2)}) collective-permute-start(bf16[288,1664]{1,0:T(8,128)(2,1)} %concatenate.70.x_even), channel_id=1, source_target_pairs={{0,16},{4,20},{8,24},{12,28},{16,0},{20,4},{24,8},{28,12},{1,17},{... | collective-permute-start | bytes 2875400 | tf_op jit(solution)/shard_map/ppermute | solution.py:445
  204.5 2.9 collective-permute-start.19
  204.5 286.6 %reduce-scatter.7.cloned.1.call-start = ((), (), s32[]{:S(2)}) async-start(), calls=%async_computation.9 | async-start | bytes 3932160 | tf_op jit(solution)/shard_map/reduce_scatter | solution.py:864
  204.7 24.8 %collective-permute-start.18 = (bf16[288,1664]{1,0:T(8,128)(2,1)}, bf16[288,1664]{1,0:T(8,128)(2,1)}, u32[]{:S(2)}, u32[]{:S(2)}) collective-permute-start(bf16[288,1664]{1,0:T(8,128)(2,1)} %collective-permute-done.14.x_even), channel_id=1, source_target_pairs={{0,8},{4,12},{8,0},{12,4},{16,24},{20,28},{24,16},{28,20},{1,9},{5... | collective-permute-start | bytes 2875400 | tf_op jit(solution)/shard_map/ppermute | solution.py:445
  229.5 4.2 collective-permute-start.21
  229.7 4.1 collective-permute-start.22
  230.1 32.2 %collective-permute-start.16 = (bf16[288,1664]{1,0:T(8,128)(2,1)}, bf16[288,1664]{1,0:T(8,128)(2,1)}, u32[]{:S(2)}, u32[]{:S(2)}) collective-permute-start(bf16[288,1664]{1,0:T(8,128)(2,1)} %collective-permute-done.14.x_even), channel_id=1, source_target_pairs={{0,4},{4,0},{8,12},{12,8},{16,20},{20,16},{24,28},{28,24},{1,5},{5... | collective-permute-start | bytes 2875400 | tf_op jit(solution)/shard_map/ppermute | solution.py:445
  230.2 25.7 %collective-permute-start.17 = (bf16[288,1664]{1,0:T(8,128)(2,1)}, bf16[288,1664]{1,0:T(8,128)(2,1)}, u32[]{:S(2)}, u32[]{:S(2)}) collective-permute-start(bf16[288,1664]{1,0:T(8,128)(2,1)} %get-tuple-element.175), channel_id=1, source_target_pairs={{0,4},{4,0},{8,12},{12,8},{16,20},{20,16},{24,28},{28,24},{1,5},{5... | collective-permute-start | bytes 2875400 | tf_op jit(solution)/shard_map/ppermute | solution.py:445
  230.6 28.0 %collective-permute-start.20 = (bf16[288,1664]{1,0:T(8,128)(2,1)}, bf16[288,1664]{1,0:T(8,128)(2,1)}, u32[]{:S(2)}, u32[]{:S(2)}) collective-permute-start(bf16[288,1664]{1,0:T(8,128)(2,1)} %get-tuple-element.188), channel_id=1, source_target_pairs={{0,4},{4,0},{8,12},{12,8},{16,20},{20,16},{24,28},{28,24},{1,5},{5... | collective-permute-start | bytes 2875400 | tf_op jit(solution)/shard_map/ppermute | solution.py:445
  255.7 5.5 collective-permute-start.23
  262.4 23.7 %collective-permute-start.24 = (bf16[288,1664]{1,0:T(8,128)(2,1)}, bf16[288,1664]{1,0:T(8,128)(2,1)}, u32[]{:S(2)}, u32[]{:S(2)}) collective-permute-start(bf16[288,1664]{1,0:T(8,128)(2,1)} %add_convert_fusion.2), channel_id=1, source_target_pairs={{0,16},{4,20},{8,24},{12,28},{16,0},{20,4},{24,8},{28,12},{1,17},{... | collective-permute-start | bytes 2875400 | tf_op jit(solution)/shard_map/ppermute | solution.py:445
  298.5 192.6 %reduce-scatter.9.cloned.1.call-start = ((), (), s32[]{:S(2)}) async-start(), calls=%async_computation.10 | async-start | bytes 3932160 | tf_op jit(solution)/shard_map/reduce_scatter | solution.py:868
  298.5 7.4 %collective-permute-start.26 = (bf16[288,1664]{1,0:T(8,128)(2,1)}, bf16[288,1664]{1,0:T(8,128)(2,1)}, u32[]{:S(2)}, u32[]{:S(2)}) collective-permute-start(bf16[288,1664]{1,0:T(8,128)(2,1)} %get-tuple-element.224), channel_id=1, source_target_pairs={{0,4},{4,0},{8,12},{12,8},{16,20},{20,16},{24,28},{28,24},{1,5},{5... | collective-permute-start | bytes 2875400 | tf_op jit(solution)/shard_map/ppermute | solution.py:445
  305.6 22.9 %collective-permute-start.25 = (bf16[288,1664]{1,0:T(8,128)(2,1)}, bf16[288,1664]{1,0:T(8,128)(2,1)}, u32[]{:S(2)}, u32[]{:S(2)}) collective-permute-start(bf16[288,1664]{1,0:T(8,128)(2,1)} %add_convert_fusion.1), channel_id=1, source_target_pairs={{0,8},{4,12},{8,0},{12,4},{16,24},{20,28},{24,16},{28,20},{1,9},{5... | collective-permute-start | bytes 2875400 | tf_op jit(solution)/shard_map/ppermute | solution.py:445
  305.9 38.2 %collective-permute-start.28 = (bf16[4,768,640]{2,1,0:T(8,128)(2,1)}, bf16[4,768,640]{2,1,0:T(8,128)(2,1)}, u32[]{:S(2)}, u32[]{:S(2)}) collective-permute-start(bf16[4,768,640]{2,1,0:T(8,128)(2,1)} %bitcast.218), channel_id=1, source_target_pairs={{0,4},{4,0},{8,12},{12,8},{16,20},{20,16},{24,28},{28,24},{1,5},{5... | collective-permute-start | bytes 11796488 | tf_op jit(solution)/shard_map/ppermute | solution.py:445
  308.3 24.0 %collective-permute-start.27 = (bf16[288,1664]{1,0:T(8,128)(2,1)}, bf16[288,1664]{1,0:T(8,128)(2,1)}, u32[]{:S(2)}, u32[]{:S(2)}) collective-permute-start(bf16[288,1664]{1,0:T(8,128)(2,1)} %add_convert_fusion), channel_id=1, source_target_pairs={{0,16},{4,20},{8,24},{12,28},{16,0},{20,4},{24,8},{28,12},{1,17},{... | collective-permute-start | bytes 2875400 | tf_op jit(solution)/shard_map/ppermute | solution.py:445
  345.2 38.1 %all-to-all-start.1 = ((bf16[288,4,384]{2,0,1:T(8,128)(2,1)}), bf16[288,4,384]{2,0,1:T(8,128)(2,1)}, u32[]{:S(2)}, u32[]{:S(2)}) async-start(bf16[288,4,384]{2,0,1:T(8,128)(2,1)} %bitcast.225), calls=%async_computation.1 | async-start | bytes 1769472 | tf_op jit(solution)/shard_map/all_to_all | solution.py:892
  349.4 204.1 %reduce-scatter.11.cloned.1.call-start = ((), (), s32[]{:S(2)}) async-start(), calls=%async_computation.11 | async-start | bytes 3932160 | tf_op jit(solution)/shard_map/reduce_scatter | solution.py:898
  349.4 22.2 %collective-permute-start.29 = (bf16[288,1536]{1,0:T(8,128)(2,1)}, bf16[288,1536]{1,0:T(8,128)(2,1)}, u32[]{:S(2)}, u32[]{:S(2)}) collective-permute-start(bf16[288,1536]{1,0:T(8,128)(2,1)} %get-tuple-element.244), channel_id=1, source_target_pairs={{0,4},{4,0},{8,12},{12,8},{16,20},{20,16},{24,28},{28,24},{1,5},{5... | collective-permute-start | bytes 2654216 | tf_op jit(solution)/shard_map/ppermute | solution.py:445
  349.5 22.7 %collective-permute-start.30 = (bf16[288,1536]{1,0:T(8,128)(2,1)}, bf16[288,1536]{1,0:T(8,128)(2,1)}, u32[]{:S(2)}, u32[]{:S(2)}) collective-permute-start(bf16[288,1536]{1,0:T(8,128)(2,1)} %get-tuple-element.245), channel_id=1, source_target_pairs={{0,4},{4,0},{8,12},{12,8},{16,20},{20,16},{24,28},{28,24},{1,5},{5... | collective-permute-start | bytes 2654216 | tf_op jit(solution)/shard_map/ppermute | solution.py:445
  350.0 22.2 %collective-permute-start.31 = (bf16[288,1536]{1,0:T(8,128)(2,1)}, bf16[288,1536]{1,0:T(8,128)(2,1)}, u32[]{:S(2)}, u32[]{:S(2)}) collective-permute-start(bf16[288,1536]{1,0:T(8,128)(2,1)} %get-tuple-element.246), channel_id=1, source_target_pairs={{0,4},{4,0},{8,12},{12,8},{16,20},{20,16},{24,28},{28,24},{1,5},{5... | collective-permute-start | bytes 2654216 | tf_op jit(solution)/shard_map/ppermute | solution.py:445
  350.1 22.1 %collective-permute-start.32 = (bf16[288,1536]{1,0:T(8,128)(2,1)}, bf16[288,1536]{1,0:T(8,128)(2,1)}, u32[]{:S(2)}, u32[]{:S(2)}) collective-permute-start(bf16[288,1536]{1,0:T(8,128)(2,1)} %get-tuple-element.247), channel_id=1, source_target_pairs={{0,4},{4,0},{8,12},{12,8},{16,20},{20,16},{24,28},{28,24},{1,5},{5... | collective-permute-start | bytes 2654216 | tf_op jit(solution)/shard_map/ppermute | solution.py:445
  357.7 25.5 %collective-permute-start.33 = (bf16[4,192,1536]{2,1,0:T(8,128)(2,1)}, bf16[4,192,1536]{2,1,0:T(8,128)(2,1)}, u32[]{:S(2)}, u32[]{:S(2)}) collective-permute-start(bf16[4,192,1536]{2,1,0:T(8,128)(2,1)} %dynamic-slice_bitcast_fusion), channel_id=1, source_target_pairs={{0,4},{4,0},{8,12},{12,8},{16,20},{20,16},{24,28},{28,24},{1,5},{5... | collective-permute-start | bytes 7077896 | tf_op jit(solution)/shard_map/ppermute | solution.py:445
  371.6 3.1 collective-permute-start.34
  384.0 43.7 %collective-permute-start.35 = (bf16[192,17]{0,1:T(8,128)(2,1)S(1)}, bf16[192,17]{0,1:T(8,128)(2,1)S(1)}, u32[]{:S(2)}, u32[]{:S(2)}) collective-permute-start(bf16[192,17]{0,1:T(8,128)(2,1)S(1)} %bitcast.247), channel_id=1, source_target_pairs={{0,16},{4,20},{8,24},{12,28},{16,0},{20,4},{24,8},{28,12},{1,17},{... | collective-permute-start | bytes 19592 | tf_op jit(solution)/shard_map/ppermute | solution.py:445
  389.8 37.9 %collective-permute-start.36 = (bf16[192,1536]{1,0:T(8,128)(2,1)S(1)}, bf16[192,1536]{1,0:T(8,128)(2,1)S(1)}, u32[]{:S(2)}, u32[]{:S(2)}) collective-permute-start(bf16[192,1536]{1,0:T(8,128)(2,1)S(1)} %get-tuple-element.379), channel_id=1, source_target_pairs={{0,16},{4,20},{8,24},{12,28},{16,0},{20,4},{24,8},{28,12},{1,17},{... | collective-permute-start | bytes 1769480 | tf_op jit(solution)/shard_map/ppermute | solution.py:445
  390.3 37.4 %collective-permute-start.37 = (bf16[288,1536]{1,0:T(8,128)(2,1)S(1)}, bf16[288,1536]{1,0:T(8,128)(2,1)S(1)}, u32[]{:S(2)}, u32[]{:S(2)}) collective-permute-start(bf16[288,1536]{1,0:T(8,128)(2,1)S(1)} %copy-done.27), channel_id=1, source_target_pairs={{0,16},{4,20},{8,24},{12,28},{16,0},{20,4},{24,8},{28,12},{1,17},{... | collective-permute-start | bytes 2654216 | tf_op jit(solution)/shard_map/ppermute | solution.py:445
  429.2 1.6 collective-permute-start.38
  431.9 4.9 collective-permute-start.39
  432.4 9.5 %collective-permute-start.41 = (bf16[128,256]{1,0:T(8,128)(2,1)S(1)}, bf16[128,256]{1,0:T(8,128)(2,1)S(1)}, u32[]{:S(2)}, u32[]{:S(2)}) collective-permute-start(bf16[128,256]{1,0:T(8,128)(2,1)S(1)} %get-tuple-element.399), channel_id=1, source_target_pairs={{0,16},{4,20},{8,24},{12,28},{16,0},{20,4},{24,8},{28,12},{1,17},{... | collective-permute-start | bytes 196616 | tf_op jit(solution)/shard_map/ppermute | solution.py:445
  436.8 5.1 collective-permute-start.40
  455.8 11.6 %collective-permute-start.42 = (bf16[4,192,640]{2,1,0:T(8,128)(2,1)}, bf16[4,192,640]{2,1,0:T(8,128)(2,1)S(1)}, u32[]{:S(2)}, u32[]{:S(2)}) collective-permute-start(bf16[4,192,640]{2,1,0:T(8,128)(2,1)} %dynamic-slice_bitcast_fusion.1), channel_id=1, source_target_pairs={{0,4},{4,0},{8,12},{12,8},{16,20},{20,16},{24,28},{28,24},{1,5},{5... | collective-permute-start | bytes 2949128 | tf_op jit(solution)/shard_map/ppermute | solution.py:445
  456.4 6.2 %collective-permute-start.51 = (bf16[192,17]{0,1:T(8,128)(2,1)S(1)}, bf16[192,17]{0,1:T(8,128)(2,1)S(1)}, u32[]{:S(2)}, u32[]{:S(2)}) collective-permute-start(bf16[192,17]{0,1:T(8,128)(2,1)S(1)} %bitcast.248), channel_id=1, source_target_pairs={{0,16},{4,20},{8,24},{12,28},{16,0},{20,4},{24,8},{28,12},{1,17},{... | collective-permute-start | bytes 19592 | tf_op jit(solution)/shard_map/ppermute | solution.py:445
  456.8 5.9 %collective-permute-start.50 = (bf16[192,17]{0,1:T(8,128)(2,1)S(1)}, bf16[192,17]{0,1:T(8,128)(2,1)S(1)}, u32[]{:S(2)}, u32[]{:S(2)}) collective-permute-start(bf16[192,17]{0,1:T(8,128)(2,1)S(1)} %fusion.73), channel_id=1, source_target_pairs={{0,8},{4,12},{8,0},{12,4},{16,24},{20,28},{24,16},{28,20},{1,9},{5... | collective-permute-start | bytes 19592 | tf_op jit(solution)/shard_map/ppermute | solution.py:445
  457.4 16.5 %collective-permute-start.49 = (bf16[192,1536]{1,0:T(8,128)(2,1)}, bf16[192,1536]{1,0:T(8,128)(2,1)}, u32[]{:S(2)}, u32[]{:S(2)}) collective-permute-start(bf16[192,1536]{1,0:T(8,128)(2,1)} %get-tuple-element.292), channel_id=1, source_target_pairs={{0,16},{4,20},{8,24},{12,28},{16,0},{20,4},{24,8},{28,12},{1,17},{... | collective-permute-start | bytes 1769480 | tf_op jit(solution)/shard_map/ppermute | solution.py:445
  461.4 15.2 %collective-permute-start.48 = (bf16[192,1536]{1,0:T(8,128)(2,1)}, bf16[192,1536]{1,0:T(8,128)(2,1)}, u32[]{:S(2)}, u32[]{:S(2)}) collective-permute-start(bf16[192,1536]{1,0:T(8,128)(2,1)} %add_convert_fusion.12), channel_id=1, source_target_pairs={{0,8},{4,12},{8,0},{12,4},{16,24},{20,28},{24,16},{28,20},{1,9},{5... | collective-permute-start | bytes 1769480 | tf_op jit(solution)/shard_map/ppermute | solution.py:445
  462.8 66.5 %all-to-all-start.2 = ((bf16[4,288,640]{2,1,0:T(8,128)(2,1)}), bf16[4,288,640]{2,1,0:T(8,128)(2,1)}, u32[]{:S(2)}, u32[]{:S(2)}) async-start(bf16[4,288,640]{2,1,0:T(8,128)(2,1)} %bitcast.49), calls=%async_computation.2 | async-start | bytes 2949120 | tf_op jit(solution)/shard_map/all_to_all | solution.py:958
  467.1 91.0 %reduce-scatter.13.cloned.1.call-start = ((), (), s32[]{:S(2)}) async-start(), calls=%async_computation.13 | async-start | bytes 983040
  468.9 10.3 %collective-permute-start.43 = (bf16[192,640]{1,0:T(8,128)(2,1)S(1)}, bf16[192,640]{1,0:T(8,128)(2,1)S(1)}, u32[]{:S(2)}, u32[]{:S(2)}) collective-permute-start(bf16[192,640]{1,0:T(8,128)(2,1)S(1)} %get-tuple-element.388), channel_id=1, source_target_pairs={{0,16},{4,20},{8,24},{12,28},{16,0},{20,4},{24,8},{28,12},{1,17},{... | collective-permute-start | bytes 737288 | tf_op jit(solution)/shard_map/ppermute | solution.py:445
  478.9 11.2 %collective-permute-start.45 = (bf16[192,640]{1,0:T(8,128)(2,1)S(1)}, bf16[192,640]{1,0:T(8,128)(2,1)S(1)}, u32[]{:S(2)}, u32[]{:S(2)}) collective-permute-start(bf16[192,640]{1,0:T(8,128)(2,1)S(1)} %get-tuple-element.389), channel_id=1, source_target_pairs={{0,16},{4,20},{8,24},{12,28},{16,0},{20,4},{24,8},{28,12},{1,17},{... | collective-permute-start | bytes 737288 | tf_op jit(solution)/shard_map/ppermute | solution.py:445
  479.3 10.9 %collective-permute-start.44 = (bf16[192,640]{1,0:T(8,128)(2,1)S(1)}, bf16[192,640]{1,0:T(8,128)(2,1)S(1)}, u32[]{:S(2)}, u32[]{:S(2)}) collective-permute-start(bf16[192,640]{1,0:T(8,128)(2,1)S(1)} %fusion.46), channel_id=1, source_target_pairs={{0,8},{4,12},{8,0},{12,4},{16,24},{20,28},{24,16},{28,20},{1,9},{5... | collective-permute-start | bytes 737288 | tf_op jit(solution)/shard_map/ppermute | solution.py:445
  483.0 58.7 %collective-permute-start.46 = (bf16[288,1536]{1,0:T(8,128)(2,1)}, bf16[288,1536]{1,0:T(8,128)(2,1)}, u32[]{:S(2)}, u32[]{:S(2)}) collective-permute-start(bf16[288,1536]{1,0:T(8,128)(2,1)} %add_convert_fusion.7), channel_id=1, source_target_pairs={{0,8},{4,12},{8,0},{12,4},{16,24},{20,28},{24,16},{28,20},{1,9},{5... | collective-permute-start | bytes 2654216 | tf_op jit(solution)/shard_map/ppermute | solution.py:445
  486.1 55.7 %collective-permute-start.47 = (bf16[288,1536]{1,0:T(8,128)(2,1)}, bf16[288,1536]{1,0:T(8,128)(2,1)}, u32[]{:S(2)}, u32[]{:S(2)}) collective-permute-start(bf16[288,1536]{1,0:T(8,128)(2,1)} %add_convert_fusion.6), channel_id=1, source_target_pairs={{0,16},{4,20},{8,24},{12,28},{16,0},{20,4},{24,8},{28,12},{1,17},{... | collective-permute-start | bytes 2654216 | tf_op jit(solution)/shard_map/ppermute | solution.py:445
  (46 other events, 313.0 us)
Sparse Core Ops, SparseCore 0:
  9.6 79.8 all-gather.6
  112.3 44.8 all-gather.8
  204.6 73.8 all-gather.10
  298.6 57.3 reduce-scatter.6
  358.2 65.9 reduce-scatter.8
  439.2 82.7 reduce-scatter.10
  524.3 28.4 reduce-scatter.12
